TPU v7x, 32 devices: a whole 2x2x4 slice. The times are simulated.
32 devices in a mesh: batch: 16 (over z, y, core), tensor: 2 (over x).
Axes of the slice: x: 2, y: 2, z: 4, core: 2. Of those that a mesh axis runs over, the one named last changes fastest.
Arguments:
- block_in: bfloat16 [2, 16384, 1024], P(None, ('batch', 'tensor')), may hold values from -6 to 6
- lengths: int32 [2, 16, 4], P(None, 'batch'), may hold values from 1 to 512, 1024 in all within a row
- norm_gains: float32 [3, 1024], replicated, may hold values from 0.5 to 1.5
- qkv_weight: bfloat16 [3, 1024, 1024], P(None, 'batch', 'tensor'), may hold values from -0.1875 to 0.1875
- head_scale: float32 [16], P('tensor'), may hold values from 0.5 to 2
- out_weight: bfloat16 [1024, 1024], P('tensor', 'batch'), may hold values from -0.1875 to 0.1875
- up_weight: bfloat16 [1024, 4096], P('batch', 'tensor'), may hold values from -0.7875 to 0.7875
- mid_gain: float32 [4096], P('tensor'), may hold values from 0.5 to 1.5
- down_weight: bfloat16 [4096, 1024], P('tensor', 'batch'), may hold values from -0.39375 to 0.39375
- cotangent: bfloat16 [2, 16384, 1024], P(None, ('batch', 'tensor')), may hold values from -6 to 6
Outputs:
- block_out: bfloat16 [2, 16384, 1024], P(None, ('batch', 'tensor'))
- grad_in: bfloat16 [2, 16384, 1024], P(None, ('batch', 'tensor'))
- grad_gains: float32 [3, 1024], replicated
- grad_qkv: float32 [3, 1024, 1024], P(None, 'batch', 'tensor')
- grad_scale: float32 [16], P('tensor')
- grad_proj: float32 [1024, 1024], P('tensor', 'batch')
- grad_up: float32 [1024, 4096], P('batch', 'tensor')
- grad_mid: float32 [4096], P('tensor')
- grad_down: float32 [4096, 1024], P('tensor', 'batch')
Inputs may be any that keep to these rules, and one draw needn't show every extreme that they name: lengths[m, b] holds the lengths of the 4 sequences packed in order into the 1024 rows of group b in micro-batch m; they sum to 1024.
All inputs are finite; a program needn't handle non-finite values.
Results may differ from a plain program's by a relative error of at most 0.019.
Values may be sent and summed in bfloat16 or wider, within the bound.
No kernel may reach another device: no remote copies, remote signals or barrier semaphores. Data moves between devices by JAX's collectives and lax.ppermute only.
A program may use at most 256 MiB of HBM per device.

v0:
```python
import jax
import jax.numpy as jnp
from jax import lax
from jax.sharding import PartitionSpec as P

eps = 1e-05


def normalize(values):
    centred = values - jnp.mean(values, axis=-1, keepdims=True)
    factor = lax.rsqrt(jnp.mean(centred * centred, axis=-1, keepdims=True) + eps)
    return (centred * factor, factor)


def norm_back(unit, factor, grad):
    return factor * (
        grad
        - jnp.mean(grad, axis=-1, keepdims=True)
        - unit * jnp.mean(grad * unit, axis=-1, keepdims=True)
    )


def segment_ids(seq_lengths, group_rows):
    places = jnp.arange(group_rows, dtype=jnp.int32)
    ends = jnp.cumsum(seq_lengths)
    seg_ids = jnp.sum((places[:, None] >= ends[None, :]).astype(jnp.int32), axis=1)
    return (seg_ids, places)


def visible_block(seg_ids, places, first_row, block_rows):
    seg_block = lax.dynamic_slice_in_dim(seg_ids, first_row, block_rows, 0)
    place_block = lax.dynamic_slice_in_dim(places, first_row, block_rows, 0)
    return (seg_block[:, None] == seg_ids[None, :]) & (place_block[:, None] >= places[None, :])


def attend_forward(queries, all_keys, values, seg_ids, places, block_rows, factor):
    group_rows = queries.shape[0]

    def one_block(first_row):
        query_block = lax.dynamic_slice_in_dim(queries, first_row, block_rows, 0)
        visible = visible_block(seg_ids, places, first_row, block_rows)
        scores = (
            jnp.einsum("qhd,khd->hqk", query_block, all_keys, preferred_element_type=jnp.float32)
            * factor
        )
        scores = jnp.where(visible[None], scores, -1e30)
        row_max = jnp.max(scores, axis=-1, keepdims=True)
        shifted = jnp.exp(scores - row_max)
        row_sum = jnp.sum(shifted, axis=-1, keepdims=True)
        weights_low = (shifted / row_sum).astype(jnp.bfloat16)
        attended = jnp.einsum(
            "hqk,khd->qhd", weights_low, values, preferred_element_type=jnp.float32
        )
        return (attended, (row_max + jnp.log(row_sum))[..., 0])

    firsts = jnp.arange(group_rows // block_rows, dtype=jnp.int32) * block_rows
    attended, log_sums = lax.map(one_block, firsts)
    return (attended.reshape(queries.shape), log_sums)


def attend_backward(
    queries, all_keys, values, seg_ids, places, block_rows, factor, log_sums, out_grad
):
    group_rows = queries.shape[0]

    def one_block(totals, pieces):
        key_grad, value_grad = totals
        first_row, log_block = pieces
        query_block = lax.dynamic_slice_in_dim(queries, first_row, block_rows, 0)
        grad_block = lax.dynamic_slice_in_dim(out_grad, first_row, block_rows, 0)
        visible = visible_block(seg_ids, places, first_row, block_rows)
        scores = (
            jnp.einsum("qhd,khd->hqk", query_block, all_keys, preferred_element_type=jnp.float32)
            * factor
        )
        scores = jnp.where(visible[None], scores, -1e30)
        probs = jnp.exp(scores - log_block[..., None])
        value_grad = value_grad + jnp.einsum(
            "hqk,qhd->khd",
            probs.astype(jnp.bfloat16),
            grad_block,
            preferred_element_type=jnp.float32,
        )
        prob_grad = jnp.einsum(
            "qhd,khd->hqk", grad_block, values, preferred_element_type=jnp.float32
        )
        inner = jnp.sum(probs * prob_grad, axis=-1, keepdims=True)
        score_grad = (probs * (prob_grad - inner)).astype(jnp.bfloat16)
        query_grad = (
            jnp.einsum("hqk,khd->qhd", score_grad, all_keys, preferred_element_type=jnp.float32)
            * factor
        )
        key_grad = (
            key_grad
            + jnp.einsum(
                "hqk,qhd->khd", score_grad, query_block, preferred_element_type=jnp.float32
            )
            * factor
        )
        return ((key_grad, value_grad), query_grad)

    zero_grad = jnp.zeros(queries.shape, jnp.float32)
    firsts = jnp.arange(group_rows // block_rows, dtype=jnp.int32) * block_rows
    (key_grad, value_grad), query_grad = lax.scan(
        one_block, (zero_grad, zero_grad), (firsts, log_sums)
    )
    return (query_grad.reshape(queries.shape), key_grad, value_grad)


def body(
    block_in,
    lengths,
    norm_gains,
    qkv_weight,
    head_scale,
    out_weight,
    up_weight,
    mid_gain,
    down_weight,
    cotangent,
):
    tensor_count = lax.axis_size("tensor")
    tensor_rank = lax.axis_index("tensor")
    qkv_full, out_full, up_full, down_full = (
        lax.all_gather(qkv_weight, "batch", axis=1, tiled=True),
        lax.all_gather(out_weight, "batch", axis=1, tiled=True),
        lax.all_gather(up_weight, "batch", axis=0, tiled=True),
        lax.all_gather(down_weight, "batch", axis=1, tiled=True),
    )
    micro_count, own_rows, model_width = block_in.shape
    group_rows = own_rows * tensor_count
    local_heads = head_scale.shape[0]
    head_size = qkv_full.shape[2] // local_heads
    local_hidden = mid_gain.shape[0]
    hidden_total = local_hidden * tensor_count
    block_rows = min(512, group_rows)
    factor = head_size ** (-0.5)
    heads_shape = (group_rows, local_heads, head_size)
    row_start = tensor_rank * own_rows
    qkv_acc = jnp.zeros(qkv_full.shape, jnp.float32)
    proj_acc = jnp.zeros(out_full.shape, jnp.float32)
    up_acc = jnp.zeros(up_full.shape, jnp.float32)
    down_acc = jnp.zeros(down_full.shape, jnp.float32)
    first_gain = jnp.zeros((model_width,), jnp.float32)
    second_gain = jnp.zeros((model_width,), jnp.float32)
    third_gain = jnp.zeros((model_width,), jnp.float32)
    mid_acc = jnp.zeros((local_hidden,), jnp.float32)
    scale_acc = jnp.zeros((local_heads,), jnp.float32)
    outputs = []
    input_grads = []
    for micro_step in range(micro_count):
        seg_ids, places = segment_ids(lengths[micro_step, 0], group_rows)
        x_rows = block_in[micro_step].astype(jnp.float32)
        input_unit, input_factor = normalize(x_rows)
        first_own = (input_unit * norm_gains[0]).astype(jnp.bfloat16)
        first_all = lax.all_gather(first_own, "tensor", axis=0, tiled=True)
        projected = jnp.einsum(
            "gd,cde->cge", first_all, qkv_full, preferred_element_type=jnp.float32
        ).astype(jnp.bfloat16)
        queries = projected[0].reshape(heads_shape)
        all_keys = projected[1].reshape(heads_shape)
        values = projected[2].reshape(heads_shape)
        attended, log_sums = attend_forward(
            queries, all_keys, values, seg_ids, places, block_rows, factor
        )
        scaled = (attended * head_scale[None, :, None]).astype(jnp.bfloat16).reshape(group_rows, -1)
        whole_mixed = lax.psum(
            jnp.dot(scaled, out_full, preferred_element_type=jnp.float32), "tensor"
        )
        mixed_own = lax.dynamic_slice_in_dim(whole_mixed, row_start, own_rows, 0)
        mixed_unit, mixed_factor = normalize(mixed_own)
        resid = x_rows + mixed_unit * norm_gains[1]
        resid_unit, resid_factor = normalize(resid)
        third_own = (resid_unit * norm_gains[2]).astype(jnp.bfloat16)
        third_all = lax.all_gather(third_own, "tensor", axis=0, tiled=True)
        hidden = jnp.dot(third_all, up_full, preferred_element_type=jnp.float32)
        activated = jax.nn.gelu(hidden)
        act_sum, act_squares = lax.psum(
            (jnp.sum(activated, axis=1), jnp.sum(activated * activated, axis=1)), "tensor"
        )
        act_mean = act_sum / hidden_total
        act_factor = lax.rsqrt(act_squares / hidden_total - act_mean * act_mean + eps)[:, None]
        act_unit = (activated - act_mean[:, None]) * act_factor
        narrow = (act_unit * mid_gain).astype(jnp.bfloat16)
        feed_own = lax.psum_scatter(
            jnp.dot(narrow, down_full, preferred_element_type=jnp.float32).astype(jnp.bfloat16),
            "tensor",
            scatter_dimension=0,
            tiled=True,
        ).astype(jnp.float32)
        outputs.append((resid + feed_own).astype(jnp.bfloat16))
        out_rows = cotangent[micro_step].astype(jnp.float32)
        feed_grad = lax.all_gather(out_rows.astype(jnp.bfloat16), "tensor", axis=0, tiled=True)
        down_acc = down_acc + jnp.einsum(
            "gf,gd->fd", narrow, feed_grad, preferred_element_type=jnp.float32
        )
        narrow_grad = jnp.einsum(
            "gd,fd->gf", feed_grad, down_full, preferred_element_type=jnp.float32
        )
        mid_acc = mid_acc + jnp.sum(narrow_grad * act_unit, axis=0)
        gained = narrow_grad * mid_gain
        back_sum, back_inner = lax.psum(
            (jnp.sum(gained, axis=1), jnp.sum(gained * act_unit, axis=1)), "tensor"
        )
        act_grad = act_factor * (
            gained
            - back_sum[:, None] / hidden_total
            - act_unit * back_inner[:, None] / hidden_total
        )
        gelu_pull = jax.vjp(jax.nn.gelu, hidden)[1]
        hidden_grad = gelu_pull(act_grad)[0].astype(jnp.bfloat16)
        up_acc = up_acc + jnp.einsum(
            "gd,gf->df", third_all, hidden_grad, preferred_element_type=jnp.float32
        )
        third_grad = lax.psum_scatter(
            jnp.einsum("gf,df->gd", hidden_grad, up_full, preferred_element_type=jnp.float32),
            "tensor",
            scatter_dimension=0,
            tiled=True,
        )
        third_gain = third_gain + jnp.sum(third_grad * resid_unit, axis=0)
        resid_grad = out_rows + norm_back(resid_unit, resid_factor, third_grad * norm_gains[2])
        second_gain = second_gain + jnp.sum(resid_grad * mixed_unit, axis=0)
        mixed_grad = norm_back(mixed_unit, mixed_factor, resid_grad * norm_gains[1]).astype(
            jnp.bfloat16
        )
        mixed_all = lax.all_gather(mixed_grad, "tensor", axis=0, tiled=True)
        proj_acc = proj_acc + jnp.einsum(
            "ge,gd->ed", scaled, mixed_all, preferred_element_type=jnp.float32
        )
        scaled_grad = jnp.einsum(
            "gd,ed->ge", mixed_all, out_full, preferred_element_type=jnp.float32
        ).reshape(heads_shape)
        scale_acc = scale_acc + jnp.sum(scaled_grad * attended, axis=(0, 2))
        attended_grad = (scaled_grad * head_scale[None, :, None]).astype(jnp.bfloat16)
        query_grad, key_grad, value_grad = attend_backward(
            queries, all_keys, values, seg_ids, places, block_rows, factor, log_sums, attended_grad
        )
        proj_grads = jnp.stack(
            [
                query_grad.reshape(group_rows, -1),
                key_grad.reshape(group_rows, -1),
                value_grad.reshape(group_rows, -1),
            ]
        ).astype(jnp.bfloat16)
        qkv_acc = qkv_acc + jnp.einsum(
            "gd,cge->cde", first_all, proj_grads, preferred_element_type=jnp.float32
        )
        first_grad = lax.psum_scatter(
            jnp.einsum(
                "cge,cde->gd", proj_grads, qkv_full, preferred_element_type=jnp.float32
            ).astype(jnp.bfloat16),
            "tensor",
            scatter_dimension=0,
            tiled=True,
        ).astype(jnp.float32)
        first_gain = first_gain + jnp.sum(first_grad * input_unit, axis=0)
        input_grads.append(
            (resid_grad + norm_back(input_unit, input_factor, first_grad * norm_gains[0])).astype(
                jnp.bfloat16
            )
        )
    qkv_grad, proj_grad, up_grad, down_grad = (
        lax.psum_scatter(
            qkv_acc.astype(jnp.bfloat16), "batch", scatter_dimension=1, tiled=True
        ).astype(jnp.float32),
        lax.psum_scatter(
            proj_acc.astype(jnp.bfloat16), "batch", scatter_dimension=1, tiled=True
        ).astype(jnp.float32),
        lax.psum_scatter(
            up_acc.astype(jnp.bfloat16), "batch", scatter_dimension=0, tiled=True
        ).astype(jnp.float32),
        lax.psum_scatter(
            down_acc.astype(jnp.bfloat16), "batch", scatter_dimension=1, tiled=True
        ).astype(jnp.float32),
    )
    mid_full = lax.dynamic_update_slice_in_dim(
        jnp.zeros((hidden_total,), jnp.float32), mid_acc, tensor_rank * local_hidden, 0
    )
    scale_full = lax.dynamic_update_slice_in_dim(
        jnp.zeros((local_heads * tensor_count,), jnp.float32),
        scale_acc,
        tensor_rank * local_heads,
        0,
    )
    gains_sum, mid_sum, scale_sum = lax.psum(
        (jnp.stack([first_gain, second_gain, third_gain]), mid_full, scale_full),
        ("batch", "tensor"),
    )
    mid_own = lax.dynamic_slice_in_dim(mid_sum, tensor_rank * local_hidden, local_hidden, 0)
    scale_own = lax.dynamic_slice_in_dim(scale_sum, tensor_rank * local_heads, local_heads, 0)
    return (
        jnp.stack(outputs),
        jnp.stack(input_grads),
        gains_sum,
        qkv_grad,
        scale_own,
        proj_grad,
        up_grad,
        mid_own,
        down_grad,
    )


def solution(mesh):
    in_specs = (
        P(None, ("batch", "tensor"), None),
        P(None, "batch", None),
        P(),
        P(None, "batch", "tensor"),
        P("tensor"),
        P("tensor", "batch"),
        P("batch", "tensor"),
        P("tensor"),
        P("tensor", "batch"),
        P(None, ("batch", "tensor"), None),
    )
    out_specs = (
        P(None, ("batch", "tensor"), None),
        P(None, ("batch", "tensor"), None),
        P(),
        P(None, "batch", "tensor"),
        P("tensor"),
        P("tensor", "batch"),
        P("batch", "tensor"),
        P("tensor"),
        P("tensor", "batch"),
    )
    return jax.shard_map(body, mesh=mesh, in_specs=in_specs, out_specs=out_specs, check_vma=False)
```

profile of v0, /device:TPU:0, one launch (start us, length us, event | category | flops | bytes accessed | tf_op | source)
XLA Modules:
  0.0 1623.8 jit_solution(3066448921522963415)
XLA Ops:
  16.8 32.0 %all-gather.15.cloned.1.call-done = bf16[1024,1024]{1,0:T(8,128)(2,1)} async-done(((bf16[512,1024]{1,0:T(8,128)(2,1)}), bf16[1024,1024]{1,0:T(8,128)(2,1)}) %all-gather.15.cloned.1.call-update) | async-done | bytes 2097168 | tf_op jit(solution)/shard_map/all_gather | solution.py:156
  48.8 47.4 %all-gather.17.cloned.1.call-done = bf16[3,1024,512]{2,1,0:T(8,128)(2,1)} async-done(((bf16[3,64,512]{2,1,0:T(8,128)(2,1)}), bf16[3,1024,512]{2,1,0:T(8,128)(2,1)}) %all-gather.17.cloned.1.call-update) | async-done | bytes 3145744 | tf_op jit(solution)/shard_map/all_gather | solution.py:125
  105.5 75.3 %while.58 = (s32[]{:T(128)}, f32[2,512,8,64]{1,0,3,2:T(2,128)}, f32[2,8,512]{2,1,0:T(8,128)S(1)}, s32[2]{0:T(128)S(1)}, s32[1024]{0:T(1024)S(1)}, /*index=5*/s32...) while((s32[]{:T(128)}, f32[2,512,8,64]{1,0,3,2:T(2,128)}, ...), condition=%wide.region_7.8_spmd.clone, body=%wide.region_4.7_spmd.clone.sunk | while | flops 1125642240 | bytes 60444856 | solution.py:57
  123.5 19.6 %dynamic_update_slice.49 = f32[2,512,8,64]{1,0,3,2:T(2,128)} dynamic-update-slice(f32[2,512,8,64]{1,0,3,2:T(2,128)} %get-tuple-element.984, f32[1,512,8,64]{1,0,3,2:T(1,128)S(1)} %copy.129, s32[]{:T(128)} %get-tuple-element.983, s32[]{:T(128)} %constant.141.clone.1..sunk, s32[]{:T(128)} %constant.141.clone.1..sunk, s32[]{:T(128)} %constant.141.clone.1..sunk) | dynamic-update-slice | bytes 2097156 | tf_op jit(solution)/shard_map/while/body/jit(dynamic_update_index_in_dim)/dynamic_update_slice | solution.py:57
  160.8 19.6 %dynamic_update_slice.49 = f32[2,512,8,64]{1,0,3,2:T(2,128)} dynamic-update-slice(f32[2,512,8,64]{1,0,3,2:T(2,128)} %get-tuple-element.984, f32[1,512,8,64]{1,0,3,2:T(1,128)S(1)} %copy.129, s32[]{:T(128)} %get-tuple-element.983, s32[]{:T(128)} %constant.141.clone.1..sunk, s32[]{:T(128)} %constant.141.clone.1..sunk, s32[]{:T(128)} %constant.141.clone.1..sunk) | dynamic-update-slice | bytes 2097156 | tf_op jit(solution)/shard_map/while/body/jit(dynamic_update_index_in_dim)/dynamic_update_slice | solution.py:57
  191.5 74.9 %while.59 = (s32[]{:T(128)}, f32[2,512,8,64]{1,0,3,2:T(2,128)}, f32[2,8,512]{2,1,0:T(8,128)S(1)}, s32[2]{0:T(128)S(1)}, s32[1024]{0:T(1024)S(1)}, /*index=5*/s32...) while((s32[]{:T(128)}, f32[2,512,8,64]{1,0,3,2:T(2,128)}, ...), condition=%wide.region_25.26_spmd.clone, body=%wide.region_22.25_spmd.clone.sunk | while | flops 1125642240 | bytes 60444856 | solution.py:57
  209.3 19.6 %dynamic_update_slice.51 = f32[2,512,8,64]{1,0,3,2:T(2,128)} dynamic-update-slice(f32[2,512,8,64]{1,0,3,2:T(2,128)} %get-tuple-element.948, f32[1,512,8,64]{1,0,3,2:T(1,128)S(1)} %copy.130, s32[]{:T(128)} %get-tuple-element.947, s32[]{:T(128)} %constant.141.clone.1..sunk.1, s32[]{:T(128)} %constant.141.clone.1..sunk.1, s32[]{:T(128)} %constant.141.clone.1..sunk.1) | dynamic-update-slice | bytes 2097156 | tf_op jit(solution)/shard_map/while/body/jit(dynamic_update_index_in_dim)/dynamic_update_slice | solution.py:57
  246.6 19.6 %dynamic_update_slice.51 = f32[2,512,8,64]{1,0,3,2:T(2,128)} dynamic-update-slice(f32[2,512,8,64]{1,0,3,2:T(2,128)} %get-tuple-element.948, f32[1,512,8,64]{1,0,3,2:T(1,128)S(1)} %copy.130, s32[]{:T(128)} %get-tuple-element.947, s32[]{:T(128)} %constant.141.clone.1..sunk.1, s32[]{:T(128)} %constant.141.clone.1..sunk.1, s32[]{:T(128)} %constant.141.clone.1..sunk.1) | dynamic-update-slice | bytes 2097156 | tf_op jit(solution)/shard_map/while/body/jit(dynamic_update_index_in_dim)/dynamic_update_slice | solution.py:57
  286.0 192.8 %all-reduce.10.cloned.1.call-done = (f32[1024,1024]{1,0:T(8,128)}, f32[1024,1024]{1,0:T(8,128)}) async-done(((f32[1024,1024]{1,0:T(8,128)}, f32[1024,1024]{1,0:T(8,128)}), (f32[1024,1024]{1,0:T(8,128)}, f32[1024,1024]{1,0:T(8,128)})) %all-reduce.10.cloned.1.call-update) | async-done | bytes 8388624 | tf_op jit(solution)/shard_map/psum | solution.py:167
  491.7 22.0 %all-gather.37.cloned.1.call-done = bf16[1,1024,1024]{2,1,0:T(8,128)(2,1)} async-done(((bf16[1,512,1024]{2,1,0:T(8,128)(2,1)}), bf16[1,1024,1024]{2,1,0:T(8,128)(2,1)}) %all-gather.37.cloned.1.call-update) | async-done | bytes 2097168 | tf_op jit(solution)/shard_map/all_gather | solution.py:193
  513.7 52.8 %all-gather.25.cloned.1.call-done = bf16[2048,1024]{0,1:T(8,128)(2,1)} async-done(((bf16[2048,64]{0,1:T(8,128)(2,1)}), bf16[2048,1024]{0,1:T(8,128)(2,1)}) %all-gather.25.cloned.1.call-update) | async-done | bytes 4194320 | tf_op jit(solution)/shard_map/all_gather | solution.py:128
  566.5 10.5 fusion.98
  577.0 40.7 %all-gather.23.cloned.1.call-done = bf16[1024,2048]{1,0:T(8,128)(2,1)} async-done(((bf16[64,2048]{1,0:T(8,128)(2,1)}), bf16[1024,2048]{1,0:T(8,128)(2,1)}) %all-gather.23.cloned.1.call-update) | async-done | bytes 4194320 | tf_op jit(solution)/shard_map/all_gather | solution.py:127
  617.7 33.8 %all-gather.21.cloned.1.call-done = bf16[1024,1024]{1,0:T(8,128)(2,1)} async-done(((bf16[512,1024]{1,0:T(8,128)(2,1)}), bf16[1024,1024]{1,0:T(8,128)(2,1)}) %all-gather.21.cloned.1.call-update) | async-done | bytes 2097168 | tf_op jit(solution)/shard_map/all_gather | solution.py:175
  651.5 10.2 fusion.120
  661.7 24.3 %all-gather.29.cloned.1.call-done = bf16[1024,1024]{1,0:T(8,128)(2,1)} async-done(((bf16[512,1024]{1,0:T(8,128)(2,1)}), bf16[1024,1024]{1,0:T(8,128)(2,1)}) %all-gather.29.cloned.1.call-update) | async-done | bytes 2097168 | tf_op jit(solution)/shard_map/all_gather | solution.py:175
  686.0 10.0 fusion.121
  703.3 17.8 %all-gather.35.cloned.1.call-done = bf16[1,1024,1024]{2,1,0:T(8,128)(2,1)} async-done(((bf16[1,512,1024]{2,1,0:T(8,128)(2,1)}), bf16[1,1024,1024]{2,1,0:T(8,128)(2,1)}) %all-gather.35.cloned.1.call-update) | async-done | bytes 2097168 | tf_op jit(solution)/shard_map/all_gather | solution.py:193
  721.1 20.2 %multiply_reduce_fusion.3 = (f32[2048]{0:T(1024)}, f32[1024]{0:T(1024)S(1)}, f32[1024]{0:T(1024)S(1)}, f32[1024]{0:T(1024)S(1)}, f32[1024]{0:T(1024)S(1)}, /*index=5*/f32[2048]{0:T(1024)}, f32[1024,2048]{1,0:T(8,128)}) fusion(f32[1024]{0:T(1024)S(1)} %get-tuple-element.645, f32[1024]{0:T(1024)S(1)} %get-tuple-element.644, ...), kind=kOutput, calls=%fused_computation.90 | convolution fusion | flops 4362067968 | bytes 39903232 | tf_op jit(solution)/shard_map/gd,fd->gf/dot_general | solution.py:197
  748.2 22.7 %fusion.54 = (bf16[1024,2048]{1,0:T(8,128)(2,1)S(1)}, bf16[1024,2048]{1,0:T(8,128)(2,1)}, bf16[1024,2048]{1,0:T(8,128)(2,1)}) fusion(f32[1024,2048]{1,0:T(8,128)} %get-tuple-element.655, f32[1024,2048]{1,0:T(8,128)} %get-tuple-element.656, f32[1024]{0:T(1024)S(1)} %get-tuple-element.592, f32[1024]{0:T(1024)S(1)} %broadcast_multiply_fusion.1, ...), kind=kLoop, calls=%fused_computation.80 | loop fusion | flops 125829120 | bytes 46178304 | tf_op jit(solution)/shard_map/convert_element_type | solution.py:211
  779.0 9.3 convolution_convert_fusion.1
  788.4 9.9 fusion.131
  798.4 11.1 convolution_convert_fusion
  809.6 25.0 %reduce-scatter.14.cloned.1.call-done = f32[512,1024]{1,0:T(8,128)} async-done(((f32[1024,1024]{1,0:T(8,128)}), f32[512,1024]{1,0:T(8,128)}) %reduce-scatter.14.cloned.1.call-update) | async-done | bytes 2097168 | tf_op jit(solution)/shard_map/reduce_scatter | solution.py:215
  837.6 31.8 %reduce-scatter.10.cloned.1.call-done = bf16[512,1024]{1,0:T(8,128)(2,1)} async-done(((bf16[1024,1024]{1,0:T(8,128)(2,1)}), bf16[512,1024]{1,0:T(8,128)(2,1)}) %reduce-scatter.10.cloned.1.call-update) | async-done | bytes 1048592 | tf_op jit(solution)/shard_map/reduce_scatter | solution.py:185
  869.3 56.5 %reduce-scatter.18.cloned.1.call-done = f32[512,1024]{1,0:T(8,128)} async-done(((f32[1024,1024]{1,0:T(8,128)}), f32[512,1024]{1,0:T(8,128)}) %reduce-scatter.18.cloned.1.call-update) | async-done | bytes 2097168 | tf_op jit(solution)/shard_map/reduce_scatter | solution.py:215
  933.1 26.8 %reduce-scatter.12.cloned.1.call-done = bf16[512,1024]{1,0:T(8,128)(2,1)} async-done(((bf16[1024,1024]{1,0:T(8,128)(2,1)}), bf16[512,1024]{1,0:T(8,128)(2,1)}) %reduce-scatter.12.cloned.1.call-update) | async-done | bytes 1048592 | tf_op jit(solution)/shard_map/reduce_scatter | solution.py:185
  976.8 10.9 add_convert_fusion
  1008.6 27.7 %all-gather.31.cloned.1.call-done = bf16[1024,1024]{1,0:T(8,128)(2,1)} async-done(((bf16[512,1024]{1,0:T(8,128)(2,1)}), bf16[1024,1024]{1,0:T(8,128)(2,1)}) %all-gather.31.cloned.1.call-update) | async-done | bytes 2097168 | tf_op jit(solution)/shard_map/all_gather | solution.py:227
  1043.9 123.0 %while.60 = (s32[]{:T(128)}, f32[1024,8,64]{0,2,1:T(8,128)}, f32[1024,8,64]{0,2,1:T(8,128)}, bf16[2,512,8,64]{1,3,2,0:T(8,128)(2,1)}, s32[2]{0:T(128)S(1)}, /*in...) while((s32[]{:T(128)}, f32[1024,8,64]{0,2,1:T(8,128)}, ...), condition=%wide.region_47.48_spmd.clone.clone, body=%wide.region_45.47_spmd.clone.clone.sunk | while | flops 2726555648 | bytes 208769808 | solution.py:104
  1047.5 10.5 fusion.228
  1058.0 13.9 multiply_reduce_fusion.30
  1071.9 14.9 multiply_convert_fusion.20
  1108.5 9.6 fusion.228
  1118.1 13.7 multiply_reduce_fusion.30
  1131.8 15.4 multiply_convert_fusion.20
  1168.0 119.8 %while.61 = (s32[]{:T(128)}, f32[1024,8,64]{0,2,1:T(8,128)}, f32[1024,8,64]{0,2,1:T(8,128)}, bf16[2,512,8,64]{1,3,2,0:T(8,128)(2,1)}, s32[2]{0:T(128)S(1)}, /*in...) while((s32[]{:T(128)}, f32[1024,8,64]{0,2,1:T(8,128)}, ...), condition=%wide.region_62.63_spmd.clone.clone, body=%wide.region_60.62_spmd.clone.clone.sunk | while | flops 2726555648 | bytes 212964144 | solution.py:104
  1171.4 9.6 fusion.239
  1181.0 13.7 multiply_reduce_fusion.31
  1194.7 14.8 multiply_convert_fusion.21
  1230.1 9.6 fusion.239
  1239.7 13.6 multiply_reduce_fusion.31
  1253.3 14.8 multiply_convert_fusion.21
  1357.3 81.9 %all-reduce.8.cloned.1.call-done = bf16[3,1024,512]{2,0,1:T(4,128)(2,1)} async-done(((bf16[3,1024,512]{2,0,1:T(4,128)(2,1)}), bf16[3,1024,512]{2,0,1:T(4,128)(2,1)}) %all-reduce.8.cloned.1.call-update) | async-done | bytes 3145744
  1441.1 58.6 %reduce-scatter.22.cloned.1.call-done = bf16[512,64]{0,1:T(8,128)(2,1)} async-done(((bf16[512,1024]{0,1:T(8,128)(2,1)}), bf16[512,64]{0,1:T(8,128)(2,1)}) %reduce-scatter.22.cloned.1.call-update) | async-done | bytes 65552 | tf_op jit(solution)/shard_map/reduce_scatter | solution.py:267
  1501.2 31.6 %reduce-scatter.20.cloned.1.call-done = bf16[512,1024]{1,0:T(8,128)(2,1)} async-done(((bf16[1024,1024]{1,0:T(8,128)(2,1)}), bf16[512,1024]{1,0:T(8,128)(2,1)}) %reduce-scatter.20.cloned.1.call-update) | async-done | bytes 1048592 | tf_op jit(solution)/shard_map/reduce_scatter | solution.py:249
  1532.8 34.8 %reduce-scatter.16.cloned.1.call-done = bf16[512,1024]{1,0:T(8,128)(2,1)} async-done(((bf16[1024,1024]{1,0:T(8,128)(2,1)}), bf16[512,1024]{1,0:T(8,128)(2,1)}) %reduce-scatter.16.cloned.1.call-update) | async-done | bytes 1048592 | tf_op jit(solution)/shard_map/reduce_scatter | solution.py:249
  1570.9 39.8 %all-reduce.1 = (f32[3,1024]{1,0:T(4,128)}, f32[16]{0:T(128)S(1)}, f32[4096]{0:T(1024)S(1)}) all-reduce(f32[3,1024]{1,0:T(4,128)S(1)} %pad_maximum_fusion.8, f32[16]{0:T(128)S(1)} %add_dynamic-update-slice_fusion.1, f32[4096]{0:T(1024)S(1)} %add_dynamic-update-slice_fusion), channel_id=1, replica_groups=mesh['batch'=16,'tensor'=2] {'batch','tensor'}, use_global_device_ids=true, to_apply=%region_72.73 | all-reduce | flops 7184 | bytes 57472 | tf_op jit(solution)/shard_map/psum | solution.py:286
  (421 shorter events, 364.9 us)
Async XLA Ops:
  7.2 41.6 %all-gather.15.cloned.1.call-start = ((), (), s32[]{:S(2)}) async-start(), calls=%async_computation.9 | async-start | bytes 3145728 | tf_op jit(solution)/shard_map/all_gather | solution.py:156
  12.8 83.4 %all-gather.17.cloned.1.call-start = ((), (), s32[]{:S(2)}) async-start(), calls=%async_computation.10 | async-start | bytes 3342336 | tf_op jit(solution)/shard_map/all_gather | solution.py:125
  13.6 167.3 %all-gather.27.cloned.1.call-start = ((), (), s32[]{:S(2)}) async-start(), calls=%async_computation.16 | async-start | bytes 3145728 | tf_op jit(solution)/shard_map/all_gather | solution.py:156
  14.3 258.1 %all-gather.19.cloned.1.call-start = ((), (), s32[]{:S(2)}) async-start(), calls=%async_computation.11 | async-start | bytes 1114112 | tf_op jit(solution)/shard_map/all_gather | solution.py:126
  14.9 463.9 %all-reduce.10.cloned.1.call-start = ((), (), s32[]{:S(2)}) async-start(), calls=%async_computation.31 | async-start | bytes 16777216 | tf_op jit(solution)/shard_map/psum | solution.py:167
  281.3 232.4 %all-gather.37.cloned.1.call-start = ((), (), s32[]{:S(2)}) async-start(), calls=%async_computation.29 | async-start | bytes 3145728 | tf_op jit(solution)/shard_map/all_gather | solution.py:193
  284.4 282.0 %all-gather.25.cloned.1.call-start = ((), (), s32[]{:S(2)}) async-start(), calls=%async_computation.14 | async-start | bytes 4456448 | tf_op jit(solution)/shard_map/all_gather | solution.py:128
  285.2 332.5 %all-gather.23.cloned.1.call-start = ((), (), s32[]{:S(2)}) async-start(), calls=%async_computation.13 | async-start | bytes 4456448 | tf_op jit(solution)/shard_map/all_gather | solution.py:127
  285.9 365.5 %all-gather.21.cloned.1.call-start = ((), (), s32[]{:S(2)}) async-start(), calls=%async_computation.12 | async-start | bytes 3145728 | tf_op jit(solution)/shard_map/all_gather | solution.py:175
  490.3 195.7 %all-gather.29.cloned.1.call-start = ((), (), s32[]{:S(2)}) async-start(), calls=%async_computation.17 | async-start | bytes 3145728 | tf_op jit(solution)/shard_map/all_gather | solution.py:175
  490.9 230.2 %all-gather.35.cloned.1.call-start = ((), (), s32[]{:S(2)}) async-start(), calls=%async_computation.28 | async-start | bytes 3145728 | tf_op jit(solution)/shard_map/all_gather | solution.py:193
  491.6 342.9 %reduce-scatter.14.cloned.1.call-start = ((), (), s32[]{:S(2)}) async-start(), calls=%async_computation.19 | async-start | bytes 6291456 | tf_op jit(solution)/shard_map/reduce_scatter | solution.py:215
  661.7 59.4 %copy-start.73 = (f32[2048]{0:T(1024)S(1)}, f32[2048]{0:T(1024)}, u32[]{:S(2)}) copy-start(f32[2048]{0:T(1024)} %param.25) | copy-start | bytes 24580
  748.2 24.7 %copy-start.77 = (bf16[1024,2048]{1,0:T(8,128)(2,1)S(1)}, bf16[1024,2048]{1,0:T(8,128)(2,1)}, u32[]{:S(2)}) copy-start(bf16[1024,2048]{1,0:T(8,128)(2,1)} %all-gather.23.cloned.1.call-done) | copy-start | bytes 12582916
  779.0 90.4 %reduce-scatter.10.cloned.1.call-start = ((), (), s32[]{:S(2)}) async-start(), calls=%async_computation.15 | async-start | bytes 3145728 | tf_op jit(solution)/shard_map/reduce_scatter | solution.py:185
  788.4 137.5 %reduce-scatter.18.cloned.1.call-start = ((), (), s32[]{:S(2)}) async-start(), calls=%async_computation.22 | async-start | bytes 6291456 | tf_op jit(solution)/shard_map/reduce_scatter | solution.py:215
  798.3 161.5 %reduce-scatter.12.cloned.1.call-start = ((), (), s32[]{:S(2)}) async-start(), calls=%async_computation.18 | async-start | bytes 3145728 | tf_op jit(solution)/shard_map/reduce_scatter | solution.py:185
  809.5 192.5 %all-gather.33.cloned.1.call-start = ((), (), s32[]{:S(2)}) async-start(), calls=%async_computation.23 | async-start | bytes 3145728 | tf_op jit(solution)/shard_map/all_gather | solution.py:227
  933.1 32.7 %copy-start.23 = (f32[512,1024]{1,0:T(8,128)S(1)}, f32[512,1024]{1,0:T(8,128)}, u32[]{:S(2)}) copy-start(f32[512,1024]{1,0:T(8,128)} %get-tuple-element.600) | copy-start | bytes 6291460
  968.5 67.8 %all-gather.31.cloned.1.call-start = ((), (), s32[]{:S(2)}) async-start(), calls=%async_computation.20 | async-start | bytes 3145728 | tf_op jit(solution)/shard_map/all_gather | solution.py:227
  969.1 381.1 %reduce-scatter.26.cloned.1.call-start = ((), (), s32[]{:S(2)}) async-start(), calls=%async_computation.27 | async-start | bytes 4456448 | tf_op jit(solution)/shard_map/reduce_scatter | solution.py:273
  987.6 364.4 %reduce-scatter.24.cloned.1.call-start = ((), (), s32[]{:S(2)}) async-start(), calls=%async_computation.26 | async-start | bytes 4456448 | tf_op jit(solution)/shard_map/reduce_scatter | solution.py:270
  1002.0 437.3 %all-reduce.8.cloned.1.call-start = ((), (), s32[]{:S(2)}) async-start(), calls=%async_computation.30 | async-start | bytes 8388608
  1008.6 32.1 %copy-start.75 = (f32[8]{0:T(128)S(1)}, f32[8]{0:T(128)}, u32[]{:S(2)}) copy-start(f32[8]{0:T(128)} %param.22) | copy-start | bytes 100
  1043.9 124.1 %copy-start.3 = (bf16[1024,8,64]{0,2,1:T(8,128)(2,1)S(1)}, bf16[1024,8,64]{0,2,1:T(8,128)(2,1)}, u32[]{:S(2)}) copy-start(bf16[1024,8,64]{0,2,1:T(8,128)(2,1)} %copy-done.2) | copy-start | bytes 3145732
  1043.9 124.1 %copy-start.37 = (s32[1024]{0:T(1024)S(1)}, s32[1024]{0:T(1024)}, u32[]{:S(2)}) copy-start(s32[1024]{0:T(1024)} %convert_reduce_fusion.2) | copy-start | bytes 12292
  1043.9 124.1 %copy-start.49 = (f32[2,8,512]{2,1,0:T(8,128)S(1)}, f32[2,8,512]{2,1,0:T(8,128)}, u32[]{:S(2)}) copy-start(f32[2,8,512]{2,1,0:T(8,128)} %copy-done.48) | copy-start | bytes 98308
  1086.9 14.3 copy-start
  1147.2 14.9 copy-start
  1209.5 14.4 copy-start.1
  1216.2 7.7 copy-start.16
  1268.1 15.0 copy-start.1
  1275.4 7.7 copy-start.16
  1287.8 7.9 copy-start.7
  1327.4 172.2 %reduce-scatter.22.cloned.1.call-start = ((), (), s32[]{:S(2)}) async-start(), calls=%async_computation.25 | async-start | bytes 1114112 | tf_op jit(solution)/shard_map/reduce_scatter | solution.py:267
  1334.2 198.6 %reduce-scatter.20.cloned.1.call-start = ((), (), s32[]{:S(2)}) async-start(), calls=%async_computation.24 | async-start | bytes 3145728 | tf_op jit(solution)/shard_map/reduce_scatter | solution.py:249
  1341.7 8.5 copy-start.69
  1341.8 8.5 copy-start.70
  1341.8 225.8 %reduce-scatter.16.cloned.1.call-start = ((), (), s32[]{:S(2)}) async-start(), calls=%async_computation.21 | async-start | bytes 3145728 | tf_op jit(solution)/shard_map/reduce_scatter | solution.py:249
  1348.9 7.9 copy-start.71
  1348.9 8.0 copy-start.72
  1353.8 213.7 %copy-start.12 = (bf16[2,512,1024]{2,1,0:T(8,128)(2,1)S(1)}, bf16[2,512,1024]{2,1,0:T(8,128)(2,1)}, u32[]{:S(2)}) copy-start(bf16[2,512,1024]{2,1,0:T(8,128)(2,1)} %param.18) | copy-start | bytes 6291460
  1353.8 213.7 %copy-start.53 = (f32[1,1024]{1,0:T(1,128)S(1)}, f32[1,1024]{1,0:T(1,128)}, u32[]{:S(2)}) copy-start(f32[1,1024]{1,0:T(1,128)} %copy-done.52) | copy-start | bytes 12292
  1353.8 213.7 %copy-start.55 = (f32[512]{0:T(512)S(1)}, f32[512]{0:T(512)}, u32[]{:S(2)}) copy-start(f32[512]{0:T(512)} %copy-done.54) | copy-start | bytes 6148
  1353.8 213.7 %copy-start.57 = (f32[512]{0:T(512)S(1)}, f32[512]{0:T(512)}, u32[]{:S(2)}) copy-start(f32[512]{0:T(512)} %copy-done.56) | copy-start | bytes 6148
  1353.8 213.7 %copy-start.61 = (f32[512]{0:T(512)S(1)}, f32[512]{0:T(512)}, u32[]{:S(2)}) copy-start(f32[512]{0:T(512)} %copy-done.60) | copy-start | bytes 6148
  1353.9 213.7 %copy-start.63 = (f32[512]{0:T(512)S(1)}, f32[512]{0:T(512)}, u32[]{:S(2)}) copy-start(f32[512]{0:T(512)} %copy-done.62) | copy-start | bytes 6148
  1532.8 79.1 %copy-start.30 = (bf16[512,1024]{1,0:T(8,128)(2,1)S(1)}, bf16[512,1024]{1,0:T(8,128)(2,1)}, u32[]{:S(2)}) copy-start(bf16[512,1024]{1,0:T(8,128)(2,1)} %reduce-scatter.20.cloned.1.call-done) | copy-start | bytes 3145732
  (63 other events, 258.8 us)
Sparse Core Ops, SparseCore 0:
  12.9 35.8 all-gather.14
  51.0 45.2 all-gather.16
  97.8 31.9 all-gather.26
  131.7 37.9 all-gather.18
  281.4 197.3 all-reduce.9
  480.2 33.4 all-gather.36
  515.9 50.5 all-gather.24
  568.6 49.0 all-gather.22
  619.8 31.5 all-gather.20
  652.9 33.1 all-gather.28
  687.6 33.4 all-gather.34
  779.1 55.4 reduce-scatter.13
  837.5 31.8 reduce-scatter.9
  871.5 54.3 reduce-scatter.17
  928.0 31.8 reduce-scatter.11
  968.6 33.1 all-gather.32
  1003.2 33.1 all-gather.30
  1040.1 72.4 reduce-scatter.25
  1116.9 71.3 reduce-scatter.23
  1327.5 111.6 all-reduce.7
  1443.3 56.3 reduce-scatter.21
  1501.9 30.8 reduce-scatter.19
  1535.7 31.8 reduce-scatter.15
where the time goes:
time: 1640 us; the launch traced here: 1620 us
  waiting for transfers between devices  844 us (51%)
  matrix products  385 us (23%)
  other arithmetic  160 us (10%)
  local copies, waits for them, and re-layouts  146 us (9%)
  blocking collectives  53.9 us (3%)
  loops' own time  17.1 us (1%)
    psum x1, waiting for transfers between devices, body(): lax.psum(jnp.dot(scaled, out_full, preferred_element_type=jnp.float32), '...  193 us
    unnamed x24, waiting for transfers between devices  87.2 us
    dynamic_update_slice x8, local copies, waits for them, and re-layouts, attend_forward(): attended, log_sums = lax.map(one_block, firsts)  82.7 us
    reduce_scatter x2, waiting for transfers between devices, body(): lax.psum_scatter(jnp.einsum('gf,df->gd', hidden_grad, up_full, preferred_...  81.5 us
    dot_general x8, matrix products, one_block(): jnp.einsum('qhd,khd->hqk', query_block, all_keys, preferred_element_type=...  73.6 us
    reduce_scatter x2, waiting for transfers between devices, body(): lax.psum_scatter(jnp.einsum('cge,cde->gd', proj_grads, qkv_full, preferre...  66.4 us
    convert_element_type x4, other arithmetic, one_block(): score_grad = (probs * (prob_grad - inner)).astype(jnp.bfloat16)  60 us
    reduce_scatter x2, waiting for transfers between devices, body(): lax.psum_scatter(jnp.dot(narrow, down_full, preferred_element_type=jnp.fl...  58.6 us
  transfers between devices with their start and end apart: 23, of which 18 were waited for; matrix products, arithmetic and copies ran while one was open for 37% of the time, Pallas kernels for 0%

commit v1 on v0

v1 whole, which is shorter than its diff:
```python
import functools
import math

import jax
import jax.numpy as jnp
from jax import lax
from jax.experimental import pallas as pl
from jax.experimental.pallas import tpu as pltpu
from jax.sharding import PartitionSpec as P

eps = 1e-05
SEQ_MOST = 512
F32 = jnp.float32
BF = jnp.bfloat16
ALL = ("batch", "tensor")
GELU_C = math.sqrt(2.0 / math.pi)
GELU_A = 0.044715


def dotf(a, b, ca, cb):
    return lax.dot_general(a, b, (((ca,), (cb,)), ((), ())), preferred_element_type=F32)


def row_loop(rows, step, fn):
    def one(i, carry):
        fn(pl.multiple_of(i * step, step))
        return carry

    lax.fori_loop(0, rows // step, one, 0)


def normalize(values):
    centred = values - jnp.mean(values, axis=-1, keepdims=True)
    factor = lax.rsqrt(jnp.mean(centred * centred, axis=-1, keepdims=True) + eps)
    return (centred * factor, factor)


def norm_back(unit, factor, grad):
    return factor * (
        grad
        - jnp.mean(grad, axis=-1, keepdims=True)
        - unit * jnp.mean(grad * unit, axis=-1, keepdims=True)
    )


def fold8(values):
    rows, width = values.shape
    return jnp.sum(values.reshape(rows // 8, 8, width), axis=0)


def bits_of(count):
    return count.bit_length() - 1


def rel_table(batch_count, tensor_count):
    batch_bits = bits_of(batch_count)
    table = []
    for core in range(2):
        for tensor in range(tensor_count):
            for rest in range(batch_count // 2):
                batch = core
                for k in range(1, batch_bits):
                    batch |= ((rest >> (batch_bits - 1 - k)) & 1) << k
                table.append((batch, tensor))
    return table


def exchange_steps(batch_count, tensor_count):
    steps = [("batch", 1)]
    steps += [("tensor", 1 << k) for k in reversed(range(bits_of(tensor_count)))]
    steps += [("batch", 1 << k) for k in range(1, bits_of(batch_count))]
    return steps


def swap(value, axis, flip):
    count = lax.axis_size(axis)
    return lax.ppermute(value, axis, [(i, i ^ flip) for i in range(count)])


def reduce_scatter(buffer, steps):
    for axis, flip in steps:
        half = buffer.shape[0] // 2
        arrived = swap(buffer[half:], axis, flip)
        buffer = (buffer[:half].astype(F32) + arrived.astype(F32)).astype(BF)
    return buffer[0].astype(F32)


def all_sum(vector, steps):
    for axis, flip in steps:
        vector = vector + swap(vector, axis, flip)
    return vector


def load_shards(src, dst, sem, table, ids_ref, lead=None, col=0):
    height, cols = dst.shape[1] // (len(table) // dst.shape[0]), dst.shape[2]
    for p, (batch, tensor) in enumerate(table):
        b = lax.bitwise_xor(jnp.int32(batch), ids_ref[0])
        t = lax.bitwise_xor(jnp.int32(tensor), ids_ref[1])
        piece = src.at[p] if lead is None else src.at[p, lead]
        pltpu.make_async_copy(
            piece.at[:, pl.ds(col, cols)],
            dst.at[t, pl.ds(pl.multiple_of(b * height, height), height), :],
            sem,
        ).start()


def wait_shards(dst, sem):
    pltpu.make_async_copy(dst, dst, sem).wait()


def qkv_kernel(table, factor, ids_ref, x_ref, gain_ref, w_hbm, h1_ref, q_ref, k_ref, v_ref, w, sem):
    first = pl.program_id(0) == 0

    @pl.when(first)
    def _():
        for c in range(3):
            load_shards(w_hbm, w.at[c], sem.at[c], table, ids_ref, lead=c)

    def chunk(r):
        unit, _ = normalize(x_ref[pl.ds(r, 32), :].astype(F32))
        h1_ref[pl.ds(r, 32), :] = (unit * gain_ref[0:1, :]).astype(BF)

    row_loop(x_ref.shape[0], 32, chunk)
    tensor_count, _, cols = w.shape[1:]
    for c, out in enumerate((q_ref, k_ref, v_ref)):

        @pl.when(first)
        def _(c=c):
            wait_shards(w.at[c], sem.at[c])

        for t in range(tensor_count):
            part = dotf(h1_ref[...], w[c, t], 1, 0).astype(BF)
            out[:, t * cols : (t + 1) * cols] = part * BF(factor) if c == 0 else part


def project(ids, x, gains, w_all, table, tensor_count, factor):
    rows, width = x.shape
    block = min(256, rows)
    cols = width // tensor_count
    row = pl.BlockSpec((block, width), lambda i, e: (i, 0))
    return pl.pallas_call(
        functools.partial(qkv_kernel, table, factor),
        grid_spec=pltpu.PrefetchScalarGridSpec(
            num_scalar_prefetch=1,
            grid=(rows // block,),
            in_specs=[
                row,
                pl.BlockSpec((3, width), lambda i, e: (0, 0)),
                pl.BlockSpec(memory_space=pl.ANY),
            ],
            out_specs=[row] * 4,
            scratch_shapes=[
                pltpu.VMEM((3, tensor_count, width, cols), BF),
                pltpu.SemaphoreType.DMA((3,)),
            ],
        ),
        out_shape=[jax.ShapeDtypeStruct((rows, width), BF)] * 4,
        compiler_params=pltpu.CompilerParams(vmem_limit_bytes=32 << 20),
        cost_estimate=pl.CostEstimate(
            flops=6 * rows * width * width, transcendentals=0, bytes_accessed=16 << 20
        ),
        name="project",
    )(ids, x, gains, w_all)


def spans(rows, block):
    return [
        (first, max(0, (first - SEQ_MOST + 1) // block * block), first + block)
        for first in range(0, rows, block)
    ]


def fill_bias(ends_ref, bias, parts, block):
    for (first, low, high), ref in zip(parts, bias):
        shape = (high - low, block)
        keys = low + lax.broadcasted_iota(jnp.int32, shape, 0)
        queries = first + lax.broadcasted_iota(jnp.int32, shape, 1)
        start = jnp.zeros(shape, jnp.int32)
        for n in range(ends_ref.shape[0]):
            end = ends_ref[n]
            start = jnp.where(queries >= end, end, start)
        ref[...] = jnp.where((keys <= queries) & (keys >= start), 0.0, -1e30).astype(F32)


def attend_kernel(rows, block, ends_ref, q_ref, k_ref, v_ref, scale_ref, o_ref, lse_ref, *bias):
    parts = spans(rows, block)

    @pl.when(pl.program_id(0) == 0)
    def _():
        fill_bias(ends_ref, bias, parts, block)

    lower = lax.broadcasted_iota(jnp.int32, (1, 128), 1) < 64
    for n, (first, low, high) in enumerate(parts):
        q = q_ref[pl.ds(first, block), :]
        heads = []
        for h in range(2):
            own = jnp.where(lower if h == 0 else ~lower, q, jnp.zeros_like(q))
            s = dotf(k_ref[pl.ds(low, high - low), :], own, 1, 1) + bias[n][...]
            most = jnp.max(s, axis=0, keepdims=True)
            p = jnp.exp(s - most)
            total = jnp.sum(p, axis=0, keepdims=True)
            probs = (p * (1.0 / total)).astype(BF)
            lse_ref[0, pl.ds(h, 1), pl.ds(first, block)] = most + jnp.log(total)
            heads.append(dotf(probs, v_ref[pl.ds(low, high - low), :], 0, 0))
        out = jnp.where(lower, heads[0], heads[1]) * scale_ref[...]
        o_ref[pl.ds(first, block), :] = out.astype(BF)


def attend_back_kernel(
    rows, block, factor, ends_ref, q_ref, k_ref, v_ref, da_ref, lse_ref,
    dq_ref, dk_ref, dv_ref, inner_ref, dk_acc, dv_acc, *bias
):
    parts = spans(rows, block)

    @pl.when(pl.program_id(0) == 0)
    def _():
        fill_bias(ends_ref, bias, parts, block)

    lower = lax.broadcasted_iota(jnp.int32, (1, 128), 1) < 64
    dk_acc[...] = jnp.zeros_like(dk_acc)
    dv_acc[...] = jnp.zeros_like(dv_acc)
    for n, (first, low, high) in enumerate(parts):
        here = pl.ds(first, block)
        keys = pl.ds(low, high - low)
        q, da, k, v = q_ref[here, :], da_ref[here, :], k_ref[keys, :], v_ref[keys, :]
        heads = []
        for h in range(2):
            mask = lower if h == 0 else ~lower
            q_own = jnp.where(mask, q, jnp.zeros_like(q))
            da_own = jnp.where(mask, da, jnp.zeros_like(da))
            s = dotf(k, q_own, 1, 1) + bias[n][...]
            p = jnp.exp(s - lse_ref[0, pl.ds(h, 1), here])
            product = p * dotf(v, da_own, 1, 1)
            inner = jnp.sum(product, axis=0, keepdims=True)
            inner_ref[0, pl.ds(h, 1), here] = inner
            ds = (product - p * inner).astype(BF)
            dv_acc[keys, :] += dotf(p.astype(BF), da_own, 1, 0)
            dk_acc[keys, :] += dotf(ds, q_own, 1, 0)
            heads.append(dotf(ds, k, 0, 0))
        dq_ref[here, :] = (jnp.where(lower, heads[0], heads[1]) * factor).astype(BF)
    dk_ref[...] = dk_acc[...].astype(BF)
    dv_ref[...] = dv_acc[...].astype(BF)


def bias_shapes(rows, block):
    return [pltpu.VMEM((high - low, block), F32) for _, low, high in spans(rows, block)]


def attend(q, k, v, scale_row, ends):
    rows, width = q.shape
    block = min(256, rows)
    pairs = width // 128
    col = pl.BlockSpec((rows, 128), lambda i, e: (0, i))
    return pl.pallas_call(
        functools.partial(attend_kernel, rows, block),
        grid_spec=pltpu.PrefetchScalarGridSpec(
            num_scalar_prefetch=1,
            grid=(pairs,),
            in_specs=[col, col, col, pl.BlockSpec((1, 128), lambda i, e: (0, i))],
            out_specs=[col, pl.BlockSpec((1, 2, rows), lambda i, e: (i, 0, 0))],
            scratch_shapes=bias_shapes(rows, block),
        ),
        out_shape=[
            jax.ShapeDtypeStruct((rows, width), BF),
            jax.ShapeDtypeStruct((pairs, 2, rows), F32),
        ],
        compiler_params=pltpu.CompilerParams(vmem_limit_bytes=40 << 20),
        cost_estimate=pl.CostEstimate(
            flops=28 * 10**9, transcendentals=0, bytes_accessed=8 << 20
        ),
        name="attend",
    )(ends, q, k, v, scale_row)


def attend_back(q, k, v, da, lse, ends, factor):
    rows, width = q.shape
    block = min(256, rows)
    pairs = width // 128
    col = pl.BlockSpec((rows, 128), lambda i, e: (0, i))
    row = pl.BlockSpec((1, 2, rows), lambda i, e: (i, 0, 0))
    out = jax.ShapeDtypeStruct((rows, width), BF)
    return pl.pallas_call(
        functools.partial(attend_back_kernel, rows, block, factor),
        grid_spec=pltpu.PrefetchScalarGridSpec(
            num_scalar_prefetch=1,
            grid=(pairs,),
            in_specs=[col, col, col, col, row],
            out_specs=[col, col, col, row],
            scratch_shapes=[pltpu.VMEM((rows, 128), F32)] * 2 + bias_shapes(rows, block),
        ),
        out_shape=[out, out, out, jax.ShapeDtypeStruct((pairs, 2, rows), F32)],
        compiler_params=pltpu.CompilerParams(vmem_limit_bytes=48 << 20),
        cost_estimate=pl.CostEstimate(
            flops=42 * 10**9, transcendentals=0, bytes_accessed=16 << 20
        ),
        name="attend_back",
    )(ends, q, k, v, da, lse)


def hidden_kernel(
    table, out_col, up_col, ids_ref, scaled_ref, x_ref, gain_ref, mid_ref, w_hbm,
    mixed_ref, h3_ref, hidden_ref, narrow_ref, stat_ref, out_w, up_w, act, sem
):
    first = pl.program_id(0) == 0
    block, width = x_ref.shape
    tensor_count, _, out_cols = out_w.shape
    up_cols = up_w.shape[2]
    total = tensor_count * up_cols

    @pl.when(first)
    def _():
        load_shards(w_hbm, out_w, sem.at[0], table, ids_ref, col=out_col)
        load_shards(w_hbm, up_w, sem.at[1], table, ids_ref, col=up_col)
        wait_shards(out_w, sem.at[0])

    mixed = dotf(scaled_ref[:, :out_cols], out_w[0], 1, 1)
    for t in range(1, tensor_count):
        mixed += dotf(scaled_ref[:, t * out_cols : (t + 1) * out_cols], out_w[t], 1, 1)
    mixed_ref[...] = mixed

    def norms(r):
        here = pl.ds(r, 32)
        unit, _ = normalize(mixed_ref[here, :])
        resid = x_ref[here, :].astype(F32) + unit * gain_ref[1:2, :]
        unit3, _ = normalize(resid)
        h3_ref[here, :] = (unit3 * gain_ref[2:3, :]).astype(BF)

    row_loop(block, 32, norms)

    @pl.when(first)
    def _():
        wait_shards(up_w, sem.at[1])

    chunk = min(512, up_cols)
    sums = jnp.zeros((block, 128), F32)
    squares = jnp.zeros((block, 128), F32)
    for c in range(total // chunk):
        t, off = divmod(c * chunk, up_cols)
        h = dotf(h3_ref[...], up_w[t, :, off : off + chunk], 1, 0)
        hidden_ref[:, c * chunk : (c + 1) * chunk] = h
        half = 0.5 * jnp.tanh(h * (GELU_C + (GELU_C * GELU_A) * (h * h))) + 0.5
        a = h * half
        act[:, c * chunk : (c + 1) * chunk] = a
        for j in range(chunk // 128):
            piece = a[:, j * 128 : (j + 1) * 128]
            sums += piece
            squares += piece * piece
    mean = jnp.sum(sums, axis=1, keepdims=True) / total
    spread = jnp.sum(squares, axis=1, keepdims=True) / total - mean * mean
    scale = lax.rsqrt(spread + eps)
    lane = lax.broadcasted_iota(jnp.int32, (1, 128), 1)
    stat_ref[...] = jnp.where(lane < 64, mean, scale)

    def narrow(r):
        here = pl.ds(r, 16)
        m = stat_ref[here, 0:1]
        s = stat_ref[here, 64:65]
        narrow_ref[here, :] = ((act[here, :] - m) * s * mid_ref[...]).astype(BF)

    row_loop(block, 16, narrow)


def hidden_forward(ids, scaled, x, gains, mid_row, w_all, table, tensor_count, cols):
    rows, width = x.shape
    block = min(256, rows)
    out_cols, up_cols, _ = cols
    total = up_cols * tensor_count
    row = pl.BlockSpec((block, width), lambda i, e: (i, 0))
    wide = pl.BlockSpec((block, total), lambda i, e: (i, 0))
    return pl.pallas_call(
        functools.partial(hidden_kernel, table, 0, out_cols),
        grid_spec=pltpu.PrefetchScalarGridSpec(
            num_scalar_prefetch=1,
            grid=(rows // block,),
            in_specs=[
                row,
                row,
                pl.BlockSpec((3, width), lambda i, e: (0, 0)),
                pl.BlockSpec((1, total), lambda i, e: (0, 0)),
                pl.BlockSpec(memory_space=pl.ANY),
            ],
            out_specs=[row, row, wide, wide, pl.BlockSpec((block, 128), lambda i, e: (i, 0))],
            scratch_shapes=[
                pltpu.VMEM((tensor_count, width, out_cols), BF),
                pltpu.VMEM((tensor_count, width, up_cols), BF),
                pltpu.VMEM((block, total), F32),
                pltpu.SemaphoreType.DMA((2,)),
            ],
        ),
        out_shape=[
            jax.ShapeDtypeStruct((rows, width), F32),
            jax.ShapeDtypeStruct((rows, width), BF),
            jax.ShapeDtypeStruct((rows, total), F32),
            jax.ShapeDtypeStruct((rows, total), BF),
            jax.ShapeDtypeStruct((rows, 128), F32),
        ],
        compiler_params=pltpu.CompilerParams(vmem_limit_bytes=48 << 20),
        cost_estimate=pl.CostEstimate(
            flops=20 * 10**9, transcendentals=0, bytes_accessed=40 << 20
        ),
        name="hidden_forward",
    )(ids, scaled, x, gains, mid_row, w_all)


def feed_kernel(
    table, offsets, ids_ref, narrow_ref, hidden_ref, stat_ref, mixed_ref, x_ref, cot_ref, gain_ref,
    mid_ref, scale_ref, w_hbm, out_ref, dhidden_ref, dresid_ref, dmixed_ref, dattended_ref,
    gains_ref, dmid_ref, out_w, up_w, down_w, grad, unit_s, slope_s, wide, sem
):
    first = pl.program_id(0) == 0
    block, width = x_ref.shape
    tensor_count, _, out_cols = out_w.shape
    up_cols = up_w.shape[2]
    total = tensor_count * up_cols

    @pl.when(first)
    def _():
        load_shards(w_hbm, down_w, sem.at[0], table, ids_ref, col=offsets[2])
        load_shards(w_hbm, up_w, sem.at[1], table, ids_ref, col=offsets[1])
        load_shards(w_hbm, out_w, sem.at[2], table, ids_ref, col=offsets[0])
        gains_ref[...] = jnp.zeros_like(gains_ref)
        dmid_ref[...] = jnp.zeros_like(dmid_ref)
        wait_shards(down_w, sem.at[0])

    feed = dotf(narrow_ref[:, :up_cols], down_w[0], 1, 1)
    for t in range(1, tensor_count):
        feed += dotf(narrow_ref[:, t * up_cols : (t + 1) * up_cols], down_w[t], 1, 1)
    wide[...] = feed

    def output(r):
        here = pl.ds(r, 32)
        unit, _ = normalize(mixed_ref[here, :])
        resid = x_ref[here, :].astype(F32) + unit * gain_ref[1:2, :]
        out_ref[here, :] = (resid + wide[here, :]).astype(BF)

    row_loop(block, 32, output)

    chunk = min(512, up_cols)
    mean = stat_ref[:, 0:1]
    scale = stat_ref[:, 64:65]
    back_sum = jnp.zeros((block, 128), F32)
    back_inner = jnp.zeros((block, 128), F32)
    for c in range(total // chunk):
        t, off = divmod(c * chunk, up_cols)
        here = slice(c * chunk, (c + 1) * chunk)
        dn = dotf(cot_ref[...], down_w[t, :, off : off + chunk], 1, 0)
        h = hidden_ref[:, here]
        square = h * h
        half = 0.5 * jnp.tanh(h * (GELU_C + (GELU_C * GELU_A) * square)) + 0.5
        a = h * half
        slope_s[:, here] = half + a * (1.0 - half) * (
            2.0 * GELU_C + (6.0 * GELU_C * GELU_A) * square
        )
        unit = (a - mean) * scale
        unit_s[:, here] = unit
        dmid_ref[:, here] += fold8(dn * unit)
        g = dn * mid_ref[:, here]
        grad[:, here] = g
        inner = g * unit
        for j in range(chunk // 128):
            back_sum += g[:, j * 128 : (j + 1) * 128]
            back_inner += inner[:, j * 128 : (j + 1) * 128]
    sum_col = jnp.sum(back_sum, axis=1, keepdims=True) / total
    inner_col = jnp.sum(back_inner, axis=1, keepdims=True) / total
    for c in range(total // chunk):
        here = slice(c * chunk, (c + 1) * chunk)
        act_grad = scale * (grad[:, here] - sum_col - unit_s[:, here] * inner_col)
        dhidden_ref[:, here] = (act_grad * slope_s[:, here]).astype(BF)

    @pl.when(first)
    def _():
        wait_shards(up_w, sem.at[1])
        wait_shards(out_w, sem.at[2])

    dh3 = dotf(dhidden_ref[:, :up_cols], up_w[0], 1, 1)
    for t in range(1, tensor_count):
        dh3 += dotf(dhidden_ref[:, t * up_cols : (t + 1) * up_cols], up_w[t], 1, 1)
    wide[...] = dh3

    def back(r):
        here = pl.ds(r, 32)
        unit, factor = normalize(mixed_ref[here, :])
        resid = x_ref[here, :].astype(F32) + unit * gain_ref[1:2, :]
        unit3, factor3 = normalize(resid)
        third = wide[here, :]
        gains_ref[8:16, :] += fold8(third * unit3)
        dresid = cot_ref[here, :].astype(F32) + norm_back(unit3, factor3, third * gain_ref[2:3, :])
        dresid_ref[here, :] = dresid
        gains_ref[0:8, :] += fold8(dresid * unit)
        dmixed_ref[here, :] = norm_back(unit, factor, dresid * gain_ref[1:2, :]).astype(BF)

    row_loop(block, 32, back)
    for t in range(tensor_count):
        here = slice(t * out_cols, (t + 1) * out_cols)
        dscaled = dotf(dmixed_ref[...], out_w[t], 1, 0)
        dattended_ref[:, here] = (dscaled * scale_ref[:, here]).astype(BF)


def feed_back(ids, narrow, hidden, stat, mixed, x, cot, gains, mid_row, scale_row, w_all, table, tensor_count, cols):
    rows, width = x.shape
    block = min(256, rows)
    out_cols, up_cols, _ = cols
    total = up_cols * tensor_count
    row = pl.BlockSpec((block, width), lambda i, e: (i, 0))
    wide = pl.BlockSpec((block, total), lambda i, e: (i, 0))
    return pl.pallas_call(
        functools.partial(feed_kernel, table, (0, out_cols, out_cols + up_cols)),
        grid_spec=pltpu.PrefetchScalarGridSpec(
            num_scalar_prefetch=1,
            grid=(rows // block,),
            in_specs=[
                wide,
                wide,
                pl.BlockSpec((block, 128), lambda i, e: (i, 0)),
                row,
                row,
                row,
                pl.BlockSpec((3, width), lambda i, e: (0, 0)),
                pl.BlockSpec((1, total), lambda i, e: (0, 0)),
                pl.BlockSpec((1, width), lambda i, e: (0, 0)),
                pl.BlockSpec(memory_space=pl.ANY),
            ],
            out_specs=[
                row,
                wide,
                row,
                row,
                row,
                pl.BlockSpec((16, width), lambda i, e: (0, 0)),
                pl.BlockSpec((8, total), lambda i, e: (0, 0)),
            ],
            scratch_shapes=[
                pltpu.VMEM((tensor_count, width, out_cols), BF),
                pltpu.VMEM((tensor_count, width, up_cols), BF),
                pltpu.VMEM((tensor_count, width, up_cols), BF),
                pltpu.VMEM((block, total), F32),
                pltpu.VMEM((block, total), F32),
                pltpu.VMEM((block, total), F32),
                pltpu.VMEM((block, width), F32),
                pltpu.SemaphoreType.DMA((3,)),
            ],
        ),
        out_shape=[
            jax.ShapeDtypeStruct((rows, width), BF),
            jax.ShapeDtypeStruct((rows, total), BF),
            jax.ShapeDtypeStruct((rows, width), F32),
            jax.ShapeDtypeStruct((rows, width), BF),
            jax.ShapeDtypeStruct((rows, width), BF),
            jax.ShapeDtypeStruct((16, width), F32),
            jax.ShapeDtypeStruct((8, total), F32),
        ],
        compiler_params=pltpu.CompilerParams(vmem_limit_bytes=60 << 20),
        cost_estimate=pl.CostEstimate(
            flops=45 * 10**9, transcendentals=0, bytes_accessed=60 << 20
        ),
        name="feed_back",
    )(ids, narrow, hidden, stat, mixed, x, cot, gains, mid_row, scale_row, w_all)


def grad_kernel(batch_table, count, ids_ref, a_ref, *refs):
    b_refs, o_ref, turned, acc = refs[:count], refs[count], refs[count + 1], refs[count + 2]
    step = pl.program_id(0)

    @pl.when(step == 0)
    def _():
        turned[...] = a_ref[...].T

    height = o_ref.shape[-2]
    for c, b_ref in enumerate(b_refs):
        acc[...] = dotf(turned[...], b_ref[...], 1, 0)
        for p, batch in enumerate(batch_table):
            b = lax.bitwise_xor(jnp.int32(batch), ids_ref[0])
            piece = acc[pl.ds(pl.multiple_of(b * height, height), height), :].astype(BF)
            core, rest = divmod(p, len(batch_table) // 2)
            if count == 1:
                o_ref[core, 0, rest] = piece
            else:
                o_ref[core, 0, rest, c] = piece


def weight_grad(ids, a, bs, table, batch_count, tensor_count, name):
    rows, width = a.shape
    cols = bs[0].shape[1] // tensor_count
    chunk = min(512, cols)
    per = cols // chunk
    height = width // batch_count
    half = batch_count // 2
    batch_table = [b for b, t in table if t == 0]
    count = len(bs)
    lead = () if count == 1 else (count,)
    zeros = (0,) * len(lead)
    return pl.pallas_call(
        functools.partial(grad_kernel, batch_table, count),
        grid_spec=pltpu.PrefetchScalarGridSpec(
            num_scalar_prefetch=1,
            grid=(tensor_count * per,),
            in_specs=[pl.BlockSpec((rows, width), lambda i, e: (0, 0))]
            + [
                pl.BlockSpec(
                    (rows, chunk),
                    lambda i, e: (0, lax.bitwise_xor(i // per, e[1]) * per + i % per),
                )
            ]
            * count,
            out_specs=pl.BlockSpec(
                (2, 1, half) + lead + (height, chunk),
                lambda i, e: (0, i // per, 0) + zeros + (0, i % per),
            ),
            scratch_shapes=[pltpu.VMEM((width, rows), BF), pltpu.VMEM((width, chunk), F32)],
        ),
        out_shape=jax.ShapeDtypeStruct((2, tensor_count, half) + lead + (height, cols), BF),
        compiler_params=pltpu.CompilerParams(vmem_limit_bytes=32 << 20),
        cost_estimate=pl.CostEstimate(
            flops=2 * rows * width * cols * tensor_count * count,
            transcendentals=0,
            bytes_accessed=2 * (rows * width + (rows + width) * cols * tensor_count * count),
        ),
        name=name,
    )(ids, a, *bs)


def input_kernel(table, ids_ref, dq_ref, dk_ref, dv_ref, x_ref, dresid_ref, gain_ref, w_hbm, out_ref, dgain_ref, w, wide, sem):
    first = pl.program_id(0) == 0
    tensor_count, _, cols = w.shape[1:]

    @pl.when(first)
    def _():
        for c in range(3):
            load_shards(w_hbm, w.at[c], sem.at[c], table, ids_ref, lead=c)
        dgain_ref[...] = jnp.zeros_like(dgain_ref)
        for c in range(3):
            wait_shards(w.at[c], sem.at[c])

    total = None
    for c, ref in enumerate((dq_ref, dk_ref, dv_ref)):
        for t in range(tensor_count):
            part = dotf(ref[:, t * cols : (t + 1) * cols], w[c, t], 1, 1)
            total = part if total is None else total + part
    wide[...] = total

    def back(r):
        here = pl.ds(r, 32)
        unit, factor = normalize(x_ref[here, :].astype(F32))
        grad = wide[here, :]
        dgain_ref[...] += fold8(grad * unit)
        out = dresid_ref[here, :] + norm_back(unit, factor, grad * gain_ref[0:1, :])
        out_ref[here, :] = out.astype(BF)

    row_loop(x_ref.shape[0], 32, back)


def input_grad(ids, dq, dk, dv, x, dresid, gains, w_all, table, tensor_count):
    rows, width = x.shape
    block = min(256, rows)
    cols = width // tensor_count
    row = pl.BlockSpec((block, width), lambda i, e: (i, 0))
    return pl.pallas_call(
        functools.partial(input_kernel, table),
        grid_spec=pltpu.PrefetchScalarGridSpec(
            num_scalar_prefetch=1,
            grid=(rows // block,),
            in_specs=[row] * 5
            + [
                pl.BlockSpec((3, width), lambda i, e: (0, 0)),
                pl.BlockSpec(memory_space=pl.ANY),
            ],
            out_specs=[row, pl.BlockSpec((8, width), lambda i, e: (0, 0))],
            scratch_shapes=[
                pltpu.VMEM((3, tensor_count, width, cols), BF),
                pltpu.VMEM((block, width), F32),
                pltpu.SemaphoreType.DMA((3,)),
            ],
        ),
        out_shape=[
            jax.ShapeDtypeStruct((rows, width), BF),
            jax.ShapeDtypeStruct((8, width), F32),
        ],
        compiler_params=pltpu.CompilerParams(vmem_limit_bytes=40 << 20),
        cost_estimate=pl.CostEstimate(
            flops=6 * rows * width * width, transcendentals=0, bytes_accessed=22 << 20
        ),
        name="input_grad",
    )(ids, dq, dk, dv, x, dresid, gains, w_all)


def take_micro(value, split):
    micro_count, own_rows, width = value.shape
    rank = lax.axis_index("tensor")
    if split == 1:
        out = jnp.zeros((micro_count, own_rows, width), value.dtype)
        mine = lax.dynamic_index_in_dim(value, rank, 0, keepdims=True)
        out = lax.dynamic_update_slice(out, mine, (rank, 0, 0))
        for flip in range(1, micro_count):
            other = lax.bitwise_xor(rank, flip)
            sent = lax.dynamic_index_in_dim(value, other, 0, keepdims=True)
            out = lax.dynamic_update_slice(out, swap(sent, "tensor", flip), (other, 0, 0))
        return out.reshape(micro_count * own_rows, width)
    whole = lax.all_gather(value, "tensor", axis=1, tiled=True)
    rows = micro_count * own_rows
    return lax.dynamic_slice(whole, (rank // split, rank % split * rows, 0), (1, rows, width))[0]


def give_micro(value, micro_count, split):
    rows, width = value.shape
    own_rows = rows // micro_count
    rank = lax.axis_index("tensor")
    if split == 1:
        pieces = value.reshape(micro_count, own_rows, width)
        out = jnp.zeros_like(pieces)
        mine = lax.dynamic_index_in_dim(pieces, rank, 0, keepdims=True)
        out = lax.dynamic_update_slice(out, mine, (rank, 0, 0))
        for flip in range(1, micro_count):
            other = lax.bitwise_xor(rank, flip)
            sent = lax.dynamic_index_in_dim(pieces, other, 0, keepdims=True)
            out = lax.dynamic_update_slice(out, swap(sent, "tensor", flip), (other, 0, 0))
        return out
    whole = lax.all_gather(value, "tensor", axis=0, tiled=True)
    whole = whole.reshape(micro_count, rows * split, width)
    return lax.dynamic_slice(whole, (0, rank * own_rows, 0), (micro_count, own_rows, width))


def gather_vector(value, tensor_count):
    rank = lax.axis_index("tensor")
    out = jnp.zeros((tensor_count,) + value.shape, value.dtype)
    for flip in range(tensor_count):
        part = value if flip == 0 else swap(value, "tensor", flip)
        out = lax.dynamic_update_slice(out, part[None], (lax.bitwise_xor(rank, flip), 0))
    return out


def body(
    block_in,
    lengths,
    norm_gains,
    qkv_weight,
    head_scale,
    out_weight,
    up_weight,
    mid_gain,
    down_weight,
    cotangent,
):
    tensor_count = lax.axis_size("tensor")
    batch_count = lax.axis_size("batch")
    tensor_rank = lax.axis_index("tensor")
    batch_rank = lax.axis_index("batch")
    micro_count, own_rows, width = block_in.shape
    if tensor_count % micro_count:
        raise NotImplementedError
    split = tensor_count // micro_count
    micro = tensor_rank // split
    local_heads = head_scale.shape[0]
    heads = local_heads * tensor_count
    head_size = width // heads
    local_hidden = mid_gain.shape[0]
    factor = head_size ** (-0.5)
    table = rel_table(batch_count, tensor_count)
    steps = exchange_steps(batch_count, tensor_count)
    own_ids = jnp.stack([batch_rank, tensor_rank]).astype(jnp.int32)
    plain = [(j // tensor_count, j % tensor_count) for j in range(batch_count * tensor_count)]
    zero_ids = jnp.zeros((2,), jnp.int32)
    out_cols = out_weight.shape[0]
    up_cols = local_hidden
    cols = (out_cols, up_cols, up_cols)

    qkv_all = lax.all_gather(qkv_weight, ALL, axis=0, tiled=False)
    rest = jnp.concatenate([out_weight.T, up_weight, down_weight.T], axis=1)
    rest_all = lax.all_gather(rest, ALL, axis=0, tiled=False)
    vectors = gather_vector(jnp.concatenate([mid_gain, head_scale]), tensor_count)
    mid_row = vectors[:, :local_hidden].reshape(1, -1)
    scale_all = vectors[:, local_hidden:].reshape(-1)
    scale_row = jnp.repeat(scale_all, head_size)[None]
    x = take_micro(block_in, split)
    cot = take_micro(cotangent, split)
    own_lengths = lax.dynamic_index_in_dim(lengths[:, 0], micro, 0, keepdims=False)
    ends = jnp.cumsum(own_lengths).astype(jnp.int32)

    def spread(value):
        if split == 1:
            return value
        groups = [[m * split + s for s in range(split)] for m in range(micro_count)]
        return lax.all_to_all(value, "tensor", 1, 0, tiled=True, axis_index_groups=groups)

    def collect(value):
        if split == 1:
            return value
        groups = [[m * split + s for s in range(split)] for m in range(micro_count)]
        return lax.all_to_all(value, "tensor", 0, 1, tiled=True, axis_index_groups=groups)

    h1, q, k, v = project(zero_ids, x, norm_gains, qkv_all, plain, tensor_count, factor)
    q, k, v = spread(q), spread(k), spread(v)
    part = width // split
    scale_part = lax.dynamic_slice(scale_row, (0, tensor_rank % split * part), (1, part))
    scaled, lse = attend(q, k, v, scale_part, ends)
    scaled = collect(scaled)
    mixed, h3, hidden, narrow, stat = hidden_forward(
        zero_ids, scaled, x, norm_gains, mid_row, rest_all, plain, tensor_count, cols
    )
    down_pieces = weight_grad(own_ids, cot, [narrow], table, batch_count, tensor_count, "grad_down")
    block_out, dhidden, dresid, dmixed, dattended, gain_sums, mid_sums = feed_back(
        zero_ids, narrow, hidden, stat, mixed, x, cot, norm_gains, mid_row, scale_row, rest_all,
        plain, tensor_count, cols,
    )
    up_pieces = weight_grad(own_ids, h3, [dhidden], table, batch_count, tensor_count, "grad_up")
    out_pieces = weight_grad(own_ids, dmixed, [scaled], table, batch_count, tensor_count, "grad_out")
    dq, dk, dv, inner = attend_back(q, k, v, spread(dattended), lse, ends, factor)
    dq, dk, dv = collect(dq), collect(dk), collect(dv)
    qkv_pieces = weight_grad(own_ids, h1, [dq, dk, dv], table, batch_count, tensor_count, "grad_qkv")
    grad_in, first_sums = input_grad(zero_ids, dq, dk, dv, x, dresid, norm_gains, qkv_all, plain, tensor_count)

    def scattered(pieces):
        return reduce_scatter(pieces.reshape((-1,) + pieces.shape[3:]), steps)

    down_grad = scattered(down_pieces).T
    up_grad = scattered(up_pieces)
    out_grad = scattered(out_pieces).T
    qkv_grad = scattered(qkv_pieces)
    head_sums = jnp.sum(inner, axis=2).reshape(-1) / lax.dynamic_slice(
        scale_all, (tensor_rank % split * (heads // split),), (heads // split,)
    )
    head_all = lax.dynamic_update_slice(
        jnp.zeros((heads,), F32), head_sums, (tensor_rank % split * (heads // split),)
    )
    gain_parts = [first_sums, gain_sums[:8], gain_sums[8:]]
    vector = jnp.concatenate(
        [jnp.sum(part, axis=0) for part in gain_parts] + [jnp.sum(mid_sums, axis=0), head_all]
    )
    vector = all_sum(vector, steps)
    gains_sum = vector[: 3 * width].reshape(3, width)
    mid_own = lax.dynamic_slice(vector, (3 * width + tensor_rank * local_hidden,), (local_hidden,))
    scale_own = lax.dynamic_slice(
        vector, (3 * width + tensor_count * local_hidden + tensor_rank * local_heads,), (local_heads,)
    )
    return (
        give_micro(block_out, micro_count, split),
        give_micro(grad_in, micro_count, split),
        gains_sum,
        qkv_grad,
        scale_own,
        out_grad,
        up_grad,
        mid_own,
        down_grad,
    )


def solution(mesh):
    in_specs = (
        P(None, ("batch", "tensor"), None),
        P(None, "batch", None),
        P(),
        P(None, "batch", "tensor"),
        P("tensor"),
        P("tensor", "batch"),
        P("batch", "tensor"),
        P("tensor"),
        P("tensor", "batch"),
        P(None, ("batch", "tensor"), None),
    )
    out_specs = (
        P(None, ("batch", "tensor"), None),
        P(None, ("batch", "tensor"), None),
        P(),
        P(None, "batch", "tensor"),
        P("tensor"),
        P("tensor", "batch"),
        P("batch", "tensor"),
        P("tensor"),
        P("tensor", "batch"),
    )
    return jax.shard_map(body, mesh=mesh, in_specs=in_specs, out_specs=out_specs, check_vma=False)
```

time: 1640 us -> 740 us (0.45)
  waiting for transfers between devices: 844 us -> 307 us
  matrix products: 385 us -> 0 us
  Pallas kernels: 0 us -> 285 us
  other arithmetic: 160 us -> 28 us
  local copies, waits for them, and re-layouts: 146 us -> 65.5 us
  blocking collectives: 53.9 us -> 0 us
  starting transfers between devices: 1.18 us -> 30.1 us
  loops' own time: 17.1 us -> 0 us
    dot_general x52 -> x0, matrix products: 385 us -> none  [the longest x8 73.6 us: one_block(): jnp.einsum('qhd,khd->hqk', query_block, all_keys, preferred_element_type=...]
    pallas_call x0 -> x10, Pallas kernels: none -> 285 us  [the longest x1 81.5 us: feed_back(): pl.pallas_call(functools.partial(feed_kernel, table, (0, out_cols, out_co...]
    reduce_scatter x9 -> x0, waiting for transfers between devices: 265 us -> none  [the longest x2 81.5 us: body(): lax.psum_scatter(jnp.einsum('gf,df->gd', hidden_grad, up_full, preferred_...]
    ppermute x0 -> x30, waiting for transfers between devices: none -> 220 us  [swap(): return lax.ppermute(value, axis, [(i, i ^ flip) for i in range(count)])]
    all_gather x12 -> x2, waiting for transfers between devices: 299 us -> 86.3 us  [the longest x1 71.5 us: body(): rest_all = lax.all_gather(rest, ALL, axis=0, tiled=False)]
    psum x1 -> x0, waiting for transfers between devices: 193 us -> none  [body(): lax.psum(jnp.dot(scaled, out_full, preferred_element_type=jnp.float32), '...]
    unnamed x24 -> x2, waiting for transfers between devices: 87.2 us -> 0.7 us
    dynamic_update_slice x8 -> x6, local copies, waits for them, and re-layouts: 82.7 us -> 7.07 us  [the longest x2 4.4 us: take_micro(): lax.dynamic_update_slice(out, swap(sent, 'tensor', flip), (other, 0, 0))]
  transfers between devices with their start and end apart: 23 -> 32, of which waited for: 18 -> 18; matrix products, arithmetic and copies ran while one was open for 37% -> 7% of each run, Pallas kernels for 0% -> 10%
where the time goes in v1:
time: 740 us; the launch traced here: 730 us
  waiting for transfers between devices  307 us (41%)
  Pallas kernels  285 us (39%)
  local copies, waits for them, and re-layouts  65.5 us (9%)
  starting transfers between devices  30.1 us (4%)
  other arithmetic  28 us (4%)
  between operations  15.3 us (2%)
    ppermute x30, waiting for transfers between devices, swap(): return lax.ppermute(value, axis, [(i, i ^ flip) for i in range(count)])  220 us
    pallas_call x1, Pallas kernels, feed_back(): pl.pallas_call(functools.partial(feed_kernel, table, (0, out_cols, out_co...  81.5 us
    all_gather x1, waiting for transfers between devices, body(): rest_all = lax.all_gather(rest, ALL, axis=0, tiled=False)  71.5 us
    pallas_call x1, Pallas kernels, attend_back(): pl.pallas_call(functools.partial(attend_back_kernel, rows, block, factor)...  49.3 us
    pallas_call x4, Pallas kernels, weight_grad(): pl.pallas_call(functools.partial(grad_kernel, batch_table, count), grid_s...  42.5 us
    pallas_call x1, Pallas kernels, hidden_forward(): pl.pallas_call(functools.partial(hidden_kernel, table, 0, out_cols), grid...  41.9 us
    unnamed x113, local copies, waits for them, and re-layouts  33.2 us
    ppermute x30, starting transfers between devices, swap(): return lax.ppermute(value, axis, [(i, i ^ flip) for i in range(count)])  30 us
  transfers between devices with their start and end apart: 32, of which 18 were waited for; matrix products, arithmetic and copies ran while one was open for 7% of the time, Pallas kernels for 10%

profile of v1, /device:TPU:0, one launch (start us, length us, event | category | flops | bytes accessed | tf_op | source)
XLA Modules:
  0.0 730.1 jit_solution(11436417910245042559)
XLA Ops:
  8.0 1.9 pad_maximum_fusion
  11.8 3.0 collective-permute-start
  20.3 50.0 %collective-permute-done.1 = f32[2056]{0:T(1024)S(1)} collective-permute-done((f32[2056]{0:T(1024)S(1)}, f32[2056]{0:T(1024)S(1)}, u32[]{:S(2)}, u32[]{:S(2)}) %collective-permute-start.1) | collective-permute-done | bytes 8256 | tf_op jit(solution)/shard_map/ppermute | solution.py:77
  72.5 3.0 constant_dynamic-update-slice_fusion.6
  75.5 14.8 %all-gather.5.cloned.1.call-done = bf16[96,64,512]{2,1,0:T(8,128)(2,1)} async-done(((bf16[3,64,512]{2,1,0:T(8,128)(2,1)}), bf16[96,64,512]{2,1,0:T(8,128)(2,1)}) %all-gather.5.cloned.1.call-update) | async-done | bytes 6291472 | tf_op jit(solution)/shard_map/all_gather | solution.py:766
  90.2 2.8 copy-done.7
  93.0 24.3 %project.1 = (bf16[1024,1024]{1,0:T(8,128)(2,1)S(1)}, bf16[1024,1024]{1,0:T(8,128)(2,1)S(1)}, bf16[1024,1024]{1,0:T(8,128)(2,1)S(1)}, bf16[1024,1024]{1,0:T(8,128)(2,1)S(1)}) custom-call(s32[2]{0:T(128)S(1)} %broadcast_5_ids_ref.2.ids_ref, bf16[1024,1024]{1,0:T(8,128)(2,1)S(1)} %bitcast.60, f32[3,1024]{1,0:T(4,128)S(1)} %copy-done.8, ...), custom_call_target="tpu_custom_call" | custom-call | flops 6442450944 | bytes 16777216 | tf_op jit(solution)/shard_map/project/pallas_call | solution.py:141
  118.7 23.4 %attend.1 = (bf16[1024,1024]{1,0:T(8,128)(2,1)S(1)}, f32[8,2,1024]{2,1,0:T(2,128)S(1)}) custom-call(s32[4]{0:T(128)S(1)} %bitcast.68, bf16[1024,1024]{1,0:T(8,128)(2,1)S(1)} %get-tuple-element.33.q_ref, bf16[1024,1024]{1,0:T(8,128)(2,1)S(1)} %get-tuple-element.34.k_ref, bf16[1024,1024]{1,0:T(8,128)(2,1)S(1)} %get-tuple-element.35.v_ref, ...), custom_call_target="tpu_custom_call" | custom-call | flops 28000000000 | bytes 8388608 | tf_op jit(solution)/shard_map/attend/pallas_call | solution.py:254
  146.3 71.5 %all-gather.7.cloned.1.call-done = bf16[2048,4608]{1,0:T(8,128)(2,1)} async-done(((bf16[64,4608]{1,0:T(8,128)(2,1)}), bf16[2048,4608]{1,0:T(8,128)(2,1)}) %all-gather.7.cloned.1.call-update) | async-done | bytes 18874384 | tf_op jit(solution)/shard_map/all_gather | solution.py:768
  217.8 41.9 %hidden_forward.1 = (f32[1024,1024]{1,0:T(8,128)}, bf16[1024,1024]{1,0:T(8,128)(2,1)S(1)}, f32[1024,4096]{1,0:T(8,128)}, bf16[1024,4096]{1,0:T(8,128)(2,1)}, f32[1024,128]{1,0:T(8,128)S(1)}) custom-call(s32[2]{0:T(128)S(1)} %broadcast_5_ids_ref.2.ids_ref, bf16[1024,1024]{1,0:T(8,128)(2,1)S(1)} %get-tuple-element.36.scaled_ref.refs_0_, ...), custom_call_target="tpu_custom_call" | custom-call | flops 20000000000 | bytes 41943040 | tf_op jit(solution)/shard_map/hidden_forward/pallas_call | solution.py:370
  261.8 3.4 copy-done.20
  265.2 15.1 %grad_down.1 = bf16[2,2,8,64,2048]{4,3,2,1,0:T(8,128)(2,1)S(1)} custom-call(s32[2]{0:T(128)S(1)} %pad_add_fusion.ids_ref, bf16[1024,1024]{1,0:T(8,128)(2,1)} %bitcast.7.cot_ref.a_ref, bf16[1024,4096]{1,0:T(8,128)(2,1)S(1)} %copy-done.20), custom_call_target="tpu_custom_call" | custom-call | flops 8589934592 | bytes 18874368 | tf_op jit(solution)/shard_map/grad_down/pallas_call | solution.py:592
  280.3 3.2 copy-done.2
  283.5 81.5 %feed_back.1 = (bf16[1024,1024]{1,0:T(8,128)(2,1)}, bf16[1024,4096]{1,0:T(8,128)(2,1)}, f32[1024,1024]{1,0:T(8,128)}, bf16[1024,1024]{1,0:T(8,128)(2,1)}, bf16[1...) custom-call(s32[2]{0:T(128)} %copy-done.10, bf16[1024,4096]{1,0:T(8,128)(2,1)} %get-tuple-element.37.narrow_ref.refs_0_, ...), custom_call_target="tpu_custom_call" | custom-call | flops 44999999488 | bytes 62914560 | tf_op jit(solution)/shard_map/feed_back/pallas_call | solution.py:506
  365.0 49.3 %attend_back.1 = (bf16[1024,1024]{1,0:T(8,128)(2,1)S(1)}, bf16[1024,1024]{1,0:T(8,128)(2,1)S(1)}, bf16[1024,1024]{1,0:T(8,128)(2,1)}, f32[8,2,1024]{2,1,0:T(2,128)S(1)}) custom-call(s32[4]{0:T(128)S(1)} %bitcast.69, bf16[1024,1024]{1,0:T(8,128)(2,1)} %copy-done.25, bf16[1024,1024]{1,0:T(8,128)(2,1)} %copy-done.26, bf16[1024,1024]{1,0:T(8,128)(2,1)} %copy-done.27, ...), custom_call_target="tpu_custom_call" | custom-call | flops 41999998976 | bytes 16777216 | tf_op jit(solution)/shard_map/attend_back/pallas_call | solution.py:282
  414.3 2.3 copy-done.17
  416.6 9.6 %grad_qkv.1 = bf16[2,2,8,3,64,512]{5,4,3,2,1,0:T(8,128)(2,1)S(1)} custom-call(s32[2]{0:T(128)S(1)} %pad_add_fusion.ids_ref, bf16[1024,1024]{1,0:T(8,128)(2,1)S(1)} %copy-done.22, bf16[1024,1024]{1,0:T(8,128)(2,1)S(1)} %get-tuple-element.44.dq_ref.refs_0_, bf16[1024,1024]{1,0:T(8,128)(2,1)S(1)} %get-tuple-element.45.dk_ref.refs_1_, ...), custom_call_target="tpu_custom_call" | custom-call | flops 6442450944 | bytes 14680064 | tf_op jit(solution)/shard_map/grad_qkv/pallas_call | solution.py:592
  426.3 3.1 fusion.13
  429.4 3.5 copy-done.19
  433.0 1.7 copy-done.24
  434.7 13.6 %grad_up.1 = bf16[2,2,8,64,2048]{4,3,2,1,0:T(8,128)(2,1)S(1)} custom-call(s32[2]{0:T(128)S(1)} %pad_add_fusion.ids_ref, bf16[1024,1024]{1,0:T(8,128)(2,1)S(1)} %copy-done.24, bf16[1024,4096]{1,0:T(8,128)(2,1)S(1)} %copy-done.19), custom_call_target="tpu_custom_call" | custom-call | flops 8589934592 | bytes 18874368 | tf_op jit(solution)/shard_map/grad_up/pallas_call | solution.py:592
  448.3 3.9 fusion.12
  452.7 3.8 fusion.11
  456.8 4.2 grad_out.1
  463.0 21.8 %input_grad.1 = (bf16[1024,1024]{1,0:T(8,128)(2,1)S(1)}, f32[8,1024]{1,0:T(8,128)S(1)}) custom-call(s32[2]{0:T(128)S(1)} %copy-done.11, bf16[1024,1024]{1,0:T(8,128)(2,1)S(1)} %get-tuple-element.44.dq_ref.refs_0_, bf16[1024,1024]{1,0:T(8,128)(2,1)S(1)} %copy-done.16, bf16[1024,1024]{1,0:T(8,128)(2,1)S(1)} %copy-done.18, bf16[1024,1024]{1,0:T(8,128)(2,1)S(1)} %bitcast.63, ...), custom_call_target="tpu_custom_call" | custom-call | flops 6442450944 | bytes 23068672 | tf_op jit(solution)/shard_map/input_grad/pallas_call | solution.py:657
  487.9 2.5 collective-permute-done.6
  491.8 2.4 collective-permute-done.7
  495.9 2.3 collective-permute-done.8
  499.6 1.9 collective-permute-start.9
  501.5 1.7 fusion.3
  503.7 3.2 fusion.2
  507.1 1.7 collective-permute-start.11
  508.9 4.1 fusion.1
  517.4 4.1 fusion
  524.3 11.4 %collective-permute-done.16 = bf16[8,64,512]{2,1,0:T(8,128)(2,1)S(1)} collective-permute-done((bf16[8,64,512]{2,1,0:T(8,128)(2,1)S(1)}, bf16[8,64,512]{2,1,0:T(8,128)(2,1)S(1)}, u32[]{:S(2)}, u32[]{:S(2)}) %collective-permute-start.16) | collective-permute-done | bytes 524320 | tf_op jit(solution)/shard_map/ppermute | solution.py:77
  538.0 31.4 %collective-permute-done.11 = bf16[8,3,64,512]{3,2,1,0:T(8,128)(2,1)S(1)} collective-permute-done((bf16[8,3,64,512]{3,2,1,0:T(8,128)(2,1)S(1)}, bf16[8,3,64,512]{3,2,1,0:T(8,128)(2,1)S(1)}, u32[]{:S(2)}, u32[]{:S(2)}) %collective-permute-start.11) | collective-permute-done | bytes 1572896 | tf_op jit(solution)/shard_map/ppermute | solution.py:77
  581.4 2.4 constant_dynamic-update-slice_fusion.5
  583.8 3.2 collective-permute-done.18
  590.6 23.9 %collective-permute-done.21 = bf16[8,64,2048]{2,1,0:T(8,128)(2,1)} collective-permute-done((bf16[8,64,2048]{2,1,0:T(8,128)(2,1)}, bf16[8,64,2048]{2,1,0:T(8,128)(2,1)}, u32[]{:S(2)}, u32[]{:S(2)}) %collective-permute-start.21) | collective-permute-done | bytes 2097184 | tf_op jit(solution)/shard_map/ppermute | solution.py:77
  614.5 2.5 add_convert_fusion.1
  618.7 40.7 %collective-permute-done.26 = bf16[8,64,2048]{2,1,0:T(8,128)(2,1)} collective-permute-done((bf16[8,64,2048]{2,1,0:T(8,128)(2,1)}, bf16[8,64,2048]{2,1,0:T(8,128)(2,1)}, u32[]{:S(2)}, u32[]{:S(2)}) %collective-permute-start.26) | collective-permute-done | bytes 2097184 | tf_op jit(solution)/shard_map/ppermute | solution.py:77
  659.4 2.4 add_convert_fusion
  663.5 14.1 %collective-permute-done.4 = bf16[1,512,1024]{2,1,0:T(8,128)(2,1)S(1)} collective-permute-done((bf16[1,512,1024]{2,1,0:T(8,128)(2,1)}, bf16[1,512,1024]{2,1,0:T(8,128)(2,1)S(1)}, u32[]{:S(2)}, u32[]{:S(2)}) %collective-permute-start.4) | collective-permute-done | bytes 1048608 | tf_op jit(solution)/shard_map/ppermute | solution.py:77
  683.2 4.2 collective-permute-done.14
  688.2 11.7 %collective-permute-done.23 = bf16[2,64,2048]{2,1,0:T(8,128)(2,1)S(1)} collective-permute-done((bf16[2,64,2048]{2,1,0:T(8,128)(2,1)S(1)}, bf16[2,64,2048]{2,1,0:T(8,128)(2,1)S(1)}, u32[]{:S(2)}, u32[]{:S(2)}) %collective-permute-start.23) | collective-permute-done | bytes 524320 | tf_op jit(solution)/shard_map/ppermute | solution.py:77
  700.1 10.5 %collective-permute-done.28 = bf16[2,64,2048]{2,1,0:T(8,128)(2,1)S(1)} collective-permute-done((bf16[2,64,2048]{2,1,0:T(8,128)(2,1)S(1)}, bf16[2,64,2048]{2,1,0:T(8,128)(2,1)S(1)}, u32[]{:S(2)}, u32[]{:S(2)}) %collective-permute-start.28) | collective-permute-done | bytes 524320 | tf_op jit(solution)/shard_map/ppermute | solution.py:77
  710.9 2.8 collective-permute-done.24
  714.6 7.5 %collective-permute-done.29 = bf16[1,64,2048]{2,1,0:T(8,128)(2,1)S(1)} collective-permute-done((bf16[1,64,2048]{2,1,0:T(8,128)(2,1)S(1)}, bf16[1,64,2048]{2,1,0:T(8,128)(2,1)S(1)}, u32[]{:S(2)}, u32[]{:S(2)}) %collective-permute-start.29) | collective-permute-done | bytes 262176 | tf_op jit(solution)/shard_map/ppermute | solution.py:77
  (224 shorter events, 65.4 us)
Async XLA Ops:
  7.2 83.0 %all-gather.5.cloned.1.call-start = ((), (), s32[]{:S(2)}) async-start(), calls=%async_computation | async-start | bytes 6488064 | tf_op jit(solution)/shard_map/all_gather | solution.py:766
  7.9 209.8 %all-gather.7.cloned.1.call-start = ((), (), s32[]{:S(2)}) async-start(), calls=%async_computation.1 | async-start | bytes 19464192 | tf_op jit(solution)/shard_map/all_gather | solution.py:768
  11.8 58.9 %collective-permute-start = (bf16[1,512,1024]{2,1,0:T(8,128)(2,1)S(1)}, bf16[1,512,1024]{2,1,0:T(8,128)(2,1)}, u32[]{:S(2)}, u32[]{:S(2)}) collective-permute-start(bf16[1,512,1024]{2,1,0:T(8,128)(2,1)S(1)} %get-tuple-element.73), channel_id=1, source_target_pairs={{0,1},{1,0},{2,3},{3,2},{4,5},{5,4},{6,7},{7,6},{8,9},{9,8},{10,11... | collective-permute-start | bytes 3145736 | tf_op jit(solution)/shard_map/ppermute | solution.py:77
  17.8 54.6 %collective-permute-start.2 = (bf16[1,512,1024]{2,1,0:T(8,128)(2,1)}, bf16[1,512,1024]{2,1,0:T(8,128)(2,1)}, u32[]{:S(2)}, u32[]{:S(2)}) collective-permute-start(bf16[1,512,1024]{2,1,0:T(8,128)(2,1)} %get-tuple-element.71), channel_id=1, source_target_pairs={{0,1},{1,0},{2,3},{3,2},{4,5},{5,4},{6,7},{7,6},{8,9},{9,8},{10,11... | collective-permute-start | bytes 3145736 | tf_op jit(solution)/shard_map/ppermute | solution.py:77
  18.4 51.9 %collective-permute-start.1 = (f32[2056]{0:T(1024)S(1)}, f32[2056]{0:T(1024)S(1)}, u32[]{:S(2)}, u32[]{:S(2)}) collective-permute-start(f32[2056]{0:T(1024)S(1)} %constant_dynamic-update-slice_fusion), channel_id=1, source_target_pairs={{0,1},{1,0},{2,3},{3,2},{4,5},{5,4},{6,7},{7,6},{8,9},{9,8},{10,11... | collective-permute-start | bytes 24680 | tf_op jit(solution)/shard_map/ppermute | solution.py:77
  70.6 48.1 %copy-start.6 = (f32[1,1024]{1,0:T(1,128)}, f32[1,1024]{1,0:T(1,128)S(1)}, u32[]{:S(2)}) copy-start(f32[1,1024]{1,0:T(1,128)S(1)} %broadcast_in_dim_reshape.3.scale_ref) | copy-start | bytes 12292
  70.7 147.1 %copy-start.5 = (f32[1,1,2,2048]{3,1,2,0:T(1,128)}, f32[1,1,2,2048]{3,1,2,0:T(1,128)S(1)}, u32[]{:S(2)}) copy-start(f32[1,1,2,2048]{3,1,2,0:T(1,128)S(1)} %copy.19) | copy-start | bytes 49156
  71.0 19.2 %copy-start.8 = (f32[3,1024]{1,0:T(4,128)S(1)}, f32[3,1024]{1,0:T(4,128)}, u32[]{:S(2)}) copy-start(f32[3,1024]{1,0:T(4,128)} %gain_ref.7) | copy-start | bytes 36868
  72.4 44.9 %copy-start.3 = (bf16[2,512,1024]{2,1,0:T(8,128)(2,1)}, bf16[2,512,1024]{2,1,0:T(8,128)(2,1)S(1)}, u32[]{:S(2)}) copy-start(bf16[2,512,1024]{2,1,0:T(8,128)(2,1)S(1)} %constant_dynamic-update-slice_fusion.7) | copy-start | bytes 6291460
  93.0 124.7 %copy-start.10 = (s32[2]{0:T(128)}, s32[2]{0:T(128)S(1)}, u32[]{:S(2)}) copy-start(s32[2]{0:T(128)S(1)} %broadcast_5_ids_ref.2.ids_ref) | copy-start | bytes 28
  146.2 113.4 %copy-start.12 = (bf16[1024,1024]{1,0:T(8,128)(2,1)}, bf16[1024,1024]{1,0:T(8,128)(2,1)S(1)}, u32[]{:S(2)}) copy-start(bf16[1024,1024]{1,0:T(8,128)(2,1)S(1)} %get-tuple-element.36.scaled_ref.refs_0_) | copy-start | bytes 6291460
  365.0 49.3 %copy-start.22 = (bf16[1024,1024]{1,0:T(8,128)(2,1)S(1)}, bf16[1024,1024]{1,0:T(8,128)(2,1)}, u32[]{:S(2)}) copy-start(bf16[1024,1024]{1,0:T(8,128)(2,1)} %copy-done.21) | copy-start | bytes 6291460
  429.4 23.2 %slice-start = ((s8[8388608]{0:T(1024)(128)(4,1)}), s8[4194304]{0:T(1024)(128)(4,1)S(1)}, s32[]{:S(2)}) async-start(s8[8388608]{0:T(1024)(128)(4,1)} %bitcast.57), calls=%async_computation.2 | async-start | bytes 8388608
  434.7 18.0 %slice-start.1 = ((s8[8388608]{0:T(1024)(128)(4,1)}), s8[4194304]{0:T(1024)(128)(4,1)S(1)}, s32[]{:S(2)}) async-start(s8[8388608]{0:T(1024)(128)(4,1)} %bitcast.57), calls=%async_computation.3 | async-start | bytes 8388608
  452.2 55.0 %collective-permute-start.20 = (bf16[16,64,2048]{2,1,0:T(8,128)(2,1)}, bf16[16,64,2048]{2,1,0:T(8,128)(2,1)}, u32[]{:S(2)}, u32[]{:S(2)}) collective-permute-start(bf16[16,64,2048]{2,1,0:T(8,128)(2,1)} %bitcast.20), channel_id=1, source_target_pairs={{0,2},{2,0},{4,6},{6,4},{8,10},{10,8},{12,14},{14,12},{16,18},{18,... | collective-permute-start | bytes 12582920 | tf_op jit(solution)/shard_map/ppermute | solution.py:77
  452.4 50.9 %collective-permute-start.10 = (bf16[16,3,64,512]{3,2,1,0:T(8,128)(2,1)}, bf16[16,3,64,512]{3,2,1,0:T(8,128)(2,1)}, u32[]{:S(2)}, u32[]{:S(2)}) collective-permute-start(bf16[16,3,64,512]{3,2,1,0:T(8,128)(2,1)} %bitcast.13), channel_id=1, source_target_pairs={{0,2},{2,0},{4,6},{6,4},{8,10},{10,8},{12,14},{14,12},{16,18},{18,... | collective-permute-start | bytes 9437192 | tf_op jit(solution)/shard_map/ppermute | solution.py:77
  456.5 59.6 %collective-permute-start.25 = (bf16[16,64,2048]{2,1,0:T(8,128)(2,1)}, bf16[16,64,2048]{2,1,0:T(8,128)(2,1)}, u32[]{:S(2)}, u32[]{:S(2)}) collective-permute-start(bf16[16,64,2048]{2,1,0:T(8,128)(2,1)} %bitcast.23), channel_id=1, source_target_pairs={{0,2},{2,0},{4,6},{6,4},{8,10},{10,8},{12,14},{14,12},{16,18},{18,... | collective-permute-start | bytes 12582920 | tf_op jit(solution)/shard_map/ppermute | solution.py:77
  462.3 37.3 %collective-permute-start.15 = (bf16[16,64,512]{2,1,0:T(8,128)(2,1)}, bf16[16,64,512]{2,1,0:T(8,128)(2,1)}, u32[]{:S(2)}, u32[]{:S(2)}) collective-permute-start(bf16[16,64,512]{2,1,0:T(8,128)(2,1)} %bitcast.16), channel_id=1, source_target_pairs={{0,2},{2,0},{4,6},{6,4},{8,10},{10,8},{12,14},{14,12},{16,18},{18,... | collective-permute-start | bytes 3145736 | tf_op jit(solution)/shard_map/ppermute | solution.py:77
  463.0 21.8 %copy-start.45 = (f32[8,4096]{1,0:T(8,128)S(1)}, f32[8,4096]{1,0:T(8,128)}, u32[]{:S(2)}) copy-start(f32[8,4096]{1,0:T(8,128)} %get-tuple-element.51) | copy-start | bytes 393220
  463.0 22.0 %copy-start.46 = (f32[16,1024]{1,0:T(8,128)S(1)}, f32[16,1024]{1,0:T(8,128)}, u32[]{:S(2)}) copy-start(f32[16,1024]{1,0:T(8,128)} %get-tuple-element.50) | copy-start | bytes 196612
  463.0 22.1 %copy-start.49 = (f32[16]{0:T(128)S(1)}, f32[16]{0:T(128)}, u32[]{:S(2)}) copy-start(f32[16]{0:T(128)} %copy-done.48) | copy-start | bytes 196
  485.2 1.3 collective-permute-start.5
  486.4 3.9 collective-permute-start.6
  490.4 3.9 collective-permute-start.7
  494.3 3.9 collective-permute-start.8
  498.2 82.3 %collective-permute-start.3 = (bf16[1,512,1024]{2,1,0:T(8,128)(2,1)}, bf16[1,512,1024]{2,1,0:T(8,128)(2,1)}, u32[]{:S(2)}, u32[]{:S(2)}) collective-permute-start(bf16[1,512,1024]{2,1,0:T(8,128)(2,1)} %get-tuple-element.69), channel_id=1, source_target_pairs={{0,1},{1,0},{2,3},{3,2},{4,5},{5,4},{6,7},{7,6},{8,9},{9,8},{10,11... | collective-permute-start | bytes 3145736 | tf_op jit(solution)/shard_map/ppermute | solution.py:77
  499.6 73.1 %collective-permute-start.9 = (f32[7184]{0:T(1024)S(1)}, f32[7184]{0:T(1024)S(1)}, u32[]{:S(2)}, u32[]{:S(2)}) collective-permute-start(f32[7184]{0:T(1024)S(1)} %add.123), channel_id=1, source_target_pairs={{0,16},{2,18},{4,20},{6,22},{8,24},{10,26},{12,28},{14,30},{16,0},... | collective-permute-start | bytes 86216 | tf_op jit(solution)/shard_map/ppermute | solution.py:77
  503.3 32.4 %collective-permute-start.16 = (bf16[8,64,512]{2,1,0:T(8,128)(2,1)S(1)}, bf16[8,64,512]{2,1,0:T(8,128)(2,1)S(1)}, u32[]{:S(2)}, u32[]{:S(2)}) collective-permute-start(bf16[8,64,512]{2,1,0:T(8,128)(2,1)S(1)} %slice.216), channel_id=1, source_target_pairs={{0,1},{1,0},{2,3},{3,2},{4,5},{5,4},{6,7},{7,6},{8,9},{9,8},{10,11... | collective-permute-start | bytes 1572872 | tf_op jit(solution)/shard_map/ppermute | solution.py:77
  507.1 62.3 %collective-permute-start.11 = (bf16[8,3,64,512]{3,2,1,0:T(8,128)(2,1)S(1)}, bf16[8,3,64,512]{3,2,1,0:T(8,128)(2,1)S(1)}, u32[]{:S(2)}, u32[]{:S(2)}) collective-permute-start(bf16[8,3,64,512]{3,2,1,0:T(8,128)(2,1)S(1)} %slice.206), channel_id=1, source_target_pairs={{0,1},{1,0},{2,3},{3,2},{4,5},{5,4},{6,7},{7,6},{8,9},{9,8},{10,11... | collective-permute-start | bytes 4718600 | tf_op jit(solution)/shard_map/ppermute | solution.py:77
  516.1 98.4 %collective-permute-start.21 = (bf16[8,64,2048]{2,1,0:T(8,128)(2,1)}, bf16[8,64,2048]{2,1,0:T(8,128)(2,1)}, u32[]{:S(2)}, u32[]{:S(2)}) collective-permute-start(bf16[8,64,2048]{2,1,0:T(8,128)(2,1)} %slice.226), channel_id=1, source_target_pairs={{0,1},{1,0},{2,3},{3,2},{4,5},{5,4},{6,7},{7,6},{8,9},{9,8},{10,11... | collective-permute-start | bytes 6291464 | tf_op jit(solution)/shard_map/ppermute | solution.py:77
  535.7 123.7 %collective-permute-start.26 = (bf16[8,64,2048]{2,1,0:T(8,128)(2,1)}, bf16[8,64,2048]{2,1,0:T(8,128)(2,1)}, u32[]{:S(2)}, u32[]{:S(2)}) collective-permute-start(bf16[8,64,2048]{2,1,0:T(8,128)(2,1)} %slice.236), channel_id=1, source_target_pairs={{0,1},{1,0},{2,3},{3,2},{4,5},{5,4},{6,7},{7,6},{8,9},{9,8},{10,11... | collective-permute-start | bytes 6291464 | tf_op jit(solution)/shard_map/ppermute | solution.py:77
  569.4 8.6 %collective-permute-start.17 = (bf16[4,64,512]{2,1,0:T(8,128)(2,1)}, bf16[4,64,512]{2,1,0:T(8,128)(2,1)}, u32[]{:S(2)}, u32[]{:S(2)}) collective-permute-start(bf16[4,64,512]{2,1,0:T(8,128)(2,1)} %slice.218), channel_id=1, source_target_pairs={{0,4},{2,6},{4,0},{6,2},{8,12},{10,14},{12,8},{14,10},{16,20},{18,... | collective-permute-start | bytes 786440 | tf_op jit(solution)/shard_map/ppermute | solution.py:77
  572.7 15.8 %collective-permute-start.12 = (bf16[4,3,64,512]{3,2,1,0:T(8,128)(2,1)S(1)}, bf16[4,3,64,512]{3,2,1,0:T(8,128)(2,1)}, u32[]{:S(2)}, u32[]{:S(2)}) collective-permute-start(bf16[4,3,64,512]{3,2,1,0:T(8,128)(2,1)S(1)} %slice.208), channel_id=1, source_target_pairs={{0,4},{2,6},{4,0},{6,2},{8,12},{10,14},{12,8},{14,10},{16,20},{18,... | collective-permute-start | bytes 2359304 | tf_op jit(solution)/shard_map/ppermute | solution.py:77
  578.1 99.5 %collective-permute-start.4 = (bf16[1,512,1024]{2,1,0:T(8,128)(2,1)}, bf16[1,512,1024]{2,1,0:T(8,128)(2,1)S(1)}, u32[]{:S(2)}, u32[]{:S(2)}) collective-permute-start(bf16[1,512,1024]{2,1,0:T(8,128)(2,1)} %get-tuple-element.67), channel_id=1, source_target_pairs={{0,1},{1,0},{2,3},{3,2},{4,5},{5,4},{6,7},{7,6},{8,9},{9,8},{10,11... | collective-permute-start | bytes 3145736 | tf_op jit(solution)/shard_map/ppermute | solution.py:77
  580.5 6.4 collective-permute-start.18
  581.4 33.1 %copy-start.30 = (bf16[16,64,2048]{2,1,0:T(8,128)(2,1)S(1)}, bf16[16,64,2048]{2,1,0:T(8,128)(2,1)}, u32[]{:S(2)}) copy-start(bf16[16,64,2048]{2,1,0:T(8,128)(2,1)} %copy-done.29) | copy-start | bytes 12582916
  587.0 90.7 %collective-permute-start.19 = (bf16[1,64,512]{2,1,0:T(8,128)(2,1)S(1)}, bf16[1,64,512]{2,1,0:T(8,128)(2,1)S(1)}, u32[]{:S(2)}, u32[]{:S(2)}) collective-permute-start(bf16[1,64,512]{2,1,0:T(8,128)(2,1)S(1)} %slice.222), channel_id=1, source_target_pairs={{0,16},{2,18},{4,20},{6,22},{8,24},{10,26},{12,28},{14,30},{16,0},... | collective-permute-start | bytes 196616 | tf_op jit(solution)/shard_map/ppermute | solution.py:77
  590.0 88.5 %collective-permute-start.13 = (bf16[2,3,64,512]{3,2,1,0:T(8,128)(2,1)S(1)}, bf16[2,3,64,512]{3,2,1,0:T(8,128)(2,1)S(1)}, u32[]{:S(2)}, u32[]{:S(2)}) collective-permute-start(bf16[2,3,64,512]{3,2,1,0:T(8,128)(2,1)S(1)} %slice.210), channel_id=1, source_target_pairs={{0,8},{2,10},{4,12},{6,14},{8,0},{10,2},{12,4},{14,6},{16,24},{18,... | collective-permute-start | bytes 1179656 | tf_op jit(solution)/shard_map/ppermute | solution.py:77
  614.5 44.9 %copy-start.32 = (bf16[16,64,2048]{2,1,0:T(8,128)(2,1)S(1)}, bf16[16,64,2048]{2,1,0:T(8,128)(2,1)}, u32[]{:S(2)}) copy-start(bf16[16,64,2048]{2,1,0:T(8,128)(2,1)} %copy-done.31) | copy-start | bytes 12582916
  617.2 63.0 %collective-permute-start.22 = (bf16[4,64,2048]{2,1,0:T(8,128)(2,1)S(1)}, bf16[4,64,2048]{2,1,0:T(8,128)(2,1)S(1)}, u32[]{:S(2)}, u32[]{:S(2)}) collective-permute-start(bf16[4,64,2048]{2,1,0:T(8,128)(2,1)S(1)} %slice.228), channel_id=1, source_target_pairs={{0,4},{2,6},{4,0},{6,2},{8,12},{10,14},{12,8},{14,10},{16,20},{18,... | collective-permute-start | bytes 3145736 | tf_op jit(solution)/shard_map/ppermute | solution.py:77
  661.9 19.2 %collective-permute-start.27 = (bf16[4,64,2048]{2,1,0:T(8,128)(2,1)S(1)}, bf16[4,64,2048]{2,1,0:T(8,128)(2,1)S(1)}, u32[]{:S(2)}, u32[]{:S(2)}) collective-permute-start(bf16[4,64,2048]{2,1,0:T(8,128)(2,1)S(1)} %slice.238), channel_id=1, source_target_pairs={{0,4},{2,6},{4,0},{6,2},{8,12},{10,14},{12,8},{14,10},{16,20},{18,... | collective-permute-start | bytes 3145736 | tf_op jit(solution)/shard_map/ppermute | solution.py:77
  677.7 22.3 %copy-start.43 = (bf16[2,512,1024]{2,1,0:T(8,128)(2,1)}, bf16[2,512,1024]{2,1,0:T(8,128)(2,1)S(1)}, u32[]{:S(2)}) copy-start(bf16[2,512,1024]{2,1,0:T(8,128)(2,1)S(1)} %constant_dynamic-update-slice_fusion.4) | copy-start | bytes 6291460
  678.6 8.8 %collective-permute-start.14 = (bf16[1,3,64,512]{3,2,1,0:T(8,128)(2,1)S(1)}, bf16[1,3,64,512]{3,2,1,0:T(8,128)(2,1)S(1)}, u32[]{:S(2)}, u32[]{:S(2)}) collective-permute-start(bf16[1,3,64,512]{3,2,1,0:T(8,128)(2,1)S(1)} %slice.212), channel_id=1, source_target_pairs={{0,16},{2,18},{4,20},{6,22},{8,24},{10,26},{12,28},{14,30},{16,0},... | collective-permute-start | bytes 589832 | tf_op jit(solution)/shard_map/ppermute | solution.py:77
  680.6 19.3 %collective-permute-start.23 = (bf16[2,64,2048]{2,1,0:T(8,128)(2,1)S(1)}, bf16[2,64,2048]{2,1,0:T(8,128)(2,1)S(1)}, u32[]{:S(2)}, u32[]{:S(2)}) collective-permute-start(bf16[2,64,2048]{2,1,0:T(8,128)(2,1)S(1)} %slice.230), channel_id=1, source_target_pairs={{0,8},{2,10},{4,12},{6,14},{8,0},{10,2},{12,4},{14,6},{16,24},{18,... | collective-permute-start | bytes 1572872 | tf_op jit(solution)/shard_map/ppermute | solution.py:77
  681.6 29.1 %collective-permute-start.28 = (bf16[2,64,2048]{2,1,0:T(8,128)(2,1)S(1)}, bf16[2,64,2048]{2,1,0:T(8,128)(2,1)S(1)}, u32[]{:S(2)}, u32[]{:S(2)}) collective-permute-start(bf16[2,64,2048]{2,1,0:T(8,128)(2,1)S(1)} %slice.240), channel_id=1, source_target_pairs={{0,8},{2,10},{4,12},{6,14},{8,0},{10,2},{12,4},{14,6},{16,24},{18,... | collective-permute-start | bytes 1572872 | tf_op jit(solution)/shard_map/ppermute | solution.py:77
  700.0 22.9 %copy-start.1 = (s32[2,1,4]{2,1,0:T(1,128)S(1)}, s32[2,1,4]{2,1,0:T(1,128)}, u32[]{:S(2)}) copy-start(s32[2,1,4]{2,1,0:T(1,128)} %param.11) | copy-start | bytes 100
  700.0 13.7 %collective-permute-start.24 = (bf16[1,64,2048]{2,1,0:T(8,128)(2,1)S(1)}, bf16[1,64,2048]{2,1,0:T(8,128)(2,1)S(1)}, u32[]{:S(2)}, u32[]{:S(2)}) collective-permute-start(bf16[1,64,2048]{2,1,0:T(8,128)(2,1)S(1)} %slice.232), channel_id=1, source_target_pairs={{0,16},{2,18},{4,20},{6,22},{8,24},{10,26},{12,28},{14,30},{16,0},... | collective-permute-start | bytes 786440 | tf_op jit(solution)/shard_map/ppermute | solution.py:77
  710.8 11.3 %collective-permute-start.29 = (bf16[1,64,2048]{2,1,0:T(8,128)(2,1)S(1)}, bf16[1,64,2048]{2,1,0:T(8,128)(2,1)S(1)}, u32[]{:S(2)}, u32[]{:S(2)}) collective-permute-start(bf16[1,64,2048]{2,1,0:T(8,128)(2,1)S(1)} %slice.242), channel_id=1, source_target_pairs={{0,16},{2,18},{4,20},{6,22},{8,24},{10,26},{12,28},{14,30},{16,0},... | collective-permute-start | bytes 786440 | tf_op jit(solution)/shard_map/ppermute | solution.py:77
  (37 other events, 151.6 us)
Sparse Core Ops, SparseCore 0:
  10.9 79.2 all-gather.4
  93.2 124.5 all-gather.6

commit v2 on v1

v2 whole, which is shorter than its diff:
```python
import functools
import math

import jax
import jax.numpy as jnp
from jax import lax
from jax.experimental import pallas as pl
from jax.experimental.pallas import tpu as pltpu
from jax.sharding import PartitionSpec as P

eps = 1e-05
SEQ_MOST = 512
F32 = jnp.float32
BF = jnp.bfloat16
ALL = ("batch", "tensor")
GELU_C = math.sqrt(2.0 / math.pi)
GELU_A = 0.044715
STEP = 64


def cost(us):
    return pl.CostEstimate(flops=int(us * 1e9), transcendentals=0, bytes_accessed=1 << 20)


def dotf(a, b, ca, cb):
    return lax.dot_general(a, b, (((ca,), (cb,)), ((), ())), preferred_element_type=F32)


def row_loop(rows, step, fn):
    def one(i, carry):
        fn(pl.multiple_of(i * step, step))
        return carry

    lax.fori_loop(0, rows // step, one, 0)


def normalize(values):
    centred = values - jnp.mean(values, axis=-1, keepdims=True)
    factor = lax.rsqrt(jnp.mean(centred * centred, axis=-1, keepdims=True) + eps)
    return (centred * factor, factor)


def norm_back(unit, factor, grad):
    return factor * (
        grad
        - jnp.mean(grad, axis=-1, keepdims=True)
        - unit * jnp.mean(grad * unit, axis=-1, keepdims=True)
    )


def fold8(values):
    rows, width = values.shape
    return jnp.sum(values.reshape(rows // 8, 8, width), axis=0)


def bits_of(count):
    return count.bit_length() - 1


def gather_steps(batch_count, tensor_count, tensor_first):
    tensor = [("tensor", 1 << k) for k in range(bits_of(tensor_count))]
    plane = [("batch", 2)]
    far = [("batch", 1 << k) for k in reversed(range(2, bits_of(batch_count)))]
    return far + (tensor + plane if tensor_first else plane + tensor) + [("batch", 1)]


def place_table(steps, batch_count, tensor_count):
    batch = jnp.arange(batch_count * tensor_count, dtype=jnp.int32) // tensor_count
    tensor = jnp.arange(batch_count * tensor_count, dtype=jnp.int32) % tensor_count
    batch = jnp.bitwise_xor(batch, lax.axis_index("batch"))
    tensor = jnp.bitwise_xor(tensor, lax.axis_index("tensor"))
    place = jnp.zeros_like(batch)
    for k, (axis, flip) in enumerate(steps):
        apart = (jnp.bitwise_and(batch if axis == "batch" else tensor, flip) != 0).astype(jnp.int32)
        place = place + apart * (1 << k)
    return place


def swap(value, axis, flip):
    count = lax.axis_size(axis)
    return lax.ppermute(value, axis, [(i, i ^ flip) for i in range(count)])


def held(value, after):
    return lax.optimization_barrier((value, after))[0]


class Gather:
    def __init__(self, buffer, steps):
        self.own, self.steps, self.parts = buffer, list(steps), None

    def outgoing(self):
        return self.arrived if len(self.steps) == 1 else self.own

    def go(self, value):
        step = self.steps.pop(0)
        self.arrived = swap(value, *step)
        if not self.steps:
            self.parts[1] = value
        else:
            self.own = value
            if len(self.steps) == 1:
                self.parts = [value, None, swap(value, *self.steps[0]), None]

    def end(self):
        if self.parts is None:
            self.own = jnp.concatenate([self.own, self.arrived], axis=0)
        elif not self.steps:
            self.parts[3] = self.arrived

    def columns(self, start, count, steps):
        return Gather(self.own[..., start : start + count], steps)


class Scatter:
    def __init__(self, keep, send, steps):
        self.keep, self.send, self.steps = keep, send, list(reversed(steps))

    def outgoing(self):
        return (self.send, self.keep)

    def go(self, value):
        send, self.keep = value
        self.arrived = swap(send, *self.steps.pop(0))

    def end(self):
        keep, arrived = self.keep, self.arrived
        half = keep.shape[0] // 2
        if self.steps:
            self.send = (keep[half:].astype(F32) + arrived[half:].astype(F32)).astype(BF)
            self.keep = (keep[:half].astype(F32) + arrived[:half].astype(F32)).astype(BF)
        else:
            self.total = keep[0].astype(F32) + arrived[0].astype(F32)


class Total:
    def __init__(self, value, steps):
        self.value, self.steps = value, list(steps)

    def outgoing(self):
        return self.value

    def go(self, value):
        self.value = value
        self.arrived = swap(value, *self.steps.pop(0))

    def end(self):
        self.value = self.value + self.arrived


class Rows:
    def __init__(self, value, micro_count, split):
        self.value, self.micro_count, self.split = value, micro_count, split
        self.taken = value.ndim == 3
        self.steps = [None]
        self.rank = lax.axis_index("tensor")

    def pieces(self):
        if self.taken:
            return self.value
        return self.value.reshape(self.micro_count, -1, self.value.shape[1])

    def outgoing(self):
        if self.split > 1:
            return []
        return [
            lax.dynamic_index_in_dim(self.pieces(), lax.bitwise_xor(self.rank, flip), 0)
            for flip in range(1, self.micro_count)
        ]

    def go(self, value):
        self.steps = []
        if self.split == 1:
            self.arrived = [swap(one, "tensor", flip + 1) for flip, one in enumerate(value)]
        else:
            self.arrived = [
                lax.all_gather(self.value, "tensor", axis=1 if self.taken else 0, tiled=True)
            ]

    def end(self):
        if self.split == 1:
            pieces = self.pieces()
            out = lax.dynamic_update_slice(
                jnp.zeros_like(pieces),
                lax.dynamic_index_in_dim(pieces, self.rank, 0),
                (self.rank, 0, 0),
            )
            for flip, one in enumerate(self.arrived):
                out = lax.dynamic_update_slice(
                    out, one, (lax.bitwise_xor(self.rank, flip + 1), 0, 0)
                )
            self.result = out.reshape(-1, out.shape[2]) if self.taken else out
            return
        whole = self.arrived[0]
        width = whole.shape[-1]
        if self.taken:
            rows = self.value.shape[0] * self.value.shape[1]
            start = (self.rank // self.split, self.rank % self.split * rows, 0)
            self.result = lax.dynamic_slice(whole, start, (1, rows, width))[0]
        else:
            own = self.value.shape[0] // self.micro_count
            whole = whole.reshape(self.micro_count, -1, width)
            start = (0, self.rank * own, 0)
            self.result = lax.dynamic_slice(whole, start, (self.micro_count, own, width))


def launch(inputs, chains):
    inputs, values = lax.optimization_barrier((inputs, [chain.outgoing() for chain in chains]))
    for chain, value in zip(chains, values):
        chain.go(value)
    return inputs


def land(inputs, chains):
    inputs, values = lax.optimization_barrier((inputs, [chain.arrived for chain in chains]))
    for chain, value in zip(chains, values):
        chain.arrived = value
        chain.end()
    return inputs


def hop(chains, after=()):
    launch(after, chains)
    for chain in chains:
        chain.end()


def columns(parts, order_ref, batch_count, tensor_count, t, start, count, lead=None):
    for first, width, which, w_ref in parts:
        if first <= start < first + width:
            break
    pieces = []
    for b in range(batch_count):
        p = order_ref[(which * batch_count + b) * tensor_count + t]
        here = pl.ds(start - first, count)
        pieces.append(w_ref[p, :, here] if lead is None else w_ref[p, lead, :, here])
    return jnp.concatenate(pieces, axis=0)


def weights(*refs):
    out, first = [], 0
    for n, ref in enumerate(refs):
        out.append((first, ref.shape[-1], n % 2, ref))
        first += ref.shape[-1]
    return out


HBM = pl.BlockSpec(memory_space=pltpu.HBM)


def whole(chain):
    part = chain.parts[0].shape
    return pltpu.VMEM((4 * part[0],) + part[1:], BF)


def in_hbm(*values):
    return [pltpu.with_memory_space_constraint(value, pltpu.HBM) for value in values]


def parts_of(chains):
    return in_hbm(*[part for chain in chains for part in chain.parts])


def load_parts(refs, w, sem):
    count = w.shape[0] // 4
    for n in range(4):
        pltpu.make_async_copy(refs[n], w.at[pl.ds(n * count, count)], sem).start()


def wait_whole(w, sem):
    pltpu.make_async_copy(w, w, sem).wait()


def qkv_kernel(grid_of, factor, count, order_ref, x_ref, gain_ref, *refs):
    batch_count, tensor_count = grid_of
    w_hbm, refs = refs[: 4 * count], refs[4 * count :]
    turned_ref, q_ref, k_ref, v_ref, h1_ref = refs[:5]
    w_refs, sem = refs[5:-1], refs[-1]
    first = pl.program_id(0) == 0

    @pl.when(first)
    def _():
        for n in range(count):
            load_parts(w_hbm[4 * n : 4 * n + 4], w_refs[n], sem.at[n])

    def chunk(r):
        here = pl.ds(r, STEP)
        unit, _ = normalize(x_ref[here, :].astype(F32))
        h1_ref[here, :] = (unit * gain_ref[0:1, :]).astype(BF)

    row_loop(x_ref.shape[0], STEP, chunk)
    turned_ref[...] = h1_ref[...].T

    @pl.when(first)
    def _():
        for n in range(count):
            wait_whole(w_refs[n], sem.at[n])

    parts = weights(*w_refs)
    cols = sum(part[1] for part in parts)
    for c, out in enumerate((q_ref, k_ref, v_ref)):
        for t in range(tensor_count):
            for start, width, _, _ in parts:
                w = columns(parts, order_ref, batch_count, tensor_count, t, start, width, lead=c)
                value = dotf(h1_ref[...], w, 1, 0).astype(BF)
                here = slice(t * cols + start, t * cols + start + width)
                out[:, here] = value * BF(factor) if c == 0 else value


def project(orders, x, gains, chains, grid_of, factor):
    rows, width = x.shape
    block = min(256, rows)
    row = pl.BlockSpec((block, width), lambda i, e: (i, 0))
    return pl.pallas_call(
        functools.partial(qkv_kernel, grid_of, factor, len(chains)),
        grid_spec=pltpu.PrefetchScalarGridSpec(
            num_scalar_prefetch=1,
            grid=(rows // block,),
            in_specs=[row, pl.BlockSpec((3, width), lambda i, e: (0, 0))]
            + [HBM] * (4 * len(chains)),
            out_specs=[pl.BlockSpec((width, block), lambda i, e: (0, i))] + [row] * 3,
            scratch_shapes=[pltpu.VMEM((block, width), BF)]
            + [whole(chain) for chain in chains]
            + [pltpu.SemaphoreType.DMA((len(chains),))],
        ),
        out_shape=[jax.ShapeDtypeStruct((width, rows), BF)]
        + [jax.ShapeDtypeStruct((rows, width), BF)] * 3,
        compiler_params=pltpu.CompilerParams(vmem_limit_bytes=24 << 20),
        cost_estimate=cost(13),
        name="project",
    )(orders, *in_hbm(x), gains, *parts_of(chains))


def spans(rows, block):
    return [
        (first, max(0, (first - SEQ_MOST + 1) // block * block), first + block)
        for first in range(0, rows, block)
    ]


def fill_bias(ends_ref, bias, parts, block):
    for (first, low, high), ref in zip(parts, bias):
        shape = (high - low, block)
        keys = low + lax.broadcasted_iota(jnp.int32, shape, 0)
        queries = first + lax.broadcasted_iota(jnp.int32, shape, 1)
        start = jnp.zeros(shape, jnp.int32)
        for n in range(ends_ref.shape[0]):
            end = ends_ref[n]
            start = jnp.where(queries >= end, end, start)
        ref[...] = jnp.where((keys <= queries) & (keys >= start), 0.0, -1e30).astype(F32)


def attend_kernel(rows, block, ends_ref, q_ref, k_ref, v_ref, scale_ref, o_ref, lse_ref, *bias):
    parts = spans(rows, block)

    @pl.when(pl.program_id(0) == 0)
    def _():
        fill_bias(ends_ref, bias, parts, block)

    lower = lax.broadcasted_iota(jnp.int32, (1, 128), 1) < 64
    for n, (first, low, high) in enumerate(parts):
        q = q_ref[pl.ds(first, block), :]
        heads = []
        for h in range(2):
            own = jnp.where(lower if h == 0 else ~lower, q, jnp.zeros_like(q))
            s = dotf(k_ref[pl.ds(low, high - low), :], own, 1, 1) + bias[n][...]
            most = jnp.max(s, axis=0, keepdims=True)
            p = jnp.exp(s - most)
            total = jnp.sum(p, axis=0, keepdims=True)
            probs = (p * (1.0 / total)).astype(BF)
            lse_ref[0, pl.ds(h, 1), pl.ds(first, block)] = most + jnp.log(total)
            heads.append(dotf(probs, v_ref[pl.ds(low, high - low), :], 0, 0))
        out = jnp.where(lower, heads[0], heads[1]) * scale_ref[...]
        o_ref[pl.ds(first, block), :] = out.astype(BF)


def attend_back_kernel(
    rows, block, factor, ends_ref, q_ref, k_ref, v_ref, da_ref, lse_ref,
    dq_ref, dk_ref, dv_ref, inner_ref, dk_acc, dv_acc, *bias
):
    parts = spans(rows, block)

    @pl.when(pl.program_id(0) == 0)
    def _():
        fill_bias(ends_ref, bias, parts, block)

    lower = lax.broadcasted_iota(jnp.int32, (1, 128), 1) < 64
    dk_acc[...] = jnp.zeros_like(dk_acc)
    dv_acc[...] = jnp.zeros_like(dv_acc)
    for n, (first, low, high) in enumerate(parts):
        here = pl.ds(first, block)
        keys = pl.ds(low, high - low)
        q, da, k, v = q_ref[here, :], da_ref[here, :], k_ref[keys, :], v_ref[keys, :]
        heads = []
        for h in range(2):
            mask = lower if h == 0 else ~lower
            q_own = jnp.where(mask, q, jnp.zeros_like(q))
            da_own = jnp.where(mask, da, jnp.zeros_like(da))
            s = dotf(k, q_own, 1, 1) + bias[n][...]
            p = jnp.exp(s - lse_ref[0, pl.ds(h, 1), here])
            product = p * dotf(v, da_own, 1, 1)
            inner = jnp.sum(product, axis=0, keepdims=True)
            inner_ref[0, pl.ds(h, 1), here] = inner
            ds = (product - p * inner).astype(BF)
            dv_acc[keys, :] += dotf(p.astype(BF), da_own, 1, 0)
            dk_acc[keys, :] += dotf(ds, q_own, 1, 0)
            heads.append(dotf(ds, k, 0, 0))
        dq_ref[here, :] = (jnp.where(lower, heads[0], heads[1]) * factor).astype(BF)
    dk_ref[...] = dk_acc[...].astype(BF)
    dv_ref[...] = dv_acc[...].astype(BF)


def bias_shapes(rows, block):
    return [pltpu.VMEM((high - low, block), F32) for _, low, high in spans(rows, block)]


def pair_of(pairs, tensor_count, parts, n):
    if parts == 1:
        return pairs, lambda i: i
    per_tensor = pairs // tensor_count
    per = per_tensor // parts
    return pairs // parts, lambda i: i // per * per_tensor + n * per + i % per


def attend(q, k, v, scale_row, ends, tensor_count, parts, n, before_out, before_lse):
    rows, width = q.shape
    block = min(256, rows)
    pairs = width // 128
    steps, pair = pair_of(pairs, tensor_count, parts, n)
    col = pl.BlockSpec((rows, 128), lambda i, e: (0, pair(i)))
    earlier = [] if before_out is None else [before_out, before_lse]
    count = len(earlier)

    def kernel(ends_ref, q_ref, k_ref, v_ref, scale_ref, *refs):
        attend_kernel(rows, block, ends_ref, q_ref, k_ref, v_ref, scale_ref, *refs[count:])

    return pl.pallas_call(
        kernel,
        grid_spec=pltpu.PrefetchScalarGridSpec(
            num_scalar_prefetch=1,
            grid=(steps,),
            in_specs=[col, col, col, pl.BlockSpec((1, 128), lambda i, e: (0, pair(i)))]
            + [HBM] * count,
            out_specs=[col, pl.BlockSpec((1, 2, rows), lambda i, e: (pair(i), 0, 0))],
            scratch_shapes=bias_shapes(rows, block),
        ),
        out_shape=[
            jax.ShapeDtypeStruct((rows, width), BF),
            jax.ShapeDtypeStruct((pairs, 2, rows), F32),
        ],
        input_output_aliases={5 + j: j for j in range(count)},
        compiler_params=pltpu.CompilerParams(vmem_limit_bytes=32 << 20),
        cost_estimate=cost(24 / parts),
        name="attend",
    )(ends, *in_hbm(q, k, v), scale_row, *earlier)


def attend_back(q, k, v, da, lse, ends, factor, tensor_count, parts, n):
    rows, width = q.shape
    block = min(256, rows)
    pairs = width // 128
    steps, pair = pair_of(pairs, tensor_count, parts, n)
    col = pl.BlockSpec((rows, 128), lambda i, e: (0, pair(i)))
    out_col = pl.BlockSpec((rows, 128), lambda i, e: (0, i))
    out = jax.ShapeDtypeStruct((rows, width // parts), BF)
    return pl.pallas_call(
        functools.partial(attend_back_kernel, rows, block, factor),
        grid_spec=pltpu.PrefetchScalarGridSpec(
            num_scalar_prefetch=1,
            grid=(steps,),
            in_specs=[col] * 4 + [pl.BlockSpec((1, 2, rows), lambda i, e: (pair(i), 0, 0))],
            out_specs=[out_col] * 3 + [pl.BlockSpec((1, 2, rows), lambda i, e: (i, 0, 0))],
            scratch_shapes=[pltpu.VMEM((rows, 128), F32)] * 2 + bias_shapes(rows, block),
        ),
        out_shape=[out, out, out, jax.ShapeDtypeStruct((steps, 2, rows), F32)],
        compiler_params=pltpu.CompilerParams(vmem_limit_bytes=40 << 20),
        cost_estimate=cost(42 / parts),
        name="attend_back",
    )(ends, *in_hbm(q, k, v, da), lse)


def put_stats(ref, here, values):
    lane = lax.broadcasted_iota(jnp.int32, (1, 128), 1)
    out = values[-1]
    for n in reversed(range(len(values) - 1)):
        out = jnp.where(lane < 16 * (n + 1), values[n], out)
    ref[here, :] = jnp.broadcast_to(out, (values[0].shape[0], 128))


def hidden_kernel(
    grid_of, order_ref, scaled_ref, x_ref, gain_ref, mid_ref, a0, a1, a2, a3, b0, b1, b2, b3,
    unit_ref, turned_ref, hidden_ref, narrow_ref, stat_ref, act, norm_stat, wide, h3_ref, wa, wb, sem
):
    batch_count, tensor_count = grid_of
    block, width = x_ref.shape
    total = hidden_ref.shape[1]
    up_cols = total // tensor_count
    out_cols = width // tensor_count
    get = functools.partial(columns, weights(wa, wb), order_ref, batch_count, tensor_count)
    first = pl.program_id(0) == 0

    @pl.when(first)
    def _():
        load_parts((a0, a1, a2, a3), wa, sem.at[0])
        load_parts((b0, b1, b2, b3), wb, sem.at[1])
        wait_whole(wa, sem.at[0])

    mixed = None
    for t in range(tensor_count):
        part = dotf(scaled_ref[:, t * out_cols : (t + 1) * out_cols], get(t, 0, out_cols), 1, 1)
        mixed = part if mixed is None else mixed + part
    wide[...] = mixed

    def norms(r):
        here = pl.ds(r, STEP)
        unit, factor = normalize(wide[here, :])
        unit_ref[here, :] = unit
        resid = x_ref[here, :].astype(F32) + unit * gain_ref[1:2, :]
        mean3 = jnp.mean(resid, axis=-1, keepdims=True)
        centred = resid - mean3
        factor3 = lax.rsqrt(jnp.mean(centred * centred, axis=-1, keepdims=True) + eps)
        h3_ref[here, :] = (centred * factor3 * gain_ref[2:3, :]).astype(BF)
        put_stats(norm_stat, here, [factor, mean3, factor3])

    row_loop(block, STEP, norms)
    turned_ref[...] = h3_ref[...].T

    @pl.when(first)
    def _():
        wait_whole(wb, sem.at[1])

    chunk = min(256, up_cols // 2)
    sums = jnp.zeros((block, 128), F32)
    squares = jnp.zeros((block, 128), F32)
    for c in range(total // chunk):
        t, off = divmod(c * chunk, up_cols)
        h = dotf(h3_ref[...], get(t, out_cols + off, chunk), 1, 0)
        hidden_ref[:, c * chunk : (c + 1) * chunk] = h
        half = 0.5 * jnp.tanh(h * (GELU_C + (GELU_C * GELU_A) * (h * h))) + 0.5
        a = h * half
        act[:, c * chunk : (c + 1) * chunk] = a
        for j in range(chunk // 128):
            piece = a[:, j * 128 : (j + 1) * 128]
            sums += piece
            squares += piece * piece
    mean = jnp.sum(sums, axis=1, keepdims=True) / total
    spread = jnp.sum(squares, axis=1, keepdims=True) / total - mean * mean
    scale = lax.rsqrt(spread + eps)
    before = norm_stat[...]
    put_stats(stat_ref, slice(None), [mean, scale, before[:, 0:1], before[:, 16:17], before[:, 32:33]])

    def narrow(r):
        here = pl.ds(r, STEP)
        m = stat_ref[here, 0:1]
        s = stat_ref[here, 16:17]
        narrow_ref[here, :] = ((act[here, :] - m) * s * mid_ref[...]).astype(BF)

    row_loop(block, STEP, narrow)


def hidden_forward(orders, scaled, x, gains, mid_row, wa, wb, grid_of, share, earlier):
    rows, width = x.shape
    block = min(256, rows)
    total = mid_row.shape[1]
    blocks = rows // block // share[1]
    first = share[0] * blocks
    row = pl.BlockSpec((block, width), lambda i, e: (first + i, 0))
    wide = pl.BlockSpec((block, total), lambda i, e: (first + i, 0))

    def kernel(order_ref, *refs):
        hidden_kernel(grid_of, order_ref, *refs[:12], *refs[12 + len(earlier) :])

    return pl.pallas_call(
        kernel,
        grid_spec=pltpu.PrefetchScalarGridSpec(
            num_scalar_prefetch=1,
            grid=(blocks,),
            in_specs=[
                row,
                row,
                pl.BlockSpec((3, width), lambda i, e: (0, 0)),
                pl.BlockSpec((1, total), lambda i, e: (0, 0)),
            ]
            + [HBM] * (8 + len(earlier)),
            out_specs=[row, pl.BlockSpec((width, block), lambda i, e: (0, first + i)), wide, wide]
            + [pl.BlockSpec((block, 128), lambda i, e: (first + i, 0))],
            scratch_shapes=[
                pltpu.VMEM((block, total), F32),
                pltpu.VMEM((block, 128), F32),
                pltpu.VMEM((block, width), F32),
                pltpu.VMEM((block, width), BF),
                whole(wa),
                whole(wb),
                pltpu.SemaphoreType.DMA((2,)),
            ],
        ),
        out_shape=[
            jax.ShapeDtypeStruct((rows, width), F32),
            jax.ShapeDtypeStruct((width, rows), BF),
            jax.ShapeDtypeStruct((rows, total), F32),
            jax.ShapeDtypeStruct((rows, total), BF),
            jax.ShapeDtypeStruct((rows, 128), F32),
        ],
        input_output_aliases={13 + n: n for n in range(len(earlier))},
        compiler_params=pltpu.CompilerParams(vmem_limit_bytes=44 << 20),
        cost_estimate=cost(30 / share[1]),
        name="hidden_forward",
    )(orders, *in_hbm(scaled, x), gains, mid_row, *parts_of((wa, wb)), *earlier)


def feed_kernel(grid_of, order_ref, narrow_ref, unit_ref, x_ref, gain_ref, a0, a1, a2, a3, b0, b1, b2, b3, out_ref, wa, wb, sem):
    batch_count, tensor_count = grid_of
    up_cols = narrow_ref.shape[1] // tensor_count
    part_cols = wa.shape[2]
    parts = weights(wa, wb)

    @pl.when(pl.program_id(0) == 0)
    def _():
        load_parts((a0, a1, a2, a3), wa, sem.at[0])
        load_parts((b0, b1, b2, b3), wb, sem.at[1])
        wait_whole(wa, sem.at[0])
        wait_whole(wb, sem.at[1])

    out = x_ref[...].astype(F32) + unit_ref[...] * gain_ref[1:2, :]
    for start in range(0, up_cols, part_cols):
        for t in range(tensor_count):
            w = columns(parts, order_ref, batch_count, tensor_count, t, start, part_cols)
            off = t * up_cols + start
            out += dotf(narrow_ref[:, off : off + part_cols], w, 1, 1)
    out_ref[...] = out.astype(BF)


def feed_forward(orders, narrow, unit, x, gains, wa, wb, grid_of):
    rows, width = x.shape
    block = min(256, rows)
    total = narrow.shape[1]
    row = pl.BlockSpec((block, width), lambda i, e: (i, 0))
    return pl.pallas_call(
        functools.partial(feed_kernel, grid_of),
        grid_spec=pltpu.PrefetchScalarGridSpec(
            num_scalar_prefetch=1,
            grid=(rows // block,),
            in_specs=[pl.BlockSpec((block, total), lambda i, e: (i, 0)), row, row]
            + [pl.BlockSpec((3, width), lambda i, e: (0, 0))]
            + [HBM] * 8,
            out_specs=row,
            scratch_shapes=[whole(wa), whole(wb), pltpu.SemaphoreType.DMA((2,))],
        ),
        out_shape=jax.ShapeDtypeStruct((rows, width), BF),
        compiler_params=pltpu.CompilerParams(vmem_limit_bytes=28 << 20),
        cost_estimate=cost(14),
        name="feed_forward",
    )(orders, *in_hbm(narrow, unit, x), gains, *parts_of((wa, wb)))


def back_kernel(
    grid_of, order_ref, hidden_ref, stat_ref, unit_ref, x_ref, cot_ref, gain_ref, mid_ref,
    scale_ref, da0, da1, da2, da3, db0, db1, db2, db3, a0, a1, a2, a3, b0, b1, b2, b3, dhidden_ref, dresid_ref, turned_ref, dattended_ref,
    gains_ref, dmid_ref, grad, unit_s, slope_s, wide, dmixed_ref, wda, wdb, wa, wb, sem
):
    batch_count, tensor_count = grid_of
    block, width = x_ref.shape
    total = hidden_ref.shape[1]
    up_cols = total // tensor_count
    out_cols = width // tensor_count
    get = functools.partial(columns, weights(wa, wb), order_ref, batch_count, tensor_count)
    get_down = functools.partial(columns, weights(wda, wdb), order_ref, batch_count, tensor_count)
    first = pl.program_id(0) == 0

    @pl.when(first)
    def _():
        load_parts((da0, da1, da2, da3), wda, sem.at[0])
        load_parts((db0, db1, db2, db3), wdb, sem.at[1])
        load_parts((a0, a1, a2, a3), wa, sem.at[2])
        load_parts((b0, b1, b2, b3), wb, sem.at[3])
        gains_ref[...] = jnp.zeros_like(gains_ref)
        dmid_ref[...] = jnp.zeros_like(dmid_ref)
        wait_whole(wda, sem.at[0])
        wait_whole(wdb, sem.at[1])

    chunk = min(256, up_cols // 2)
    mean = stat_ref[:, 0:1]
    scale = stat_ref[:, 16:17]
    back_sum = jnp.zeros((block, 128), F32)
    back_inner = jnp.zeros((block, 128), F32)
    for c in range(total // chunk):
        t, off = divmod(c * chunk, up_cols)
        here = slice(c * chunk, (c + 1) * chunk)
        dn = dotf(cot_ref[...], get_down(t, off, chunk), 1, 0)
        h = hidden_ref[:, here]
        square = h * h
        half = 0.5 * jnp.tanh(h * (GELU_C + (GELU_C * GELU_A) * square)) + 0.5
        a = h * half
        slope_s[:, here] = half + a * (1.0 - half) * (
            2.0 * GELU_C + (6.0 * GELU_C * GELU_A) * square
        )
        unit = (a - mean) * scale
        unit_s[:, here] = unit
        dmid_ref[:, here] += fold8(dn * unit)
        g = dn * mid_ref[:, here]
        grad[:, here] = g
        inner = g * unit
        for j in range(chunk // 128):
            back_sum += g[:, j * 128 : (j + 1) * 128]
            back_inner += inner[:, j * 128 : (j + 1) * 128]
    sum_col = jnp.sum(back_sum, axis=1, keepdims=True) / total
    inner_col = jnp.sum(back_inner, axis=1, keepdims=True) / total

    @pl.when(first)
    def _():
        wait_whole(wa, sem.at[2])
        wait_whole(wb, sem.at[3])

    dh3 = None
    for c in range(total // chunk):
        t, off = divmod(c * chunk, up_cols)
        here = slice(c * chunk, (c + 1) * chunk)
        act_grad = scale * (grad[:, here] - sum_col - unit_s[:, here] * inner_col)
        dhidden = (act_grad * slope_s[:, here]).astype(BF)
        dhidden_ref[:, here] = dhidden
        part = dotf(dhidden, get(t, out_cols + off, chunk), 1, 1)
        dh3 = part if dh3 is None else dh3 + part
    wide[...] = dh3

    def back(r):
        here = pl.ds(r, STEP)
        unit = unit_ref[here, :]
        resid = x_ref[here, :].astype(F32) + unit * gain_ref[1:2, :]
        unit3 = (resid - stat_ref[here, 48:49]) * stat_ref[here, 64:65]
        third = wide[here, :]
        gains_ref[8:16, :] += fold8(third * unit3)
        dresid = cot_ref[here, :].astype(F32) + norm_back(
            unit3, stat_ref[here, 64:65], third * gain_ref[2:3, :]
        )
        dresid_ref[here, :] = dresid
        gains_ref[0:8, :] += fold8(dresid * unit)
        dmixed = norm_back(unit, stat_ref[here, 32:33], dresid * gain_ref[1:2, :])
        dmixed_ref[here, :] = dmixed.astype(BF)

    row_loop(block, STEP, back)
    turned_ref[...] = dmixed_ref[...].T
    for t in range(tensor_count):
        here = slice(t * out_cols, (t + 1) * out_cols)
        dscaled = dotf(dmixed_ref[...], get(t, 0, out_cols), 1, 0)
        dattended_ref[:, here] = (dscaled * scale_ref[:, here]).astype(BF)


def feed_back(orders, hidden, stat, unit, x, cot, gains, mid_row, scale_row, wda, wdb, wa, wb, grid_of):
    rows, width = x.shape
    block = min(256, rows)
    total = mid_row.shape[1]
    row = pl.BlockSpec((block, width), lambda i, e: (i, 0))
    wide = pl.BlockSpec((block, total), lambda i, e: (i, 0))
    return pl.pallas_call(
        functools.partial(back_kernel, grid_of),
        grid_spec=pltpu.PrefetchScalarGridSpec(
            num_scalar_prefetch=1,
            grid=(rows // block,),
            in_specs=[
                wide,
                pl.BlockSpec((block, 128), lambda i, e: (i, 0)),
                row,
                row,
                row,
                pl.BlockSpec((3, width), lambda i, e: (0, 0)),
                pl.BlockSpec((1, total), lambda i, e: (0, 0)),
                pl.BlockSpec((1, width), lambda i, e: (0, 0)),
            ]
            + [HBM] * 16,
            out_specs=[
                wide,
                row,
                pl.BlockSpec((width, block), lambda i, e: (0, i)),
                row,
                pl.BlockSpec((16, width), lambda i, e: (0, 0)),
                pl.BlockSpec((8, total), lambda i, e: (0, 0)),
            ],
            scratch_shapes=[
                pltpu.VMEM((block, total), F32),
                pltpu.VMEM((block, total), F32),
                pltpu.VMEM((block, total), F32),
                pltpu.VMEM((block, width), F32),
                pltpu.VMEM((block, width), BF),
            ]
            + [whole(chain) for chain in (wda, wdb, wa, wb)]
            + [pltpu.SemaphoreType.DMA((4,))],
        ),
        out_shape=[
            jax.ShapeDtypeStruct((rows, total), BF),
            jax.ShapeDtypeStruct((rows, width), F32),
            jax.ShapeDtypeStruct((width, rows), BF),
            jax.ShapeDtypeStruct((rows, width), BF),
            jax.ShapeDtypeStruct((16, width), F32),
            jax.ShapeDtypeStruct((8, total), F32),
        ],
        compiler_params=pltpu.CompilerParams(vmem_limit_bytes=60 << 20),
        cost_estimate=cost(60),
        name="feed_back",
    )(
        orders, *in_hbm(hidden, stat, unit, x, cot), gains, mid_row, scale_row,
        *parts_of((wda, wdb, wa, wb)),
    )


def grad_kernel(grid_of, count, turn, order_ref, a_ref, *refs):
    batch_count, tensor_count = grid_of
    b_refs, keep_ref, send_ref = refs[:count], refs[count], refs[count + 1]
    tensor = pl.program_id(1)
    if turn:
        turned = refs[count + 2]

        @pl.when((pl.program_id(0) == 0) & (tensor == 0))
        def _():
            turned[...] = a_ref[...].T

        a_ref = turned
    half = batch_count * tensor_count // 2
    height = keep_ref.shape[-2]
    second = order_ref[0] >= half
    for c, b_ref in enumerate(b_refs):
        acc = dotf(a_ref[...], b_ref[...], 1, 0).astype(BF)
        for core in range(2):

            @pl.when(second if core else jnp.logical_not(second))
            def _(acc=acc, core=core, c=c):
                for b in range(batch_count):
                    place = lax.bitwise_and(order_ref[b * tensor_count + tensor], half - 1)
                    ref = keep_ref if b % 2 == core else send_ref
                    ref[(place,) if count == 1 else (place, c)] = acc[b * height : (b + 1) * height]


def weight_grad(order, a, bs, grid_of, start, cols, name, turn=False):
    batch_count, tensor_count = grid_of
    width, rows = a.shape[::-1] if turn else a.shape
    part = bs[0].shape[1] // tensor_count
    chunk = min(512, cols)
    per = part // chunk
    height = width // batch_count
    count = len(bs)
    lead = (batch_count * tensor_count // 2,) + (() if count == 1 else (count,)) + (height,)
    zeros = (0,) * len(lead)
    out_spec = pl.BlockSpec(lead + (chunk,), lambda i, t, e: zeros + (i,))
    out = jax.ShapeDtypeStruct(lead + (cols,), BF)
    b_spec = pl.BlockSpec((rows, chunk), lambda i, t, e: (0, t * per + start // chunk + i))
    return pl.pallas_call(
        functools.partial(grad_kernel, grid_of, count, turn),
        grid_spec=pltpu.PrefetchScalarGridSpec(
            num_scalar_prefetch=1,
            grid=(cols // chunk, tensor_count),
            in_specs=[pl.BlockSpec(a.shape, lambda i, t, e: (0, 0))] + [b_spec] * count,
            out_specs=[out_spec, out_spec],
            scratch_shapes=[pltpu.VMEM((width, rows), BF)] if turn else [],
        ),
        out_shape=[out, out],
        compiler_params=pltpu.CompilerParams(vmem_limit_bytes=36 << 20),
        cost_estimate=cost(2.4 * count * cols * tensor_count / 1024),
        name=name,
    )(order, *in_hbm(a, *bs))


def input_kernel(grid_of, count, order_ref, *refs):
    batch_count, tensor_count = grid_of
    grads, refs = refs[: 3 * count], refs[3 * count :]
    x_ref, dresid_ref, gain_ref = refs[:3]
    w_hbm, refs = refs[3 : 3 + 4 * count], refs[3 + 4 * count :]
    out_ref, dgain_ref, wide = refs[:3]
    w_refs, sem = refs[3:-1], refs[-1]
    first = pl.program_id(0) == 0

    @pl.when(first)
    def _():
        for n in range(count):
            load_parts(w_hbm[4 * n : 4 * n + 4], w_refs[n], sem.at[n])
        dgain_ref[...] = jnp.zeros_like(dgain_ref)
        for n in range(count):
            wait_whole(w_refs[n], sem.at[n])

    parts = weights(*w_refs)
    total = None
    for n, (start, width, _, _) in enumerate(parts):
        for c in range(3):
            for t in range(tensor_count):
                w = columns(parts, order_ref, batch_count, tensor_count, t, start, width, lead=c)
                part = dotf(grads[3 * n + c][:, t * width : (t + 1) * width], w, 1, 1)
                total = part if total is None else total + part
    wide[...] = total

    def back(r):
        here = pl.ds(r, STEP)
        unit, factor = normalize(x_ref[here, :].astype(F32))
        grad = wide[here, :]
        dgain_ref[...] += fold8(grad * unit)
        out = dresid_ref[here, :] + norm_back(unit, factor, grad * gain_ref[0:1, :])
        out_ref[here, :] = out.astype(BF)

    row_loop(x_ref.shape[0], STEP, back)


def input_grad(orders, grads, x, dresid, gains, chains, grid_of):
    rows, width = x.shape
    block = min(256, rows)
    row = pl.BlockSpec((block, width), lambda i, e: (i, 0))
    part = pl.BlockSpec((block, width // len(chains)), lambda i, e: (i, 0))
    return pl.pallas_call(
        functools.partial(input_kernel, grid_of, len(chains)),
        grid_spec=pltpu.PrefetchScalarGridSpec(
            num_scalar_prefetch=1,
            grid=(rows // block,),
            in_specs=[part] * len(grads)
            + [row, row, pl.BlockSpec((3, width), lambda i, e: (0, 0))]
            + [HBM] * (4 * len(chains)),
            out_specs=[row, pl.BlockSpec((8, width), lambda i, e: (0, 0))],
            scratch_shapes=[pltpu.VMEM((block, width), F32)]
            + [whole(chain) for chain in chains]
            + [pltpu.SemaphoreType.DMA((len(chains),))],
        ),
        out_shape=[
            jax.ShapeDtypeStruct((rows, width), BF),
            jax.ShapeDtypeStruct((8, width), F32),
        ],
        compiler_params=pltpu.CompilerParams(vmem_limit_bytes=32 << 20),
        cost_estimate=cost(15),
        name="input_grad",
    )(orders, *in_hbm(*grads, x, dresid), gains, *parts_of(chains))


def gather_vector(value, tensor_count):
    rank = lax.axis_index("tensor")
    out = jnp.zeros((tensor_count,) + value.shape, value.dtype)
    for flip in range(tensor_count):
        part = value if flip == 0 else swap(value, "tensor", flip)
        out = lax.dynamic_update_slice(out, part[None], (lax.bitwise_xor(rank, flip), 0))
    return out


def body(
    block_in,
    lengths,
    norm_gains,
    qkv_weight,
    head_scale,
    out_weight,
    up_weight,
    mid_gain,
    down_weight,
    cotangent,
):
    tensor_count = lax.axis_size("tensor")
    batch_count = lax.axis_size("batch")
    tensor_rank = lax.axis_index("tensor")
    batch_rank = lax.axis_index("batch")
    micro_count, own_rows, width = block_in.shape
    if tensor_count % micro_count:
        raise NotImplementedError
    split = tensor_count // micro_count
    micro = tensor_rank // split
    local_heads = head_scale.shape[0]
    heads = local_heads * tensor_count
    head_size = width // heads
    local_hidden = mid_gain.shape[0]
    factor = head_size ** (-0.5)
    grid_of = (batch_count, tensor_count)
    half_cols = local_hidden // 2
    qkv_cols = width // tensor_count
    parts = 2 if qkv_cols % 256 == 0 and split == 1 else 1
    steps = [gather_steps(batch_count, tensor_count, first) for first in (True, False)]
    tables = [place_table(one, batch_count, tensor_count) for one in steps]
    orders = jnp.concatenate(tables)
    far = len(steps[0]) - 2 - bits_of(tensor_count)
    near = bits_of(tensor_count) + 1

    def more(chains, count):
        for _ in range(count):
            hop(chains)

    part_cols = qkv_cols // parts
    up_chunk = min(256, local_hidden // 2)
    out_cols = out_weight.shape[0]
    cut = out_cols + ((local_hidden - out_cols) // 2) // up_chunk * up_chunk
    rows_in = Rows(block_in, micro_count, split)
    qkv = Gather(qkv_weight[None], steps[0])
    launch((), [rows_in, qkv])
    qkv.end()
    for _ in range(far - 1):
        hop([qkv])
    qkv_chains = [
        qkv.columns(n * part_cols, part_cols, steps[n % 2][far:]) for n in range(parts)
    ]
    launch(rows_in.arrived, qkv_chains)
    vectors = gather_vector(
        held(jnp.concatenate([mid_gain, head_scale]), rows_in.arrived), tensor_count
    )
    out_up = Gather(
        held(jnp.concatenate([out_weight.T, up_weight], axis=1)[None], qkv.arrived), steps[0]
    )
    hop([out_up])
    for n in range(near - 1):
        for chain in qkv_chains:
            chain.end()
        launch((), qkv_chains)
    for _ in range(far - 1):
        hop([out_up])
    for chain in qkv_chains:
        chain.end()
    down = Gather(held(down_weight.T[None], out_up.arrived), steps[0])
    wa = out_up.columns(0, cut, steps[0][far:])
    wb = out_up.columns(cut, out_weight.shape[0] + local_hidden - cut, steps[1][far:])
    rows_in.end()
    x = launch(rows_in.result, qkv_chains)
    for chain in qkv_chains:
        chain.end()
    x = launch(x, [wa, wb])

    mid_row = vectors[:, :local_hidden].reshape(1, -1)
    scale_all = vectors[:, local_hidden:].reshape(-1)
    scale_row = jnp.repeat(scale_all, head_size)[None]
    own_lengths = lax.dynamic_index_in_dim(lengths[:, 0], micro, 0, keepdims=False)
    ends = jnp.cumsum(own_lengths).astype(jnp.int32)

    def spread(value):
        if split == 1:
            return value
        groups = [[m * split + s for s in range(split)] for m in range(micro_count)]
        return lax.all_to_all(value, "tensor", 1, 0, tiled=True, axis_index_groups=groups)

    def collect(value):
        if split == 1:
            return value
        groups = [[m * split + s for s in range(split)] for m in range(micro_count)]
        return lax.all_to_all(value, "tensor", 0, 1, tiled=True, axis_index_groups=groups)

    h1, q, k, v = project(orders, x, norm_gains, qkv_chains, grid_of, factor)
    q, k, v = land((q, k, v), [wa, wb])
    q, k, v = spread(q), spread(k), spread(v)
    more([wa, wb], near - 2)
    q = launch(q, [wa, wb, down])
    part = width // split
    scale_part = lax.dynamic_slice(scale_row, (0, tensor_rank % split * part), (1, part))
    scaled, lse = None, None
    for n in range(parts):
        scaled, lse = attend(q, k, v, scale_part, ends, tensor_count, parts, n, scaled, lse)
        if n == 0:
            scaled = land(scaled, [down])
            more([down], far - 2)
            scaled = launch(scaled, [down])
    scaled = land(scaled, [wa, wb, down])
    wda = down.columns(0, half_cols, steps[0][far:])
    wdb = down.columns(half_cols, half_cols, steps[1][far:])
    rows_cot = Rows(cotangent, micro_count, split)
    scaled = launch(scaled, [wa, wb])
    scaled = land(scaled, [wa, wb])
    scaled = collect(launch(scaled, [wda, wdb, rows_cot]))
    forward = []
    shares = 2 if x.shape[0] % 512 == 0 else 1
    for n in range(shares):
        if n:
            forward[0] = land(forward[0], [wda, wdb])
            more([wda, wdb], near - 2)
            forward[0] = launch(forward[0], [wda, wdb])
        forward = list(
            hidden_forward(orders, scaled, x, norm_gains, mid_row, wa, wb, grid_of, (n, shares), forward)
        )
    unit, h3, hidden, narrow, stat = forward
    if shares == 1:
        narrow = land(narrow, [wda, wdb])
        more([wda, wdb], near - 2)
        narrow = launch(narrow, [wda, wdb])
    narrow = land(narrow, [rows_cot, wda])
    cot = rows_cot.result

    def grad_half(n, a, b, name, turn=False):
        keep, send = weight_grad(tables[n], a, [b], grid_of, n * half_cols, half_cols, name, turn)
        return Scatter(keep, send, steps[n])

    def flush(chains):
        for chain in chains:
            while chain.steps:
                hop([chain])
        return [chain.total for chain in chains]

    cot_held = launch(cot, [wda])
    d0 = grad_half(0, cot_held, narrow, "grad_down", True)
    cot_held = launch(cot_held, [d0])
    d1 = grad_half(1, cot_held, narrow, "grad_down", True)
    d1.send = land(d1.send, [d0, wda, wdb])
    hidden = launch(hidden, [d1, d0, wdb])
    hidden = land(hidden, [d1, wdb])
    hidden = launch(hidden, [d1])
    dhidden, dresid, dmixed, dattended, gain_sums, mid_sums = feed_back(
        orders, hidden, stat, unit, x, cot, norm_gains, mid_row, scale_row, wda, wdb, wa, wb, grid_of
    )
    dhidden = land(dhidden, [d0, d1])
    more([d0, d1], near - 2)
    dhidden = launch(dhidden, [d0, d1])
    u0 = grad_half(0, h3, dhidden, "grad_up")
    dhidden = launch(dhidden, [u0])
    u1 = grad_half(1, h3, dhidden, "grad_up")
    u1.send = land(u1.send, [u0, d0, d1])
    narrow = launch(narrow, [u1, u0, d0, d1])
    block_out = feed_forward(orders, narrow, unit, x, norm_gains, wda, wdb, grid_of)
    rows_out = Rows(block_out, micro_count, split)
    dmixed, rows_out.value = land((dmixed, rows_out.value), [u1, d0, d1])
    dmixed = launch(dmixed, [u1, d0, d1])
    keep, send = weight_grad(
        tables[0], dmixed, [scaled], grid_of, 0, out_weight.shape[0], "grad_out"
    )
    o0 = Scatter(keep, send, steps[0])
    o0.send = land(o0.send, [u0])
    da = launch(spread(dattended), [u0, o0])
    halves, grads, inners = [], [], []
    for n in range(parts):
        *three, inner = attend_back(q, k, v, da, lse, ends, factor, tensor_count, parts, n)
        inners.append(inner)
        three = [collect(one) for one in three]
        if n == 0:
            three = land(three, [u0, u1, d0, d1, o0])
            three = launch(three, [o0])
        else:
            three = land(three, [rows_out, halves[0], u0, u1])
            three = launch(three, [halves[0], u0, u1, o0])
        keep, send = weight_grad(tables[n % 2], h1, three, grid_of, 0, part_cols, "grad_qkv")
        halves.append(Scatter(keep, send, steps[n % 2]))
        grads += three
        if n < parts - 1:
            da, halves[0].send = land((da, halves[0].send), [o0])
            da = launch(da, [halves[0], u0, u1, rows_out])
    q_last = halves[-1]
    beside = [u0, u1, o0] if parts > 1 else [o0]
    q_last.send = land(q_last.send, beside)
    dresid = launch(dresid, [q_last])
    dresid = land(dresid, [q_last])
    beside = [one for one in beside if one.steps]
    dresid = launch(dresid, [q_last] + beside)
    grad_in, first_sums = input_grad(orders, grads, x, dresid, norm_gains, qkv_chains, grid_of)
    local = heads // split
    if parts == 1:
        head_sums = jnp.sum(inners[0], axis=-1).reshape(-1)
    else:
        shaped = [jnp.sum(one, axis=-1).reshape(tensor_count, -1) for one in inners]
        head_sums = jnp.concatenate(shaped, axis=1).reshape(-1)
    first_head = tensor_rank % split * local
    head_sums = head_sums / lax.dynamic_slice(scale_all, (first_head,), (local,))
    head_all = lax.dynamic_update_slice(jnp.zeros((heads,), F32), head_sums, (first_head,))
    last = jnp.concatenate(
        [jnp.sum(one, axis=0) for one in (first_sums, gain_sums[:8], gain_sums[8:], mid_sums)]
        + [head_all]
    )
    last = Total(last, steps[0])
    rows_back = Rows(grad_in, micro_count, split)
    last.value = land(last.value, halves + beside)
    launch((), [last, rows_back] + ([] if parts > 1 else [rows_out]) + [one for one in halves + [o0] if one.steps])
    while last.steps:
        tail = [one for one in [last] + halves + [o0] if one.steps]
        for one in tail:
            one.end()
        launch((), tail)
    last.end()
    for one in halves + [o0]:
        if not hasattr(one, "total"):
            one.end()
    if parts == 1:
        rows_out.end()
    rows_back.end()
    block_out, grad_in = rows_out.result, rows_back.result
    vector = last.value
    d_totals, u_totals, o_totals, q_totals = (
        flush([d0, d1]), flush([u0, u1]), flush([o0]), flush(halves)
    )
    down_grad = jnp.concatenate(d_totals, axis=1).T
    up_grad = jnp.concatenate(u_totals, axis=1)
    out_grad = o_totals[0].T
    qkv_grad = jnp.concatenate(q_totals, axis=2)
    gains_sum = vector[: 3 * width].reshape(3, width)
    mid_own = lax.dynamic_slice(vector, (3 * width + tensor_rank * local_hidden,), (local_hidden,))
    scale_own = lax.dynamic_slice(
        vector, (3 * width + tensor_count * local_hidden + tensor_rank * local_heads,), (local_heads,)
    )
    return (
        block_out,
        grad_in,
        gains_sum,
        qkv_grad,
        scale_own,
        out_grad,
        up_grad,
        mid_own,
        down_grad,
    )


def solution(mesh):
    in_specs = (
        P(None, ("batch", "tensor"), None),
        P(None, "batch", None),
        P(),
        P(None, "batch", "tensor"),
        P("tensor"),
        P("tensor", "batch"),
        P("batch", "tensor"),
        P("tensor"),
        P("tensor", "batch"),
        P(None, ("batch", "tensor"), None),
    )
    out_specs = (
        P(None, ("batch", "tensor"), None),
        P(None, ("batch", "tensor"), None),
        P(),
        P(None, "batch", "tensor"),
        P("tensor"),
        P("tensor", "batch"),
        P("batch", "tensor"),
        P("tensor"),
        P("tensor", "batch"),
    )
    return jax.shard_map(body, mesh=mesh, in_specs=in_specs, out_specs=out_specs, check_vma=False)
```

time: 740 us -> 541 us (0.73)
  waiting for transfers between devices: 307 us -> 129 us
  starting transfers between devices: 30.1 us -> 68.5 us
  local copies, waits for them, and re-layouts: 65.5 us -> 30.5 us
  Pallas kernels: 285 us -> 265 us
  between operations: 15.3 us -> 2.4 us
  other arithmetic: 28 us -> 37.4 us
    ppermute x30 -> x75, waiting for transfers between devices: 220 us -> 129 us  [swap(): return lax.ppermute(value, axis, [(i, i ^ flip) for i in range(count)])]
    all_gather x2 -> x0, waiting for transfers between devices: 86.3 us -> none  [the longest x1 71.5 us: body(): rest_all = lax.all_gather(rest, ALL, axis=0, tiled=False)]
    ppermute x30 -> x75, starting transfers between devices: 30 us -> 68.5 us  [swap(): return lax.ppermute(value, axis, [(i, i ^ flip) for i in range(count)])]
    slice x20 -> x1, local copies, waits for them, and re-layouts: 16.5 us -> 0.08 us  [columns(): return Gather(self.own[..., start:start + count], steps)]
    unnamed x113 -> x149, local copies, waits for them, and re-layouts: 33.2 us -> 20.3 us
    pallas_call x9 -> x15, Pallas kernels: 235 us -> 224 us  [the longest x7 59.3 us: weight_grad(): pl.pallas_call(functools.partial(grad_kernel, grid_of, count, turn), grid...]
    pallas_call x1 -> x2, Pallas kernels: 49.3 us -> 41.1 us  [attend_back(): pl.pallas_call(functools.partial(attend_back_kernel, rows, block, factor)...]
    convert_element_type x18 -> x28, other arithmetic: 24 us -> 25.3 us  [end(): (keep[:half].astype(F32) + arrived[:half].astype(F32)).astype(BF)]
  transfers between devices with their start and end apart: 32 -> 75, of which waited for: 18 -> 29; matrix products, arithmetic and copies ran while one was open for 7% -> 6% of each run, Pallas kernels for 10% -> 46%
where the time goes in v2:
time: 541 us; the launch traced here: 532 us
  Pallas kernels  265 us (49%)
  waiting for transfers between devices  129 us (24%)
  starting transfers between devices  68.5 us (13%)
  other arithmetic  37.4 us (7%)
  local copies, waits for them, and re-layouts  30.5 us (6%)
    ppermute x75, waiting for transfers between devices, swap(): return lax.ppermute(value, axis, [(i, i ^ flip) for i in range(count)])  129 us
    ppermute x75, starting transfers between devices, swap(): return lax.ppermute(value, axis, [(i, i ^ flip) for i in range(count)])  68.5 us
    pallas_call x7, Pallas kernels, weight_grad(): pl.pallas_call(functools.partial(grad_kernel, grid_of, count, turn), grid...  59.3 us
    pallas_call x1, Pallas kernels, feed_back(): pl.pallas_call(functools.partial(back_kernel, grid_of), grid_spec=pltpu.P...  48.4 us
    pallas_call x2, Pallas kernels, hidden_forward(): pl.pallas_call(kernel, grid_spec=pltpu.PrefetchScalarGridSpec(num_scalar_...  41.6 us
    pallas_call x2, Pallas kernels, attend_back(): pl.pallas_call(functools.partial(attend_back_kernel, rows, block, factor)...  41.1 us
    convert_element_type x28, other arithmetic, end(): (keep[:half].astype(F32) + arrived[:half].astype(F32)).astype(BF)  25.3 us
    pallas_call x2, Pallas kernels, attend(): pl.pallas_call(kernel, grid_spec=pltpu.PrefetchScalarGridSpec(num_scalar_...  25 us
  transfers between devices with their start and end apart: 75, of which 29 were waited for; matrix products, arithmetic and copies ran while one was open for 6% of the time, Pallas kernels for 46%

profile of v2, /device:TPU:0, one launch (start us, length us, event | category | flops | bytes accessed | tf_op | source)
XLA Modules:
  0.0 532.4 jit_solution(122993795059327112)
XLA Ops:
  4.2 2.9 collective-permute-start
  7.1 2.6 collective-permute-start.1
  9.7 8.9 %collective-permute-done.1 = bf16[1,3,64,512]{3,2,1,0:T(8,128)(2,1)S(1)} collective-permute-done((bf16[1,3,64,512]{3,2,1,0:T(8,128)(2,1)S(1)}, bf16[1,3,64,512]{3,2,1,0:T(8,128)(2,1)S(1)}, u32[]{:S(2)}, u32[]{:S(2)}) %collective-permute-start.1) | collective-permute-done | bytes 196640 | tf_op jit(solution)/shard_map/ppermute | solution.py:81
  19.4 9.3 %collective-permute-done.2 = bf16[2,3,64,512]{3,2,1,0:T(8,128)(2,1)S(1)} collective-permute-done((bf16[2,3,64,512]{3,2,1,0:T(8,128)(2,1)S(1)}, bf16[2,3,64,512]{3,2,1,0:T(8,128)(2,1)S(1)}, u32[]{:S(2)}, u32[]{:S(2)}) %collective-permute-start.2) | collective-permute-done | bytes 393248 | tf_op jit(solution)/shard_map/ppermute | solution.py:81
  33.6 2.7 collective-permute-start.7
  36.2 4.3 collective-permute-done.4
  45.5 4.1 collective-permute-done.7
  52.0 8.6 %collective-permute-done.5.refs_1_.refs_10_ = bf16[8,3,64,256]{3,2,1,0:T(8,128)(2,1)} collective-permute-done((bf16[8,3,64,256]{3,2,1,0:T(8,128)(2,1)}, bf16[8,3,64,256]{3,2,1,0:T(8,128)(2,1)}, u32[]{:S(2)}, u32[]{:S(2)}) %collective-permute-start.5) | collective-permute-done | bytes 786464 | tf_op jit(solution)/shard_map/ppermute | solution.py:81
  62.9 2.5 collective-permute-done.8
  68.1 15.1 %project.1 = (bf16[1024,1024]{1,0:T(8,128)(2,1)S(1)}, bf16[1024,1024]{1,0:T(8,128)(2,1)S(1)}, bf16[1024,1024]{1,0:T(8,128)(2,1)S(1)}, bf16[1024,1024]{1,0:T(8,128)(2,1)S(1)}) custom-call(s32[64]{0:T(128)S(1)} %pad_add_fusion.order_ref, bf16[1024,1024]{1,0:T(8,128)(2,1)} %bitcast.3.x_ref.refs_1_.refs_6_, f32[3,1024]{1,0:T(4,128)S(1)} %copy-done.4, ...), custom_call_target="tpu_custom_call" | custom-call | flops 12999999488 | bytes 1048576 | tf_op jit(solution)/shard_map/project/pallas_call | solution.py:314
  90.8 3.4 collective-permute-start.16
  94.2 12.5 %attend.2 = (bf16[1024,1024]{1,0:T(8,128)(2,1)S(1)}, f32[8,2,1024]{2,1,0:T(2,128)S(1)}) custom-call(s32[4]{0:T(128)S(1)} %bitcast.41, bf16[1024,1024]{1,0:T(8,128)(2,1)} %copy-done.19, bf16[1024,1024]{1,0:T(8,128)(2,1)} %copy-done.20, bf16[1024,1024]{1,0:T(8,128)(2,1)} %copy-done.21, f32[1,1024]{1,0:T(1,128)S(1)} %broadcast_in_dim_reshape.3.scale_ref), custom_call_target="tpu_custom_call" | custom-call | flops 12000000000 | bytes 1048576 | tf_op jit(solution)/shard_map/attend/pallas_call | solution.py:437
  108.6 12.5 %attend.3 = (bf16[1024,1024]{1,0:T(8,128)(2,1)S(1)}, f32[8,2,1024]{2,1,0:T(2,128)S(1)}) custom-call(s32[4]{0:T(128)S(1)} %bitcast.42, bf16[1024,1024]{1,0:T(8,128)(2,1)} %copy-done.19, bf16[1024,1024]{1,0:T(8,128)(2,1)} %copy-done.20, bf16[1024,1024]{1,0:T(8,128)(2,1)} %copy-done.21, ...), custom_call_target="tpu_custom_call", output_to_operand_aliasing={{0}: (5, {}), {1}: (6, {})} | custom-call | flops 12000000000 | bytes 1048576 | tf_op jit(solution)/shard_map/attend/pallas_call | solution.py:437
  122.0 2.3 copy-done.24
  131.2 20.9 %hidden_forward.2 = (f32[1024,1024]{1,0:T(8,128)S(1)}, bf16[1024,1024]{1,0:T(8,128)(2,1)S(1)}, f32[1024,4096]{1,0:T(8,128)}, bf16[1024,4096]{1,0:T(8,128)(2,1)}, f32[1024,128]{1,0:T(8,128)S(1)}) custom-call(s32[64]{0:T(128)S(1)} %pad_add_fusion.order_ref, bf16[1024,1024]{1,0:T(8,128)(2,1)} %copy-done.8, bf16[1024,1024]{1,0:T(8,128)(2,1)} %bitcast.3.x_ref.refs_1_.refs_6_, ...), custom_call_target="tpu_custom_call" | custom-call | flops 15000000512 | bytes 1048576 | tf_op jit(solution)/shard_map/hidden_forward/pallas_call | solution.py:573
  153.6 20.7 %hidden_forward.3 = (f32[1024,1024]{1,0:T(8,128)S(1)}, bf16[1024,1024]{1,0:T(8,128)(2,1)S(1)}, f32[1024,4096]{1,0:T(8,128)}, bf16[1024,4096]{1,0:T(8,128)(2,1)}, f32[1024,128]{1,0:T(8,128)S(1)}) custom-call(s32[64]{0:T(128)S(1)} %pad_add_fusion.order_ref, ...), custom_call_target="tpu_custom_call", output_to_operand_aliasing={{0}: (13, {}), {1}: (14, {}), {2}: (15, {}), {3}: (16, {}),... | custom-call | flops 15000000512 | bytes 1048576 | tf_op jit(solution)/shard_map/hidden_forward/pallas_call | solution.py:573
  174.3 2.0 copy-done.9
  176.9 2.0 copy-done.31
  178.9 9.0 %grad_down.2 = (bf16[16,64,1024]{2,1,0:T(8,128)(2,1)S(1)}, bf16[16,64,1024]{2,1,0:T(8,128)(2,1)S(1)}) custom-call(s32[32]{0:T(128)S(1)} %get-tuple-element.570.order_ref, bf16[1024,1024]{1,0:T(8,128)(2,1)} %bitcast.45, bf16[1024,4096]{1,0:T(8,128)(2,1)} %get-tuple-element.366.refs_0_.narrow_ref), custom_call_target="tpu_custom_call" | custom-call | flops 4800000000 | bytes 1048576 | tf_op jit(solution)/shard_map/grad_down/pallas_call | solution.py:845
  188.7 9.4 %grad_down.3 = (bf16[16,64,1024]{2,1,0:T(8,128)(2,1)S(1)}, bf16[16,64,1024]{2,1,0:T(8,128)(2,1)S(1)}) custom-call(s32[32]{0:T(128)S(1)} %get-tuple-element.569.order_ref, bf16[1024,1024]{1,0:T(8,128)(2,1)} %bitcast.46, bf16[1024,4096]{1,0:T(8,128)(2,1)} %get-tuple-element.366.refs_0_.narrow_ref), custom_call_target="tpu_custom_call" | custom-call | flops 4800000000 | bytes 1048576 | tf_op jit(solution)/shard_map/grad_down/pallas_call | solution.py:845
  198.1 15.4 %collective-permute-done.30.db1.b1 = bf16[8,64,1024]{2,1,0:T(8,128)(2,1)S(1)} collective-permute-done((bf16[8,64,1024]{2,1,0:T(8,128)(2,1)S(1)}, bf16[8,64,1024]{2,1,0:T(8,128)(2,1)S(1)}, u32[]{:S(2)}, u32[]{:S(2)}) %collective-permute-start.30) | collective-permute-done | bytes 1048608 | tf_op jit(solution)/shard_map/ppermute | solution.py:81
  218.8 3.8 collective-permute-done.32.db3.b3
  222.5 2.0 add_convert_fusion.4
  227.1 48.4 %feed_back.1 = (bf16[1024,4096]{1,0:T(8,128)(2,1)}, f32[1024,1024]{1,0:T(8,128)}, bf16[1024,1024]{1,0:T(8,128)(2,1)}, bf16[1024,1024]{1,0:T(8,128)(2,1)}, f32[16,1024]{1,0:T(8,128)}, /*index=5*/f32[8,4096]{1,0:T(8,128)}) custom-call(s32[64]{0:T(128)} %copy-done.6, f32[1024,4096]{1,0:T(8,128)} %get-tuple-element.335.hidden_ref, f32[1024,128]{1,0:T(8,128)} %copy-done.18, ...), custom_call_target="tpu_custom_call" | custom-call | flops 60000002048 | bytes 1048576 | tf_op jit(solution)/shard_map/feed_back/pallas_call | solution.py:754
  278.7 8.5 %grad_up.2 = (bf16[16,64,1024]{2,1,0:T(8,128)(2,1)S(1)}, bf16[16,64,1024]{2,1,0:T(8,128)(2,1)S(1)}) custom-call(s32[32]{0:T(128)S(1)} %get-tuple-element.570.order_ref, bf16[1024,1024]{1,0:T(8,128)(2,1)} %copy-done.10, bf16[1024,4096]{1,0:T(8,128)(2,1)} %get-tuple-element.353.refs_0_), custom_call_target="tpu_custom_call" | custom-call | flops 4800000000 | bytes 1048576 | tf_op jit(solution)/shard_map/grad_up/pallas_call | solution.py:845
  289.8 8.3 %grad_up.3 = (bf16[16,64,1024]{2,1,0:T(8,128)(2,1)S(1)}, bf16[16,64,1024]{2,1,0:T(8,128)(2,1)S(1)}) custom-call(s32[32]{0:T(128)S(1)} %get-tuple-element.569.order_ref, bf16[1024,1024]{1,0:T(8,128)(2,1)} %copy-done.10, bf16[1024,4096]{1,0:T(8,128)(2,1)} %get-tuple-element.353.refs_0_), custom_call_target="tpu_custom_call" | custom-call | flops 4800000000 | bytes 1048576 | tf_op jit(solution)/shard_map/grad_up/pallas_call | solution.py:845
  298.1 3.5 collective-permute-done.38
  307.4 15.9 %feed_forward.1 = bf16[1024,1024]{1,0:T(8,128)(2,1)S(1)} custom-call(s32[64]{0:T(128)S(1)} %copy-done.7, bf16[1024,4096]{1,0:T(8,128)(2,1)} %get-tuple-element.366.refs_0_.narrow_ref, f32[1024,1024]{1,0:T(8,128)} %copy-done.9, bf16[1024,1024]{1,0:T(8,128)(2,1)} %bitcast.3.x_ref.refs_1_.refs_6_, f32[3,1024]{1,0:T(4,128)S(1)} %copy-done.5, ...), custom_call_target="tpu_custom_call" | custom-call | flops 14000000000 | bytes 1048576 | tf_op jit(solution)/shard_map/feed_forward/pallas_call | solution.py:638
  325.8 5.2 grad_out.1
  334.1 2.4 collective-permute-start.46
  337.0 20.5 %attend_back.2 = (bf16[1024,512]{1,0:T(8,128)(2,1)S(1)}, bf16[1024,512]{1,0:T(8,128)(2,1)S(1)}, bf16[1024,512]{1,0:T(8,128)(2,1)S(1)}, f32[4,2,1024]{2,1,0:T(2,128)S(1)}) custom-call(s32[4]{0:T(128)S(1)} %bitcast.43, bf16[1024,1024]{1,0:T(8,128)(2,1)} %copy-done.19, bf16[1024,1024]{1,0:T(8,128)(2,1)} %copy-done.20, bf16[1024,1024]{1,0:T(8,128)(2,1)} %copy-done.21, ...), custom_call_target="tpu_custom_call" | custom-call | flops 20999999488 | bytes 1048576 | tf_op jit(solution)/shard_map/attend_back/pallas_call | solution.py:466
  359.2 9.5 %collective-permute-done.45 = bf16[8,64,1024]{2,1,0:T(8,128)(2,1)S(1)} collective-permute-done((bf16[8,64,1024]{2,1,0:T(8,128)(2,1)S(1)}, bf16[8,64,1024]{2,1,0:T(8,128)(2,1)S(1)}, u32[]{:S(2)}, u32[]{:S(2)}) %collective-permute-start.45) | collective-permute-done | bytes 1048608 | tf_op jit(solution)/shard_map/ppermute | solution.py:81
  370.7 9.4 %grad_qkv.2 = (bf16[16,3,64,256]{3,2,1,0:T(8,128)(2,1)S(1)}, bf16[16,3,64,256]{3,2,1,0:T(8,128)(2,1)S(1)}) custom-call(s32[32]{0:T(128)S(1)} %get-tuple-element.570.order_ref, bf16[1024,1024]{1,0:T(8,128)(2,1)} %copy-done.11, bf16[1024,512]{1,0:T(8,128)(2,1)} %copy-done.12, bf16[1024,512]{1,0:T(8,128)(2,1)} %copy-done.13, bf16[1024,512]{1,0:T(8,128)(2,1)} %copy-done.14), custom_call_target="tpu_custom_call" | custom-call | flops 3600000000 | bytes 1048576 | tf_op jit(solution)/shard_map/grad_qkv/pallas_call | solution.py:845
  380.2 2.5 collective-permute-done.49
  385.8 20.6 %attend_back.3 = (bf16[1024,512]{1,0:T(8,128)(2,1)S(1)}, bf16[1024,512]{1,0:T(8,128)(2,1)S(1)}, bf16[1024,512]{1,0:T(8,128)(2,1)S(1)}, f32[4,2,1024]{2,1,0:T(2,128)S(1)}) custom-call(s32[4]{0:T(128)S(1)} %bitcast.44, bf16[1024,1024]{1,0:T(8,128)(2,1)} %copy-done.19, bf16[1024,1024]{1,0:T(8,128)(2,1)} %copy-done.20, bf16[1024,1024]{1,0:T(8,128)(2,1)} %copy-done.21, ...), custom_call_target="tpu_custom_call" | custom-call | flops 20999999488 | bytes 1048576 | tf_op jit(solution)/shard_map/attend_back/pallas_call | solution.py:466
  414.2 3.4 collective-permute-start.54
  417.6 9.4 %grad_qkv.3 = (bf16[16,3,64,256]{3,2,1,0:T(8,128)(2,1)S(1)}, bf16[16,3,64,256]{3,2,1,0:T(8,128)(2,1)S(1)}) custom-call(s32[32]{0:T(128)S(1)} %get-tuple-element.569.order_ref, bf16[1024,1024]{1,0:T(8,128)(2,1)} %copy-done.11, bf16[1024,512]{1,0:T(8,128)(2,1)} %copy-done.15, bf16[1024,512]{1,0:T(8,128)(2,1)} %copy-done.16, bf16[1024,512]{1,0:T(8,128)(2,1)} %copy-done.17), custom_call_target="tpu_custom_call" | custom-call | flops 3600000000 | bytes 1048576 | tf_op jit(solution)/shard_map/grad_qkv/pallas_call | solution.py:845
  435.6 2.8 add_convert_fusion.8
  438.5 18.6 %input_grad.1 = (bf16[1024,1024]{1,0:T(8,128)(2,1)S(1)}, f32[8,1024]{1,0:T(8,128)S(1)}) custom-call(s32[64]{0:T(128)S(1)} %copy-done.7, bf16[1024,512]{1,0:T(8,128)(2,1)} %copy-done.12, bf16[1024,512]{1,0:T(8,128)(2,1)} %copy-done.13, bf16[1024,512]{1,0:T(8,128)(2,1)} %copy-done.14, bf16[1024,512]{1,0:T(8,128)(2,1)} %copy-done.15, ...), custom_call_target="tpu_custom_call" | custom-call | flops 15000000512 | bytes 1048576 | tf_op jit(solution)/shard_map/input_grad/pallas_call | solution.py:904
  460.0 6.7 %collective-permute-done.60 = bf16[1,64,1024]{2,1,0:T(8,128)(2,1)S(1)} collective-permute-done((bf16[1,64,1024]{2,1,0:T(8,128)(2,1)S(1)}, bf16[1,64,1024]{2,1,0:T(8,128)(2,1)S(1)}, u32[]{:S(2)}, u32[]{:S(2)}) %collective-permute-start.60) | collective-permute-done | bytes 131104 | tf_op jit(solution)/shard_map/ppermute | solution.py:81
  466.8 10.3 %collective-permute-done.59 = bf16[8,3,64,256]{3,2,1,0:T(8,128)(2,1)S(1)} collective-permute-done((bf16[8,3,64,256]{3,2,1,0:T(8,128)(2,1)}, bf16[8,3,64,256]{3,2,1,0:T(8,128)(2,1)S(1)}, u32[]{:S(2)}, u32[]{:S(2)}) %collective-permute-start.59) | collective-permute-done | bytes 786464 | tf_op jit(solution)/shard_map/ppermute | solution.py:81
  481.8 4.7 collective-permute-done.63
  486.6 2.9 collective-permute-done.65
  494.1 5.7 %collective-permute-done.66 = f32[7184]{0:T(1024)S(1)} collective-permute-done((f32[7184]{0:T(1024)S(1)}, f32[7184]{0:T(1024)S(1)}, u32[]{:S(2)}, u32[]{:S(2)}) %collective-permute-start.66) | collective-permute-done | bytes 28768 | tf_op jit(solution)/shard_map/ppermute | solution.py:81
  503.5 12.9 %collective-permute-done.69 = f32[7184]{0:T(1024)S(1)} collective-permute-done((f32[7184]{0:T(1024)S(1)}, f32[7184]{0:T(1024)S(1)}, u32[]{:S(2)}, u32[]{:S(2)}) %collective-permute-start.69) | collective-permute-done | bytes 28768 | tf_op jit(solution)/shard_map/ppermute | solution.py:81
  518.1 2.6 collective-permute-start.72
  521.5 2.1 collective-permute-start.73
  526.5 3.2 collective-permute-done.73
  (365 shorter events, 113.0 us)
Async XLA Ops:
  4.2 26.1 %collective-permute-start = (bf16[1,512,1024]{2,1,0:T(8,128)(2,1)S(1)}, bf16[1,512,1024]{2,1,0:T(8,128)(2,1)S(1)}, u32[]{:S(2)}, u32[]{:S(2)}) collective-permute-start(bf16[1,512,1024]{2,1,0:T(8,128)(2,1)S(1)} %get-tuple-element.253), channel_id=1, source_target_pairs={{0,1},{1,0},{2,3},{3,2},{4,5},{5,4},{6,7},{7,6},{8,9},{9,8},{10,11... | collective-permute-start | bytes 3145736 | tf_op jit(solution)/shard_map/ppermute | solution.py:81
  33.6 16.0 %collective-permute-start.7 = (bf16[1,64,2560]{2,1,0:T(8,128)(2,1)S(1)}, bf16[1,64,2560]{2,1,0:T(8,128)(2,1)S(1)}, u32[]{:S(2)}, u32[]{:S(2)}) collective-permute-start(bf16[1,64,2560]{2,1,0:T(8,128)(2,1)S(1)} %maximum_bitcast_fusion.1), channel_id=1, source_target_pairs={{0,16},{2,18},{4,20},{6,22},{8,24},{10,26},{12,28},{14,30},{16,0},... | collective-permute-start | bytes 983048 | tf_op jit(solution)/shard_map/ppermute | solution.py:81
  42.7 17.9 %collective-permute-start.5 = (bf16[8,3,64,256]{3,2,1,0:T(8,128)(2,1)}, bf16[8,3,64,256]{3,2,1,0:T(8,128)(2,1)}, u32[]{:S(2)}, u32[]{:S(2)}) collective-permute-start(bf16[8,3,64,256]{3,2,1,0:T(8,128)(2,1)} %pad_maximum_fusion.4.refs_0_.refs_9_), channel_id=1, source_target_pairs={{0,4},{2,6},{4,0},{6,2},{8,12},{10,14},{12,8},{14,10},{16,20},{18,... | collective-permute-start | bytes 2359304 | tf_op jit(solution)/shard_map/ppermute | solution.py:81
  44.0 17.7 %collective-permute-start.6 = (bf16[8,3,64,256]{3,2,1,0:T(8,128)(2,1)}, bf16[8,3,64,256]{3,2,1,0:T(8,128)(2,1)}, u32[]{:S(2)}, u32[]{:S(2)}) collective-permute-start(bf16[8,3,64,256]{3,2,1,0:T(8,128)(2,1)} %pad_maximum_fusion.5.refs_4_.refs_13_), channel_id=1, source_target_pairs={{0,1},{1,0},{2,3},{3,2},{4,5},{5,4},{6,7},{7,6},{8,9},{9,8},{10,11... | collective-permute-start | bytes 2359304 | tf_op jit(solution)/shard_map/ppermute | solution.py:81
  49.6 15.8 %collective-permute-start.8 = (bf16[2,64,2560]{2,1,0:T(8,128)(2,1)S(1)}, bf16[2,64,2560]{2,1,0:T(8,128)(2,1)}, u32[]{:S(2)}, u32[]{:S(2)}) collective-permute-start(bf16[2,64,2560]{2,1,0:T(8,128)(2,1)S(1)} %pad_maximum_fusion.7), channel_id=1, source_target_pairs={{0,8},{2,10},{4,12},{6,14},{8,0},{10,2},{12,4},{14,6},{16,24},{18,... | collective-permute-start | bytes 1966088 | tf_op jit(solution)/shard_map/ppermute | solution.py:81
  52.0 15.2 %collective-permute-start.11 = (bf16[8,3,64,256]{3,2,1,0:T(8,128)(2,1)}, bf16[8,3,64,256]{3,2,1,0:T(8,128)(2,1)S(1)}, u32[]{:S(2)}, u32[]{:S(2)}) collective-permute-start(bf16[8,3,64,256]{3,2,1,0:T(8,128)(2,1)} %pad_maximum_fusion.5.refs_4_.refs_13_), channel_id=1, source_target_pairs={{0,2},{2,0},{4,6},{6,4},{8,10},{10,8},{12,14},{14,12},{16,18},{18,... | collective-permute-start | bytes 2359304 | tf_op jit(solution)/shard_map/ppermute | solution.py:81
  66.6 19.3 %collective-permute-start.13 = (bf16[4,64,1280]{2,1,0:T(8,128)(2,1)S(1)}, bf16[4,64,1280]{2,1,0:T(8,128)(2,1)S(1)}, u32[]{:S(2)}, u32[]{:S(2)}) collective-permute-start(bf16[4,64,1280]{2,1,0:T(8,128)(2,1)S(1)} %get-tuple-element.267), channel_id=1, source_target_pairs={{0,1},{1,0},{2,3},{3,2},{4,5},{5,4},{6,7},{7,6},{8,9},{9,8},{10,11... | collective-permute-start | bytes 1966088 | tf_op jit(solution)/shard_map/ppermute | solution.py:81
  67.2 18.7 %collective-permute-start.14 = (bf16[4,64,1280]{2,1,0:T(8,128)(2,1)S(1)}, bf16[4,64,1280]{2,1,0:T(8,128)(2,1)S(1)}, u32[]{:S(2)}, u32[]{:S(2)}) collective-permute-start(bf16[4,64,1280]{2,1,0:T(8,128)(2,1)S(1)} %get-tuple-element.268), channel_id=1, source_target_pairs={{0,4},{2,6},{4,0},{6,2},{8,12},{10,14},{12,8},{14,10},{16,20},{18,... | collective-permute-start | bytes 1966088 | tf_op jit(solution)/shard_map/ppermute | solution.py:81
  87.9 33.2 %collective-permute-start.17 = (bf16[8,64,1280]{2,1,0:T(8,128)(2,1)S(1)}, bf16[8,64,1280]{2,1,0:T(8,128)(2,1)S(1)}, u32[]{:S(2)}, u32[]{:S(2)}) collective-permute-start(bf16[8,64,1280]{2,1,0:T(8,128)(2,1)S(1)} %pad_maximum_fusion.refs_4_.a0), channel_id=1, source_target_pairs={{0,4},{2,6},{4,0},{6,2},{8,12},{10,14},{12,8},{14,10},{16,20},{18,... | collective-permute-start | bytes 3932168 | tf_op jit(solution)/shard_map/ppermute | solution.py:81
  89.1 40.0 %collective-permute-start.22 = (bf16[8,64,1280]{2,1,0:T(8,128)(2,1)S(1)}, bf16[8,64,1280]{2,1,0:T(8,128)(2,1)S(1)}, u32[]{:S(2)}, u32[]{:S(2)}) collective-permute-start(bf16[8,64,1280]{2,1,0:T(8,128)(2,1)S(1)} %pad_maximum_fusion.refs_4_.a0), channel_id=1, source_target_pairs={{0,2},{2,0},{4,6},{6,4},{8,10},{10,8},{12,14},{14,12},{16,18},{18,... | collective-permute-start | bytes 3932168 | tf_op jit(solution)/shard_map/ppermute | solution.py:81
  89.1 32.1 %collective-permute-start.18 = (bf16[8,64,1280]{2,1,0:T(8,128)(2,1)S(1)}, bf16[8,64,1280]{2,1,0:T(8,128)(2,1)S(1)}, u32[]{:S(2)}, u32[]{:S(2)}) collective-permute-start(bf16[8,64,1280]{2,1,0:T(8,128)(2,1)S(1)} %pad_maximum_fusion.1.refs_8_.b0), channel_id=1, source_target_pairs={{0,1},{1,0},{2,3},{3,2},{4,5},{5,4},{6,7},{7,6},{8,9},{9,8},{10,11... | collective-permute-start | bytes 3932168 | tf_op jit(solution)/shard_map/ppermute | solution.py:81
  90.6 38.5 %collective-permute-start.23 = (bf16[8,64,1280]{2,1,0:T(8,128)(2,1)S(1)}, bf16[8,64,1280]{2,1,0:T(8,128)(2,1)S(1)}, u32[]{:S(2)}, u32[]{:S(2)}) collective-permute-start(bf16[8,64,1280]{2,1,0:T(8,128)(2,1)S(1)} %pad_maximum_fusion.1.refs_8_.b0), channel_id=1, source_target_pairs={{0,2},{2,0},{4,6},{6,4},{8,10},{10,8},{12,14},{14,12},{16,18},{18,... | collective-permute-start | bytes 3932168 | tf_op jit(solution)/shard_map/ppermute | solution.py:81
  90.8 15.9 %collective-permute-start.16 = (bf16[1,64,2048]{2,1,0:T(8,128)(2,1)S(1)}, bf16[1,64,2048]{2,1,0:T(8,128)(2,1)S(1)}, u32[]{:S(2)}, u32[]{:S(2)}) collective-permute-start(bf16[1,64,2048]{2,1,0:T(8,128)(2,1)S(1)} %bitcast.48), channel_id=1, source_target_pairs={{0,16},{2,18},{4,20},{6,22},{8,24},{10,26},{12,28},{14,30},{16,0},... | collective-permute-start | bytes 786440 | tf_op jit(solution)/shard_map/ppermute | solution.py:81
  106.8 14.3 %collective-permute-start.19 = (bf16[2,64,2048]{2,1,0:T(8,128)(2,1)S(1)}, bf16[2,64,2048]{2,1,0:T(8,128)(2,1)S(1)}, u32[]{:S(2)}, u32[]{:S(2)}) collective-permute-start(bf16[2,64,2048]{2,1,0:T(8,128)(2,1)S(1)} %pad_maximum_fusion.8), channel_id=1, source_target_pairs={{0,8},{2,10},{4,12},{6,14},{8,0},{10,2},{12,4},{14,6},{16,24},{18,... | collective-permute-start | bytes 1572872 | tf_op jit(solution)/shard_map/ppermute | solution.py:81
  126.1 25.9 %collective-permute-start.24 = (bf16[4,64,1024]{2,1,0:T(8,128)(2,1)S(1)}, bf16[4,64,1024]{2,1,0:T(8,128)(2,1)S(1)}, u32[]{:S(2)}, u32[]{:S(2)}) collective-permute-start(bf16[4,64,1024]{2,1,0:T(8,128)(2,1)S(1)} %get-tuple-element.299), channel_id=1, source_target_pairs={{0,1},{1,0},{2,3},{3,2},{4,5},{5,4},{6,7},{7,6},{8,9},{9,8},{10,11... | collective-permute-start | bytes 1572872 | tf_op jit(solution)/shard_map/ppermute | solution.py:81
  126.7 25.4 %collective-permute-start.25 = (bf16[4,64,1024]{2,1,0:T(8,128)(2,1)S(1)}, bf16[4,64,1024]{2,1,0:T(8,128)(2,1)S(1)}, u32[]{:S(2)}, u32[]{:S(2)}) collective-permute-start(bf16[4,64,1024]{2,1,0:T(8,128)(2,1)S(1)} %get-tuple-element.300), channel_id=1, source_target_pairs={{0,4},{2,6},{4,0},{6,2},{8,12},{10,14},{12,8},{14,10},{16,20},{18,... | collective-permute-start | bytes 1572872 | tf_op jit(solution)/shard_map/ppermute | solution.py:81
  127.6 48.8 %collective-permute-start.26 = (bf16[1,512,1024]{2,1,0:T(8,128)(2,1)}, bf16[1,512,1024]{2,1,0:T(8,128)(2,1)S(1)}, u32[]{:S(2)}, u32[]{:S(2)}) collective-permute-start(bf16[1,512,1024]{2,1,0:T(8,128)(2,1)} %get-tuple-element.311), channel_id=1, source_target_pairs={{0,1},{1,0},{2,3},{3,2},{4,5},{5,4},{6,7},{7,6},{8,9},{9,8},{10,11... | collective-permute-start | bytes 3145736 | tf_op jit(solution)/shard_map/ppermute | solution.py:81
  152.3 24.4 %collective-permute-start.27 = (bf16[8,64,1024]{2,1,0:T(8,128)(2,1)S(1)}, bf16[8,64,1024]{2,1,0:T(8,128)(2,1)S(1)}, u32[]{:S(2)}, u32[]{:S(2)}) collective-permute-start(bf16[8,64,1024]{2,1,0:T(8,128)(2,1)S(1)} %pad_maximum_fusion.2.da0.a0), channel_id=1, source_target_pairs={{0,4},{2,6},{4,0},{6,2},{8,12},{10,14},{12,8},{14,10},{16,20},{18,... | collective-permute-start | bytes 3145736 | tf_op jit(solution)/shard_map/ppermute | solution.py:81
  187.9 25.7 %collective-permute-start.28 = (bf16[16,64,1024]{2,1,0:T(8,128)(2,1)S(1)}, bf16[16,64,1024]{2,1,0:T(8,128)(2,1)S(1)}, u32[]{:S(2)}, u32[]{:S(2)}) collective-permute-start(bf16[16,64,1024]{2,1,0:T(8,128)(2,1)S(1)} %get-tuple-element.321), channel_id=1, source_target_pairs={{0,2},{2,0},{4,6},{6,4},{8,10},{10,8},{12,14},{14,12},{16,18},{18,... | collective-permute-start | bytes 6291464 | tf_op jit(solution)/shard_map/ppermute | solution.py:81
  188.0 25.6 %collective-permute-start.30 = (bf16[8,64,1024]{2,1,0:T(8,128)(2,1)S(1)}, bf16[8,64,1024]{2,1,0:T(8,128)(2,1)S(1)}, u32[]{:S(2)}, u32[]{:S(2)}) collective-permute-start(bf16[8,64,1024]{2,1,0:T(8,128)(2,1)S(1)} %pad_maximum_fusion.3.db0.b0), channel_id=1, source_target_pairs={{0,1},{1,0},{2,3},{3,2},{4,5},{5,4},{6,7},{7,6},{8,9},{9,8},{10,11... | collective-permute-start | bytes 3145736 | tf_op jit(solution)/shard_map/ppermute | solution.py:81
  188.6 25.0 %collective-permute-start.29 = (bf16[8,64,1024]{2,1,0:T(8,128)(2,1)S(1)}, bf16[8,64,1024]{2,1,0:T(8,128)(2,1)S(1)}, u32[]{:S(2)}, u32[]{:S(2)}) collective-permute-start(bf16[8,64,1024]{2,1,0:T(8,128)(2,1)S(1)} %collective-permute-done.27.da1.a1), channel_id=1, source_target_pairs={{0,2},{2,0},{4,6},{6,4},{8,10},{10,8},{12,14},{14,12},{16,18},{18,... | collective-permute-start | bytes 3145736 | tf_op jit(solution)/shard_map/ppermute | solution.py:81
  217.9 57.6 %collective-permute-start.35 = (bf16[8,64,1024]{2,1,0:T(8,128)(2,1)}, bf16[8,64,1024]{2,1,0:T(8,128)(2,1)}, u32[]{:S(2)}, u32[]{:S(2)}) collective-permute-start(bf16[8,64,1024]{2,1,0:T(8,128)(2,1)} %get-tuple-element.343), channel_id=1, source_target_pairs={{0,4},{2,6},{4,0},{6,2},{8,12},{10,14},{12,8},{14,10},{16,20},{18,... | collective-permute-start | bytes 3145736 | tf_op jit(solution)/shard_map/ppermute | solution.py:81
  224.5 51.0 %collective-permute-start.36 = (bf16[8,64,1024]{2,1,0:T(8,128)(2,1)}, bf16[8,64,1024]{2,1,0:T(8,128)(2,1)}, u32[]{:S(2)}, u32[]{:S(2)}) collective-permute-start(bf16[8,64,1024]{2,1,0:T(8,128)(2,1)} %get-tuple-element.344), channel_id=1, source_target_pairs={{0,1},{1,0},{2,3},{3,2},{4,5},{5,4},{6,7},{7,6},{8,9},{9,8},{10,11... | collective-permute-start | bytes 3145736 | tf_op jit(solution)/shard_map/ppermute | solution.py:81
  287.3 15.6 %collective-permute-start.37 = (bf16[16,64,1024]{2,1,0:T(8,128)(2,1)S(1)}, bf16[16,64,1024]{2,1,0:T(8,128)(2,1)S(1)}, u32[]{:S(2)}, u32[]{:S(2)}) collective-permute-start(bf16[16,64,1024]{2,1,0:T(8,128)(2,1)S(1)} %get-tuple-element.355), channel_id=1, source_target_pairs={{0,2},{2,0},{4,6},{6,4},{8,10},{10,8},{12,14},{14,12},{16,18},{18,... | collective-permute-start | bytes 6291464 | tf_op jit(solution)/shard_map/ppermute | solution.py:81
  287.3 14.3 %collective-permute-start.38 = (bf16[4,64,1024]{2,1,0:T(8,128)(2,1)S(1)}, bf16[4,64,1024]{2,1,0:T(8,128)(2,1)S(1)}, u32[]{:S(2)}, u32[]{:S(2)}) collective-permute-start(bf16[4,64,1024]{2,1,0:T(8,128)(2,1)S(1)} %get-tuple-element.356), channel_id=1, source_target_pairs={{0,1},{1,0},{2,3},{3,2},{4,5},{5,4},{6,7},{7,6},{8,9},{9,8},{10,11... | collective-permute-start | bytes 1572872 | tf_op jit(solution)/shard_map/ppermute | solution.py:81
  288.9 14.0 %collective-permute-start.39 = (bf16[4,64,1024]{2,1,0:T(8,128)(2,1)S(1)}, bf16[4,64,1024]{2,1,0:T(8,128)(2,1)S(1)}, u32[]{:S(2)}, u32[]{:S(2)}) collective-permute-start(bf16[4,64,1024]{2,1,0:T(8,128)(2,1)S(1)} %get-tuple-element.357), channel_id=1, source_target_pairs={{0,4},{2,6},{4,0},{6,2},{8,12},{10,14},{12,8},{14,10},{16,20},{18,... | collective-permute-start | bytes 1572872 | tf_op jit(solution)/shard_map/ppermute | solution.py:81
  304.4 19.0 %collective-permute-start.40 = (bf16[16,64,1024]{2,1,0:T(8,128)(2,1)S(1)}, bf16[16,64,1024]{2,1,0:T(8,128)(2,1)S(1)}, u32[]{:S(2)}, u32[]{:S(2)}) collective-permute-start(bf16[16,64,1024]{2,1,0:T(8,128)(2,1)S(1)} %get-tuple-element.367), channel_id=1, source_target_pairs={{0,2},{2,0},{4,6},{6,4},{8,10},{10,8},{12,14},{14,12},{16,18},{18,... | collective-permute-start | bytes 6291464 | tf_op jit(solution)/shard_map/ppermute | solution.py:81
  304.4 18.9 %collective-permute-start.41 = (bf16[2,64,1024]{2,1,0:T(8,128)(2,1)S(1)}, bf16[2,64,1024]{2,1,0:T(8,128)(2,1)S(1)}, u32[]{:S(2)}, u32[]{:S(2)}) collective-permute-start(bf16[2,64,1024]{2,1,0:T(8,128)(2,1)S(1)} %get-tuple-element.368), channel_id=1, source_target_pairs={{0,8},{2,10},{4,12},{6,14},{8,0},{10,2},{12,4},{14,6},{16,24},{18,... | collective-permute-start | bytes 786440 | tf_op jit(solution)/shard_map/ppermute | solution.py:81
  305.8 17.5 %collective-permute-start.42 = (bf16[2,64,1024]{2,1,0:T(8,128)(2,1)S(1)}, bf16[2,64,1024]{2,1,0:T(8,128)(2,1)S(1)}, u32[]{:S(2)}, u32[]{:S(2)}) collective-permute-start(bf16[2,64,1024]{2,1,0:T(8,128)(2,1)S(1)} %get-tuple-element.369), channel_id=1, source_target_pairs={{0,8},{2,10},{4,12},{6,14},{8,0},{10,2},{12,4},{14,6},{16,24},{18,... | collective-permute-start | bytes 786440 | tf_op jit(solution)/shard_map/ppermute | solution.py:81
  306.5 24.9 %collective-permute-start.43 = (bf16[8,64,1024]{2,1,0:T(8,128)(2,1)S(1)}, bf16[8,64,1024]{2,1,0:T(8,128)(2,1)S(1)}, u32[]{:S(2)}, u32[]{:S(2)}) collective-permute-start(bf16[8,64,1024]{2,1,0:T(8,128)(2,1)S(1)} %get-tuple-element.382), channel_id=1, source_target_pairs={{0,4},{2,6},{4,0},{6,2},{8,12},{10,14},{12,8},{14,10},{16,20},{18,... | collective-permute-start | bytes 3145736 | tf_op jit(solution)/shard_map/ppermute | solution.py:81
  331.9 27.4 %collective-permute-start.48 = (bf16[16,64,512]{2,1,0:T(8,128)(2,1)S(1)}, bf16[16,64,512]{2,1,0:T(8,128)(2,1)S(1)}, u32[]{:S(2)}, u32[]{:S(2)}) collective-permute-start(bf16[16,64,512]{2,1,0:T(8,128)(2,1)S(1)} %get-tuple-element.396), channel_id=1, source_target_pairs={{0,2},{2,0},{4,6},{6,4},{8,10},{10,8},{12,14},{14,12},{16,18},{18,... | collective-permute-start | bytes 3145736 | tf_op jit(solution)/shard_map/ppermute | solution.py:81
  332.0 27.3 %collective-permute-start.44 = (bf16[4,64,1024]{2,1,0:T(8,128)(2,1)S(1)}, bf16[4,64,1024]{2,1,0:T(8,128)(2,1)S(1)}, u32[]{:S(2)}, u32[]{:S(2)}) collective-permute-start(bf16[4,64,1024]{2,1,0:T(8,128)(2,1)S(1)} %get-tuple-element.392), channel_id=1, source_target_pairs={{0,1},{1,0},{2,3},{3,2},{4,5},{5,4},{6,7},{7,6},{8,9},{9,8},{10,11... | collective-permute-start | bytes 1572872 | tf_op jit(solution)/shard_map/ppermute | solution.py:81
  332.6 36.2 %collective-permute-start.45 = (bf16[8,64,1024]{2,1,0:T(8,128)(2,1)S(1)}, bf16[8,64,1024]{2,1,0:T(8,128)(2,1)S(1)}, u32[]{:S(2)}, u32[]{:S(2)}) collective-permute-start(bf16[8,64,1024]{2,1,0:T(8,128)(2,1)S(1)} %get-tuple-element.393), channel_id=1, source_target_pairs={{0,1},{1,0},{2,3},{3,2},{4,5},{5,4},{6,7},{7,6},{8,9},{9,8},{10,11... | collective-permute-start | bytes 3145736 | tf_op jit(solution)/shard_map/ppermute | solution.py:81
  334.1 25.1 %collective-permute-start.46 = (bf16[1,64,1024]{2,1,0:T(8,128)(2,1)S(1)}, bf16[1,64,1024]{2,1,0:T(8,128)(2,1)S(1)}, u32[]{:S(2)}, u32[]{:S(2)}) collective-permute-start(bf16[1,64,1024]{2,1,0:T(8,128)(2,1)S(1)} %get-tuple-element.394), channel_id=1, source_target_pairs={{0,16},{2,18},{4,20},{6,22},{8,24},{10,26},{12,28},{14,30},{16,0},... | collective-permute-start | bytes 393224 | tf_op jit(solution)/shard_map/ppermute | solution.py:81
  336.5 22.7 %collective-permute-start.47 = (bf16[1,64,1024]{2,1,0:T(8,128)(2,1)S(1)}, bf16[1,64,1024]{2,1,0:T(8,128)(2,1)S(1)}, u32[]{:S(2)}, u32[]{:S(2)}) collective-permute-start(bf16[1,64,1024]{2,1,0:T(8,128)(2,1)S(1)} %get-tuple-element.395), channel_id=1, source_target_pairs={{0,16},{2,18},{4,20},{6,22},{8,24},{10,26},{12,28},{14,30},{16,0},... | collective-permute-start | bytes 393224 | tf_op jit(solution)/shard_map/ppermute | solution.py:81
  369.1 13.6 %collective-permute-start.49 = (bf16[8,64,512]{2,1,0:T(8,128)(2,1)S(1)}, bf16[8,64,512]{2,1,0:T(8,128)(2,1)S(1)}, u32[]{:S(2)}, u32[]{:S(2)}) collective-permute-start(bf16[8,64,512]{2,1,0:T(8,128)(2,1)S(1)} %get-tuple-element.406), channel_id=1, source_target_pairs={{0,4},{2,6},{4,0},{6,2},{8,12},{10,14},{12,8},{14,10},{16,20},{18,... | collective-permute-start | bytes 1572872 | tf_op jit(solution)/shard_map/ppermute | solution.py:81
  382.7 25.6 %collective-permute-start.51 = (bf16[16,3,64,256]{3,2,1,0:T(8,128)(2,1)S(1)}, bf16[16,3,64,256]{3,2,1,0:T(8,128)(2,1)S(1)}, u32[]{:S(2)}, u32[]{:S(2)}) collective-permute-start(bf16[16,3,64,256]{3,2,1,0:T(8,128)(2,1)S(1)} %get-tuple-element.419), channel_id=1, source_target_pairs={{0,2},{2,0},{4,6},{6,4},{8,10},{10,8},{12,14},{14,12},{16,18},{18,... | collective-permute-start | bytes 4718600 | tf_op jit(solution)/shard_map/ppermute | solution.py:81
  382.7 25.6 %collective-permute-start.50 = (bf16[1,512,1024]{2,1,0:T(8,128)(2,1)S(1)}, bf16[1,512,1024]{2,1,0:T(8,128)(2,1)S(1)}, u32[]{:S(2)}, u32[]{:S(2)}) collective-permute-start(bf16[1,512,1024]{2,1,0:T(8,128)(2,1)S(1)} %get-tuple-element.418), channel_id=1, source_target_pairs={{0,1},{1,0},{2,3},{3,2},{4,5},{5,4},{6,7},{7,6},{8,9},{9,8},{10,11... | collective-permute-start | bytes 3145736 | tf_op jit(solution)/shard_map/ppermute | solution.py:81
  383.2 23.4 %collective-permute-start.53 = (bf16[4,64,1024]{2,1,0:T(8,128)(2,1)S(1)}, bf16[4,64,1024]{2,1,0:T(8,128)(2,1)S(1)}, u32[]{:S(2)}, u32[]{:S(2)}) collective-permute-start(bf16[4,64,1024]{2,1,0:T(8,128)(2,1)S(1)} %get-tuple-element.421), channel_id=1, source_target_pairs={{0,4},{2,6},{4,0},{6,2},{8,12},{10,14},{12,8},{14,10},{16,20},{18,... | collective-permute-start | bytes 1572872 | tf_op jit(solution)/shard_map/ppermute | solution.py:81
  384.1 22.5 %collective-permute-start.52 = (bf16[2,64,1024]{2,1,0:T(8,128)(2,1)S(1)}, bf16[2,64,1024]{2,1,0:T(8,128)(2,1)S(1)}, u32[]{:S(2)}, u32[]{:S(2)}) collective-permute-start(bf16[2,64,1024]{2,1,0:T(8,128)(2,1)S(1)} %get-tuple-element.420), channel_id=1, source_target_pairs={{0,8},{2,10},{4,12},{6,14},{8,0},{10,2},{12,4},{14,6},{16,24},{18,... | collective-permute-start | bytes 786440 | tf_op jit(solution)/shard_map/ppermute | solution.py:81
  411.9 15.2 %collective-permute-start.55 = (bf16[2,64,1024]{2,1,0:T(8,128)(2,1)S(1)}, bf16[2,64,1024]{2,1,0:T(8,128)(2,1)S(1)}, u32[]{:S(2)}, u32[]{:S(2)}) collective-permute-start(bf16[2,64,1024]{2,1,0:T(8,128)(2,1)S(1)} %get-tuple-element.440), channel_id=1, source_target_pairs={{0,8},{2,10},{4,12},{6,14},{8,0},{10,2},{12,4},{14,6},{16,24},{18,... | collective-permute-start | bytes 786440 | tf_op jit(solution)/shard_map/ppermute | solution.py:81
  413.2 13.9 %collective-permute-start.56 = (bf16[4,64,512]{2,1,0:T(8,128)(2,1)S(1)}, bf16[4,64,512]{2,1,0:T(8,128)(2,1)S(1)}, u32[]{:S(2)}, u32[]{:S(2)}) collective-permute-start(bf16[4,64,512]{2,1,0:T(8,128)(2,1)S(1)} %get-tuple-element.441), channel_id=1, source_target_pairs={{0,1},{1,0},{2,3},{3,2},{4,5},{5,4},{6,7},{7,6},{8,9},{9,8},{10,11... | collective-permute-start | bytes 786440 | tf_op jit(solution)/shard_map/ppermute | solution.py:81
  414.2 12.8 %collective-permute-start.54 = (bf16[1,64,1024]{2,1,0:T(8,128)(2,1)S(1)}, bf16[1,64,1024]{2,1,0:T(8,128)(2,1)S(1)}, u32[]{:S(2)}, u32[]{:S(2)}) collective-permute-start(bf16[1,64,1024]{2,1,0:T(8,128)(2,1)S(1)} %get-tuple-element.439), channel_id=1, source_target_pairs={{0,16},{2,18},{4,20},{6,22},{8,24},{10,26},{12,28},{14,30},{16,0},... | collective-permute-start | bytes 393224 | tf_op jit(solution)/shard_map/ppermute | solution.py:81
  431.9 28.2 %collective-permute-start.58 = (bf16[8,3,64,256]{3,2,1,0:T(8,128)(2,1)}, bf16[8,3,64,256]{3,2,1,0:T(8,128)(2,1)}, u32[]{:S(2)}, u32[]{:S(2)}) collective-permute-start(bf16[8,3,64,256]{3,2,1,0:T(8,128)(2,1)} %get-tuple-element.460), channel_id=1, source_target_pairs={{0,4},{2,6},{4,0},{6,2},{8,12},{10,14},{12,8},{14,10},{16,20},{18,... | collective-permute-start | bytes 2359304 | tf_op jit(solution)/shard_map/ppermute | solution.py:81
  457.1 20.0 %collective-permute-start.59 = (bf16[8,3,64,256]{3,2,1,0:T(8,128)(2,1)}, bf16[8,3,64,256]{3,2,1,0:T(8,128)(2,1)S(1)}, u32[]{:S(2)}, u32[]{:S(2)}) collective-permute-start(bf16[8,3,64,256]{3,2,1,0:T(8,128)(2,1)} %get-tuple-element.461), channel_id=1, source_target_pairs={{0,1},{1,0},{2,3},{3,2},{4,5},{5,4},{6,7},{7,6},{8,9},{9,8},{10,11... | collective-permute-start | bytes 2359304 | tf_op jit(solution)/shard_map/ppermute | solution.py:81
  492.7 28.1 %collective-permute-start.74 = (bf16[1,64,512]{2,1,0:T(8,128)(2,1)S(1)}, bf16[1,64,512]{2,1,0:T(8,128)(2,1)S(1)}, u32[]{:S(2)}, u32[]{:S(2)}) collective-permute-start(bf16[1,64,512]{2,1,0:T(8,128)(2,1)S(1)} %get-tuple-element.488), channel_id=1, source_target_pairs={{0,16},{2,18},{4,20},{6,22},{8,24},{10,26},{12,28},{14,30},{16,0},... | collective-permute-start | bytes 196616 | tf_op jit(solution)/shard_map/ppermute | solution.py:81
  492.7 37.8 %collective-permute-start.62 = (bf16[1,512,1024]{2,1,0:T(8,128)(2,1)}, bf16[1,512,1024]{2,1,0:T(8,128)(2,1)S(1)}, u32[]{:S(2)}, u32[]{:S(2)}) collective-permute-start(bf16[1,512,1024]{2,1,0:T(8,128)(2,1)} %get-tuple-element.471), channel_id=1, source_target_pairs={{0,1},{1,0},{2,3},{3,2},{4,5},{5,4},{6,7},{7,6},{8,9},{9,8},{10,11... | collective-permute-start | bytes 3145736 | tf_op jit(solution)/shard_map/ppermute | solution.py:81
  502.7 13.7 %collective-permute-start.69 = (f32[7184]{0:T(1024)S(1)}, f32[7184]{0:T(1024)S(1)}, u32[]{:S(2)}, u32[]{:S(2)}) collective-permute-start(f32[7184]{0:T(1024)S(1)} %add.361), channel_id=1, source_target_pairs={{0,1},{1,0},{2,3},{3,2},{4,5},{5,4},{6,7},{7,6},{8,9},{9,8},{10,11... | collective-permute-start | bytes 86216 | tf_op jit(solution)/shard_map/ppermute | solution.py:81
  (98 other events, 1116.3 us)

commit v3 on v2

--- a/solution.py
+++ b/solution.py
@@ -133,24 +133,49 @@
             self.total = keep[0].astype(F32) + arrived[0].astype(F32)
 
 
+def merged(chains):
+    keep = jnp.concatenate([chain.keep for chain in chains], axis=-1)
+    send = jnp.concatenate([chain.send for chain in chains], axis=-1)
+    return Scatter(keep, send, list(reversed(chains[0].steps)))
+
+
 class Total:
-    def __init__(self, value, steps):
-        self.value, self.steps = value, list(steps)
+    def __init__(self, value, batch_count, tensor_count):
+        self.value, self.grid_of = value, (batch_count, tensor_count)
+        bits = [(flip, 0) for flip in (1 << k for k in range(2, bits_of(batch_count)))]
+        plane = [(2, 0)] + [(0, 1 << k) for k in range(bits_of(tensor_count))]
+        self.steps = [[(1, 0)]]
+        for group in (plane, bits):
+            if len(group) <= 2:
+                spans = [(0, 0)]
+                for flip in group:
+                    spans += [(one[0] ^ flip[0], one[1] ^ flip[1]) for one in spans]
+                self.steps.append(spans[1:])
+            else:
+                self.steps += [[flip] for flip in group]
 
     def outgoing(self):
         return self.value
 
     def go(self, value):
-        self.value = value
-        self.arrived = swap(value, *self.steps.pop(0))
+        batch_count, tensor_count = self.grid_of
+        self.value, self.arrived = value, []
+        for batch, tensor in self.steps.pop(0):
+            pairs = [
+                (b * tensor_count + t, (b ^ batch) * tensor_count + (t ^ tensor))
+                for b in range(batch_count)
+                for t in range(tensor_count)
+            ]
+            self.arrived.append(lax.ppermute(value, ALL, pairs))
 
     def end(self):
-        self.value = self.value + self.arrived
+        for one in self.arrived:
+            self.value = self.value + one
 
 
 class Rows:
-    def __init__(self, value, micro_count, split):
-        self.value, self.micro_count, self.split = value, micro_count, split
+    def __init__(self, value, micro_count, split, cuts=1):
+        self.value, self.micro_count, self.split, self.cuts = value, micro_count, split, cuts
         self.taken = value.ndim == 3
         self.steps = [None]
         self.rank = lax.axis_index("tensor")
@@ -163,15 +188,18 @@
     def outgoing(self):
         if self.split > 1:
             return []
-        return [
-            lax.dynamic_index_in_dim(self.pieces(), lax.bitwise_xor(self.rank, flip), 0)
-            for flip in range(1, self.micro_count)
-        ]
+        sent = []
+        for flip in range(1, self.micro_count):
+            one = lax.dynamic_index_in_dim(self.pieces(), lax.bitwise_xor(self.rank, flip), 0)
+            sent += [one[:, n * (one.shape[1] // self.cuts) :][:, : one.shape[1] // self.cuts] for n in range(self.cuts)]
+        return sent
 
     def go(self, value):
         self.steps = []
         if self.split == 1:
-            self.arrived = [swap(one, "tensor", flip + 1) for flip, one in enumerate(value)]
+            self.arrived = [
+                swap(one, "tensor", n // self.cuts + 1) for n, one in enumerate(value)
+            ]
         else:
             self.arrived = [
                 lax.all_gather(self.value, "tensor", axis=1 if self.taken else 0, tiled=True)
@@ -185,9 +213,10 @@
                 lax.dynamic_index_in_dim(pieces, self.rank, 0),
                 (self.rank, 0, 0),
             )
-            for flip, one in enumerate(self.arrived):
+            for n, one in enumerate(self.arrived):
+                other = lax.bitwise_xor(self.rank, n // self.cuts + 1)
                 out = lax.dynamic_update_slice(
-                    out, one, (lax.bitwise_xor(self.rank, flip + 1), 0, 0)
+                    out, one, (other, n % self.cuts * one.shape[1], 0)
                 )
             self.result = out.reshape(-1, out.shape[2]) if self.taken else out
             return
@@ -323,8 +352,8 @@
             + [whole(chain) for chain in chains]
             + [pltpu.SemaphoreType.DMA((len(chains),))],
         ),
-        out_shape=[jax.ShapeDtypeStruct((width, rows), BF)]
-        + [jax.ShapeDtypeStruct((rows, width), BF)] * 3,
+        out_shape=[pltpu.HBM((width, rows), BF)]
+        + [pltpu.HBM((rows, width), BF)] * 3,
         compiler_params=pltpu.CompilerParams(vmem_limit_bytes=24 << 20),
         cost_estimate=cost(13),
         name="project",
@@ -445,8 +474,8 @@
             scratch_shapes=bias_shapes(rows, block),
         ),
         out_shape=[
-            jax.ShapeDtypeStruct((rows, width), BF),
-            jax.ShapeDtypeStruct((pairs, 2, rows), F32),
+            pltpu.HBM((rows, width), BF),
+            pltpu.HBM((pairs, 2, rows), F32),
         ],
         input_output_aliases={5 + j: j for j in range(count)},
         compiler_params=pltpu.CompilerParams(vmem_limit_bytes=32 << 20),
@@ -462,7 +491,7 @@
     steps, pair = pair_of(pairs, tensor_count, parts, n)
     col = pl.BlockSpec((rows, 128), lambda i, e: (0, pair(i)))
     out_col = pl.BlockSpec((rows, 128), lambda i, e: (0, i))
-    out = jax.ShapeDtypeStruct((rows, width // parts), BF)
+    out = pltpu.HBM((rows, width // parts), BF)
     return pl.pallas_call(
         functools.partial(attend_back_kernel, rows, block, factor),
         grid_spec=pltpu.PrefetchScalarGridSpec(
@@ -472,7 +501,7 @@
             out_specs=[out_col] * 3 + [pl.BlockSpec((1, 2, rows), lambda i, e: (i, 0, 0))],
             scratch_shapes=[pltpu.VMEM((rows, 128), F32)] * 2 + bias_shapes(rows, block),
         ),
-        out_shape=[out, out, out, jax.ShapeDtypeStruct((steps, 2, rows), F32)],
+        out_shape=[out, out, out, pltpu.HBM((steps, 2, rows), F32)],
         compiler_params=pltpu.CompilerParams(vmem_limit_bytes=40 << 20),
         cost_estimate=cost(42 / parts),
         name="attend_back",
@@ -595,11 +624,11 @@
             ],
         ),
         out_shape=[
-            jax.ShapeDtypeStruct((rows, width), F32),
-            jax.ShapeDtypeStruct((width, rows), BF),
-            jax.ShapeDtypeStruct((rows, total), F32),
-            jax.ShapeDtypeStruct((rows, total), BF),
-            jax.ShapeDtypeStruct((rows, 128), F32),
+            pltpu.HBM((rows, width), F32),
+            pltpu.HBM((width, rows), BF),
+            pltpu.HBM((rows, total), F32),
+            pltpu.HBM((rows, total), BF),
+            pltpu.HBM((rows, 128), F32),
         ],
         input_output_aliases={13 + n: n for n in range(len(earlier))},
         compiler_params=pltpu.CompilerParams(vmem_limit_bytes=44 << 20),
@@ -611,7 +640,6 @@
 def feed_kernel(grid_of, order_ref, narrow_ref, unit_ref, x_ref, gain_ref, a0, a1, a2, a3, b0, b1, b2, b3, out_ref, wa, wb, sem):
     batch_count, tensor_count = grid_of
     up_cols = narrow_ref.shape[1] // tensor_count
-    part_cols = wa.shape[2]
     parts = weights(wa, wb)
 
     @pl.when(pl.program_id(0) == 0)
@@ -622,11 +650,11 @@
         wait_whole(wb, sem.at[1])
 
     out = x_ref[...].astype(F32) + unit_ref[...] * gain_ref[1:2, :]
-    for start in range(0, up_cols, part_cols):
+    for start, width, _, _ in parts:
         for t in range(tensor_count):
-            w = columns(parts, order_ref, batch_count, tensor_count, t, start, part_cols)
+            w = columns(parts, order_ref, batch_count, tensor_count, t, start, width)
             off = t * up_cols + start
-            out += dotf(narrow_ref[:, off : off + part_cols], w, 1, 1)
+            out += dotf(narrow_ref[:, off : off + width], w, 1, 1)
     out_ref[...] = out.astype(BF)
 
 
@@ -646,7 +674,7 @@
             out_specs=row,
             scratch_shapes=[whole(wa), whole(wb), pltpu.SemaphoreType.DMA((2,))],
         ),
-        out_shape=jax.ShapeDtypeStruct((rows, width), BF),
+        out_shape=pltpu.HBM((rows, width), BF),
         compiler_params=pltpu.CompilerParams(vmem_limit_bytes=28 << 20),
         cost_estimate=cost(14),
         name="feed_forward",
@@ -786,12 +814,12 @@
             + [pltpu.SemaphoreType.DMA((4,))],
         ),
         out_shape=[
-            jax.ShapeDtypeStruct((rows, total), BF),
-            jax.ShapeDtypeStruct((rows, width), F32),
-            jax.ShapeDtypeStruct((width, rows), BF),
-            jax.ShapeDtypeStruct((rows, width), BF),
-            jax.ShapeDtypeStruct((16, width), F32),
-            jax.ShapeDtypeStruct((8, total), F32),
+            pltpu.HBM((rows, total), BF),
+            pltpu.HBM((rows, width), F32),
+            pltpu.HBM((width, rows), BF),
+            pltpu.HBM((rows, width), BF),
+            pltpu.HBM((16, width), F32),
+            pltpu.HBM((8, total), F32),
         ],
         compiler_params=pltpu.CompilerParams(vmem_limit_bytes=60 << 20),
         cost_estimate=cost(60),
@@ -840,7 +868,7 @@
     lead = (batch_count * tensor_count // 2,) + (() if count == 1 else (count,)) + (height,)
     zeros = (0,) * len(lead)
     out_spec = pl.BlockSpec(lead + (chunk,), lambda i, t, e: zeros + (i,))
-    out = jax.ShapeDtypeStruct(lead + (cols,), BF)
+    out = pltpu.HBM(lead + (cols,), BF)
     b_spec = pl.BlockSpec((rows, chunk), lambda i, t, e: (0, t * per + start // chunk + i))
     return pl.pallas_call(
         functools.partial(grad_kernel, grid_of, count, turn),
@@ -915,8 +943,8 @@
             + [pltpu.SemaphoreType.DMA((len(chains),))],
         ),
         out_shape=[
-            jax.ShapeDtypeStruct((rows, width), BF),
-            jax.ShapeDtypeStruct((8, width), F32),
+            pltpu.HBM((rows, width), BF),
+            pltpu.HBM((8, width), F32),
         ],
         compiler_params=pltpu.CompilerParams(vmem_limit_bytes=32 << 20),
         cost_estimate=cost(15),
@@ -1044,8 +1072,9 @@
             more([down], far - 2)
             scaled = launch(scaled, [down])
     scaled = land(scaled, [wa, wb, down])
-    wda = down.columns(0, half_cols, steps[0][far:])
-    wdb = down.columns(half_cols, half_cols, steps[1][far:])
+    down_cut = half_cols + (up_chunk if half_cols % 1024 == 0 else 0)
+    wda = down.columns(0, down_cut, steps[0][far:])
+    wdb = down.columns(down_cut, local_hidden - down_cut, steps[1][far:])
     rows_cot = Rows(cotangent, micro_count, split)
     scaled = launch(scaled, [wa, wb])
     scaled = land(scaled, [wa, wb])
@@ -1065,7 +1094,7 @@
         narrow = land(narrow, [wda, wdb])
         more([wda, wdb], near - 2)
         narrow = launch(narrow, [wda, wdb])
-    narrow = land(narrow, [rows_cot, wda])
+    unit, h3, hidden, narrow, stat = land([unit, h3, hidden, narrow, stat], [rows_cot, wda, wdb])
     cot = rows_cot.result
 
     def grad_half(n, a, b, name, turn=False):
@@ -1078,60 +1107,67 @@
                 hop([chain])
         return [chain.total for chain in chains]
 
-    cot_held = launch(cot, [wda])
+    cot_held = launch(cot, [wda, wdb])
     d0 = grad_half(0, cot_held, narrow, "grad_down", True)
     cot_held = launch(cot_held, [d0])
     d1 = grad_half(1, cot_held, narrow, "grad_down", True)
-    d1.send = land(d1.send, [d0, wda, wdb])
-    hidden = launch(hidden, [d1, d0, wdb])
-    hidden = land(hidden, [d1, wdb])
+    d1.keep, d1.send = land((d1.keep, d1.send), [d0, wda, wdb])
+    hidden = launch(hidden, [d1, d0])
+    hidden = land(hidden, [d1])
     hidden = launch(hidden, [d1])
-    dhidden, dresid, dmixed, dattended, gain_sums, mid_sums = feed_back(
+    back = feed_back(
         orders, hidden, stat, unit, x, cot, norm_gains, mid_row, scale_row, wda, wdb, wa, wb, grid_of
     )
-    dhidden = land(dhidden, [d0, d1])
+    dhidden, dresid, dmixed, dattended, gain_sums, mid_sums = land(back, [d0, d1])
     more([d0, d1], near - 2)
     dhidden = launch(dhidden, [d0, d1])
     u0 = grad_half(0, h3, dhidden, "grad_up")
-    dhidden = launch(dhidden, [u0])
+    u0.keep, u0.send = land((u0.keep, u0.send), [d0, d1])
+    down_sum = merged([d0, d1])
+    dhidden = launch(dhidden, [u0, down_sum])
     u1 = grad_half(1, h3, dhidden, "grad_up")
-    u1.send = land(u1.send, [u0, d0, d1])
-    narrow = launch(narrow, [u1, u0, d0, d1])
-    block_out = feed_forward(orders, narrow, unit, x, norm_gains, wda, wdb, grid_of)
-    rows_out = Rows(block_out, micro_count, split)
-    dmixed, rows_out.value = land((dmixed, rows_out.value), [u1, d0, d1])
-    dmixed = launch(dmixed, [u1, d0, d1])
+    u1.keep, u1.send = land((u1.keep, u1.send), [u0, down_sum])
+    dmixed = launch(dmixed, [u1] + ([down_sum] if down_sum.steps else []))
     keep, send = weight_grad(
         tables[0], dmixed, [scaled], grid_of, 0, out_weight.shape[0], "grad_out"
     )
     o0 = Scatter(keep, send, steps[0])
-    o0.send = land(o0.send, [u0])
-    da = launch(spread(dattended), [u0, o0])
+    flying = [u1, down_sum] if far > 1 else [u1]
+    o0.keep, o0.send = land((o0.keep, o0.send), flying)
+    da = launch(spread(dattended), [u0, u1, o0])
     halves, grads, inners = [], [], []
     for n in range(parts):
         *three, inner = attend_back(q, k, v, da, lse, ends, factor, tensor_count, parts, n)
         inners.append(inner)
-        three = [collect(one) for one in three]
         if n == 0:
-            three = land(three, [u0, u1, d0, d1, o0])
-            three = launch(three, [o0])
+            three = land(three, [u0, u1, o0])
+            narrow = launch(narrow, [u0, u1])
+            block_out = feed_forward(orders, narrow, unit, x, norm_gains, wda, wdb, grid_of)
+            block_out = land(block_out, [u0, u1])
+            more([u0, u1], near - 2)
+            up_sum = merged([u0, u1])
+            rows_out = Rows(block_out, micro_count, split)
+            three = [collect(one) for one in three]
+            three = launch(three, [up_sum, o0])
+            flying = [up_sum, o0]
         else:
-            three = land(three, [rows_out, halves[0], u0, u1])
-            three = launch(three, [halves[0], u0, u1, o0])
+            three = land(three, flying)
+            flying = [o0]
+            three = launch(three, flying)
         keep, send = weight_grad(tables[n % 2], h1, three, grid_of, 0, part_cols, "grad_qkv")
         halves.append(Scatter(keep, send, steps[n % 2]))
         grads += three
+        halves[-1].keep, halves[-1].send = land((halves[-1].keep, halves[-1].send), flying)
         if n < parts - 1:
-            da, halves[0].send = land((da, halves[0].send), [o0])
-            da = launch(da, [halves[0], u0, u1, rows_out])
+            flying = [halves[0], up_sum, o0, rows_out]
+            da = launch(da, flying)
     q_last = halves[-1]
-    beside = [u0, u1, o0] if parts > 1 else [o0]
-    q_last.send = land(q_last.send, beside)
     dresid = launch(dresid, [q_last])
     dresid = land(dresid, [q_last])
-    beside = [one for one in beside if one.steps]
-    dresid = launch(dresid, [q_last] + beside)
+    beside = halves + [o0] + ([] if parts > 1 else [rows_out])
+    dresid = launch(dresid, beside)
     grad_in, first_sums = input_grad(orders, grads, x, dresid, norm_gains, qkv_chains, grid_of)
+    grad_in, first_sums = land((grad_in, first_sums), beside)
     local = heads // split
     if parts == 1:
         head_sums = jnp.sum(inners[0], axis=-1).reshape(-1)
@@ -1145,31 +1181,34 @@
         [jnp.sum(one, axis=0) for one in (first_sums, gain_sums[:8], gain_sums[8:], mid_sums)]
         + [head_all]
     )
-    last = Total(last, steps[0])
-    rows_back = Rows(grad_in, micro_count, split)
-    last.value = land(last.value, halves + beside)
-    launch((), [last, rows_back] + ([] if parts > 1 else [rows_out]) + [one for one in halves + [o0] if one.steps])
+    last = Total(last, batch_count, tensor_count)
+    rows_back = Rows(grad_in, micro_count, split, 2)
+    tail = [last] + halves + ([o0] if o0.steps else [])
+    launch((), tail + [rows_back])
+    for one in tail:
+        one.end()
+    if parts > 1:
+        halves = [merged(halves)]
+    after = ()
     while last.steps:
         tail = [one for one in [last] + halves + [o0] if one.steps]
+        launch(after, tail)
         for one in tail:
             one.end()
-        launch((), tail)
-    last.end()
-    for one in halves + [o0]:
-        if not hasattr(one, "total"):
-            one.end()
-    if parts == 1:
-        rows_out.end()
+        after = rows_back.arrived[:1]
     rows_back.end()
     block_out, grad_in = rows_out.result, rows_back.result
+    d_totals, u_totals, o_totals, q_totals = (
+        flush([down_sum]), flush([up_sum]), flush([o0]), flush(halves)
+    )
+    down_grad = d_totals[0].T
+    up_grad = u_totals[0]
+    out_grad = o_totals[0].T
+    qkv_grad = q_totals[0]
     vector = last.value
     d_totals, u_totals, o_totals, q_totals = (
         flush([d0, d1]), flush([u0, u1]), flush([o0]), flush(halves)
     )
-    down_grad = jnp.concatenate(d_totals, axis=1).T
-    up_grad = jnp.concatenate(u_totals, axis=1)
-    out_grad = o_totals[0].T
-    qkv_grad = jnp.concatenate(q_totals, axis=2)
     gains_sum = vector[: 3 * width].reshape(3, width)
     mid_own = lax.dynamic_slice(vector, (3 * width + tensor_rank * local_hidden,), (local_hidden,))
     scale_own = lax.dynamic_slice(

time: 541 us -> 514 us (0.950)
  waiting for transfers between devices: 129 us -> 108 us
  Pallas kernels: 265 us -> 284 us
  local copies, waits for them, and re-layouts: 30.5 us -> 19.2 us
  other arithmetic: 37.4 us -> 26.8 us
    ppermute x75 -> x65, waiting for transfers between devices: 129 us -> 103 us  [swap(): return lax.ppermute(value, axis, [(i, i ^ flip) for i in range(count)])]
    ppermute x75 -> x65, starting transfers between devices: 68.5 us -> 56.3 us  [swap(): return lax.ppermute(value, axis, [(i, i ^ flip) for i in range(count)])]
    pallas_call x7, Pallas kernels: 59.3 us -> 70.9 us  [weight_grad(): pl.pallas_call(functools.partial(grad_kernel, grid_of, count, turn), grid...]
    unnamed x149 -> x141, local copies, waits for them, and re-layouts: 20.3 us -> 11 us
    ppermute x0 -> x7, starting transfers between devices: none -> 8.01 us  [go(): self.arrived.append(lax.ppermute(value, ALL, pairs))]
    convert_element_type x28 -> x25, other arithmetic: 25.3 us -> 19.4 us  [end(): (keep[:half].astype(F32) + arrived[:half].astype(F32)).astype(BF)]
  transfers between devices with their start and end apart: 75 -> 72, of which waited for: 29 -> 29; matrix products, arithmetic and copies ran while one was open for 6% -> 3% of each run, Pallas kernels for 46% -> 54%
where the time goes in v3:
time: 514 us; the launch traced here: 505 us
  Pallas kernels  284 us (55%)
  waiting for transfers between devices  108 us (21%)
  starting transfers between devices  64.3 us (13%)
  other arithmetic  26.8 us (5%)
  local copies, waits for them, and re-layouts  19.2 us (4%)
    ppermute x65, waiting for transfers between devices, swap(): return lax.ppermute(value, axis, [(i, i ^ flip) for i in range(count)])  103 us
    pallas_call x7, Pallas kernels, weight_grad(): pl.pallas_call(functools.partial(grad_kernel, grid_of, count, turn), grid...  70.9 us
    ppermute x65, starting transfers between devices, swap(): return lax.ppermute(value, axis, [(i, i ^ flip) for i in range(count)])  56.3 us
    pallas_call x1, Pallas kernels, feed_back(): pl.pallas_call(functools.partial(back_kernel, grid_of), grid_spec=pltpu.P...  50.2 us
    pallas_call x2, Pallas kernels, hidden_forward(): pl.pallas_call(kernel, grid_spec=pltpu.PrefetchScalarGridSpec(num_scalar_...  43.2 us
    pallas_call x2, Pallas kernels, attend_back(): pl.pallas_call(functools.partial(attend_back_kernel, rows, block, factor)...  41.3 us
    pallas_call x2, Pallas kernels, attend(): pl.pallas_call(kernel, grid_spec=pltpu.PrefetchScalarGridSpec(num_scalar_...  26.2 us
    convert_element_type x25, other arithmetic, end(): (keep[:half].astype(F32) + arrived[:half].astype(F32)).astype(BF)  19.4 us
  transfers between devices with their start and end apart: 72, of which 29 were waited for; matrix products, arithmetic and copies ran while one was open for 3% of the time, Pallas kernels for 54%

profile of v3, /device:TPU:0, one launch (start us, length us, event | category | flops | bytes accessed | tf_op | source)
XLA Modules:
  0.0 504.7 jit_solution(770542703947607138)
XLA Ops:
  4.2 2.9 collective-permute-start
  7.1 2.6 collective-permute-start.1
  9.7 8.9 %collective-permute-done.1 = bf16[1,3,64,512]{3,2,1,0:T(8,128)(2,1)S(1)} collective-permute-done((bf16[1,3,64,512]{3,2,1,0:T(8,128)(2,1)S(1)}, bf16[1,3,64,512]{3,2,1,0:T(8,128)(2,1)S(1)}, u32[]{:S(2)}, u32[]{:S(2)}) %collective-permute-start.1) | collective-permute-done | bytes 196640 | tf_op jit(solution)/shard_map/ppermute | solution.py:81
  19.4 9.3 %collective-permute-done.2 = bf16[2,3,64,512]{3,2,1,0:T(8,128)(2,1)S(1)} collective-permute-done((bf16[2,3,64,512]{3,2,1,0:T(8,128)(2,1)S(1)}, bf16[2,3,64,512]{3,2,1,0:T(8,128)(2,1)S(1)}, u32[]{:S(2)}, u32[]{:S(2)}) %collective-permute-start.2) | collective-permute-done | bytes 393248 | tf_op jit(solution)/shard_map/ppermute | solution.py:81
  30.3 1.8 collective-permute-start.4
  33.6 2.7 collective-permute-start.7
  36.2 4.3 collective-permute-done.4
  43.9 5.7 %collective-permute-done.7 = bf16[1,64,2560]{2,1,0:T(8,128)(2,1)S(1)} collective-permute-done((bf16[1,64,2560]{2,1,0:T(8,128)(2,1)S(1)}, bf16[1,64,2560]{2,1,0:T(8,128)(2,1)S(1)}, u32[]{:S(2)}, u32[]{:S(2)}) %collective-permute-start.7) | collective-permute-done | bytes 327712 | tf_op jit(solution)/shard_map/ppermute | solution.py:81
  52.0 7.2 %collective-permute-done.5.refs_1_.refs_10_ = bf16[8,3,64,256]{3,2,1,0:T(8,128)(2,1)} collective-permute-done((bf16[8,3,64,256]{3,2,1,0:T(8,128)(2,1)S(1)}, bf16[8,3,64,256]{3,2,1,0:T(8,128)(2,1)}, u32[]{:S(2)}, u32[]{:S(2)}) %collective-permute-start.5) | collective-permute-done | bytes 786464 | tf_op jit(solution)/shard_map/ppermute | solution.py:81
  61.2 4.1 collective-permute-done.8
  66.7 16.1 %project.1 = (bf16[1024,1024]{1,0:T(8,128)(2,1)}, bf16[1024,1024]{1,0:T(8,128)(2,1)}, bf16[1024,1024]{1,0:T(8,128)(2,1)}, bf16[1024,1024]{1,0:T(8,128)(2,1)}) custom-call(s32[64]{0:T(128)S(1)} %pad_add_fusion.order_ref, bf16[1024,1024]{1,0:T(8,128)(2,1)} %bitcast.3.x_ref.refs_1_.refs_6_, f32[3,1024]{1,0:T(4,128)S(1)} %copy-done.4, ...), custom_call_target="tpu_custom_call" | custom-call | flops 12999999488 | bytes 1048576 | tf_op jit(solution)/shard_map/project/pallas_call | solution.py:343
  83.8 3.3 collective-permute-start.16
  90.0 13.1 %attend.2 = (bf16[1024,1024]{1,0:T(8,128)(2,1)}, f32[8,2,1024]{2,1,0:T(2,128)}) custom-call(s32[4]{0:T(128)S(1)} %bitcast.33, bf16[1024,1024]{1,0:T(8,128)(2,1)} %get-tuple-element.274.q_ref, bf16[1024,1024]{1,0:T(8,128)(2,1)} %get-tuple-element.275.k_ref, bf16[1024,1024]{1,0:T(8,128)(2,1)} %get-tuple-element.276.v_ref, ...), custom_call_target="tpu_custom_call" | custom-call | flops 12000000000 | bytes 1048576 | tf_op jit(solution)/shard_map/attend/pallas_call | solution.py:466
  103.2 1.8 collective-permute-start.19
  105.0 13.1 %attend.3 = (bf16[1024,1024]{1,0:T(8,128)(2,1)}, f32[8,2,1024]{2,1,0:T(2,128)}) custom-call(s32[4]{0:T(128)S(1)} %bitcast.34, bf16[1024,1024]{1,0:T(8,128)(2,1)} %get-tuple-element.274.q_ref, bf16[1024,1024]{1,0:T(8,128)(2,1)} %get-tuple-element.275.k_ref, ...), custom_call_target="tpu_custom_call", output_to_operand_aliasing={{0}: (5, {}), {1}: (6, {})} | custom-call | flops 12000000000 | bytes 1048576 | tf_op jit(solution)/shard_map/attend/pallas_call | solution.py:466
  121.2 1.9 collective-permute-done.21.refs_11_.b3
  128.0 21.7 %hidden_forward.2 = (f32[1024,1024]{1,0:T(8,128)}, bf16[1024,1024]{1,0:T(8,128)(2,1)}, f32[1024,4096]{1,0:T(8,128)}, bf16[1024,4096]{1,0:T(8,128)(2,1)}, f32[1024,128]{1,0:T(8,128)}) custom-call(s32[64]{0:T(128)S(1)} %pad_add_fusion.order_ref, bf16[1024,1024]{1,0:T(8,128)(2,1)} %get-tuple-element.296.refs_0_, ...), custom_call_target="tpu_custom_call" | custom-call | flops 15000000512 | bytes 1048576 | tf_op jit(solution)/shard_map/hidden_forward/pallas_call | solution.py:602
  151.6 21.5 %hidden_forward.3 = (f32[1024,1024]{1,0:T(8,128)}, bf16[1024,1024]{1,0:T(8,128)(2,1)}, f32[1024,4096]{1,0:T(8,128)}, bf16[1024,4096]{1,0:T(8,128)(2,1)}, f32[1024,128]{1,0:T(8,128)}) custom-call(s32[64]{0:T(128)S(1)} %pad_add_fusion.order_ref, ...), custom_call_target="tpu_custom_call", output_to_operand_aliasing={{0}: (13, {}), {1}: (14, {}), {2}: (15, {}), {3}: (16, {}),... | custom-call | flops 15000000512 | bytes 1048576 | tf_op jit(solution)/shard_map/hidden_forward/pallas_call | solution.py:602
  173.2 6.0 %collective-permute-done.28.db1.b1 = bf16[8,64,768]{2,1,0:T(8,128)(2,1)S(1)} collective-permute-done((bf16[8,64,768]{2,1,0:T(8,128)(2,1)S(1)}, bf16[8,64,768]{2,1,0:T(8,128)(2,1)S(1)}, u32[]{:S(2)}, u32[]{:S(2)}) %collective-permute-start.28) | collective-permute-done | bytes 786464 | tf_op jit(solution)/shard_map/ppermute | solution.py:81
  182.6 10.6 %grad_down.2 = (bf16[16,64,1024]{2,1,0:T(8,128)(2,1)}, bf16[16,64,1024]{2,1,0:T(8,128)(2,1)}) custom-call(s32[32]{0:T(128)S(1)} %get-tuple-element.564.order_ref, bf16[1024,1024]{1,0:T(8,128)(2,1)} %bitcast.38, bf16[1024,4096]{1,0:T(8,128)(2,1)} %get-tuple-element.405.refs_0_.narrow_ref), custom_call_target="tpu_custom_call" | custom-call | flops 4800000000 | bytes 1048576 | tf_op jit(solution)/shard_map/grad_down/pallas_call | solution.py:873
  193.8 10.9 %grad_down.3 = (bf16[16,64,1024]{2,1,0:T(8,128)(2,1)}, bf16[16,64,1024]{2,1,0:T(8,128)(2,1)}) custom-call(s32[32]{0:T(128)S(1)} %get-tuple-element.563.order_ref, bf16[1024,1024]{1,0:T(8,128)(2,1)} %bitcast.39, bf16[1024,4096]{1,0:T(8,128)(2,1)} %get-tuple-element.405.refs_0_.narrow_ref), custom_call_target="tpu_custom_call" | custom-call | flops 4800000000 | bytes 1048576 | tf_op jit(solution)/shard_map/grad_down/pallas_call | solution.py:873
  204.8 2.0 add_convert_fusion.6
  209.0 4.6 collective-permute-done.32
  213.6 2.0 add_convert_fusion.4
  217.4 50.2 %feed_back.1 = (bf16[1024,4096]{1,0:T(8,128)(2,1)}, f32[1024,1024]{1,0:T(8,128)}, bf16[1024,1024]{1,0:T(8,128)(2,1)}, bf16[1024,1024]{1,0:T(8,128)(2,1)}, f32[16,1024]{1,0:T(8,128)}, /*index=5*/f32[8,4096]{1,0:T(8,128)}) custom-call(s32[64]{0:T(128)} %copy-done.6, f32[1024,4096]{1,0:T(8,128)} %get-tuple-element.341.hidden_ref, ...), custom_call_target="tpu_custom_call" | custom-call | flops 60000002048 | bytes 1048576 | tf_op jit(solution)/shard_map/feed_back/pallas_call | solution.py:782
  272.6 10.1 %grad_up.2 = (bf16[16,64,1024]{2,1,0:T(8,128)(2,1)}, bf16[16,64,1024]{2,1,0:T(8,128)(2,1)}) custom-call(s32[32]{0:T(128)S(1)} %get-tuple-element.564.order_ref, bf16[1024,1024]{1,0:T(8,128)(2,1)} %get-tuple-element.361.a_ref, bf16[1024,4096]{1,0:T(8,128)(2,1)} %get-tuple-element.373.refs_0_), custom_call_target="tpu_custom_call" | custom-call | flops 4800000000 | bytes 1048576 | tf_op jit(solution)/shard_map/grad_up/pallas_call | solution.py:873
  282.7 2.1 collective-permute-done.37
  288.3 10.0 %grad_up.3 = (bf16[16,64,1024]{2,1,0:T(8,128)(2,1)}, bf16[16,64,1024]{2,1,0:T(8,128)(2,1)}) custom-call(s32[32]{0:T(128)S(1)} %get-tuple-element.563.order_ref, bf16[1024,1024]{1,0:T(8,128)(2,1)} %get-tuple-element.361.a_ref, bf16[1024,4096]{1,0:T(8,128)(2,1)} %get-tuple-element.373.refs_0_), custom_call_target="tpu_custom_call" | custom-call | flops 4800000000 | bytes 1048576 | tf_op jit(solution)/shard_map/grad_up/pallas_call | solution.py:873
  298.4 3.5 collective-permute-done.40
  303.2 6.6 %grad_out.1 = (bf16[16,64,512]{2,1,0:T(8,128)(2,1)}, bf16[16,64,512]{2,1,0:T(8,128)(2,1)}) custom-call(s32[32]{0:T(128)S(1)} %get-tuple-element.564.order_ref, bf16[1024,1024]{1,0:T(8,128)(2,1)} %get-tuple-element.385.a_ref, bf16[1024,1024]{1,0:T(8,128)(2,1)} %get-tuple-element.296.refs_0_), custom_call_target="tpu_custom_call" | custom-call | flops 2400000000 | bytes 1048576 | tf_op jit(solution)/shard_map/grad_out/pallas_call | solution.py:873
  309.8 7.5 %collective-permute-done.42 = bf16[1,64,2048]{2,1,0:T(8,128)(2,1)S(1)} collective-permute-done((bf16[1,64,2048]{2,1,0:T(8,128)(2,1)S(1)}, bf16[1,64,2048]{2,1,0:T(8,128)(2,1)S(1)}, u32[]{:S(2)}, u32[]{:S(2)}) %collective-permute-start.42) | collective-permute-done | bytes 262176 | tf_op jit(solution)/shard_map/ppermute | solution.py:81
  319.9 20.6 %attend_back.2 = (bf16[1024,512]{1,0:T(8,128)(2,1)}, bf16[1024,512]{1,0:T(8,128)(2,1)}, bf16[1024,512]{1,0:T(8,128)(2,1)}, f32[4,2,1024]{2,1,0:T(2,128)}) custom-call(s32[4]{0:T(128)S(1)} %bitcast.35, bf16[1024,1024]{1,0:T(8,128)(2,1)} %get-tuple-element.274.q_ref, bf16[1024,1024]{1,0:T(8,128)(2,1)} %get-tuple-element.275.k_ref, ...), custom_call_target="tpu_custom_call" | custom-call | flops 20999999488 | bytes 1048576 | tf_op jit(solution)/shard_map/attend_back/pallas_call | solution.py:495
  340.5 2.8 collective-permute-done.43
  346.8 16.9 %feed_forward.1 = bf16[1024,1024]{1,0:T(8,128)(2,1)} custom-call(s32[64]{0:T(128)S(1)} %copy-done.7, bf16[1024,4096]{1,0:T(8,128)(2,1)} %get-tuple-element.405.refs_0_.narrow_ref, f32[1024,1024]{1,0:T(8,128)} %get-tuple-element.343.unit_ref, bf16[1024,1024]{1,0:T(8,128)(2,1)} %bitcast.3.x_ref.refs_1_.refs_6_, f32[3,1024]{1,0:T(4,128)S(1)} %copy-done.5, ...), custom_call_target="tpu_custom_call" | custom-call | flops 14000000000 | bytes 1048576 | tf_op jit(solution)/shard_map/feed_forward/pallas_call | solution.py:666
  366.3 11.2 %grad_qkv.2 = (bf16[16,3,64,256]{3,2,1,0:T(8,128)(2,1)}, bf16[16,3,64,256]{3,2,1,0:T(8,128)(2,1)}) custom-call(s32[32]{0:T(128)S(1)} %get-tuple-element.564.order_ref, bf16[1024,1024]{1,0:T(8,128)(2,1)} %get-tuple-element.409.a_ref, bf16[1024,512]{1,0:T(8,128)(2,1)} %get-tuple-element.419.refs_0_, bf16[1024,512]{1,0:T(8,128)(2,1)} %get-tuple-element.420.refs_1_, ...), custom_call_target="tpu_custom_call" | custom-call | flops 3600000000 | bytes 1048576 | tf_op jit(solution)/shard_map/grad_qkv/pallas_call | solution.py:873
  380.6 1.7 collective-permute-start.52
  382.4 20.7 %attend_back.3 = (bf16[1024,512]{1,0:T(8,128)(2,1)}, bf16[1024,512]{1,0:T(8,128)(2,1)}, bf16[1024,512]{1,0:T(8,128)(2,1)}, f32[4,2,1024]{2,1,0:T(2,128)}) custom-call(s32[4]{0:T(128)S(1)} %bitcast.36, bf16[1024,1024]{1,0:T(8,128)(2,1)} %get-tuple-element.274.q_ref, bf16[1024,1024]{1,0:T(8,128)(2,1)} %get-tuple-element.275.k_ref, ...), custom_call_target="tpu_custom_call" | custom-call | flops 20999999488 | bytes 1048576 | tf_op jit(solution)/shard_map/attend_back/pallas_call | solution.py:495
  403.1 7.1 %collective-permute-done.52 = bf16[4,64,512]{2,1,0:T(8,128)(2,1)S(1)} collective-permute-done((bf16[4,64,512]{2,1,0:T(8,128)(2,1)S(1)}, bf16[4,64,512]{2,1,0:T(8,128)(2,1)S(1)}, u32[]{:S(2)}, u32[]{:S(2)}) %collective-permute-start.52) | collective-permute-done | bytes 262176 | tf_op jit(solution)/shard_map/ppermute | solution.py:81
  412.4 11.4 %grad_qkv.3 = (bf16[16,3,64,256]{3,2,1,0:T(8,128)(2,1)}, bf16[16,3,64,256]{3,2,1,0:T(8,128)(2,1)}) custom-call(s32[32]{0:T(128)S(1)} %get-tuple-element.563.order_ref, bf16[1024,1024]{1,0:T(8,128)(2,1)} %get-tuple-element.409.a_ref, bf16[1024,512]{1,0:T(8,128)(2,1)} %get-tuple-element.446.refs_0_.refs_3_, ...), custom_call_target="tpu_custom_call" | custom-call | flops 3600000000 | bytes 1048576 | tf_op jit(solution)/shard_map/grad_qkv/pallas_call | solution.py:873
  427.6 2.1 add_convert_fusion.10
  429.7 2.0 add_convert_fusion.8
  434.6 19.2 %input_grad.1 = (bf16[1024,1024]{1,0:T(8,128)(2,1)}, f32[8,1024]{1,0:T(8,128)}) custom-call(s32[64]{0:T(128)S(1)} %copy-done.7, bf16[1024,512]{1,0:T(8,128)(2,1)} %get-tuple-element.419.refs_0_, bf16[1024,512]{1,0:T(8,128)(2,1)} %get-tuple-element.420.refs_1_, bf16[1024,512]{1,0:T(8,128)(2,1)} %get-tuple-element.421.refs_2_, ...), custom_call_target="tpu_custom_call" | custom-call | flops 15000000512 | bytes 1048576 | tf_op jit(solution)/shard_map/input_grad/pallas_call | solution.py:932
  461.9 7.7 %collective-permute-done.62 = bf16[4,3,64,256]{3,2,1,0:T(8,128)(2,1)S(1)} collective-permute-done((bf16[4,3,64,256]{3,2,1,0:T(8,128)(2,1)S(1)}, bf16[4,3,64,256]{3,2,1,0:T(8,128)(2,1)S(1)}, u32[]{:S(2)}, u32[]{:S(2)}) %collective-permute-start.62) | collective-permute-done | bytes 393248 | tf_op jit(solution)/shard_map/ppermute | solution.py:81
  472.2 1.8 collective-permute-start.66
  476.9 4.6 collective-permute-done.65
  487.5 4.9 collective-permute-done.60
  492.5 2.7 collective-permute-start.71
  497.2 6.3 %collective-permute-done.71 = bf16[1,3,64,512]{3,2,1,0:T(8,128)(2,1)S(1)} collective-permute-done((bf16[1,3,64,512]{3,2,1,0:T(8,128)(2,1)S(1)}, bf16[1,3,64,512]{3,2,1,0:T(8,128)(2,1)S(1)}, u32[]{:S(2)}, u32[]{:S(2)}) %collective-permute-start.71) | collective-permute-done | bytes 196640 | tf_op jit(solution)/shard_map/ppermute | solution.py:81
  (349 shorter events, 90.3 us)
Async XLA Ops:
  4.2 26.1 %collective-permute-start = (bf16[1,512,1024]{2,1,0:T(8,128)(2,1)S(1)}, bf16[1,512,1024]{2,1,0:T(8,128)(2,1)S(1)}, u32[]{:S(2)}, u32[]{:S(2)}) collective-permute-start(bf16[1,512,1024]{2,1,0:T(8,128)(2,1)S(1)} %get-tuple-element.254), channel_id=1, source_target_pairs={{0,1},{1,0},{2,3},{3,2},{4,5},{5,4},{6,7},{7,6},{8,9},{9,8},{10,11... | collective-permute-start | bytes 3145736 | tf_op jit(solution)/shard_map/ppermute | solution.py:81
  7.1 11.5 %collective-permute-start.1 = (bf16[1,3,64,512]{3,2,1,0:T(8,128)(2,1)S(1)}, bf16[1,3,64,512]{3,2,1,0:T(8,128)(2,1)S(1)}, u32[]{:S(2)}, u32[]{:S(2)}) collective-permute-start(bf16[1,3,64,512]{3,2,1,0:T(8,128)(2,1)S(1)} %bitcast.45), channel_id=1, source_target_pairs={{0,16},{2,18},{4,20},{6,22},{8,24},{10,26},{12,28},{14,30},{16,0},... | collective-permute-start | bytes 589832 | tf_op jit(solution)/shard_map/ppermute | solution.py:81
  33.6 16.0 %collective-permute-start.7 = (bf16[1,64,2560]{2,1,0:T(8,128)(2,1)S(1)}, bf16[1,64,2560]{2,1,0:T(8,128)(2,1)S(1)}, u32[]{:S(2)}, u32[]{:S(2)}) collective-permute-start(bf16[1,64,2560]{2,1,0:T(8,128)(2,1)S(1)} %maximum_bitcast_fusion), channel_id=1, source_target_pairs={{0,16},{2,18},{4,20},{6,22},{8,24},{10,26},{12,28},{14,30},{16,0},... | collective-permute-start | bytes 983048 | tf_op jit(solution)/shard_map/ppermute | solution.py:81
  41.8 17.4 %collective-permute-start.5 = (bf16[8,3,64,256]{3,2,1,0:T(8,128)(2,1)S(1)}, bf16[8,3,64,256]{3,2,1,0:T(8,128)(2,1)}, u32[]{:S(2)}, u32[]{:S(2)}) collective-permute-start(bf16[8,3,64,256]{3,2,1,0:T(8,128)(2,1)S(1)} %pad_maximum_fusion.3.refs_0_.refs_9_), channel_id=1, source_target_pairs={{0,4},{2,6},{4,0},{6,2},{8,12},{10,14},{12,8},{14,10},{16,20},{18,... | collective-permute-start | bytes 2359304 | tf_op jit(solution)/shard_map/ppermute | solution.py:81
  42.5 17.5 %collective-permute-start.6 = (bf16[8,3,64,256]{3,2,1,0:T(8,128)(2,1)S(1)}, bf16[8,3,64,256]{3,2,1,0:T(8,128)(2,1)}, u32[]{:S(2)}, u32[]{:S(2)}) collective-permute-start(bf16[8,3,64,256]{3,2,1,0:T(8,128)(2,1)S(1)} %pad_maximum_fusion.4.refs_4_.refs_13_), channel_id=1, source_target_pairs={{0,1},{1,0},{2,3},{3,2},{4,5},{5,4},{6,7},{7,6},{8,9},{9,8},{10,11... | collective-permute-start | bytes 2359304 | tf_op jit(solution)/shard_map/ppermute | solution.py:81
  49.6 15.7 %collective-permute-start.8 = (bf16[2,64,2560]{2,1,0:T(8,128)(2,1)S(1)}, bf16[2,64,2560]{2,1,0:T(8,128)(2,1)S(1)}, u32[]{:S(2)}, u32[]{:S(2)}) collective-permute-start(bf16[2,64,2560]{2,1,0:T(8,128)(2,1)S(1)} %pad_maximum_fusion.7), channel_id=1, source_target_pairs={{0,8},{2,10},{4,12},{6,14},{8,0},{10,2},{12,4},{14,6},{16,24},{18,... | collective-permute-start | bytes 1966088 | tf_op jit(solution)/shard_map/ppermute | solution.py:81
  52.0 14.0 %collective-permute-start.11 = (bf16[8,3,64,256]{3,2,1,0:T(8,128)(2,1)S(1)}, bf16[8,3,64,256]{3,2,1,0:T(8,128)(2,1)}, u32[]{:S(2)}, u32[]{:S(2)}) collective-permute-start(bf16[8,3,64,256]{3,2,1,0:T(8,128)(2,1)S(1)} %pad_maximum_fusion.4.refs_4_.refs_13_), channel_id=1, source_target_pairs={{0,2},{2,0},{4,6},{6,4},{8,10},{10,8},{12,14},{14,12},{16,18},{18,... | collective-permute-start | bytes 2359304 | tf_op jit(solution)/shard_map/ppermute | solution.py:81
  65.4 17.4 %collective-permute-start.13 = (bf16[4,64,1280]{2,1,0:T(8,128)(2,1)S(1)}, bf16[4,64,1280]{2,1,0:T(8,128)(2,1)S(1)}, u32[]{:S(2)}, u32[]{:S(2)}) collective-permute-start(bf16[4,64,1280]{2,1,0:T(8,128)(2,1)S(1)} %get-tuple-element.268), channel_id=1, source_target_pairs={{0,1},{1,0},{2,3},{3,2},{4,5},{5,4},{6,7},{7,6},{8,9},{9,8},{10,11... | collective-permute-start | bytes 1966088 | tf_op jit(solution)/shard_map/ppermute | solution.py:81
  66.0 16.8 %collective-permute-start.14 = (bf16[4,64,1280]{2,1,0:T(8,128)(2,1)S(1)}, bf16[4,64,1280]{2,1,0:T(8,128)(2,1)S(1)}, u32[]{:S(2)}, u32[]{:S(2)}) collective-permute-start(bf16[4,64,1280]{2,1,0:T(8,128)(2,1)S(1)} %get-tuple-element.269), channel_id=1, source_target_pairs={{0,4},{2,6},{4,0},{6,2},{8,12},{10,14},{12,8},{14,10},{16,20},{18,... | collective-permute-start | bytes 1966088 | tf_op jit(solution)/shard_map/ppermute | solution.py:81
  83.8 19.4 %collective-permute-start.16 = (bf16[1,64,2048]{2,1,0:T(8,128)(2,1)S(1)}, bf16[1,64,2048]{2,1,0:T(8,128)(2,1)S(1)}, u32[]{:S(2)}, u32[]{:S(2)}) collective-permute-start(bf16[1,64,2048]{2,1,0:T(8,128)(2,1)S(1)} %bitcast.43), channel_id=1, source_target_pairs={{0,16},{2,18},{4,20},{6,22},{8,24},{10,26},{12,28},{14,30},{16,0},... | collective-permute-start | bytes 786440 | tf_op jit(solution)/shard_map/ppermute | solution.py:81
  87.0 31.1 %collective-permute-start.17 = (bf16[8,64,1280]{2,1,0:T(8,128)(2,1)S(1)}, bf16[8,64,1280]{2,1,0:T(8,128)(2,1)S(1)}, u32[]{:S(2)}, u32[]{:S(2)}) collective-permute-start(bf16[8,64,1280]{2,1,0:T(8,128)(2,1)S(1)} %pad_maximum_fusion.refs_4_.a0), channel_id=1, source_target_pairs={{0,4},{2,6},{4,0},{6,2},{8,12},{10,14},{12,8},{14,10},{16,20},{18,... | collective-permute-start | bytes 3932168 | tf_op jit(solution)/shard_map/ppermute | solution.py:81
  88.5 29.6 %collective-permute-start.18 = (bf16[8,64,1280]{2,1,0:T(8,128)(2,1)S(1)}, bf16[8,64,1280]{2,1,0:T(8,128)(2,1)S(1)}, u32[]{:S(2)}, u32[]{:S(2)}) collective-permute-start(bf16[8,64,1280]{2,1,0:T(8,128)(2,1)S(1)} %pad_maximum_fusion.1.refs_8_.b0), channel_id=1, source_target_pairs={{0,1},{1,0},{2,3},{3,2},{4,5},{5,4},{6,7},{7,6},{8,9},{9,8},{10,11... | collective-permute-start | bytes 3932168 | tf_op jit(solution)/shard_map/ppermute | solution.py:81
  103.2 14.9 %collective-permute-start.19 = (bf16[2,64,2048]{2,1,0:T(8,128)(2,1)S(1)}, bf16[2,64,2048]{2,1,0:T(8,128)(2,1)S(1)}, u32[]{:S(2)}, u32[]{:S(2)}) collective-permute-start(bf16[2,64,2048]{2,1,0:T(8,128)(2,1)S(1)} %pad_maximum_fusion.8), channel_id=1, source_target_pairs={{0,8},{2,10},{4,12},{6,14},{8,0},{10,2},{12,4},{14,6},{16,24},{18,... | collective-permute-start | bytes 1572872 | tf_op jit(solution)/shard_map/ppermute | solution.py:81
  123.1 26.6 %collective-permute-start.24 = (bf16[4,64,1280]{2,1,0:T(8,128)(2,1)S(1)}, bf16[4,64,1280]{2,1,0:T(8,128)(2,1)S(1)}, u32[]{:S(2)}, u32[]{:S(2)}) collective-permute-start(bf16[4,64,1280]{2,1,0:T(8,128)(2,1)S(1)} %slice.457), channel_id=1, source_target_pairs={{0,1},{1,0},{2,3},{3,2},{4,5},{5,4},{6,7},{7,6},{8,9},{9,8},{10,11... | collective-permute-start | bytes 1966088 | tf_op jit(solution)/shard_map/ppermute | solution.py:81
  124.0 25.7 %collective-permute-start.25 = (bf16[4,64,768]{2,1,0:T(8,128)(2,1)S(1)}, bf16[4,64,768]{2,1,0:T(8,128)(2,1)S(1)}, u32[]{:S(2)}, u32[]{:S(2)}) collective-permute-start(bf16[4,64,768]{2,1,0:T(8,128)(2,1)S(1)} %slice.458), channel_id=1, source_target_pairs={{0,4},{2,6},{4,0},{6,2},{8,12},{10,14},{12,8},{14,10},{16,20},{18,... | collective-permute-start | bytes 1179656 | tf_op jit(solution)/shard_map/ppermute | solution.py:81
  124.5 48.6 %collective-permute-start.26 = (bf16[1,512,1024]{2,1,0:T(8,128)(2,1)S(1)}, bf16[1,512,1024]{2,1,0:T(8,128)(2,1)S(1)}, u32[]{:S(2)}, u32[]{:S(2)}) collective-permute-start(bf16[1,512,1024]{2,1,0:T(8,128)(2,1)S(1)} %get-tuple-element.315), channel_id=1, source_target_pairs={{0,1},{1,0},{2,3},{3,2},{4,5},{5,4},{6,7},{7,6},{8,9},{9,8},{10,11... | collective-permute-start | bytes 3145736 | tf_op jit(solution)/shard_map/ppermute | solution.py:81
  149.9 30.9 %collective-permute-start.27 = (bf16[8,64,1280]{2,1,0:T(8,128)(2,1)S(1)}, bf16[8,64,1280]{2,1,0:T(8,128)(2,1)S(1)}, u32[]{:S(2)}, u32[]{:S(2)}) collective-permute-start(bf16[8,64,1280]{2,1,0:T(8,128)(2,1)S(1)} %pad_maximum_fusion.2.da0.a0), channel_id=1, source_target_pairs={{0,4},{2,6},{4,0},{6,2},{8,12},{10,14},{12,8},{14,10},{16,20},{18,... | collective-permute-start | bytes 3932168 | tf_op jit(solution)/shard_map/ppermute | solution.py:81
  150.7 28.5 %collective-permute-start.28 = (bf16[8,64,768]{2,1,0:T(8,128)(2,1)S(1)}, bf16[8,64,768]{2,1,0:T(8,128)(2,1)S(1)}, u32[]{:S(2)}, u32[]{:S(2)}) collective-permute-start(bf16[8,64,768]{2,1,0:T(8,128)(2,1)S(1)} %pad_maximum_fusion.5.db0.b0), channel_id=1, source_target_pairs={{0,1},{1,0},{2,3},{3,2},{4,5},{5,4},{6,7},{7,6},{8,9},{9,8},{10,11... | collective-permute-start | bytes 2359304 | tf_op jit(solution)/shard_map/ppermute | solution.py:81
  193.2 11.6 %collective-permute-start.29 = (bf16[16,64,1024]{2,1,0:T(8,128)(2,1)}, bf16[16,64,1024]{2,1,0:T(8,128)(2,1)S(1)}, u32[]{:S(2)}, u32[]{:S(2)}) collective-permute-start(bf16[16,64,1024]{2,1,0:T(8,128)(2,1)} %get-tuple-element.329), channel_id=1, source_target_pairs={{0,2},{2,0},{4,6},{6,4},{8,10},{10,8},{12,14},{14,12},{16,18},{18,... | collective-permute-start | bytes 6291464 | tf_op jit(solution)/shard_map/ppermute | solution.py:81
  193.2 11.6 %collective-permute-start.30 = (bf16[8,64,1280]{2,1,0:T(8,128)(2,1)S(1)}, bf16[8,64,1280]{2,1,0:T(8,128)(2,1)S(1)}, u32[]{:S(2)}, u32[]{:S(2)}) collective-permute-start(bf16[8,64,1280]{2,1,0:T(8,128)(2,1)S(1)} %collective-permute-done.27.da1.a1), channel_id=1, source_target_pairs={{0,2},{2,0},{4,6},{6,4},{8,10},{10,8},{12,14},{14,12},{16,18},{18,... | collective-permute-start | bytes 3932168 | tf_op jit(solution)/shard_map/ppermute | solution.py:81
  193.7 11.0 %collective-permute-start.31 = (bf16[8,64,768]{2,1,0:T(8,128)(2,1)S(1)}, bf16[8,64,768]{2,1,0:T(8,128)(2,1)S(1)}, u32[]{:S(2)}, u32[]{:S(2)}) collective-permute-start(bf16[8,64,768]{2,1,0:T(8,128)(2,1)S(1)} %collective-permute-done.28.db1.b1), channel_id=1, source_target_pairs={{0,2},{2,0},{4,6},{6,4},{8,10},{10,8},{12,14},{14,12},{16,18},{18,... | collective-permute-start | bytes 2359304 | tf_op jit(solution)/shard_map/ppermute | solution.py:81
  208.5 59.1 %collective-permute-start.35 = (bf16[8,64,1024]{2,1,0:T(8,128)(2,1)}, bf16[8,64,1024]{2,1,0:T(8,128)(2,1)}, u32[]{:S(2)}, u32[]{:S(2)}) collective-permute-start(bf16[8,64,1024]{2,1,0:T(8,128)(2,1)} %get-tuple-element.352), channel_id=1, source_target_pairs={{0,4},{2,6},{4,0},{6,2},{8,12},{10,14},{12,8},{14,10},{16,20},{18,... | collective-permute-start | bytes 3145736 | tf_op jit(solution)/shard_map/ppermute | solution.py:81
  215.6 52.0 %collective-permute-start.36 = (bf16[8,64,1024]{2,1,0:T(8,128)(2,1)}, bf16[8,64,1024]{2,1,0:T(8,128)(2,1)}, u32[]{:S(2)}, u32[]{:S(2)}) collective-permute-start(bf16[8,64,1024]{2,1,0:T(8,128)(2,1)} %get-tuple-element.353), channel_id=1, source_target_pairs={{0,1},{1,0},{2,3},{3,2},{4,5},{5,4},{6,7},{7,6},{8,9},{9,8},{10,11... | collective-permute-start | bytes 3145736 | tf_op jit(solution)/shard_map/ppermute | solution.py:81
  270.9 14.0 %collective-permute-start.37 = (bf16[4,64,1024]{2,1,0:T(8,128)(2,1)S(1)}, bf16[4,64,1024]{2,1,0:T(8,128)(2,1)S(1)}, u32[]{:S(2)}, u32[]{:S(2)}) collective-permute-start(bf16[4,64,1024]{2,1,0:T(8,128)(2,1)S(1)} %get-tuple-element.364), channel_id=1, source_target_pairs={{0,1},{1,0},{2,3},{3,2},{4,5},{5,4},{6,7},{7,6},{8,9},{9,8},{10,11... | collective-permute-start | bytes 1572872 | tf_op jit(solution)/shard_map/ppermute | solution.py:81
  272.1 13.6 %collective-permute-start.38 = (bf16[4,64,1024]{2,1,0:T(8,128)(2,1)S(1)}, bf16[4,64,1024]{2,1,0:T(8,128)(2,1)S(1)}, u32[]{:S(2)}, u32[]{:S(2)}) collective-permute-start(bf16[4,64,1024]{2,1,0:T(8,128)(2,1)S(1)} %get-tuple-element.365), channel_id=1, source_target_pairs={{0,4},{2,6},{4,0},{6,2},{8,12},{10,14},{12,8},{14,10},{16,20},{18,... | collective-permute-start | bytes 1572872 | tf_op jit(solution)/shard_map/ppermute | solution.py:81
  287.5 14.3 %collective-permute-start.39 = (bf16[16,64,1024]{2,1,0:T(8,128)(2,1)S(1)}, bf16[16,64,1024]{2,1,0:T(8,128)(2,1)S(1)}, u32[]{:S(2)}, u32[]{:S(2)}) collective-permute-start(bf16[16,64,1024]{2,1,0:T(8,128)(2,1)S(1)} %copy-done.52), channel_id=1, source_target_pairs={{0,2},{2,0},{4,6},{6,4},{8,10},{10,8},{12,14},{14,12},{16,18},{18,... | collective-permute-start | bytes 6291464 | tf_op jit(solution)/shard_map/ppermute | solution.py:81
  287.5 14.3 %collective-permute-start.40 = (bf16[2,64,2048]{2,1,0:T(8,128)(2,1)S(1)}, bf16[2,64,2048]{2,1,0:T(8,128)(2,1)S(1)}, u32[]{:S(2)}, u32[]{:S(2)}) collective-permute-start(bf16[2,64,2048]{2,1,0:T(8,128)(2,1)S(1)} %pad_maximum_fusion.9), channel_id=1, source_target_pairs={{0,8},{2,10},{4,12},{6,14},{8,0},{10,2},{12,4},{14,6},{16,24},{18,... | collective-permute-start | bytes 1572872 | tf_op jit(solution)/shard_map/ppermute | solution.py:81
  302.0 15.3 %collective-permute-start.41 = (bf16[16,64,1024]{2,1,0:T(8,128)(2,1)}, bf16[16,64,1024]{2,1,0:T(8,128)(2,1)S(1)}, u32[]{:S(2)}, u32[]{:S(2)}) collective-permute-start(bf16[16,64,1024]{2,1,0:T(8,128)(2,1)} %get-tuple-element.388), channel_id=1, source_target_pairs={{0,2},{2,0},{4,6},{6,4},{8,10},{10,8},{12,14},{14,12},{16,18},{18,... | collective-permute-start | bytes 6291464 | tf_op jit(solution)/shard_map/ppermute | solution.py:81
  302.1 15.2 %collective-permute-start.42 = (bf16[1,64,2048]{2,1,0:T(8,128)(2,1)S(1)}, bf16[1,64,2048]{2,1,0:T(8,128)(2,1)S(1)}, u32[]{:S(2)}, u32[]{:S(2)}) collective-permute-start(bf16[1,64,2048]{2,1,0:T(8,128)(2,1)S(1)} %get-tuple-element.389), channel_id=1, source_target_pairs={{0,16},{2,18},{4,20},{6,22},{8,24},{10,26},{12,28},{14,30},{16,0},... | collective-permute-start | bytes 786440 | tf_op jit(solution)/shard_map/ppermute | solution.py:81
  318.4 24.9 %collective-permute-start.43 = (bf16[8,64,1024]{2,1,0:T(8,128)(2,1)S(1)}, bf16[8,64,1024]{2,1,0:T(8,128)(2,1)S(1)}, u32[]{:S(2)}, u32[]{:S(2)}) collective-permute-start(bf16[8,64,1024]{2,1,0:T(8,128)(2,1)S(1)} %get-tuple-element.399), channel_id=1, source_target_pairs={{0,4},{2,6},{4,0},{6,2},{8,12},{10,14},{12,8},{14,10},{16,20},{18,... | collective-permute-start | bytes 3145736 | tf_op jit(solution)/shard_map/ppermute | solution.py:81
  318.9 24.6 %collective-permute-start.44 = (bf16[8,64,1024]{2,1,0:T(8,128)(2,1)S(1)}, bf16[8,64,1024]{2,1,0:T(8,128)(2,1)S(1)}, u32[]{:S(2)}, u32[]{:S(2)}) collective-permute-start(bf16[8,64,1024]{2,1,0:T(8,128)(2,1)S(1)} %get-tuple-element.400), channel_id=1, source_target_pairs={{0,1},{1,0},{2,3},{3,2},{4,5},{5,4},{6,7},{7,6},{8,9},{9,8},{10,11... | collective-permute-start | bytes 3145736 | tf_op jit(solution)/shard_map/ppermute | solution.py:81
  319.9 23.7 %collective-permute-start.45 = (bf16[16,64,512]{2,1,0:T(8,128)(2,1)S(1)}, bf16[16,64,512]{2,1,0:T(8,128)(2,1)S(1)}, u32[]{:S(2)}, u32[]{:S(2)}) collective-permute-start(bf16[16,64,512]{2,1,0:T(8,128)(2,1)S(1)} %copy-done.63), channel_id=1, source_target_pairs={{0,2},{2,0},{4,6},{6,4},{8,10},{10,8},{12,14},{14,12},{16,18},{18,... | collective-permute-start | bytes 3145736 | tf_op jit(solution)/shard_map/ppermute | solution.py:81
  344.4 19.6 %collective-permute-start.46 = (bf16[4,64,1024]{2,1,0:T(8,128)(2,1)S(1)}, bf16[4,64,1024]{2,1,0:T(8,128)(2,1)S(1)}, u32[]{:S(2)}, u32[]{:S(2)}) collective-permute-start(bf16[4,64,1024]{2,1,0:T(8,128)(2,1)S(1)} %get-tuple-element.406), channel_id=1, source_target_pairs={{0,1},{1,0},{2,3},{3,2},{4,5},{5,4},{6,7},{7,6},{8,9},{9,8},{10,11... | collective-permute-start | bytes 1572872 | tf_op jit(solution)/shard_map/ppermute | solution.py:81
  345.2 18.8 %collective-permute-start.47 = (bf16[4,64,1024]{2,1,0:T(8,128)(2,1)S(1)}, bf16[4,64,1024]{2,1,0:T(8,128)(2,1)S(1)}, u32[]{:S(2)}, u32[]{:S(2)}) collective-permute-start(bf16[4,64,1024]{2,1,0:T(8,128)(2,1)S(1)} %get-tuple-element.407), channel_id=1, source_target_pairs={{0,4},{2,6},{4,0},{6,2},{8,12},{10,14},{12,8},{14,10},{16,20},{18,... | collective-permute-start | bytes 1572872 | tf_op jit(solution)/shard_map/ppermute | solution.py:81
  364.6 12.9 %collective-permute-start.48 = (bf16[2,64,2048]{2,1,0:T(8,128)(2,1)S(1)}, bf16[2,64,2048]{2,1,0:T(8,128)(2,1)S(1)}, u32[]{:S(2)}, u32[]{:S(2)}) collective-permute-start(bf16[2,64,2048]{2,1,0:T(8,128)(2,1)S(1)} %pad_maximum_fusion.11), channel_id=1, source_target_pairs={{0,8},{2,10},{4,12},{6,14},{8,0},{10,2},{12,4},{14,6},{16,24},{18,... | collective-permute-start | bytes 1572872 | tf_op jit(solution)/shard_map/ppermute | solution.py:81
  364.6 12.8 %collective-permute-start.49 = (bf16[8,64,512]{2,1,0:T(8,128)(2,1)S(1)}, bf16[8,64,512]{2,1,0:T(8,128)(2,1)S(1)}, u32[]{:S(2)}, u32[]{:S(2)}) collective-permute-start(bf16[8,64,512]{2,1,0:T(8,128)(2,1)S(1)} %get-tuple-element.425), channel_id=1, source_target_pairs={{0,4},{2,6},{4,0},{6,2},{8,12},{10,14},{12,8},{14,10},{16,20},{18,... | collective-permute-start | bytes 1572872 | tf_op jit(solution)/shard_map/ppermute | solution.py:81
  379.0 31.2 %collective-permute-start.50 = (bf16[16,3,64,256]{3,2,1,0:T(8,128)(2,1)S(1)}, bf16[16,3,64,256]{3,2,1,0:T(8,128)(2,1)S(1)}, u32[]{:S(2)}, u32[]{:S(2)}) collective-permute-start(bf16[16,3,64,256]{3,2,1,0:T(8,128)(2,1)S(1)} %copy-done.54), channel_id=1, source_target_pairs={{0,2},{2,0},{4,6},{6,4},{8,10},{10,8},{12,14},{14,12},{16,18},{18,... | collective-permute-start | bytes 4718600 | tf_op jit(solution)/shard_map/ppermute | solution.py:81
  379.0 31.2 %collective-permute-start.53 = (bf16[1,512,1024]{2,1,0:T(8,128)(2,1)S(1)}, bf16[1,512,1024]{2,1,0:T(8,128)(2,1)S(1)}, u32[]{:S(2)}, u32[]{:S(2)}) collective-permute-start(bf16[1,512,1024]{2,1,0:T(8,128)(2,1)S(1)} %get-tuple-element.439), channel_id=1, source_target_pairs={{0,1},{1,0},{2,3},{3,2},{4,5},{5,4},{6,7},{7,6},{8,9},{9,8},{10,11... | collective-permute-start | bytes 3145736 | tf_op jit(solution)/shard_map/ppermute | solution.py:81
  380.3 22.8 %collective-permute-start.51 = (bf16[1,64,2048]{2,1,0:T(8,128)(2,1)S(1)}, bf16[1,64,2048]{2,1,0:T(8,128)(2,1)S(1)}, u32[]{:S(2)}, u32[]{:S(2)}) collective-permute-start(bf16[1,64,2048]{2,1,0:T(8,128)(2,1)S(1)} %get-tuple-element.437), channel_id=1, source_target_pairs={{0,16},{2,18},{4,20},{6,22},{8,24},{10,26},{12,28},{14,30},{16,0},... | collective-permute-start | bytes 786440 | tf_op jit(solution)/shard_map/ppermute | solution.py:81
  380.6 29.6 %collective-permute-start.52 = (bf16[4,64,512]{2,1,0:T(8,128)(2,1)S(1)}, bf16[4,64,512]{2,1,0:T(8,128)(2,1)S(1)}, u32[]{:S(2)}, u32[]{:S(2)}) collective-permute-start(bf16[4,64,512]{2,1,0:T(8,128)(2,1)S(1)} %get-tuple-element.438), channel_id=1, source_target_pairs={{0,1},{1,0},{2,3},{3,2},{4,5},{5,4},{6,7},{7,6},{8,9},{9,8},{10,11... | collective-permute-start | bytes 786440 | tf_op jit(solution)/shard_map/ppermute | solution.py:81
  411.0 12.8 %collective-permute-start.54 = (bf16[2,64,512]{2,1,0:T(8,128)(2,1)S(1)}, bf16[2,64,512]{2,1,0:T(8,128)(2,1)S(1)}, u32[]{:S(2)}, u32[]{:S(2)}) collective-permute-start(bf16[2,64,512]{2,1,0:T(8,128)(2,1)S(1)} %get-tuple-element.452), channel_id=1, source_target_pairs={{0,8},{2,10},{4,12},{6,14},{8,0},{10,2},{12,4},{14,6},{16,24},{18,... | collective-permute-start | bytes 393224 | tf_op jit(solution)/shard_map/ppermute | solution.py:81
  431.7 22.1 %collective-permute-start.56 = (bf16[8,3,64,256]{3,2,1,0:T(8,128)(2,1)S(1)}, bf16[8,3,64,256]{3,2,1,0:T(8,128)(2,1)S(1)}, u32[]{:S(2)}, u32[]{:S(2)}) collective-permute-start(bf16[8,3,64,256]{3,2,1,0:T(8,128)(2,1)S(1)} %get-tuple-element.467), channel_id=1, source_target_pairs={{0,4},{2,6},{4,0},{6,2},{8,12},{10,14},{12,8},{14,10},{16,20},{18,... | collective-permute-start | bytes 2359304 | tf_op jit(solution)/shard_map/ppermute | solution.py:81
  433.3 20.5 %collective-permute-start.57 = (bf16[8,3,64,256]{3,2,1,0:T(8,128)(2,1)S(1)}, bf16[8,3,64,256]{3,2,1,0:T(8,128)(2,1)}, u32[]{:S(2)}, u32[]{:S(2)}) collective-permute-start(bf16[8,3,64,256]{3,2,1,0:T(8,128)(2,1)S(1)} %get-tuple-element.468), channel_id=1, source_target_pairs={{0,1},{1,0},{2,3},{3,2},{4,5},{5,4},{6,7},{7,6},{8,9},{9,8},{10,11... | collective-permute-start | bytes 2359304 | tf_op jit(solution)/shard_map/ppermute | solution.py:81
  434.6 19.2 %collective-permute-start.58 = (bf16[1,64,512]{2,1,0:T(8,128)(2,1)S(1)}, bf16[1,64,512]{2,1,0:T(8,128)(2,1)S(1)}, u32[]{:S(2)}, u32[]{:S(2)}) collective-permute-start(bf16[1,64,512]{2,1,0:T(8,128)(2,1)S(1)} %get-tuple-element.469), channel_id=1, source_target_pairs={{0,16},{2,18},{4,20},{6,22},{8,24},{10,26},{12,28},{14,30},{16,0},... | collective-permute-start | bytes 196616 | tf_op jit(solution)/shard_map/ppermute | solution.py:81
  457.6 12.1 %collective-permute-start.62 = (bf16[4,3,64,256]{3,2,1,0:T(8,128)(2,1)S(1)}, bf16[4,3,64,256]{3,2,1,0:T(8,128)(2,1)S(1)}, u32[]{:S(2)}, u32[]{:S(2)}) collective-permute-start(bf16[4,3,64,256]{3,2,1,0:T(8,128)(2,1)S(1)} %get-tuple-element.484), channel_id=1, source_target_pairs={{0,1},{1,0},{2,3},{3,2},{4,5},{5,4},{6,7},{7,6},{8,9},{9,8},{10,11... | collective-permute-start | bytes 1179656 | tf_op jit(solution)/shard_map/ppermute | solution.py:81
  460.6 21.6 %collective-permute-start.59 = (bf16[1,256,1024]{2,1,0:T(8,128)(2,1)S(1)}, bf16[1,256,1024]{2,1,0:T(8,128)(2,1)S(1)}, u32[]{:S(2)}, u32[]{:S(2)}) collective-permute-start(bf16[1,256,1024]{2,1,0:T(8,128)(2,1)S(1)} %get-tuple-element.480), channel_id=1, source_target_pairs={{0,1},{1,0},{2,3},{3,2},{4,5},{5,4},{6,7},{7,6},{8,9},{9,8},{10,11... | collective-permute-start | bytes 1572872 | tf_op jit(solution)/shard_map/ppermute | solution.py:81
  476.0 16.5 %collective-permute-start.60 = (bf16[1,256,1024]{2,1,0:T(8,128)(2,1)S(1)}, bf16[1,256,1024]{2,1,0:T(8,128)(2,1)S(1)}, u32[]{:S(2)}, u32[]{:S(2)}) collective-permute-start(bf16[1,256,1024]{2,1,0:T(8,128)(2,1)S(1)} %get-tuple-element.481), channel_id=1, source_target_pairs={{0,1},{1,0},{2,3},{3,2},{4,5},{5,4},{6,7},{7,6},{8,9},{9,8},{10,11... | collective-permute-start | bytes 1572872 | tf_op jit(solution)/shard_map/ppermute | solution.py:81
  483.1 12.2 %collective-permute-start.68 = (f32[7184]{0:T(1024)S(1)}, f32[7184]{0:T(1024)S(1)}, u32[]{:S(2)}, u32[]{:S(2)}) collective-permute-start(f32[7184]{0:T(1024)S(1)} %add_add_fusion.1), channel_id=1, source_target_pairs={{0,8},{1,9},{2,10},{3,11},{4,12},{5,13},{6,14},{7,15},{8,0},{9,1},... | collective-permute-start | bytes 86216 | tf_op jit(solution)/shard_map/ppermute | solution.py:169
  (91 other events, 1071.4 us)

commit v4 on v3

--- a/solution.py
+++ b/solution.py
@@ -15,7 +15,7 @@
 ALL = ("batch", "tensor")
 GELU_C = math.sqrt(2.0 / math.pi)
 GELU_A = 0.044715
-STEP = 64
+STEP = 256
 
 
 def cost(us):
@@ -1072,7 +1072,7 @@
             more([down], far - 2)
             scaled = launch(scaled, [down])
     scaled = land(scaled, [wa, wb, down])
-    down_cut = half_cols + (up_chunk if half_cols % 1024 == 0 else 0)
+    down_cut = half_cols
     wda = down.columns(0, down_cut, steps[0][far:])
     wdb = down.columns(down_cut, local_hidden - down_cut, steps[1][far:])
     rows_cot = Rows(cotangent, micro_count, split)
@@ -1094,7 +1094,7 @@
         narrow = land(narrow, [wda, wdb])
         more([wda, wdb], near - 2)
         narrow = launch(narrow, [wda, wdb])
-    unit, h3, hidden, narrow, stat = land([unit, h3, hidden, narrow, stat], [rows_cot, wda, wdb])
+    unit, h3, hidden, narrow, stat = land([unit, h3, hidden, narrow, stat], [rows_cot, wda])
     cot = rows_cot.result
 
     def grad_half(n, a, b, name, turn=False):
@@ -1107,9 +1107,10 @@
                 hop([chain])
         return [chain.total for chain in chains]
 
-    cot_held = launch(cot, [wda, wdb])
+    cot_held = launch(cot, [wda])
     d0 = grad_half(0, cot_held, narrow, "grad_down", True)
-    cot_held = launch(cot_held, [d0])
+    d0.keep, d0.send = land((d0.keep, d0.send), [wdb])
+    cot_held = launch(cot_held, [d0, wdb])
     d1 = grad_half(1, cot_held, narrow, "grad_down", True)
     d1.keep, d1.send = land((d1.keep, d1.send), [d0, wda, wdb])
     hidden = launch(hidden, [d1, d0])
@@ -1127,31 +1128,33 @@
     dhidden = launch(dhidden, [u0, down_sum])
     u1 = grad_half(1, h3, dhidden, "grad_up")
     u1.keep, u1.send = land((u1.keep, u1.send), [u0, down_sum])
-    dmixed = launch(dmixed, [u1] + ([down_sum] if down_sum.steps else []))
+    dmixed = launch(dmixed, [u1])
     keep, send = weight_grad(
         tables[0], dmixed, [scaled], grid_of, 0, out_weight.shape[0], "grad_out"
     )
     o0 = Scatter(keep, send, steps[0])
-    flying = [u1, down_sum] if far > 1 else [u1]
-    o0.keep, o0.send = land((o0.keep, o0.send), flying)
-    da = launch(spread(dattended), [u0, u1, o0])
+    o0.keep, o0.send = land((o0.keep, o0.send), [u1])
+    flying = [u0, u1, o0] + ([down_sum] if down_sum.steps else [])
+    da = launch(spread(dattended), flying)
     halves, grads, inners = [], [], []
     for n in range(parts):
         *three, inner = attend_back(q, k, v, da, lse, ends, factor, tensor_count, parts, n)
         inners.append(inner)
         if n == 0:
-            three = land(three, [u0, u1, o0])
+            three = land(three, flying)
             narrow = launch(narrow, [u0, u1])
             block_out = feed_forward(orders, narrow, unit, x, norm_gains, wda, wdb, grid_of)
             block_out = land(block_out, [u0, u1])
             more([u0, u1], near - 2)
             up_sum = merged([u0, u1])
-            rows_out = Rows(block_out, micro_count, split)
+            rows_out = Rows(block_out, micro_count, split, 2)
             three = [collect(one) for one in three]
             three = launch(three, [up_sum, o0])
             flying = [up_sum, o0]
         else:
             three = land(three, flying)
+            three, first_out = lax.optimization_barrier((three, rows_out.arrived[0]))
+            rows_out.arrived[0] = first_out
             flying = [o0]
             three = launch(three, flying)
         keep, send = weight_grad(tables[n % 2], h1, three, grid_of, 0, part_cols, "grad_qkv")
@@ -1159,9 +1162,14 @@
         grads += three
         halves[-1].keep, halves[-1].send = land((halves[-1].keep, halves[-1].send), flying)
         if n < parts - 1:
-            flying = [halves[0], up_sum, o0, rows_out]
-            da = launch(da, flying)
+            flying = [halves[0], up_sum, o0]
+            da = launch(da, flying + [rows_out])
     q_last = halves[-1]
+    if parts > 1:
+        q_last.keep, q_last.send, rows_out.arrived = lax.optimization_barrier(
+            (q_last.keep, q_last.send, rows_out.arrived)
+        )
+        rows_out.end()
     dresid = launch(dresid, [q_last])
     dresid = land(dresid, [q_last])
     beside = halves + [o0] + ([] if parts > 1 else [rows_out])
@@ -1195,7 +1203,6 @@
         launch(after, tail)
         for one in tail:
             one.end()
-        after = rows_back.arrived[:1]
     rows_back.end()
     block_out, grad_in = rows_out.result, rows_back.result
     d_totals, u_totals, o_totals, q_totals = (

time: 514 us -> 487 us (0.947)
  waiting for transfers between devices: 108 us -> 87.7 us
  Pallas kernels: 284 us -> 266 us
    ppermute x65 -> x66, waiting for transfers between devices: 103 us -> 83 us  [swap(): return lax.ppermute(value, axis, [(i, i ^ flip) for i in range(count)])]
    pallas_call x2, Pallas kernels: 43.2 us -> 34.3 us  [hidden_forward(): pl.pallas_call(kernel, grid_spec=pltpu.PrefetchScalarGridSpec(num_scalar_...]
    ppermute x65 -> x66, starting transfers between devices: 56.3 us -> 61.1 us  [swap(): return lax.ppermute(value, axis, [(i, i ^ flip) for i in range(count)])]
    unnamed x141 -> x135, local copies, waits for them, and re-layouts: 11 us -> 9.2 us
  transfers between devices with their start and end apart: 72 -> 73, of which waited for: 29 -> 28; matrix products, arithmetic and copies ran while one was open for 3% -> 5% of each run, Pallas kernels for 54% -> 56%
where the time goes in v4:
time: 487 us; the launch traced here: 478 us
  Pallas kernels  266 us (55%)
  waiting for transfers between devices  87.7 us (18%)
  starting transfers between devices  69.1 us (14%)
  other arithmetic  28.7 us (6%)
  local copies, waits for them, and re-layouts  24 us (5%)
    ppermute x66, waiting for transfers between devices, swap(): return lax.ppermute(value, axis, [(i, i ^ flip) for i in range(count)])  83 us
    pallas_call x7, Pallas kernels, weight_grad(): pl.pallas_call(functools.partial(grad_kernel, grid_of, count, turn), grid...  70.7 us
    ppermute x66, starting transfers between devices, swap(): return lax.ppermute(value, axis, [(i, i ^ flip) for i in range(count)])  61.1 us
    pallas_call x1, Pallas kernels, feed_back(): pl.pallas_call(functools.partial(back_kernel, grid_of), grid_spec=pltpu.P...  46.9 us
    pallas_call x2, Pallas kernels, attend_back(): pl.pallas_call(functools.partial(attend_back_kernel, rows, block, factor)...  41.5 us
    pallas_call x2, Pallas kernels, hidden_forward(): pl.pallas_call(kernel, grid_spec=pltpu.PrefetchScalarGridSpec(num_scalar_...  34.3 us
    pallas_call x2, Pallas kernels, attend(): pl.pallas_call(kernel, grid_spec=pltpu.PrefetchScalarGridSpec(num_scalar_...  26.2 us
    convert_element_type x25, other arithmetic, end(): (keep[:half].astype(F32) + arrived[:half].astype(F32)).astype(BF)  20.1 us
  transfers between devices with their start and end apart: 73, of which 28 were waited for; matrix products, arithmetic and copies ran while one was open for 5% of the time, Pallas kernels for 56%

profile of v4, /device:TPU:0, one launch (start us, length us, event | category | flops | bytes accessed | tf_op | source)
XLA Modules:
  0.0 477.9 jit_solution(17547969931655562590)
XLA Ops:
  4.2 2.9 collective-permute-start
  7.1 2.6 collective-permute-start.1
  9.7 8.9 %collective-permute-done.1 = bf16[1,3,64,512]{3,2,1,0:T(8,128)(2,1)S(1)} collective-permute-done((bf16[1,3,64,512]{3,2,1,0:T(8,128)(2,1)S(1)}, bf16[1,3,64,512]{3,2,1,0:T(8,128)(2,1)S(1)}, u32[]{:S(2)}, u32[]{:S(2)}) %collective-permute-start.1) | collective-permute-done | bytes 196640 | tf_op jit(solution)/shard_map/ppermute | solution.py:81
  19.4 9.3 %collective-permute-done.2 = bf16[2,3,64,512]{3,2,1,0:T(8,128)(2,1)S(1)} collective-permute-done((bf16[2,3,64,512]{3,2,1,0:T(8,128)(2,1)S(1)}, bf16[2,3,64,512]{3,2,1,0:T(8,128)(2,1)S(1)}, u32[]{:S(2)}, u32[]{:S(2)}) %collective-permute-start.2) | collective-permute-done | bytes 393248 | tf_op jit(solution)/shard_map/ppermute | solution.py:81
  30.3 1.8 collective-permute-start.4
  33.6 2.7 collective-permute-start.7
  36.2 4.3 collective-permute-done.4
  43.9 5.7 %collective-permute-done.7 = bf16[1,64,2560]{2,1,0:T(8,128)(2,1)S(1)} collective-permute-done((bf16[1,64,2560]{2,1,0:T(8,128)(2,1)S(1)}, bf16[1,64,2560]{2,1,0:T(8,128)(2,1)S(1)}, u32[]{:S(2)}, u32[]{:S(2)}) %collective-permute-start.7) | collective-permute-done | bytes 327712 | tf_op jit(solution)/shard_map/ppermute | solution.py:81
  52.0 7.2 %collective-permute-done.5.refs_1_.refs_10_ = bf16[8,3,64,256]{3,2,1,0:T(8,128)(2,1)} collective-permute-done((bf16[8,3,64,256]{3,2,1,0:T(8,128)(2,1)S(1)}, bf16[8,3,64,256]{3,2,1,0:T(8,128)(2,1)}, u32[]{:S(2)}, u32[]{:S(2)}) %collective-permute-start.5) | collective-permute-done | bytes 786464 | tf_op jit(solution)/shard_map/ppermute | solution.py:81
  61.2 4.1 collective-permute-done.8
  66.7 14.4 %project.1 = (bf16[1024,1024]{1,0:T(8,128)(2,1)}, bf16[1024,1024]{1,0:T(8,128)(2,1)}, bf16[1024,1024]{1,0:T(8,128)(2,1)}, bf16[1024,1024]{1,0:T(8,128)(2,1)}) custom-call(s32[64]{0:T(128)S(1)} %pad_add_fusion.order_ref, bf16[1024,1024]{1,0:T(8,128)(2,1)} %bitcast.3.x_ref.refs_1_.refs_6_, f32[3,1024]{1,0:T(4,128)S(1)} %copy-done.4, ...), custom_call_target="tpu_custom_call" | custom-call | flops 12999999488 | bytes 1048576 | tf_op jit(solution)/shard_map/project/pallas_call | solution.py:343
  84.5 3.4 collective-permute-start.16
  87.9 13.1 %attend.2 = (bf16[1024,1024]{1,0:T(8,128)(2,1)}, f32[8,2,1024]{2,1,0:T(2,128)}) custom-call(s32[4]{0:T(128)S(1)} %bitcast.33, bf16[1024,1024]{1,0:T(8,128)(2,1)} %get-tuple-element.284.q_ref, bf16[1024,1024]{1,0:T(8,128)(2,1)} %get-tuple-element.285.k_ref, bf16[1024,1024]{1,0:T(8,128)(2,1)} %get-tuple-element.286.v_ref, ...), custom_call_target="tpu_custom_call" | custom-call | flops 12000000000 | bytes 1048576 | tf_op jit(solution)/shard_map/attend/pallas_call | solution.py:466
  101.1 1.8 collective-permute-start.19
  102.9 13.1 %attend.3 = (bf16[1024,1024]{1,0:T(8,128)(2,1)}, f32[8,2,1024]{2,1,0:T(2,128)}) custom-call(s32[4]{0:T(128)S(1)} %bitcast.34, bf16[1024,1024]{1,0:T(8,128)(2,1)} %get-tuple-element.284.q_ref, bf16[1024,1024]{1,0:T(8,128)(2,1)} %get-tuple-element.285.k_ref, ...), custom_call_target="tpu_custom_call", output_to_operand_aliasing={{0}: (5, {}), {1}: (6, {})} | custom-call | flops 12000000000 | bytes 1048576 | tf_op jit(solution)/shard_map/attend/pallas_call | solution.py:466
  119.1 1.9 collective-permute-done.21.refs_11_.b3
  125.6 17.3 %hidden_forward.2 = (f32[1024,1024]{1,0:T(8,128)}, bf16[1024,1024]{1,0:T(8,128)(2,1)}, f32[1024,4096]{1,0:T(8,128)}, bf16[1024,4096]{1,0:T(8,128)(2,1)}, f32[1024,128]{1,0:T(8,128)}) custom-call(s32[64]{0:T(128)S(1)} %pad_add_fusion.order_ref, bf16[1024,1024]{1,0:T(8,128)(2,1)} %get-tuple-element.306.refs_0_, ...), custom_call_target="tpu_custom_call" | custom-call | flops 15000000512 | bytes 1048576 | tf_op jit(solution)/shard_map/hidden_forward/pallas_call | solution.py:602
  144.7 17.0 %hidden_forward.3 = (f32[1024,1024]{1,0:T(8,128)}, bf16[1024,1024]{1,0:T(8,128)(2,1)}, f32[1024,4096]{1,0:T(8,128)}, bf16[1024,4096]{1,0:T(8,128)(2,1)}, f32[1024,128]{1,0:T(8,128)}) custom-call(s32[64]{0:T(128)S(1)} %pad_add_fusion.order_ref, ...), custom_call_target="tpu_custom_call", output_to_operand_aliasing={{0}: (13, {}), {1}: (14, {}), {2}: (15, {}), {3}: (16, {}),... | custom-call | flops 15000000512 | bytes 1048576 | tf_op jit(solution)/shard_map/hidden_forward/pallas_call | solution.py:602
  161.7 5.8 %collective-permute-done.27.da1.a1 = bf16[8,64,1024]{2,1,0:T(8,128)(2,1)S(1)} collective-permute-done((bf16[8,64,1024]{2,1,0:T(8,128)(2,1)S(1)}, bf16[8,64,1024]{2,1,0:T(8,128)(2,1)S(1)}, u32[]{:S(2)}, u32[]{:S(2)}) %collective-permute-start.27) | collective-permute-done | bytes 1048608 | tf_op jit(solution)/shard_map/ppermute | solution.py:81
  169.2 10.6 %grad_down.2 = (bf16[16,64,1024]{2,1,0:T(8,128)(2,1)}, bf16[16,64,1024]{2,1,0:T(8,128)(2,1)}) custom-call(s32[32]{0:T(128)S(1)} %get-tuple-element.586.order_ref, bf16[1024,1024]{1,0:T(8,128)(2,1)} %bitcast.37, bf16[1024,4096]{1,0:T(8,128)(2,1)} %get-tuple-element.417.refs_0_.narrow_ref), custom_call_target="tpu_custom_call" | custom-call | flops 4800000000 | bytes 1048576 | tf_op jit(solution)/shard_map/grad_down/pallas_call | solution.py:873
  180.5 11.0 %grad_down.3 = (bf16[16,64,1024]{2,1,0:T(8,128)(2,1)}, bf16[16,64,1024]{2,1,0:T(8,128)(2,1)}) custom-call(s32[32]{0:T(128)S(1)} %get-tuple-element.585.order_ref, bf16[1024,1024]{1,0:T(8,128)(2,1)} %bitcast.38, bf16[1024,4096]{1,0:T(8,128)(2,1)} %get-tuple-element.417.refs_0_.narrow_ref), custom_call_target="tpu_custom_call" | custom-call | flops 4800000000 | bytes 1048576 | tf_op jit(solution)/shard_map/grad_down/pallas_call | solution.py:873
  191.6 2.0 add_convert_fusion.6
  196.3 2.2 collective-permute-done.32
  198.5 2.0 add_convert_fusion.4
  202.5 46.9 %feed_back.1 = (bf16[1024,4096]{1,0:T(8,128)(2,1)}, f32[1024,1024]{1,0:T(8,128)}, bf16[1024,1024]{1,0:T(8,128)(2,1)}, bf16[1024,1024]{1,0:T(8,128)(2,1)}, f32[16,1024]{1,0:T(8,128)}, /*index=5*/f32[8,4096]{1,0:T(8,128)}) custom-call(s32[64]{0:T(128)} %copy-done.6, f32[1024,4096]{1,0:T(8,128)} %get-tuple-element.353.hidden_ref, ...), custom_call_target="tpu_custom_call" | custom-call | flops 60000002048 | bytes 1048576 | tf_op jit(solution)/shard_map/feed_back/pallas_call | solution.py:782
  253.7 10.0 %grad_up.2 = (bf16[16,64,1024]{2,1,0:T(8,128)(2,1)}, bf16[16,64,1024]{2,1,0:T(8,128)(2,1)}) custom-call(s32[32]{0:T(128)S(1)} %get-tuple-element.586.order_ref, bf16[1024,1024]{1,0:T(8,128)(2,1)} %get-tuple-element.373.a_ref, bf16[1024,4096]{1,0:T(8,128)(2,1)} %get-tuple-element.385.refs_0_), custom_call_target="tpu_custom_call" | custom-call | flops 4800000000 | bytes 1048576 | tf_op jit(solution)/shard_map/grad_up/pallas_call | solution.py:873
  263.7 2.1 collective-permute-done.37
  268.8 10.0 %grad_up.3 = (bf16[16,64,1024]{2,1,0:T(8,128)(2,1)}, bf16[16,64,1024]{2,1,0:T(8,128)(2,1)}) custom-call(s32[32]{0:T(128)S(1)} %get-tuple-element.585.order_ref, bf16[1024,1024]{1,0:T(8,128)(2,1)} %get-tuple-element.373.a_ref, bf16[1024,4096]{1,0:T(8,128)(2,1)} %get-tuple-element.385.refs_0_), custom_call_target="tpu_custom_call" | custom-call | flops 4800000000 | bytes 1048576 | tf_op jit(solution)/shard_map/grad_up/pallas_call | solution.py:873
  278.8 3.6 collective-permute-done.40
  282.5 6.6 %grad_out.1 = (bf16[16,64,512]{2,1,0:T(8,128)(2,1)}, bf16[16,64,512]{2,1,0:T(8,128)(2,1)}) custom-call(s32[32]{0:T(128)S(1)} %get-tuple-element.586.order_ref, bf16[1024,1024]{1,0:T(8,128)(2,1)} %get-tuple-element.395.a_ref, bf16[1024,1024]{1,0:T(8,128)(2,1)} %get-tuple-element.306.refs_0_), custom_call_target="tpu_custom_call" | custom-call | flops 2400000000 | bytes 1048576 | tf_op jit(solution)/shard_map/grad_out/pallas_call | solution.py:873
  290.7 2.3 add_convert_fusion
  295.3 1.9 collective-permute-start.45
  297.2 20.8 %attend_back.2 = (bf16[1024,512]{1,0:T(8,128)(2,1)}, bf16[1024,512]{1,0:T(8,128)(2,1)}, bf16[1024,512]{1,0:T(8,128)(2,1)}, f32[4,2,1024]{2,1,0:T(2,128)}) custom-call(s32[4]{0:T(128)S(1)} %bitcast.35, bf16[1024,1024]{1,0:T(8,128)(2,1)} %get-tuple-element.284.q_ref, bf16[1024,1024]{1,0:T(8,128)(2,1)} %get-tuple-element.285.k_ref, ...), custom_call_target="tpu_custom_call" | custom-call | flops 20999999488 | bytes 1048576 | tf_op jit(solution)/shard_map/attend_back/pallas_call | solution.py:495
  322.5 16.8 %feed_forward.1 = bf16[1024,1024]{1,0:T(8,128)(2,1)} custom-call(s32[64]{0:T(128)S(1)} %copy-done.7, bf16[1024,4096]{1,0:T(8,128)(2,1)} %get-tuple-element.417.refs_0_.narrow_ref, f32[1024,1024]{1,0:T(8,128)} %get-tuple-element.355.unit_ref, bf16[1024,1024]{1,0:T(8,128)(2,1)} %bitcast.3.x_ref.refs_1_.refs_6_, f32[3,1024]{1,0:T(4,128)S(1)} %copy-done.5, ...), custom_call_target="tpu_custom_call" | custom-call | flops 14000000000 | bytes 1048576 | tf_op jit(solution)/shard_map/feed_forward/pallas_call | solution.py:666
  346.7 11.1 %grad_qkv.2 = (bf16[16,3,64,256]{3,2,1,0:T(8,128)(2,1)}, bf16[16,3,64,256]{3,2,1,0:T(8,128)(2,1)}) custom-call(s32[32]{0:T(128)S(1)} %get-tuple-element.586.order_ref, bf16[1024,1024]{1,0:T(8,128)(2,1)} %get-tuple-element.421.a_ref, bf16[1024,512]{1,0:T(8,128)(2,1)} %get-tuple-element.431.refs_0_, bf16[1024,512]{1,0:T(8,128)(2,1)} %get-tuple-element.432.refs_1_, ...), custom_call_target="tpu_custom_call" | custom-call | flops 3600000000 | bytes 1048576 | tf_op jit(solution)/shard_map/grad_qkv/pallas_call | solution.py:873
  360.3 2.5 collective-permute-start.51
  364.9 20.7 %attend_back.3 = (bf16[1024,512]{1,0:T(8,128)(2,1)}, bf16[1024,512]{1,0:T(8,128)(2,1)}, bf16[1024,512]{1,0:T(8,128)(2,1)}, f32[4,2,1024]{2,1,0:T(2,128)}) custom-call(s32[4]{0:T(128)S(1)} %bitcast.36, bf16[1024,1024]{1,0:T(8,128)(2,1)} %get-tuple-element.284.q_ref, bf16[1024,1024]{1,0:T(8,128)(2,1)} %get-tuple-element.285.k_ref, ...), custom_call_target="tpu_custom_call" | custom-call | flops 20999999488 | bytes 1048576 | tf_op jit(solution)/shard_map/attend_back/pallas_call | solution.py:495
  387.6 11.4 %grad_qkv.3 = (bf16[16,3,64,256]{3,2,1,0:T(8,128)(2,1)}, bf16[16,3,64,256]{3,2,1,0:T(8,128)(2,1)}) custom-call(s32[32]{0:T(128)S(1)} %get-tuple-element.585.order_ref, bf16[1024,1024]{1,0:T(8,128)(2,1)} %get-tuple-element.421.a_ref, bf16[1024,512]{1,0:T(8,128)(2,1)} %get-tuple-element.460.refs_0_.refs_3_, ...), custom_call_target="tpu_custom_call" | custom-call | flops 3600000000 | bytes 1048576 | tf_op jit(solution)/shard_map/grad_qkv/pallas_call | solution.py:873
  403.0 2.6 add_convert_fusion.10
  406.6 1.9 add_convert_fusion.8
  411.4 15.3 %input_grad.1 = (bf16[1024,1024]{1,0:T(8,128)(2,1)}, f32[8,1024]{1,0:T(8,128)}) custom-call(s32[64]{0:T(128)S(1)} %copy-done.7, bf16[1024,512]{1,0:T(8,128)(2,1)} %get-tuple-element.431.refs_0_, bf16[1024,512]{1,0:T(8,128)(2,1)} %get-tuple-element.432.refs_1_, bf16[1024,512]{1,0:T(8,128)(2,1)} %get-tuple-element.433.refs_2_, ...), custom_call_target="tpu_custom_call" | custom-call | flops 15000000512 | bytes 1048576 | tf_op jit(solution)/shard_map/input_grad/pallas_call | solution.py:932
  433.2 1.9 constant_dynamic-update-slice_fusion.6
  438.5 5.6 %collective-permute-done.63 = bf16[4,3,64,256]{3,2,1,0:T(8,128)(2,1)S(1)} collective-permute-done((bf16[4,3,64,256]{3,2,1,0:T(8,128)(2,1)S(1)}, bf16[4,3,64,256]{3,2,1,0:T(8,128)(2,1)S(1)}, u32[]{:S(2)}, u32[]{:S(2)}) %collective-permute-start.63) | collective-permute-done | bytes 393248 | tf_op jit(solution)/shard_map/ppermute | solution.py:81
  444.2 1.7 collective-permute-done.64
  452.5 3.5 collective-permute-done.66
  460.0 2.9 collective-permute-start.71
  462.9 3.3 collective-permute-done.61
  468.9 7.8 %collective-permute-done.72 = bf16[1,3,64,512]{3,2,1,0:T(8,128)(2,1)S(1)} collective-permute-done((bf16[1,3,64,512]{3,2,1,0:T(8,128)(2,1)S(1)}, bf16[1,3,64,512]{3,2,1,0:T(8,128)(2,1)S(1)}, u32[]{:S(2)}, u32[]{:S(2)}) %collective-permute-start.72) | collective-permute-done | bytes 196640 | tf_op jit(solution)/shard_map/ppermute | solution.py:81
  (346 shorter events, 97.2 us)
Async XLA Ops:
  4.2 26.1 %collective-permute-start = (bf16[1,512,1024]{2,1,0:T(8,128)(2,1)S(1)}, bf16[1,512,1024]{2,1,0:T(8,128)(2,1)S(1)}, u32[]{:S(2)}, u32[]{:S(2)}) collective-permute-start(bf16[1,512,1024]{2,1,0:T(8,128)(2,1)S(1)} %get-tuple-element.264), channel_id=1, source_target_pairs={{0,1},{1,0},{2,3},{3,2},{4,5},{5,4},{6,7},{7,6},{8,9},{9,8},{10,11... | collective-permute-start | bytes 3145736 | tf_op jit(solution)/shard_map/ppermute | solution.py:81
  7.1 11.5 %collective-permute-start.1 = (bf16[1,3,64,512]{3,2,1,0:T(8,128)(2,1)S(1)}, bf16[1,3,64,512]{3,2,1,0:T(8,128)(2,1)S(1)}, u32[]{:S(2)}, u32[]{:S(2)}) collective-permute-start(bf16[1,3,64,512]{3,2,1,0:T(8,128)(2,1)S(1)} %bitcast.46), channel_id=1, source_target_pairs={{0,16},{2,18},{4,20},{6,22},{8,24},{10,26},{12,28},{14,30},{16,0},... | collective-permute-start | bytes 589832 | tf_op jit(solution)/shard_map/ppermute | solution.py:81
  33.6 16.0 %collective-permute-start.7 = (bf16[1,64,2560]{2,1,0:T(8,128)(2,1)S(1)}, bf16[1,64,2560]{2,1,0:T(8,128)(2,1)S(1)}, u32[]{:S(2)}, u32[]{:S(2)}) collective-permute-start(bf16[1,64,2560]{2,1,0:T(8,128)(2,1)S(1)} %maximum_bitcast_fusion), channel_id=1, source_target_pairs={{0,16},{2,18},{4,20},{6,22},{8,24},{10,26},{12,28},{14,30},{16,0},... | collective-permute-start | bytes 983048 | tf_op jit(solution)/shard_map/ppermute | solution.py:81
  41.8 17.4 %collective-permute-start.5 = (bf16[8,3,64,256]{3,2,1,0:T(8,128)(2,1)S(1)}, bf16[8,3,64,256]{3,2,1,0:T(8,128)(2,1)}, u32[]{:S(2)}, u32[]{:S(2)}) collective-permute-start(bf16[8,3,64,256]{3,2,1,0:T(8,128)(2,1)S(1)} %pad_maximum_fusion.4.refs_0_.refs_9_), channel_id=1, source_target_pairs={{0,4},{2,6},{4,0},{6,2},{8,12},{10,14},{12,8},{14,10},{16,20},{18,... | collective-permute-start | bytes 2359304 | tf_op jit(solution)/shard_map/ppermute | solution.py:81
  42.5 17.5 %collective-permute-start.6 = (bf16[8,3,64,256]{3,2,1,0:T(8,128)(2,1)S(1)}, bf16[8,3,64,256]{3,2,1,0:T(8,128)(2,1)}, u32[]{:S(2)}, u32[]{:S(2)}) collective-permute-start(bf16[8,3,64,256]{3,2,1,0:T(8,128)(2,1)S(1)} %pad_maximum_fusion.5.refs_4_.refs_13_), channel_id=1, source_target_pairs={{0,1},{1,0},{2,3},{3,2},{4,5},{5,4},{6,7},{7,6},{8,9},{9,8},{10,11... | collective-permute-start | bytes 2359304 | tf_op jit(solution)/shard_map/ppermute | solution.py:81
  49.6 15.7 %collective-permute-start.8 = (bf16[2,64,2560]{2,1,0:T(8,128)(2,1)S(1)}, bf16[2,64,2560]{2,1,0:T(8,128)(2,1)S(1)}, u32[]{:S(2)}, u32[]{:S(2)}) collective-permute-start(bf16[2,64,2560]{2,1,0:T(8,128)(2,1)S(1)} %pad_maximum_fusion.7), channel_id=1, source_target_pairs={{0,8},{2,10},{4,12},{6,14},{8,0},{10,2},{12,4},{14,6},{16,24},{18,... | collective-permute-start | bytes 1966088 | tf_op jit(solution)/shard_map/ppermute | solution.py:81
  52.0 14.0 %collective-permute-start.11 = (bf16[8,3,64,256]{3,2,1,0:T(8,128)(2,1)S(1)}, bf16[8,3,64,256]{3,2,1,0:T(8,128)(2,1)}, u32[]{:S(2)}, u32[]{:S(2)}) collective-permute-start(bf16[8,3,64,256]{3,2,1,0:T(8,128)(2,1)S(1)} %pad_maximum_fusion.5.refs_4_.refs_13_), channel_id=1, source_target_pairs={{0,2},{2,0},{4,6},{6,4},{8,10},{10,8},{12,14},{14,12},{16,18},{18,... | collective-permute-start | bytes 2359304 | tf_op jit(solution)/shard_map/ppermute | solution.py:81
  65.4 15.6 %collective-permute-start.13 = (bf16[4,64,1280]{2,1,0:T(8,128)(2,1)S(1)}, bf16[4,64,1280]{2,1,0:T(8,128)(2,1)S(1)}, u32[]{:S(2)}, u32[]{:S(2)}) collective-permute-start(bf16[4,64,1280]{2,1,0:T(8,128)(2,1)S(1)} %get-tuple-element.278), channel_id=1, source_target_pairs={{0,1},{1,0},{2,3},{3,2},{4,5},{5,4},{6,7},{7,6},{8,9},{9,8},{10,11... | collective-permute-start | bytes 1966088 | tf_op jit(solution)/shard_map/ppermute | solution.py:81
  66.0 15.1 %collective-permute-start.14 = (bf16[4,64,1280]{2,1,0:T(8,128)(2,1)S(1)}, bf16[4,64,1280]{2,1,0:T(8,128)(2,1)S(1)}, u32[]{:S(2)}, u32[]{:S(2)}) collective-permute-start(bf16[4,64,1280]{2,1,0:T(8,128)(2,1)S(1)} %get-tuple-element.279), channel_id=1, source_target_pairs={{0,4},{2,6},{4,0},{6,2},{8,12},{10,14},{12,8},{14,10},{16,20},{18,... | collective-permute-start | bytes 1966088 | tf_op jit(solution)/shard_map/ppermute | solution.py:81
  81.3 34.6 %collective-permute-start.17 = (bf16[8,64,1280]{2,1,0:T(8,128)(2,1)S(1)}, bf16[8,64,1280]{2,1,0:T(8,128)(2,1)S(1)}, u32[]{:S(2)}, u32[]{:S(2)}) collective-permute-start(bf16[8,64,1280]{2,1,0:T(8,128)(2,1)S(1)} %pad_maximum_fusion.refs_4_.a0), channel_id=1, source_target_pairs={{0,4},{2,6},{4,0},{6,2},{8,12},{10,14},{12,8},{14,10},{16,20},{18,... | collective-permute-start | bytes 3932168 | tf_op jit(solution)/shard_map/ppermute | solution.py:81
  82.8 41.3 %collective-permute-start.22 = (bf16[8,64,1280]{2,1,0:T(8,128)(2,1)S(1)}, bf16[8,64,1280]{2,1,0:T(8,128)(2,1)S(1)}, u32[]{:S(2)}, u32[]{:S(2)}) collective-permute-start(bf16[8,64,1280]{2,1,0:T(8,128)(2,1)S(1)} %pad_maximum_fusion.refs_4_.a0), channel_id=1, source_target_pairs={{0,2},{2,0},{4,6},{6,4},{8,10},{10,8},{12,14},{14,12},{16,18},{18,... | collective-permute-start | bytes 3932168 | tf_op jit(solution)/shard_map/ppermute | solution.py:81
  82.8 33.2 %collective-permute-start.18 = (bf16[8,64,1280]{2,1,0:T(8,128)(2,1)S(1)}, bf16[8,64,1280]{2,1,0:T(8,128)(2,1)S(1)}, u32[]{:S(2)}, u32[]{:S(2)}) collective-permute-start(bf16[8,64,1280]{2,1,0:T(8,128)(2,1)S(1)} %pad_maximum_fusion.1.refs_8_.b0), channel_id=1, source_target_pairs={{0,1},{1,0},{2,3},{3,2},{4,5},{5,4},{6,7},{7,6},{8,9},{9,8},{10,11... | collective-permute-start | bytes 3932168 | tf_op jit(solution)/shard_map/ppermute | solution.py:81
  84.3 39.8 %collective-permute-start.23 = (bf16[8,64,1280]{2,1,0:T(8,128)(2,1)S(1)}, bf16[8,64,1280]{2,1,0:T(8,128)(2,1)S(1)}, u32[]{:S(2)}, u32[]{:S(2)}) collective-permute-start(bf16[8,64,1280]{2,1,0:T(8,128)(2,1)S(1)} %pad_maximum_fusion.1.refs_8_.b0), channel_id=1, source_target_pairs={{0,2},{2,0},{4,6},{6,4},{8,10},{10,8},{12,14},{14,12},{16,18},{18,... | collective-permute-start | bytes 3932168 | tf_op jit(solution)/shard_map/ppermute | solution.py:81
  84.5 16.5 %collective-permute-start.16 = (bf16[1,64,2048]{2,1,0:T(8,128)(2,1)S(1)}, bf16[1,64,2048]{2,1,0:T(8,128)(2,1)S(1)}, u32[]{:S(2)}, u32[]{:S(2)}) collective-permute-start(bf16[1,64,2048]{2,1,0:T(8,128)(2,1)S(1)} %bitcast.44), channel_id=1, source_target_pairs={{0,16},{2,18},{4,20},{6,22},{8,24},{10,26},{12,28},{14,30},{16,0},... | collective-permute-start | bytes 786440 | tf_op jit(solution)/shard_map/ppermute | solution.py:81
  101.1 14.9 %collective-permute-start.19 = (bf16[2,64,2048]{2,1,0:T(8,128)(2,1)S(1)}, bf16[2,64,2048]{2,1,0:T(8,128)(2,1)S(1)}, u32[]{:S(2)}, u32[]{:S(2)}) collective-permute-start(bf16[2,64,2048]{2,1,0:T(8,128)(2,1)S(1)} %pad_maximum_fusion.8), channel_id=1, source_target_pairs={{0,8},{2,10},{4,12},{6,14},{8,0},{10,2},{12,4},{14,6},{16,24},{18,... | collective-permute-start | bytes 1572872 | tf_op jit(solution)/shard_map/ppermute | solution.py:81
  121.0 21.9 %collective-permute-start.24 = (bf16[4,64,1024]{2,1,0:T(8,128)(2,1)S(1)}, bf16[4,64,1024]{2,1,0:T(8,128)(2,1)S(1)}, u32[]{:S(2)}, u32[]{:S(2)}) collective-permute-start(bf16[4,64,1024]{2,1,0:T(8,128)(2,1)S(1)} %get-tuple-element.310), channel_id=1, source_target_pairs={{0,1},{1,0},{2,3},{3,2},{4,5},{5,4},{6,7},{7,6},{8,9},{9,8},{10,11... | collective-permute-start | bytes 1572872 | tf_op jit(solution)/shard_map/ppermute | solution.py:81
  121.5 21.3 %collective-permute-start.25 = (bf16[4,64,1024]{2,1,0:T(8,128)(2,1)S(1)}, bf16[4,64,1024]{2,1,0:T(8,128)(2,1)S(1)}, u32[]{:S(2)}, u32[]{:S(2)}) collective-permute-start(bf16[4,64,1024]{2,1,0:T(8,128)(2,1)S(1)} %get-tuple-element.311), channel_id=1, source_target_pairs={{0,4},{2,6},{4,0},{6,2},{8,12},{10,14},{12,8},{14,10},{16,20},{18,... | collective-permute-start | bytes 1572872 | tf_op jit(solution)/shard_map/ppermute | solution.py:81
  122.6 39.1 %collective-permute-start.26 = (bf16[1,512,1024]{2,1,0:T(8,128)(2,1)S(1)}, bf16[1,512,1024]{2,1,0:T(8,128)(2,1)S(1)}, u32[]{:S(2)}, u32[]{:S(2)}) collective-permute-start(bf16[1,512,1024]{2,1,0:T(8,128)(2,1)S(1)} %get-tuple-element.325), channel_id=1, source_target_pairs={{0,1},{1,0},{2,3},{3,2},{4,5},{5,4},{6,7},{7,6},{8,9},{9,8},{10,11... | collective-permute-start | bytes 3145736 | tf_op jit(solution)/shard_map/ppermute | solution.py:81
  143.1 24.4 %collective-permute-start.27 = (bf16[8,64,1024]{2,1,0:T(8,128)(2,1)S(1)}, bf16[8,64,1024]{2,1,0:T(8,128)(2,1)S(1)}, u32[]{:S(2)}, u32[]{:S(2)}) collective-permute-start(bf16[8,64,1024]{2,1,0:T(8,128)(2,1)S(1)} %pad_maximum_fusion.2.da0.a0), channel_id=1, source_target_pairs={{0,4},{2,6},{4,0},{6,2},{8,12},{10,14},{12,8},{14,10},{16,20},{18,... | collective-permute-start | bytes 3145736 | tf_op jit(solution)/shard_map/ppermute | solution.py:81
  144.1 35.8 %collective-permute-start.28 = (bf16[8,64,1024]{2,1,0:T(8,128)(2,1)S(1)}, bf16[8,64,1024]{2,1,0:T(8,128)(2,1)S(1)}, u32[]{:S(2)}, u32[]{:S(2)}) collective-permute-start(bf16[8,64,1024]{2,1,0:T(8,128)(2,1)S(1)} %pad_maximum_fusion.3.db0.b0), channel_id=1, source_target_pairs={{0,1},{1,0},{2,3},{3,2},{4,5},{5,4},{6,7},{7,6},{8,9},{9,8},{10,11... | collective-permute-start | bytes 3145736 | tf_op jit(solution)/shard_map/ppermute | solution.py:81
  179.9 11.6 %collective-permute-start.29 = (bf16[16,64,1024]{2,1,0:T(8,128)(2,1)}, bf16[16,64,1024]{2,1,0:T(8,128)(2,1)S(1)}, u32[]{:S(2)}, u32[]{:S(2)}) collective-permute-start(bf16[16,64,1024]{2,1,0:T(8,128)(2,1)} %get-tuple-element.341), channel_id=1, source_target_pairs={{0,2},{2,0},{4,6},{6,4},{8,10},{10,8},{12,14},{14,12},{16,18},{18,... | collective-permute-start | bytes 6291464 | tf_op jit(solution)/shard_map/ppermute | solution.py:81
  180.0 11.6 %collective-permute-start.31 = (bf16[8,64,1024]{2,1,0:T(8,128)(2,1)S(1)}, bf16[8,64,1024]{2,1,0:T(8,128)(2,1)S(1)}, u32[]{:S(2)}, u32[]{:S(2)}) collective-permute-start(bf16[8,64,1024]{2,1,0:T(8,128)(2,1)S(1)} %collective-permute-done.28.db1.b1), channel_id=1, source_target_pairs={{0,2},{2,0},{4,6},{6,4},{8,10},{10,8},{12,14},{14,12},{16,18},{18,... | collective-permute-start | bytes 3145736 | tf_op jit(solution)/shard_map/ppermute | solution.py:81
  195.2 54.2 %collective-permute-start.35 = (bf16[8,64,1024]{2,1,0:T(8,128)(2,1)}, bf16[8,64,1024]{2,1,0:T(8,128)(2,1)S(1)}, u32[]{:S(2)}, u32[]{:S(2)}) collective-permute-start(bf16[8,64,1024]{2,1,0:T(8,128)(2,1)} %get-tuple-element.364), channel_id=1, source_target_pairs={{0,4},{2,6},{4,0},{6,2},{8,12},{10,14},{12,8},{14,10},{16,20},{18,... | collective-permute-start | bytes 3145736 | tf_op jit(solution)/shard_map/ppermute | solution.py:81
  200.5 48.9 %collective-permute-start.36 = (bf16[8,64,1024]{2,1,0:T(8,128)(2,1)}, bf16[8,64,1024]{2,1,0:T(8,128)(2,1)}, u32[]{:S(2)}, u32[]{:S(2)}) collective-permute-start(bf16[8,64,1024]{2,1,0:T(8,128)(2,1)} %get-tuple-element.365), channel_id=1, source_target_pairs={{0,1},{1,0},{2,3},{3,2},{4,5},{5,4},{6,7},{7,6},{8,9},{9,8},{10,11... | collective-permute-start | bytes 3145736 | tf_op jit(solution)/shard_map/ppermute | solution.py:81
  251.6 14.3 %collective-permute-start.37 = (bf16[4,64,1024]{2,1,0:T(8,128)(2,1)S(1)}, bf16[4,64,1024]{2,1,0:T(8,128)(2,1)S(1)}, u32[]{:S(2)}, u32[]{:S(2)}) collective-permute-start(bf16[4,64,1024]{2,1,0:T(8,128)(2,1)S(1)} %get-tuple-element.376), channel_id=1, source_target_pairs={{0,1},{1,0},{2,3},{3,2},{4,5},{5,4},{6,7},{7,6},{8,9},{9,8},{10,11... | collective-permute-start | bytes 1572872 | tf_op jit(solution)/shard_map/ppermute | solution.py:81
  252.7 13.6 %collective-permute-start.38 = (bf16[4,64,1024]{2,1,0:T(8,128)(2,1)S(1)}, bf16[4,64,1024]{2,1,0:T(8,128)(2,1)S(1)}, u32[]{:S(2)}, u32[]{:S(2)}) collective-permute-start(bf16[4,64,1024]{2,1,0:T(8,128)(2,1)S(1)} %get-tuple-element.377), channel_id=1, source_target_pairs={{0,4},{2,6},{4,0},{6,2},{8,12},{10,14},{12,8},{14,10},{16,20},{18,... | collective-permute-start | bytes 1572872 | tf_op jit(solution)/shard_map/ppermute | solution.py:81
  268.1 14.3 %collective-permute-start.39 = (bf16[16,64,1024]{2,1,0:T(8,128)(2,1)S(1)}, bf16[16,64,1024]{2,1,0:T(8,128)(2,1)S(1)}, u32[]{:S(2)}, u32[]{:S(2)}) collective-permute-start(bf16[16,64,1024]{2,1,0:T(8,128)(2,1)S(1)} %copy-done.49), channel_id=1, source_target_pairs={{0,2},{2,0},{4,6},{6,4},{8,10},{10,8},{12,14},{14,12},{16,18},{18,... | collective-permute-start | bytes 6291464 | tf_op jit(solution)/shard_map/ppermute | solution.py:81
  268.1 14.3 %collective-permute-start.40 = (bf16[2,64,2048]{2,1,0:T(8,128)(2,1)S(1)}, bf16[2,64,2048]{2,1,0:T(8,128)(2,1)S(1)}, u32[]{:S(2)}, u32[]{:S(2)}) collective-permute-start(bf16[2,64,2048]{2,1,0:T(8,128)(2,1)S(1)} %pad_maximum_fusion.9), channel_id=1, source_target_pairs={{0,8},{2,10},{4,12},{6,14},{8,0},{10,2},{12,4},{14,6},{16,24},{18,... | collective-permute-start | bytes 1572872 | tf_op jit(solution)/shard_map/ppermute | solution.py:81
  292.9 25.6 %collective-permute-start.42 = (bf16[8,64,1024]{2,1,0:T(8,128)(2,1)S(1)}, bf16[8,64,1024]{2,1,0:T(8,128)(2,1)S(1)}, u32[]{:S(2)}, u32[]{:S(2)}) collective-permute-start(bf16[8,64,1024]{2,1,0:T(8,128)(2,1)S(1)} %get-tuple-element.410), channel_id=1, source_target_pairs={{0,4},{2,6},{4,0},{6,2},{8,12},{10,14},{12,8},{14,10},{16,20},{18,... | collective-permute-start | bytes 3145736 | tf_op jit(solution)/shard_map/ppermute | solution.py:81
  294.0 25.3 %collective-permute-start.43 = (bf16[8,64,1024]{2,1,0:T(8,128)(2,1)S(1)}, bf16[8,64,1024]{2,1,0:T(8,128)(2,1)S(1)}, u32[]{:S(2)}, u32[]{:S(2)}) collective-permute-start(bf16[8,64,1024]{2,1,0:T(8,128)(2,1)S(1)} %get-tuple-element.411), channel_id=1, source_target_pairs={{0,1},{1,0},{2,3},{3,2},{4,5},{5,4},{6,7},{7,6},{8,9},{9,8},{10,11... | collective-permute-start | bytes 3145736 | tf_op jit(solution)/shard_map/ppermute | solution.py:81
  295.3 24.0 %collective-permute-start.44 = (bf16[16,64,512]{2,1,0:T(8,128)(2,1)S(1)}, bf16[16,64,512]{2,1,0:T(8,128)(2,1)S(1)}, u32[]{:S(2)}, u32[]{:S(2)}) collective-permute-start(bf16[16,64,512]{2,1,0:T(8,128)(2,1)S(1)} %copy-done.63), channel_id=1, source_target_pairs={{0,2},{2,0},{4,6},{6,4},{8,10},{10,8},{12,14},{14,12},{16,18},{18,... | collective-permute-start | bytes 3145736 | tf_op jit(solution)/shard_map/ppermute | solution.py:81
  295.3 22.8 %collective-permute-start.45 = (bf16[1,64,2048]{2,1,0:T(8,128)(2,1)S(1)}, bf16[1,64,2048]{2,1,0:T(8,128)(2,1)S(1)}, u32[]{:S(2)}, u32[]{:S(2)}) collective-permute-start(bf16[1,64,2048]{2,1,0:T(8,128)(2,1)S(1)} %get-tuple-element.413), channel_id=1, source_target_pairs={{0,16},{2,18},{4,20},{6,22},{8,24},{10,26},{12,28},{14,30},{16,0},... | collective-permute-start | bytes 786440 | tf_op jit(solution)/shard_map/ppermute | solution.py:81
  320.2 20.2 %collective-permute-start.46 = (bf16[4,64,1024]{2,1,0:T(8,128)(2,1)S(1)}, bf16[4,64,1024]{2,1,0:T(8,128)(2,1)S(1)}, u32[]{:S(2)}, u32[]{:S(2)}) collective-permute-start(bf16[4,64,1024]{2,1,0:T(8,128)(2,1)S(1)} %get-tuple-element.418), channel_id=1, source_target_pairs={{0,1},{1,0},{2,3},{3,2},{4,5},{5,4},{6,7},{7,6},{8,9},{9,8},{10,11... | collective-permute-start | bytes 1572872 | tf_op jit(solution)/shard_map/ppermute | solution.py:81
  321.5 18.9 %collective-permute-start.47 = (bf16[4,64,1024]{2,1,0:T(8,128)(2,1)S(1)}, bf16[4,64,1024]{2,1,0:T(8,128)(2,1)S(1)}, u32[]{:S(2)}, u32[]{:S(2)}) collective-permute-start(bf16[4,64,1024]{2,1,0:T(8,128)(2,1)S(1)} %get-tuple-element.419), channel_id=1, source_target_pairs={{0,4},{2,6},{4,0},{6,2},{8,12},{10,14},{12,8},{14,10},{16,20},{18,... | collective-permute-start | bytes 1572872 | tf_op jit(solution)/shard_map/ppermute | solution.py:81
  341.7 16.0 %collective-permute-start.48 = (bf16[2,64,2048]{2,1,0:T(8,128)(2,1)}, bf16[2,64,2048]{2,1,0:T(8,128)(2,1)}, u32[]{:S(2)}, u32[]{:S(2)}) collective-permute-start(bf16[2,64,2048]{2,1,0:T(8,128)(2,1)} %pad_maximum_fusion.11), channel_id=1, source_target_pairs={{0,8},{2,10},{4,12},{6,14},{8,0},{10,2},{12,4},{14,6},{16,24},{18,... | collective-permute-start | bytes 1572872 | tf_op jit(solution)/shard_map/ppermute | solution.py:81
  342.6 15.2 %collective-permute-start.49 = (bf16[8,64,512]{2,1,0:T(8,128)(2,1)}, bf16[8,64,512]{2,1,0:T(8,128)(2,1)}, u32[]{:S(2)}, u32[]{:S(2)}) collective-permute-start(bf16[8,64,512]{2,1,0:T(8,128)(2,1)} %get-tuple-element.437), channel_id=1, source_target_pairs={{0,4},{2,6},{4,0},{6,2},{8,12},{10,14},{12,8},{14,10},{16,20},{18,... | collective-permute-start | bytes 1572872 | tf_op jit(solution)/shard_map/ppermute | solution.py:81
  360.2 26.6 %collective-permute-start.50 = (bf16[16,3,64,256]{3,2,1,0:T(8,128)(2,1)S(1)}, bf16[16,3,64,256]{3,2,1,0:T(8,128)(2,1)S(1)}, u32[]{:S(2)}, u32[]{:S(2)}) collective-permute-start(bf16[16,3,64,256]{3,2,1,0:T(8,128)(2,1)S(1)} %copy-done.51), channel_id=1, source_target_pairs={{0,2},{2,0},{4,6},{6,4},{8,10},{10,8},{12,14},{14,12},{16,18},{18,... | collective-permute-start | bytes 4718600 | tf_op jit(solution)/shard_map/ppermute | solution.py:81
  360.3 26.5 %collective-permute-start.51 = (bf16[1,64,2048]{2,1,0:T(8,128)(2,1)S(1)}, bf16[1,64,2048]{2,1,0:T(8,128)(2,1)S(1)}, u32[]{:S(2)}, u32[]{:S(2)}) collective-permute-start(bf16[1,64,2048]{2,1,0:T(8,128)(2,1)S(1)} %get-tuple-element.449), channel_id=1, source_target_pairs={{0,16},{2,18},{4,20},{6,22},{8,24},{10,26},{12,28},{14,30},{16,0},... | collective-permute-start | bytes 786440 | tf_op jit(solution)/shard_map/ppermute | solution.py:81
  362.8 24.0 %collective-permute-start.52 = (bf16[4,64,512]{2,1,0:T(8,128)(2,1)S(1)}, bf16[4,64,512]{2,1,0:T(8,128)(2,1)S(1)}, u32[]{:S(2)}, u32[]{:S(2)}) collective-permute-start(bf16[4,64,512]{2,1,0:T(8,128)(2,1)S(1)} %get-tuple-element.450), channel_id=1, source_target_pairs={{0,1},{1,0},{2,3},{3,2},{4,5},{5,4},{6,7},{7,6},{8,9},{9,8},{10,11... | collective-permute-start | bytes 786440 | tf_op jit(solution)/shard_map/ppermute | solution.py:81
  364.1 22.8 %collective-permute-start.53 = (bf16[1,256,1024]{2,1,0:T(8,128)(2,1)S(1)}, bf16[1,256,1024]{2,1,0:T(8,128)(2,1)}, u32[]{:S(2)}, u32[]{:S(2)}) collective-permute-start(bf16[1,256,1024]{2,1,0:T(8,128)(2,1)S(1)} %get-tuple-element.454), channel_id=1, source_target_pairs={{0,1},{1,0},{2,3},{3,2},{4,5},{5,4},{6,7},{7,6},{8,9},{9,8},{10,11... | collective-permute-start | bytes 1572872 | tf_op jit(solution)/shard_map/ppermute | solution.py:81
  385.5 13.5 %collective-permute-start.55 = (bf16[1,256,1024]{2,1,0:T(8,128)(2,1)S(1)}, bf16[1,256,1024]{2,1,0:T(8,128)(2,1)S(1)}, u32[]{:S(2)}, u32[]{:S(2)}) collective-permute-start(bf16[1,256,1024]{2,1,0:T(8,128)(2,1)S(1)} %get-tuple-element.469), channel_id=1, source_target_pairs={{0,1},{1,0},{2,3},{3,2},{4,5},{5,4},{6,7},{7,6},{8,9},{9,8},{10,11... | collective-permute-start | bytes 1572872 | tf_op jit(solution)/shard_map/ppermute | solution.py:81
  387.0 12.1 %collective-permute-start.54 = (bf16[2,64,512]{2,1,0:T(8,128)(2,1)S(1)}, bf16[2,64,512]{2,1,0:T(8,128)(2,1)S(1)}, u32[]{:S(2)}, u32[]{:S(2)}) collective-permute-start(bf16[2,64,512]{2,1,0:T(8,128)(2,1)S(1)} %get-tuple-element.465), channel_id=1, source_target_pairs={{0,8},{2,10},{4,12},{6,14},{8,0},{10,2},{12,4},{14,6},{16,24},{18,... | collective-permute-start | bytes 393224 | tf_op jit(solution)/shard_map/ppermute | solution.py:81
  408.5 20.0 %collective-permute-start.57 = (bf16[8,3,64,256]{3,2,1,0:T(8,128)(2,1)S(1)}, bf16[8,3,64,256]{3,2,1,0:T(8,128)(2,1)S(1)}, u32[]{:S(2)}, u32[]{:S(2)}) collective-permute-start(bf16[8,3,64,256]{3,2,1,0:T(8,128)(2,1)S(1)} %get-tuple-element.487), channel_id=1, source_target_pairs={{0,4},{2,6},{4,0},{6,2},{8,12},{10,14},{12,8},{14,10},{16,20},{18,... | collective-permute-start | bytes 2359304 | tf_op jit(solution)/shard_map/ppermute | solution.py:81
  409.5 19.6 %collective-permute-start.58 = (bf16[8,3,64,256]{3,2,1,0:T(8,128)(2,1)S(1)}, bf16[8,3,64,256]{3,2,1,0:T(8,128)(2,1)S(1)}, u32[]{:S(2)}, u32[]{:S(2)}) collective-permute-start(bf16[8,3,64,256]{3,2,1,0:T(8,128)(2,1)S(1)} %get-tuple-element.488), channel_id=1, source_target_pairs={{0,1},{1,0},{2,3},{3,2},{4,5},{5,4},{6,7},{7,6},{8,9},{9,8},{10,11... | collective-permute-start | bytes 2359304 | tf_op jit(solution)/shard_map/ppermute | solution.py:81
  410.7 16.0 %collective-permute-start.59 = (bf16[1,64,512]{2,1,0:T(8,128)(2,1)S(1)}, bf16[1,64,512]{2,1,0:T(8,128)(2,1)S(1)}, u32[]{:S(2)}, u32[]{:S(2)}) collective-permute-start(bf16[1,64,512]{2,1,0:T(8,128)(2,1)S(1)} %get-tuple-element.489), channel_id=1, source_target_pairs={{0,16},{2,18},{4,20},{6,22},{8,24},{10,26},{12,28},{14,30},{16,0},... | collective-permute-start | bytes 196616 | tf_op jit(solution)/shard_map/ppermute | solution.py:81
  431.9 12.1 %collective-permute-start.63 = (bf16[4,3,64,256]{3,2,1,0:T(8,128)(2,1)S(1)}, bf16[4,3,64,256]{3,2,1,0:T(8,128)(2,1)S(1)}, u32[]{:S(2)}, u32[]{:S(2)}) collective-permute-start(bf16[4,3,64,256]{3,2,1,0:T(8,128)(2,1)S(1)} %get-tuple-element.504), channel_id=1, source_target_pairs={{0,1},{1,0},{2,3},{3,2},{4,5},{5,4},{6,7},{7,6},{8,9},{9,8},{10,11... | collective-permute-start | bytes 1179656 | tf_op jit(solution)/shard_map/ppermute | solution.py:81
  436.9 20.3 %collective-permute-start.60 = (bf16[1,256,1024]{2,1,0:T(8,128)(2,1)S(1)}, bf16[1,256,1024]{2,1,0:T(8,128)(2,1)S(1)}, u32[]{:S(2)}, u32[]{:S(2)}) collective-permute-start(bf16[1,256,1024]{2,1,0:T(8,128)(2,1)S(1)} %get-tuple-element.500), channel_id=1, source_target_pairs={{0,1},{1,0},{2,3},{3,2},{4,5},{5,4},{6,7},{7,6},{8,9},{9,8},{10,11... | collective-permute-start | bytes 1572872 | tf_op jit(solution)/shard_map/ppermute | solution.py:81
  451.1 15.1 %collective-permute-start.61 = (bf16[1,256,1024]{2,1,0:T(8,128)(2,1)S(1)}, bf16[1,256,1024]{2,1,0:T(8,128)(2,1)S(1)}, u32[]{:S(2)}, u32[]{:S(2)}) collective-permute-start(bf16[1,256,1024]{2,1,0:T(8,128)(2,1)S(1)} %get-tuple-element.501), channel_id=1, source_target_pairs={{0,1},{1,0},{2,3},{3,2},{4,5},{5,4},{6,7},{7,6},{8,9},{9,8},{10,11... | collective-permute-start | bytes 1572872 | tf_op jit(solution)/shard_map/ppermute | solution.py:81
  (89 other events, 948.8 us)

commit v5 on v4

--- a/solution.py
+++ b/solution.py
@@ -320,16 +320,16 @@
     row_loop(x_ref.shape[0], STEP, chunk)
     turned_ref[...] = h1_ref[...].T
 
-    @pl.when(first)
-    def _():
-        for n in range(count):
-            wait_whole(w_refs[n], sem.at[n])
-
     parts = weights(*w_refs)
     cols = sum(part[1] for part in parts)
-    for c, out in enumerate((q_ref, k_ref, v_ref)):
-        for t in range(tensor_count):
-            for start, width, _, _ in parts:
+    for n, (start, width, _, _) in enumerate(parts):
+
+        @pl.when(first)
+        def _(n=n):
+            wait_whole(w_refs[n], sem.at[n])
+
+        for c, out in enumerate((q_ref, k_ref, v_ref)):
+            for t in range(tensor_count):
                 w = columns(parts, order_ref, batch_count, tensor_count, t, start, width, lead=c)
                 value = dotf(h1_ref[...], w, 1, 0).astype(BF)
                 here = slice(t * cols + start, t * cols + start + width)
@@ -646,11 +646,14 @@
     def _():
         load_parts((a0, a1, a2, a3), wa, sem.at[0])
         load_parts((b0, b1, b2, b3), wb, sem.at[1])
-        wait_whole(wa, sem.at[0])
-        wait_whole(wb, sem.at[1])
 
     out = x_ref[...].astype(F32) + unit_ref[...] * gain_ref[1:2, :]
-    for start, width, _, _ in parts:
+    for n, (start, width, _, w_ref) in enumerate(parts):
+
+        @pl.when(pl.program_id(0) == 0)
+        def _(n=n, w_ref=w_ref):
+            wait_whole(w_ref, sem.at[n])
+
         for t in range(tensor_count):
             w = columns(parts, order_ref, batch_count, tensor_count, t, start, width)
             off = t * up_cols + start
@@ -704,16 +707,24 @@
         gains_ref[...] = jnp.zeros_like(gains_ref)
         dmid_ref[...] = jnp.zeros_like(dmid_ref)
         wait_whole(wda, sem.at[0])
-        wait_whole(wdb, sem.at[1])
 
     chunk = min(256, up_cols // 2)
     mean = stat_ref[:, 0:1]
     scale = stat_ref[:, 16:17]
     back_sum = jnp.zeros((block, 128), F32)
     back_inner = jnp.zeros((block, 128), F32)
-    for c in range(total // chunk):
-        t, off = divmod(c * chunk, up_cols)
-        here = slice(c * chunk, (c + 1) * chunk)
+    turns = [divmod(c * chunk, up_cols) for c in range(total // chunk)]
+    turns.sort(key=lambda turn: turn[1] >= wda.shape[2])
+    waited = False
+    for t, off in turns:
+        if off >= wda.shape[2] and not waited:
+            waited = True
+
+            @pl.when(first)
+            def _():
+                wait_whole(wdb, sem.at[1])
+
+        here = slice(t * up_cols + off, t * up_cols + off + chunk)
         dn = dotf(cot_ref[...], get_down(t, off, chunk), 1, 0)
         h = hidden_ref[:, here]
         square = h * h
@@ -830,7 +841,7 @@
     )
 
 
-def grad_kernel(grid_of, count, turn, order_ref, a_ref, *refs):
+def grad_kernel(grid_of, count, turn, chunk, order_ref, a_ref, *refs):
     batch_count, tensor_count = grid_of
     b_refs, keep_ref, send_ref = refs[:count], refs[count], refs[count + 1]
     tensor = pl.program_id(1)
@@ -854,10 +865,14 @@
                 for b in range(batch_count):
                     place = lax.bitwise_and(order_ref[b * tensor_count + tensor], half - 1)
                     ref = keep_ref if b % 2 == core else send_ref
-                    ref[(place,) if count == 1 else (place, c)] = acc[b * height : (b + 1) * height]
-
-
-def weight_grad(order, a, bs, grid_of, start, cols, name, turn=False):
+                    at = (place,) if count == 1 else (place, c)
+                    if chunk:
+                        start = pl.multiple_of(pl.program_id(0) * chunk, chunk)
+                        at += (slice(None), pl.ds(start, chunk))
+                    ref[at] = acc[b * height : (b + 1) * height]
+
+
+def weight_grad(order, a, bs, grid_of, start, cols, name, turn=False, near=False):
     batch_count, tensor_count = grid_of
     width, rows = a.shape[::-1] if turn else a.shape
     part = bs[0].shape[1] // tensor_count
@@ -867,11 +882,15 @@
     count = len(bs)
     lead = (batch_count * tensor_count // 2,) + (() if count == 1 else (count,)) + (height,)
     zeros = (0,) * len(lead)
-    out_spec = pl.BlockSpec(lead + (chunk,), lambda i, t, e: zeros + (i,))
-    out = pltpu.HBM(lead + (cols,), BF)
+    if near:
+        out_spec = pl.BlockSpec(memory_space=pltpu.VMEM)
+        out = pltpu.VMEM(lead + (cols,), BF)
+    else:
+        out_spec = pl.BlockSpec(lead + (chunk,), lambda i, t, e: zeros + (i,))
+        out = pltpu.HBM(lead + (cols,), BF)
     b_spec = pl.BlockSpec((rows, chunk), lambda i, t, e: (0, t * per + start // chunk + i))
     return pl.pallas_call(
-        functools.partial(grad_kernel, grid_of, count, turn),
+        functools.partial(grad_kernel, grid_of, count, turn, chunk if near else None),
         grid_spec=pltpu.PrefetchScalarGridSpec(
             num_scalar_prefetch=1,
             grid=(cols // chunk, tensor_count),
@@ -900,12 +919,15 @@
         for n in range(count):
             load_parts(w_hbm[4 * n : 4 * n + 4], w_refs[n], sem.at[n])
         dgain_ref[...] = jnp.zeros_like(dgain_ref)
-        for n in range(count):
-            wait_whole(w_refs[n], sem.at[n])
 
     parts = weights(*w_refs)
     total = None
     for n, (start, width, _, _) in enumerate(parts):
+
+        @pl.when(first)
+        def _(n=n):
+            wait_whole(w_refs[n], sem.at[n])
+
         for c in range(3):
             for t in range(tensor_count):
                 w = columns(parts, order_ref, batch_count, tensor_count, t, start, width, lead=c)
@@ -1098,7 +1120,9 @@
     cot = rows_cot.result
 
     def grad_half(n, a, b, name, turn=False):
-        keep, send = weight_grad(tables[n], a, [b], grid_of, n * half_cols, half_cols, name, turn)
+        keep, send = weight_grad(
+            tables[n], a, [b], grid_of, n * half_cols, half_cols, name, turn, not turn
+        )
         return Scatter(keep, send, steps[n])
 
     def flush(chains):
@@ -1130,7 +1154,7 @@
     u1.keep, u1.send = land((u1.keep, u1.send), [u0, down_sum])
     dmixed = launch(dmixed, [u1])
     keep, send = weight_grad(
-        tables[0], dmixed, [scaled], grid_of, 0, out_weight.shape[0], "grad_out"
+        tables[0], dmixed, [scaled], grid_of, 0, out_weight.shape[0], "grad_out", near=True
     )
     o0 = Scatter(keep, send, steps[0])
     o0.keep, o0.send = land((o0.keep, o0.send), [u1])
@@ -1157,7 +1181,7 @@
             rows_out.arrived[0] = first_out
             flying = [o0]
             three = launch(three, flying)
-        keep, send = weight_grad(tables[n % 2], h1, three, grid_of, 0, part_cols, "grad_qkv")
+        keep, send = weight_grad(tables[n % 2], h1, three, grid_of, 0, part_cols, "grad_qkv", near=True)
         halves.append(Scatter(keep, send, steps[n % 2]))
         grads += three
         halves[-1].keep, halves[-1].send = land((halves[-1].keep, halves[-1].send), flying)
@@ -1191,18 +1215,30 @@
     )
     last = Total(last, batch_count, tensor_count)
     rows_back = Rows(grad_in, micro_count, split, 2)
-    tail = [last] + halves + ([o0] if o0.steps else [])
-    launch((), tail + [rows_back])
+    tail = halves + ([o0] if o0.steps else [])
+    launch((), tail + [last])
+    last.end()
+    launch((), [last])
+    land((), tail + [last])
+    if parts > 1:
+        halves = [merged(halves)]
+    sent = rows_back.outgoing()
+    tail = [one for one in halves + [o0, last] if one.steps]
+    values, sent = lax.optimization_barrier(([one.outgoing() for one in tail], sent))
+    for one, value in zip(tail, values):
+        one.go(value)
+    rows_back.go(sent)
     for one in tail:
         one.end()
-    if parts > 1:
-        halves = [merged(halves)]
-    after = ()
     while last.steps:
-        tail = [one for one in [last] + halves + [o0] if one.steps]
-        launch(after, tail)
-        for one in tail:
-            one.end()
+        hop([last])
+    tail = [one for one in halves + [o0] if one.steps]
+    launch((), tail)
+    arrived = [one.arrived for one in tail]
+    rows_back.arrived = held(rows_back.arrived, arrived)
+    last.value = held(last.value, arrived)
+    for one in tail:
+        one.end()
     rows_back.end()
     block_out, grad_in = rows_out.result, rows_back.result
     d_totals, u_totals, o_totals, q_totals = (

time: 487 us -> 476 us (0.977)
  Pallas kernels: 266 us -> 258 us
    pallas_call x7, Pallas kernels: 70.7 us -> 63.1 us  [weight_grad(): pl.pallas_call(functools.partial(grad_kernel, grid_of, count, turn, chunk...]
    ppermute x66, waiting for transfers between devices: 83 us -> 78.1 us  [swap(): return lax.ppermute(value, axis, [(i, i ^ flip) for i in range(count)])]
  transfers between devices with their start and end apart: 73 -> 73, of which waited for: 28 -> 31; matrix products, arithmetic and copies ran while one was open for 5% -> 6% of each run, Pallas kernels for 56% -> 55%
where the time goes in v5:
time: 476 us; the launch traced here: 467 us
  Pallas kernels  258 us (54%)
  waiting for transfers between devices  84.6 us (18%)
  starting transfers between devices  68 us (14%)
  other arithmetic  27.9 us (6%)
  local copies, waits for them, and re-layouts  26.3 us (6%)
    ppermute x66, waiting for transfers between devices, swap(): return lax.ppermute(value, axis, [(i, i ^ flip) for i in range(count)])  78.1 us
    pallas_call x7, Pallas kernels, weight_grad(): pl.pallas_call(functools.partial(grad_kernel, grid_of, count, turn, chunk...  63.1 us
    ppermute x66, starting transfers between devices, swap(): return lax.ppermute(value, axis, [(i, i ^ flip) for i in range(count)])  61.9 us
    pallas_call x1, Pallas kernels, feed_back(): pl.pallas_call(functools.partial(back_kernel, grid_of), grid_spec=pltpu.P...  46.5 us
    pallas_call x2, Pallas kernels, attend_back(): pl.pallas_call(functools.partial(attend_back_kernel, rows, block, factor)...  41.6 us
    pallas_call x2, Pallas kernels, hidden_forward(): pl.pallas_call(kernel, grid_spec=pltpu.PrefetchScalarGridSpec(num_scalar_...  34.7 us
    pallas_call x2, Pallas kernels, attend(): pl.pallas_call(kernel, grid_spec=pltpu.PrefetchScalarGridSpec(num_scalar_...  26.2 us
    convert_element_type x25, other arithmetic, end(): (keep[:half].astype(F32) + arrived[:half].astype(F32)).astype(BF)  19.3 us
  transfers between devices with their start and end apart: 73, of which 31 were waited for; matrix products, arithmetic and copies ran while one was open for 6% of the time, Pallas kernels for 55%

profile of v5, /device:TPU:0, one launch (start us, length us, event | category | flops | bytes accessed | tf_op | source)
XLA Modules:
  0.0 466.7 jit_solution(11749293593892349432)
XLA Ops:
  4.2 2.9 collective-permute-start
  7.1 2.6 collective-permute-start.1
  9.7 8.9 %collective-permute-done.1 = bf16[1,3,64,512]{3,2,1,0:T(8,128)(2,1)S(1)} collective-permute-done((bf16[1,3,64,512]{3,2,1,0:T(8,128)(2,1)S(1)}, bf16[1,3,64,512]{3,2,1,0:T(8,128)(2,1)S(1)}, u32[]{:S(2)}, u32[]{:S(2)}) %collective-permute-start.1) | collective-permute-done | bytes 196640 | tf_op jit(solution)/shard_map/ppermute | solution.py:81
  19.4 9.3 %collective-permute-done.2 = bf16[2,3,64,512]{3,2,1,0:T(8,128)(2,1)S(1)} collective-permute-done((bf16[2,3,64,512]{3,2,1,0:T(8,128)(2,1)S(1)}, bf16[2,3,64,512]{3,2,1,0:T(8,128)(2,1)S(1)}, u32[]{:S(2)}, u32[]{:S(2)}) %collective-permute-start.2) | collective-permute-done | bytes 393248 | tf_op jit(solution)/shard_map/ppermute | solution.py:81
  30.3 1.8 collective-permute-start.4
  33.6 2.7 collective-permute-start.7
  36.2 4.3 collective-permute-done.4
  43.9 5.7 %collective-permute-done.7 = bf16[1,64,2560]{2,1,0:T(8,128)(2,1)S(1)} collective-permute-done((bf16[1,64,2560]{2,1,0:T(8,128)(2,1)S(1)}, bf16[1,64,2560]{2,1,0:T(8,128)(2,1)S(1)}, u32[]{:S(2)}, u32[]{:S(2)}) %collective-permute-start.7) | collective-permute-done | bytes 327712 | tf_op jit(solution)/shard_map/ppermute | solution.py:81
  52.0 7.2 %collective-permute-done.5.refs_1_.refs_10_ = bf16[8,3,64,256]{3,2,1,0:T(8,128)(2,1)} collective-permute-done((bf16[8,3,64,256]{3,2,1,0:T(8,128)(2,1)S(1)}, bf16[8,3,64,256]{3,2,1,0:T(8,128)(2,1)}, u32[]{:S(2)}, u32[]{:S(2)}) %collective-permute-start.5) | collective-permute-done | bytes 786464 | tf_op jit(solution)/shard_map/ppermute | solution.py:81
  61.2 4.1 collective-permute-done.8
  66.7 14.3 %project.1 = (bf16[1024,1024]{1,0:T(8,128)(2,1)}, bf16[1024,1024]{1,0:T(8,128)(2,1)}, bf16[1024,1024]{1,0:T(8,128)(2,1)}, bf16[1024,1024]{1,0:T(8,128)(2,1)}) custom-call(s32[64]{0:T(128)S(1)} %pad_add_fusion.order_ref, bf16[1024,1024]{1,0:T(8,128)(2,1)} %bitcast.3.x_ref.refs_1_.refs_6_, f32[3,1024]{1,0:T(4,128)S(1)} %copy-done.4, ...), custom_call_target="tpu_custom_call" | custom-call | flops 12999999488 | bytes 1048576 | tf_op jit(solution)/shard_map/project/pallas_call | solution.py:343
  84.5 3.4 collective-permute-start.16
  87.9 13.1 %attend.2 = (bf16[1024,1024]{1,0:T(8,128)(2,1)}, f32[8,2,1024]{2,1,0:T(2,128)}) custom-call(s32[4]{0:T(128)S(1)} %bitcast.33, bf16[1024,1024]{1,0:T(8,128)(2,1)} %get-tuple-element.291.q_ref, bf16[1024,1024]{1,0:T(8,128)(2,1)} %get-tuple-element.292.k_ref, bf16[1024,1024]{1,0:T(8,128)(2,1)} %get-tuple-element.293.v_ref, ...), custom_call_target="tpu_custom_call" | custom-call | flops 12000000000 | bytes 1048576 | tf_op jit(solution)/shard_map/attend/pallas_call | solution.py:466
  101.0 1.8 collective-permute-start.19
  102.8 13.1 %attend.3 = (bf16[1024,1024]{1,0:T(8,128)(2,1)}, f32[8,2,1024]{2,1,0:T(2,128)}) custom-call(s32[4]{0:T(128)S(1)} %bitcast.34, bf16[1024,1024]{1,0:T(8,128)(2,1)} %get-tuple-element.291.q_ref, bf16[1024,1024]{1,0:T(8,128)(2,1)} %get-tuple-element.292.k_ref, ...), custom_call_target="tpu_custom_call", output_to_operand_aliasing={{0}: (5, {}), {1}: (6, {})} | custom-call | flops 12000000000 | bytes 1048576 | tf_op jit(solution)/shard_map/attend/pallas_call | solution.py:466
  116.8 1.7 copy-done.13
  119.1 1.9 collective-permute-done.21.refs_11_.b3
  125.6 17.5 %hidden_forward.2 = (f32[1024,1024]{1,0:T(8,128)}, bf16[1024,1024]{1,0:T(8,128)(2,1)}, f32[1024,4096]{1,0:T(8,128)}, bf16[1024,4096]{1,0:T(8,128)(2,1)}, f32[1024,128]{1,0:T(8,128)}) custom-call(s32[64]{0:T(128)S(1)} %pad_add_fusion.order_ref, bf16[1024,1024]{1,0:T(8,128)(2,1)} %get-tuple-element.313.refs_0_, ...), custom_call_target="tpu_custom_call" | custom-call | flops 15000000512 | bytes 1048576 | tf_op jit(solution)/shard_map/hidden_forward/pallas_call | solution.py:602
  144.8 17.2 %hidden_forward.3 = (f32[1024,1024]{1,0:T(8,128)}, bf16[1024,1024]{1,0:T(8,128)(2,1)}, f32[1024,4096]{1,0:T(8,128)}, bf16[1024,4096]{1,0:T(8,128)(2,1)}, f32[1024,128]{1,0:T(8,128)}) custom-call(s32[64]{0:T(128)S(1)} %pad_add_fusion.order_ref, ...), custom_call_target="tpu_custom_call", output_to_operand_aliasing={{0}: (13, {}), {1}: (14, {}), {2}: (15, {}), {3}: (16, {}),... | custom-call | flops 15000000512 | bytes 1048576 | tf_op jit(solution)/shard_map/hidden_forward/pallas_call | solution.py:602
  162.0 5.7 %collective-permute-done.27.da1.a1 = bf16[8,64,1024]{2,1,0:T(8,128)(2,1)S(1)} collective-permute-done((bf16[8,64,1024]{2,1,0:T(8,128)(2,1)S(1)}, bf16[8,64,1024]{2,1,0:T(8,128)(2,1)S(1)}, u32[]{:S(2)}, u32[]{:S(2)}) %collective-permute-start.27) | collective-permute-done | bytes 1048608 | tf_op jit(solution)/shard_map/ppermute | solution.py:81
  169.5 10.6 %grad_down.2 = (bf16[16,64,1024]{2,1,0:T(8,128)(2,1)}, bf16[16,64,1024]{2,1,0:T(8,128)(2,1)}) custom-call(s32[32]{0:T(128)S(1)} %get-tuple-element.600.order_ref, bf16[1024,1024]{1,0:T(8,128)(2,1)} %bitcast.37, bf16[1024,4096]{1,0:T(8,128)(2,1)} %get-tuple-element.424.refs_0_.narrow_ref), custom_call_target="tpu_custom_call" | custom-call | flops 4800000000 | bytes 1048576 | tf_op jit(solution)/shard_map/grad_down/pallas_call | solution.py:892
  180.8 10.9 %grad_down.3 = (bf16[16,64,1024]{2,1,0:T(8,128)(2,1)}, bf16[16,64,1024]{2,1,0:T(8,128)(2,1)}) custom-call(s32[32]{0:T(128)S(1)} %get-tuple-element.599.order_ref, bf16[1024,1024]{1,0:T(8,128)(2,1)} %bitcast.38, bf16[1024,4096]{1,0:T(8,128)(2,1)} %get-tuple-element.424.refs_0_.narrow_ref), custom_call_target="tpu_custom_call" | custom-call | flops 4800000000 | bytes 1048576 | tf_op jit(solution)/shard_map/grad_down/pallas_call | solution.py:892
  191.8 2.0 add_convert_fusion.6
  196.3 2.4 collective-permute-done.32
  198.7 2.0 add_convert_fusion.4
  202.7 46.5 %feed_back.1 = (bf16[1024,4096]{1,0:T(8,128)(2,1)}, f32[1024,1024]{1,0:T(8,128)}, bf16[1024,1024]{1,0:T(8,128)(2,1)}, bf16[1024,1024]{1,0:T(8,128)(2,1)}, f32[16,1024]{1,0:T(8,128)}, /*index=5*/f32[8,4096]{1,0:T(8,128)}) custom-call(s32[64]{0:T(128)} %copy-done.6, f32[1024,4096]{1,0:T(8,128)} %get-tuple-element.360.hidden_ref, ...), custom_call_target="tpu_custom_call" | custom-call | flops 60000002048 | bytes 1048576 | tf_op jit(solution)/shard_map/feed_back/pallas_call | solution.py:793
  253.2 8.0 %grad_up.2 = (bf16[16,64,1024]{2,1,0:T(8,128)(2,1)S(1)}, bf16[16,64,1024]{2,1,0:T(8,128)(2,1)S(1)}) custom-call(s32[32]{0:T(128)S(1)} %get-tuple-element.600.order_ref, bf16[1024,1024]{1,0:T(8,128)(2,1)} %get-tuple-element.380.a_ref, bf16[1024,4096]{1,0:T(8,128)(2,1)} %get-tuple-element.392.refs_0_), custom_call_target="tpu_custom_call" | custom-call | flops 4800000000 | bytes 1048576 | tf_op jit(solution)/shard_map/grad_up/pallas_call | solution.py:892
  261.2 4.3 collective-permute-done.37
  267.3 8.0 %grad_up.3 = (bf16[16,64,1024]{2,1,0:T(8,128)(2,1)S(1)}, bf16[16,64,1024]{2,1,0:T(8,128)(2,1)S(1)}) custom-call(s32[32]{0:T(128)S(1)} %get-tuple-element.599.order_ref, bf16[1024,1024]{1,0:T(8,128)(2,1)} %get-tuple-element.380.a_ref, bf16[1024,4096]{1,0:T(8,128)(2,1)} %get-tuple-element.392.refs_0_), custom_call_target="tpu_custom_call" | custom-call | flops 4800000000 | bytes 1048576 | tf_op jit(solution)/shard_map/grad_up/pallas_call | solution.py:892
  275.3 5.5 %collective-permute-done.40 = bf16[2,64,2048]{2,1,0:T(8,128)(2,1)S(1)} collective-permute-done((bf16[2,64,2048]{2,1,0:T(8,128)(2,1)S(1)}, bf16[2,64,2048]{2,1,0:T(8,128)(2,1)S(1)}, u32[]{:S(2)}, u32[]{:S(2)}) %collective-permute-start.40) | collective-permute-done | bytes 524320 | tf_op jit(solution)/shard_map/ppermute | solution.py:81
  280.8 5.2 %grad_out.1 = (bf16[16,64,512]{2,1,0:T(8,128)(2,1)S(1)}, bf16[16,64,512]{2,1,0:T(8,128)(2,1)S(1)}) custom-call(s32[32]{0:T(128)S(1)} %get-tuple-element.600.order_ref, bf16[1024,1024]{1,0:T(8,128)(2,1)} %get-tuple-element.402.a_ref, bf16[1024,1024]{1,0:T(8,128)(2,1)} %get-tuple-element.313.refs_0_), custom_call_target="tpu_custom_call" | custom-call | flops 2400000000 | bytes 1048576 | tf_op jit(solution)/shard_map/grad_out/pallas_call | solution.py:892
  290.5 1.9 collective-permute-start.45
  292.4 20.9 %attend_back.2 = (bf16[1024,512]{1,0:T(8,128)(2,1)}, bf16[1024,512]{1,0:T(8,128)(2,1)}, bf16[1024,512]{1,0:T(8,128)(2,1)}, f32[4,2,1024]{2,1,0:T(2,128)}) custom-call(s32[4]{0:T(128)S(1)} %bitcast.35, bf16[1024,1024]{1,0:T(8,128)(2,1)} %get-tuple-element.291.q_ref, bf16[1024,1024]{1,0:T(8,128)(2,1)} %get-tuple-element.292.k_ref, ...), custom_call_target="tpu_custom_call" | custom-call | flops 20999999488 | bytes 1048576 | tf_op jit(solution)/shard_map/attend_back/pallas_call | solution.py:495
  317.9 16.4 %feed_forward.1 = bf16[1024,1024]{1,0:T(8,128)(2,1)} custom-call(s32[64]{0:T(128)S(1)} %copy-done.7, bf16[1024,4096]{1,0:T(8,128)(2,1)} %get-tuple-element.424.refs_0_.narrow_ref, f32[1024,1024]{1,0:T(8,128)} %get-tuple-element.362.unit_ref, bf16[1024,1024]{1,0:T(8,128)(2,1)} %bitcast.3.x_ref.refs_1_.refs_6_, f32[3,1024]{1,0:T(4,128)S(1)} %copy-done.5, ...), custom_call_target="tpu_custom_call" | custom-call | flops 14000000000 | bytes 1048576 | tf_op jit(solution)/shard_map/feed_forward/pallas_call | solution.py:669
  339.6 9.4 %grad_qkv.2 = (bf16[16,3,64,256]{3,2,1,0:T(8,128)(2,1)S(1)}, bf16[16,3,64,256]{3,2,1,0:T(8,128)(2,1)S(1)}) custom-call(s32[32]{0:T(128)S(1)} %get-tuple-element.600.order_ref, bf16[1024,1024]{1,0:T(8,128)(2,1)} %get-tuple-element.428.a_ref, bf16[1024,512]{1,0:T(8,128)(2,1)} %get-tuple-element.438.refs_0_, bf16[1024,512]{1,0:T(8,128)(2,1)} %get-tuple-element.439.refs_1_, ...), custom_call_target="tpu_custom_call" | custom-call | flops 3600000000 | bytes 1048576 | tf_op jit(solution)/shard_map/grad_qkv/pallas_call | solution.py:892
  352.5 2.3 collective-permute-start.51
  356.8 20.7 %attend_back.3 = (bf16[1024,512]{1,0:T(8,128)(2,1)}, bf16[1024,512]{1,0:T(8,128)(2,1)}, bf16[1024,512]{1,0:T(8,128)(2,1)}, f32[4,2,1024]{2,1,0:T(2,128)}) custom-call(s32[4]{0:T(128)S(1)} %bitcast.36, bf16[1024,1024]{1,0:T(8,128)(2,1)} %get-tuple-element.291.q_ref, bf16[1024,1024]{1,0:T(8,128)(2,1)} %get-tuple-element.292.k_ref, ...), custom_call_target="tpu_custom_call" | custom-call | flops 20999999488 | bytes 1048576 | tf_op jit(solution)/shard_map/attend_back/pallas_call | solution.py:495
  380.3 10.8 %grad_qkv.3 = (bf16[16,3,64,256]{3,2,1,0:T(8,128)(2,1)S(1)}, bf16[16,3,64,256]{3,2,1,0:T(8,128)(2,1)}) custom-call(s32[32]{0:T(128)S(1)} %get-tuple-element.599.order_ref, bf16[1024,1024]{1,0:T(8,128)(2,1)} %get-tuple-element.428.a_ref, bf16[1024,512]{1,0:T(8,128)(2,1)} %get-tuple-element.467.refs_0_.refs_3_, ...), custom_call_target="tpu_custom_call" | custom-call | flops 3600000000 | bytes 1048576 | tf_op jit(solution)/shard_map/grad_qkv/pallas_call | solution.py:892
  393.0 1.9 add_bitcast_fusion
  397.9 2.8 add_convert_fusion.10
  400.8 1.8 add_convert_fusion.8
  405.4 14.7 %input_grad.1 = (bf16[1024,1024]{1,0:T(8,128)(2,1)}, f32[8,1024]{1,0:T(8,128)}) custom-call(s32[64]{0:T(128)S(1)} %copy-done.7, bf16[1024,512]{1,0:T(8,128)(2,1)} %get-tuple-element.438.refs_0_, bf16[1024,512]{1,0:T(8,128)(2,1)} %get-tuple-element.439.refs_1_, bf16[1024,512]{1,0:T(8,128)(2,1)} %get-tuple-element.440.refs_2_, ...), custom_call_target="tpu_custom_call" | custom-call | flops 15000000512 | bytes 1048576 | tf_op jit(solution)/shard_map/input_grad/pallas_call | solution.py:954
  420.2 2.5 collective-permute-done.57
  433.4 3.4 collective-permute-done.63
  439.0 1.9 constant_dynamic-update-slice_fusion.5
  445.6 1.9 collective-permute-done.68
  448.7 2.3 collective-permute-start.69
  453.4 5.3 %collective-permute-done.69 = bf16[1,3,64,512]{3,2,1,0:T(8,128)(2,1)S(1)} collective-permute-done((bf16[1,3,64,512]{3,2,1,0:T(8,128)(2,1)S(1)}, bf16[1,3,64,512]{3,2,1,0:T(8,128)(2,1)S(1)}, u32[]{:S(2)}, u32[]{:S(2)}) %collective-permute-start.69) | collective-permute-done | bytes 196640 | tf_op jit(solution)/shard_map/ppermute | solution.py:81
  (334 shorter events, 99.0 us)
Async XLA Ops:
  4.2 26.1 %collective-permute-start = (bf16[1,512,1024]{2,1,0:T(8,128)(2,1)S(1)}, bf16[1,512,1024]{2,1,0:T(8,128)(2,1)S(1)}, u32[]{:S(2)}, u32[]{:S(2)}) collective-permute-start(bf16[1,512,1024]{2,1,0:T(8,128)(2,1)S(1)} %get-tuple-element.271), channel_id=1, source_target_pairs={{0,1},{1,0},{2,3},{3,2},{4,5},{5,4},{6,7},{7,6},{8,9},{9,8},{10,11... | collective-permute-start | bytes 3145736 | tf_op jit(solution)/shard_map/ppermute | solution.py:81
  7.1 11.5 %collective-permute-start.1 = (bf16[1,3,64,512]{3,2,1,0:T(8,128)(2,1)S(1)}, bf16[1,3,64,512]{3,2,1,0:T(8,128)(2,1)S(1)}, u32[]{:S(2)}, u32[]{:S(2)}) collective-permute-start(bf16[1,3,64,512]{3,2,1,0:T(8,128)(2,1)S(1)} %bitcast.46), channel_id=1, source_target_pairs={{0,16},{2,18},{4,20},{6,22},{8,24},{10,26},{12,28},{14,30},{16,0},... | collective-permute-start | bytes 589832 | tf_op jit(solution)/shard_map/ppermute | solution.py:81
  33.6 16.0 %collective-permute-start.7 = (bf16[1,64,2560]{2,1,0:T(8,128)(2,1)S(1)}, bf16[1,64,2560]{2,1,0:T(8,128)(2,1)S(1)}, u32[]{:S(2)}, u32[]{:S(2)}) collective-permute-start(bf16[1,64,2560]{2,1,0:T(8,128)(2,1)S(1)} %maximum_bitcast_fusion), channel_id=1, source_target_pairs={{0,16},{2,18},{4,20},{6,22},{8,24},{10,26},{12,28},{14,30},{16,0},... | collective-permute-start | bytes 983048 | tf_op jit(solution)/shard_map/ppermute | solution.py:81
  41.8 17.4 %collective-permute-start.5 = (bf16[8,3,64,256]{3,2,1,0:T(8,128)(2,1)S(1)}, bf16[8,3,64,256]{3,2,1,0:T(8,128)(2,1)}, u32[]{:S(2)}, u32[]{:S(2)}) collective-permute-start(bf16[8,3,64,256]{3,2,1,0:T(8,128)(2,1)S(1)} %pad_maximum_fusion.4.refs_0_.refs_9_), channel_id=1, source_target_pairs={{0,4},{2,6},{4,0},{6,2},{8,12},{10,14},{12,8},{14,10},{16,20},{18,... | collective-permute-start | bytes 2359304 | tf_op jit(solution)/shard_map/ppermute | solution.py:81
  42.5 17.5 %collective-permute-start.6 = (bf16[8,3,64,256]{3,2,1,0:T(8,128)(2,1)S(1)}, bf16[8,3,64,256]{3,2,1,0:T(8,128)(2,1)}, u32[]{:S(2)}, u32[]{:S(2)}) collective-permute-start(bf16[8,3,64,256]{3,2,1,0:T(8,128)(2,1)S(1)} %pad_maximum_fusion.5.refs_4_.refs_13_), channel_id=1, source_target_pairs={{0,1},{1,0},{2,3},{3,2},{4,5},{5,4},{6,7},{7,6},{8,9},{9,8},{10,11... | collective-permute-start | bytes 2359304 | tf_op jit(solution)/shard_map/ppermute | solution.py:81
  49.6 15.7 %collective-permute-start.8 = (bf16[2,64,2560]{2,1,0:T(8,128)(2,1)S(1)}, bf16[2,64,2560]{2,1,0:T(8,128)(2,1)S(1)}, u32[]{:S(2)}, u32[]{:S(2)}) collective-permute-start(bf16[2,64,2560]{2,1,0:T(8,128)(2,1)S(1)} %pad_maximum_fusion.7), channel_id=1, source_target_pairs={{0,8},{2,10},{4,12},{6,14},{8,0},{10,2},{12,4},{14,6},{16,24},{18,... | collective-permute-start | bytes 1966088 | tf_op jit(solution)/shard_map/ppermute | solution.py:81
  52.0 14.0 %collective-permute-start.11 = (bf16[8,3,64,256]{3,2,1,0:T(8,128)(2,1)S(1)}, bf16[8,3,64,256]{3,2,1,0:T(8,128)(2,1)}, u32[]{:S(2)}, u32[]{:S(2)}) collective-permute-start(bf16[8,3,64,256]{3,2,1,0:T(8,128)(2,1)S(1)} %pad_maximum_fusion.5.refs_4_.refs_13_), channel_id=1, source_target_pairs={{0,2},{2,0},{4,6},{6,4},{8,10},{10,8},{12,14},{14,12},{16,18},{18,... | collective-permute-start | bytes 2359304 | tf_op jit(solution)/shard_map/ppermute | solution.py:81
  65.4 15.6 %collective-permute-start.13 = (bf16[4,64,1280]{2,1,0:T(8,128)(2,1)S(1)}, bf16[4,64,1280]{2,1,0:T(8,128)(2,1)S(1)}, u32[]{:S(2)}, u32[]{:S(2)}) collective-permute-start(bf16[4,64,1280]{2,1,0:T(8,128)(2,1)S(1)} %get-tuple-element.285), channel_id=1, source_target_pairs={{0,1},{1,0},{2,3},{3,2},{4,5},{5,4},{6,7},{7,6},{8,9},{9,8},{10,11... | collective-permute-start | bytes 1966088 | tf_op jit(solution)/shard_map/ppermute | solution.py:81
  66.0 15.0 %collective-permute-start.14 = (bf16[4,64,1280]{2,1,0:T(8,128)(2,1)S(1)}, bf16[4,64,1280]{2,1,0:T(8,128)(2,1)S(1)}, u32[]{:S(2)}, u32[]{:S(2)}) collective-permute-start(bf16[4,64,1280]{2,1,0:T(8,128)(2,1)S(1)} %get-tuple-element.286), channel_id=1, source_target_pairs={{0,4},{2,6},{4,0},{6,2},{8,12},{10,14},{12,8},{14,10},{16,20},{18,... | collective-permute-start | bytes 1966088 | tf_op jit(solution)/shard_map/ppermute | solution.py:81
  81.3 34.6 %collective-permute-start.17 = (bf16[8,64,1280]{2,1,0:T(8,128)(2,1)S(1)}, bf16[8,64,1280]{2,1,0:T(8,128)(2,1)S(1)}, u32[]{:S(2)}, u32[]{:S(2)}) collective-permute-start(bf16[8,64,1280]{2,1,0:T(8,128)(2,1)S(1)} %pad_maximum_fusion.refs_4_.a0), channel_id=1, source_target_pairs={{0,4},{2,6},{4,0},{6,2},{8,12},{10,14},{12,8},{14,10},{16,20},{18,... | collective-permute-start | bytes 3932168 | tf_op jit(solution)/shard_map/ppermute | solution.py:81
  82.7 41.4 %collective-permute-start.22 = (bf16[8,64,1280]{2,1,0:T(8,128)(2,1)S(1)}, bf16[8,64,1280]{2,1,0:T(8,128)(2,1)S(1)}, u32[]{:S(2)}, u32[]{:S(2)}) collective-permute-start(bf16[8,64,1280]{2,1,0:T(8,128)(2,1)S(1)} %pad_maximum_fusion.refs_4_.a0), channel_id=1, source_target_pairs={{0,2},{2,0},{4,6},{6,4},{8,10},{10,8},{12,14},{14,12},{16,18},{18,... | collective-permute-start | bytes 3932168 | tf_op jit(solution)/shard_map/ppermute | solution.py:81
  82.8 33.2 %collective-permute-start.18 = (bf16[8,64,1280]{2,1,0:T(8,128)(2,1)S(1)}, bf16[8,64,1280]{2,1,0:T(8,128)(2,1)S(1)}, u32[]{:S(2)}, u32[]{:S(2)}) collective-permute-start(bf16[8,64,1280]{2,1,0:T(8,128)(2,1)S(1)} %pad_maximum_fusion.1.refs_8_.b0), channel_id=1, source_target_pairs={{0,1},{1,0},{2,3},{3,2},{4,5},{5,4},{6,7},{7,6},{8,9},{9,8},{10,11... | collective-permute-start | bytes 3932168 | tf_op jit(solution)/shard_map/ppermute | solution.py:81
  84.2 39.9 %collective-permute-start.23 = (bf16[8,64,1280]{2,1,0:T(8,128)(2,1)S(1)}, bf16[8,64,1280]{2,1,0:T(8,128)(2,1)S(1)}, u32[]{:S(2)}, u32[]{:S(2)}) collective-permute-start(bf16[8,64,1280]{2,1,0:T(8,128)(2,1)S(1)} %pad_maximum_fusion.1.refs_8_.b0), channel_id=1, source_target_pairs={{0,2},{2,0},{4,6},{6,4},{8,10},{10,8},{12,14},{14,12},{16,18},{18,... | collective-permute-start | bytes 3932168 | tf_op jit(solution)/shard_map/ppermute | solution.py:81
  84.5 16.5 %collective-permute-start.16 = (bf16[1,64,2048]{2,1,0:T(8,128)(2,1)S(1)}, bf16[1,64,2048]{2,1,0:T(8,128)(2,1)S(1)}, u32[]{:S(2)}, u32[]{:S(2)}) collective-permute-start(bf16[1,64,2048]{2,1,0:T(8,128)(2,1)S(1)} %bitcast.44), channel_id=1, source_target_pairs={{0,16},{2,18},{4,20},{6,22},{8,24},{10,26},{12,28},{14,30},{16,0},... | collective-permute-start | bytes 786440 | tf_op jit(solution)/shard_map/ppermute | solution.py:81
  101.0 14.9 %collective-permute-start.19 = (bf16[2,64,2048]{2,1,0:T(8,128)(2,1)S(1)}, bf16[2,64,2048]{2,1,0:T(8,128)(2,1)S(1)}, u32[]{:S(2)}, u32[]{:S(2)}) collective-permute-start(bf16[2,64,2048]{2,1,0:T(8,128)(2,1)S(1)} %pad_maximum_fusion.8), channel_id=1, source_target_pairs={{0,8},{2,10},{4,12},{6,14},{8,0},{10,2},{12,4},{14,6},{16,24},{18,... | collective-permute-start | bytes 1572872 | tf_op jit(solution)/shard_map/ppermute | solution.py:81
  120.9 22.1 %collective-permute-start.24 = (bf16[4,64,1024]{2,1,0:T(8,128)(2,1)S(1)}, bf16[4,64,1024]{2,1,0:T(8,128)(2,1)S(1)}, u32[]{:S(2)}, u32[]{:S(2)}) collective-permute-start(bf16[4,64,1024]{2,1,0:T(8,128)(2,1)S(1)} %get-tuple-element.317), channel_id=1, source_target_pairs={{0,1},{1,0},{2,3},{3,2},{4,5},{5,4},{6,7},{7,6},{8,9},{9,8},{10,11... | collective-permute-start | bytes 1572872 | tf_op jit(solution)/shard_map/ppermute | solution.py:81
  121.5 21.6 %collective-permute-start.25 = (bf16[4,64,1024]{2,1,0:T(8,128)(2,1)S(1)}, bf16[4,64,1024]{2,1,0:T(8,128)(2,1)S(1)}, u32[]{:S(2)}, u32[]{:S(2)}) collective-permute-start(bf16[4,64,1024]{2,1,0:T(8,128)(2,1)S(1)} %get-tuple-element.318), channel_id=1, source_target_pairs={{0,4},{2,6},{4,0},{6,2},{8,12},{10,14},{12,8},{14,10},{16,20},{18,... | collective-permute-start | bytes 1572872 | tf_op jit(solution)/shard_map/ppermute | solution.py:81
  122.6 39.4 %collective-permute-start.26 = (bf16[1,512,1024]{2,1,0:T(8,128)(2,1)S(1)}, bf16[1,512,1024]{2,1,0:T(8,128)(2,1)S(1)}, u32[]{:S(2)}, u32[]{:S(2)}) collective-permute-start(bf16[1,512,1024]{2,1,0:T(8,128)(2,1)S(1)} %get-tuple-element.332), channel_id=1, source_target_pairs={{0,1},{1,0},{2,3},{3,2},{4,5},{5,4},{6,7},{7,6},{8,9},{9,8},{10,11... | collective-permute-start | bytes 3145736 | tf_op jit(solution)/shard_map/ppermute | solution.py:81
  143.3 24.4 %collective-permute-start.27 = (bf16[8,64,1024]{2,1,0:T(8,128)(2,1)S(1)}, bf16[8,64,1024]{2,1,0:T(8,128)(2,1)S(1)}, u32[]{:S(2)}, u32[]{:S(2)}) collective-permute-start(bf16[8,64,1024]{2,1,0:T(8,128)(2,1)S(1)} %pad_maximum_fusion.2.da0.a0), channel_id=1, source_target_pairs={{0,4},{2,6},{4,0},{6,2},{8,12},{10,14},{12,8},{14,10},{16,20},{18,... | collective-permute-start | bytes 3145736 | tf_op jit(solution)/shard_map/ppermute | solution.py:81
  144.3 35.8 %collective-permute-start.28 = (bf16[8,64,1024]{2,1,0:T(8,128)(2,1)S(1)}, bf16[8,64,1024]{2,1,0:T(8,128)(2,1)S(1)}, u32[]{:S(2)}, u32[]{:S(2)}) collective-permute-start(bf16[8,64,1024]{2,1,0:T(8,128)(2,1)S(1)} %pad_maximum_fusion.3.db0.b0), channel_id=1, source_target_pairs={{0,1},{1,0},{2,3},{3,2},{4,5},{5,4},{6,7},{7,6},{8,9},{9,8},{10,11... | collective-permute-start | bytes 3145736 | tf_op jit(solution)/shard_map/ppermute | solution.py:81
  180.1 11.6 %collective-permute-start.29 = (bf16[16,64,1024]{2,1,0:T(8,128)(2,1)}, bf16[16,64,1024]{2,1,0:T(8,128)(2,1)S(1)}, u32[]{:S(2)}, u32[]{:S(2)}) collective-permute-start(bf16[16,64,1024]{2,1,0:T(8,128)(2,1)} %get-tuple-element.348), channel_id=1, source_target_pairs={{0,2},{2,0},{4,6},{6,4},{8,10},{10,8},{12,14},{14,12},{16,18},{18,... | collective-permute-start | bytes 6291464 | tf_op jit(solution)/shard_map/ppermute | solution.py:81
  180.2 11.5 %collective-permute-start.31 = (bf16[8,64,1024]{2,1,0:T(8,128)(2,1)S(1)}, bf16[8,64,1024]{2,1,0:T(8,128)(2,1)S(1)}, u32[]{:S(2)}, u32[]{:S(2)}) collective-permute-start(bf16[8,64,1024]{2,1,0:T(8,128)(2,1)S(1)} %collective-permute-done.28.db1.b1), channel_id=1, source_target_pairs={{0,2},{2,0},{4,6},{6,4},{8,10},{10,8},{12,14},{14,12},{16,18},{18,... | collective-permute-start | bytes 3145736 | tf_op jit(solution)/shard_map/ppermute | solution.py:81
  195.4 53.8 %collective-permute-start.35 = (bf16[8,64,1024]{2,1,0:T(8,128)(2,1)}, bf16[8,64,1024]{2,1,0:T(8,128)(2,1)S(1)}, u32[]{:S(2)}, u32[]{:S(2)}) collective-permute-start(bf16[8,64,1024]{2,1,0:T(8,128)(2,1)} %get-tuple-element.371), channel_id=1, source_target_pairs={{0,4},{2,6},{4,0},{6,2},{8,12},{10,14},{12,8},{14,10},{16,20},{18,... | collective-permute-start | bytes 3145736 | tf_op jit(solution)/shard_map/ppermute | solution.py:81
  200.7 48.5 %collective-permute-start.36 = (bf16[8,64,1024]{2,1,0:T(8,128)(2,1)}, bf16[8,64,1024]{2,1,0:T(8,128)(2,1)}, u32[]{:S(2)}, u32[]{:S(2)}) collective-permute-start(bf16[8,64,1024]{2,1,0:T(8,128)(2,1)} %get-tuple-element.372), channel_id=1, source_target_pairs={{0,1},{1,0},{2,3},{3,2},{4,5},{5,4},{6,7},{7,6},{8,9},{9,8},{10,11... | collective-permute-start | bytes 3145736 | tf_op jit(solution)/shard_map/ppermute | solution.py:81
  251.2 14.3 %collective-permute-start.37 = (bf16[4,64,1024]{2,1,0:T(8,128)(2,1)S(1)}, bf16[4,64,1024]{2,1,0:T(8,128)(2,1)S(1)}, u32[]{:S(2)}, u32[]{:S(2)}) collective-permute-start(bf16[4,64,1024]{2,1,0:T(8,128)(2,1)S(1)} %get-tuple-element.383), channel_id=1, source_target_pairs={{0,1},{1,0},{2,3},{3,2},{4,5},{5,4},{6,7},{7,6},{8,9},{9,8},{10,11... | collective-permute-start | bytes 1572872 | tf_op jit(solution)/shard_map/ppermute | solution.py:81
  252.3 13.6 %collective-permute-start.38 = (bf16[4,64,1024]{2,1,0:T(8,128)(2,1)S(1)}, bf16[4,64,1024]{2,1,0:T(8,128)(2,1)S(1)}, u32[]{:S(2)}, u32[]{:S(2)}) collective-permute-start(bf16[4,64,1024]{2,1,0:T(8,128)(2,1)S(1)} %get-tuple-element.384), channel_id=1, source_target_pairs={{0,4},{2,6},{4,0},{6,2},{8,12},{10,14},{12,8},{14,10},{16,20},{18,... | collective-permute-start | bytes 1572872 | tf_op jit(solution)/shard_map/ppermute | solution.py:81
  266.4 14.4 %collective-permute-start.39 = (bf16[16,64,1024]{2,1,0:T(8,128)(2,1)S(1)}, bf16[16,64,1024]{2,1,0:T(8,128)(2,1)S(1)}, u32[]{:S(2)}, u32[]{:S(2)}) collective-permute-start(bf16[16,64,1024]{2,1,0:T(8,128)(2,1)S(1)} %get-tuple-element.395), channel_id=1, source_target_pairs={{0,2},{2,0},{4,6},{6,4},{8,10},{10,8},{12,14},{14,12},{16,18},{18,... | collective-permute-start | bytes 6291464 | tf_op jit(solution)/shard_map/ppermute | solution.py:81
  266.5 14.3 %collective-permute-start.40 = (bf16[2,64,2048]{2,1,0:T(8,128)(2,1)S(1)}, bf16[2,64,2048]{2,1,0:T(8,128)(2,1)S(1)}, u32[]{:S(2)}, u32[]{:S(2)}) collective-permute-start(bf16[2,64,2048]{2,1,0:T(8,128)(2,1)S(1)} %pad_maximum_fusion.9), channel_id=1, source_target_pairs={{0,8},{2,10},{4,12},{6,14},{8,0},{10,2},{12,4},{14,6},{16,24},{18,... | collective-permute-start | bytes 1572872 | tf_op jit(solution)/shard_map/ppermute | solution.py:81
  288.3 25.7 %collective-permute-start.42 = (bf16[8,64,1024]{2,1,0:T(8,128)(2,1)S(1)}, bf16[8,64,1024]{2,1,0:T(8,128)(2,1)S(1)}, u32[]{:S(2)}, u32[]{:S(2)}) collective-permute-start(bf16[8,64,1024]{2,1,0:T(8,128)(2,1)S(1)} %get-tuple-element.417), channel_id=1, source_target_pairs={{0,4},{2,6},{4,0},{6,2},{8,12},{10,14},{12,8},{14,10},{16,20},{18,... | collective-permute-start | bytes 3145736 | tf_op jit(solution)/shard_map/ppermute | solution.py:81
  289.2 25.3 %collective-permute-start.43 = (bf16[8,64,1024]{2,1,0:T(8,128)(2,1)S(1)}, bf16[8,64,1024]{2,1,0:T(8,128)(2,1)S(1)}, u32[]{:S(2)}, u32[]{:S(2)}) collective-permute-start(bf16[8,64,1024]{2,1,0:T(8,128)(2,1)S(1)} %get-tuple-element.418), channel_id=1, source_target_pairs={{0,1},{1,0},{2,3},{3,2},{4,5},{5,4},{6,7},{7,6},{8,9},{9,8},{10,11... | collective-permute-start | bytes 3145736 | tf_op jit(solution)/shard_map/ppermute | solution.py:81
  290.5 24.0 %collective-permute-start.44 = (bf16[16,64,512]{2,1,0:T(8,128)(2,1)S(1)}, bf16[16,64,512]{2,1,0:T(8,128)(2,1)S(1)}, u32[]{:S(2)}, u32[]{:S(2)}) collective-permute-start(bf16[16,64,512]{2,1,0:T(8,128)(2,1)S(1)} %get-tuple-element.419), channel_id=1, source_target_pairs={{0,2},{2,0},{4,6},{6,4},{8,10},{10,8},{12,14},{14,12},{16,18},{18,... | collective-permute-start | bytes 3145736 | tf_op jit(solution)/shard_map/ppermute | solution.py:81
  290.5 22.8 %collective-permute-start.45 = (bf16[1,64,2048]{2,1,0:T(8,128)(2,1)S(1)}, bf16[1,64,2048]{2,1,0:T(8,128)(2,1)S(1)}, u32[]{:S(2)}, u32[]{:S(2)}) collective-permute-start(bf16[1,64,2048]{2,1,0:T(8,128)(2,1)S(1)} %get-tuple-element.420), channel_id=1, source_target_pairs={{0,16},{2,18},{4,20},{6,22},{8,24},{10,26},{12,28},{14,30},{16,0},... | collective-permute-start | bytes 786440 | tf_op jit(solution)/shard_map/ppermute | solution.py:81
  315.4 20.0 %collective-permute-start.46 = (bf16[4,64,1024]{2,1,0:T(8,128)(2,1)S(1)}, bf16[4,64,1024]{2,1,0:T(8,128)(2,1)S(1)}, u32[]{:S(2)}, u32[]{:S(2)}) collective-permute-start(bf16[4,64,1024]{2,1,0:T(8,128)(2,1)S(1)} %get-tuple-element.425), channel_id=1, source_target_pairs={{0,1},{1,0},{2,3},{3,2},{4,5},{5,4},{6,7},{7,6},{8,9},{9,8},{10,11... | collective-permute-start | bytes 1572872 | tf_op jit(solution)/shard_map/ppermute | solution.py:81
  316.8 18.7 %collective-permute-start.47 = (bf16[4,64,1024]{2,1,0:T(8,128)(2,1)S(1)}, bf16[4,64,1024]{2,1,0:T(8,128)(2,1)S(1)}, u32[]{:S(2)}, u32[]{:S(2)}) collective-permute-start(bf16[4,64,1024]{2,1,0:T(8,128)(2,1)S(1)} %get-tuple-element.426), channel_id=1, source_target_pairs={{0,4},{2,6},{4,0},{6,2},{8,12},{10,14},{12,8},{14,10},{16,20},{18,... | collective-permute-start | bytes 1572872 | tf_op jit(solution)/shard_map/ppermute | solution.py:81
  336.7 12.9 %collective-permute-start.48 = (bf16[2,64,2048]{2,1,0:T(8,128)(2,1)}, bf16[2,64,2048]{2,1,0:T(8,128)(2,1)S(1)}, u32[]{:S(2)}, u32[]{:S(2)}) collective-permute-start(bf16[2,64,2048]{2,1,0:T(8,128)(2,1)} %pad_maximum_fusion.11), channel_id=1, source_target_pairs={{0,8},{2,10},{4,12},{6,14},{8,0},{10,2},{12,4},{14,6},{16,24},{18,... | collective-permute-start | bytes 1572872 | tf_op jit(solution)/shard_map/ppermute | solution.py:81
  337.5 13.0 %collective-permute-start.49 = (bf16[8,64,512]{2,1,0:T(8,128)(2,1)}, bf16[8,64,512]{2,1,0:T(8,128)(2,1)}, u32[]{:S(2)}, u32[]{:S(2)}) collective-permute-start(bf16[8,64,512]{2,1,0:T(8,128)(2,1)} %get-tuple-element.444), channel_id=1, source_target_pairs={{0,4},{2,6},{4,0},{6,2},{8,12},{10,14},{12,8},{14,10},{16,20},{18,... | collective-permute-start | bytes 1572872 | tf_op jit(solution)/shard_map/ppermute | solution.py:81
  352.5 26.3 %collective-permute-start.50 = (bf16[16,3,64,256]{3,2,1,0:T(8,128)(2,1)S(1)}, bf16[16,3,64,256]{3,2,1,0:T(8,128)(2,1)S(1)}, u32[]{:S(2)}, u32[]{:S(2)}) collective-permute-start(bf16[16,3,64,256]{3,2,1,0:T(8,128)(2,1)S(1)} %get-tuple-element.455), channel_id=1, source_target_pairs={{0,2},{2,0},{4,6},{6,4},{8,10},{10,8},{12,14},{14,12},{16,18},{18,... | collective-permute-start | bytes 4718600 | tf_op jit(solution)/shard_map/ppermute | solution.py:81
  352.5 26.3 %collective-permute-start.51 = (bf16[1,64,2048]{2,1,0:T(8,128)(2,1)S(1)}, bf16[1,64,2048]{2,1,0:T(8,128)(2,1)S(1)}, u32[]{:S(2)}, u32[]{:S(2)}) collective-permute-start(bf16[1,64,2048]{2,1,0:T(8,128)(2,1)S(1)} %get-tuple-element.456), channel_id=1, source_target_pairs={{0,16},{2,18},{4,20},{6,22},{8,24},{10,26},{12,28},{14,30},{16,0},... | collective-permute-start | bytes 786440 | tf_op jit(solution)/shard_map/ppermute | solution.py:81
  354.8 24.0 %collective-permute-start.52 = (bf16[4,64,512]{2,1,0:T(8,128)(2,1)S(1)}, bf16[4,64,512]{2,1,0:T(8,128)(2,1)S(1)}, u32[]{:S(2)}, u32[]{:S(2)}) collective-permute-start(bf16[4,64,512]{2,1,0:T(8,128)(2,1)S(1)} %get-tuple-element.457), channel_id=1, source_target_pairs={{0,1},{1,0},{2,3},{3,2},{4,5},{5,4},{6,7},{7,6},{8,9},{9,8},{10,11... | collective-permute-start | bytes 786440 | tf_op jit(solution)/shard_map/ppermute | solution.py:81
  356.0 22.8 %collective-permute-start.53 = (bf16[1,256,1024]{2,1,0:T(8,128)(2,1)S(1)}, bf16[1,256,1024]{2,1,0:T(8,128)(2,1)S(1)}, u32[]{:S(2)}, u32[]{:S(2)}) collective-permute-start(bf16[1,256,1024]{2,1,0:T(8,128)(2,1)S(1)} %get-tuple-element.461), channel_id=1, source_target_pairs={{0,1},{1,0},{2,3},{3,2},{4,5},{5,4},{6,7},{7,6},{8,9},{9,8},{10,11... | collective-permute-start | bytes 1572872 | tf_op jit(solution)/shard_map/ppermute | solution.py:81
  377.5 13.7 %collective-permute-start.55 = (bf16[1,256,1024]{2,1,0:T(8,128)(2,1)S(1)}, bf16[1,256,1024]{2,1,0:T(8,128)(2,1)}, u32[]{:S(2)}, u32[]{:S(2)}) collective-permute-start(bf16[1,256,1024]{2,1,0:T(8,128)(2,1)S(1)} %get-tuple-element.476), channel_id=1, source_target_pairs={{0,1},{1,0},{2,3},{3,2},{4,5},{5,4},{6,7},{7,6},{8,9},{9,8},{10,11... | collective-permute-start | bytes 1572872 | tf_op jit(solution)/shard_map/ppermute | solution.py:81
  402.6 20.0 %collective-permute-start.57 = (bf16[8,3,64,256]{3,2,1,0:T(8,128)(2,1)S(1)}, bf16[8,3,64,256]{3,2,1,0:T(8,128)(2,1)S(1)}, u32[]{:S(2)}, u32[]{:S(2)}) collective-permute-start(bf16[8,3,64,256]{3,2,1,0:T(8,128)(2,1)S(1)} %get-tuple-element.494), channel_id=1, source_target_pairs={{0,4},{2,6},{4,0},{6,2},{8,12},{10,14},{12,8},{14,10},{16,20},{18,... | collective-permute-start | bytes 2359304 | tf_op jit(solution)/shard_map/ppermute | solution.py:81
  403.5 19.7 %collective-permute-start.58 = (bf16[8,3,64,256]{3,2,1,0:T(8,128)(2,1)S(1)}, bf16[8,3,64,256]{3,2,1,0:T(8,128)(2,1)S(1)}, u32[]{:S(2)}, u32[]{:S(2)}) collective-permute-start(bf16[8,3,64,256]{3,2,1,0:T(8,128)(2,1)S(1)} %get-tuple-element.495), channel_id=1, source_target_pairs={{0,1},{1,0},{2,3},{3,2},{4,5},{5,4},{6,7},{7,6},{8,9},{9,8},{10,11... | collective-permute-start | bytes 2359304 | tf_op jit(solution)/shard_map/ppermute | solution.py:81
  404.3 15.8 %collective-permute-start.59 = (bf16[1,64,512]{2,1,0:T(8,128)(2,1)S(1)}, bf16[1,64,512]{2,1,0:T(8,128)(2,1)S(1)}, u32[]{:S(2)}, u32[]{:S(2)}) collective-permute-start(bf16[1,64,512]{2,1,0:T(8,128)(2,1)S(1)} %get-tuple-element.496), channel_id=1, source_target_pairs={{0,16},{2,18},{4,20},{6,22},{8,24},{10,26},{12,28},{14,30},{16,0},... | collective-permute-start | bytes 196616 | tf_op jit(solution)/shard_map/ppermute | solution.py:81
  424.6 12.6 %collective-permute-start.60 = (bf16[4,3,64,256]{3,2,1,0:T(8,128)(2,1)S(1)}, bf16[4,3,64,256]{3,2,1,0:T(8,128)(2,1)S(1)}, u32[]{:S(2)}, u32[]{:S(2)}) collective-permute-start(bf16[4,3,64,256]{3,2,1,0:T(8,128)(2,1)S(1)} %get-tuple-element.508), channel_id=1, source_target_pairs={{0,1},{1,0},{2,3},{3,2},{4,5},{5,4},{6,7},{7,6},{8,9},{9,8},{10,11... | collective-permute-start | bytes 1179656 | tf_op jit(solution)/shard_map/ppermute | solution.py:81
  425.6 11.7 %collective-permute-start.61 = (bf16[4,3,64,256]{3,2,1,0:T(8,128)(2,1)S(1)}, bf16[4,3,64,256]{3,2,1,0:T(8,128)(2,1)S(1)}, u32[]{:S(2)}, u32[]{:S(2)}) collective-permute-start(bf16[4,3,64,256]{3,2,1,0:T(8,128)(2,1)S(1)} %get-tuple-element.509), channel_id=1, source_target_pairs={{0,4},{2,6},{4,0},{6,2},{8,12},{10,14},{12,8},{14,10},{16,20},{18,... | collective-permute-start | bytes 1179656 | tf_op jit(solution)/shard_map/ppermute | solution.py:81
  441.6 21.7 %collective-permute-start.66 = (bf16[1,256,1024]{2,1,0:T(8,128)(2,1)}, bf16[1,256,1024]{2,1,0:T(8,128)(2,1)S(1)}, u32[]{:S(2)}, u32[]{:S(2)}) collective-permute-start(bf16[1,256,1024]{2,1,0:T(8,128)(2,1)} %get-tuple-element.517), channel_id=1, source_target_pairs={{0,1},{1,0},{2,3},{3,2},{4,5},{5,4},{6,7},{7,6},{8,9},{9,8},{10,11... | collective-permute-start | bytes 1572872 | tf_op jit(solution)/shard_map/ppermute | solution.py:81
  442.7 22.0 %collective-permute-start.67 = (bf16[1,256,1024]{2,1,0:T(8,128)(2,1)}, bf16[1,256,1024]{2,1,0:T(8,128)(2,1)S(1)}, u32[]{:S(2)}, u32[]{:S(2)}) collective-permute-start(bf16[1,256,1024]{2,1,0:T(8,128)(2,1)} %get-tuple-element.518), channel_id=1, source_target_pairs={{0,1},{1,0},{2,3},{3,2},{4,5},{5,4},{6,7},{7,6},{8,9},{9,8},{10,11... | collective-permute-start | bytes 1572872 | tf_op jit(solution)/shard_map/ppermute | solution.py:81
  (83 other events, 952.3 us)

commit v6 on v5

--- a/solution.py
+++ b/solution.py
@@ -420,21 +420,27 @@
         here = pl.ds(first, block)
         keys = pl.ds(low, high - low)
         q, da, k, v = q_ref[here, :], da_ref[here, :], k_ref[keys, :], v_ref[keys, :]
-        heads = []
+        probs, scores, q_own, da_own, k_own = [], [], [], [], []
         for h in range(2):
             mask = lower if h == 0 else ~lower
-            q_own = jnp.where(mask, q, jnp.zeros_like(q))
-            da_own = jnp.where(mask, da, jnp.zeros_like(da))
-            s = dotf(k, q_own, 1, 1) + bias[n][...]
+            q_own.append(jnp.where(mask, q, jnp.zeros_like(q)))
+            da_own.append(jnp.where(mask, da, jnp.zeros_like(da)))
+            k_own.append(jnp.where(mask, k, jnp.zeros_like(k)))
+            s = dotf(k, q_own[h], 1, 1) + bias[n][...]
             p = jnp.exp(s - lse_ref[0, pl.ds(h, 1), here])
-            product = p * dotf(v, da_own, 1, 1)
+            product = p * dotf(v, da_own[h], 1, 1)
             inner = jnp.sum(product, axis=0, keepdims=True)
             inner_ref[0, pl.ds(h, 1), here] = inner
-            ds = (product - p * inner).astype(BF)
-            dv_acc[keys, :] += dotf(p.astype(BF), da_own, 1, 0)
-            dk_acc[keys, :] += dotf(ds, q_own, 1, 0)
-            heads.append(dotf(ds, k, 0, 0))
-        dq_ref[here, :] = (jnp.where(lower, heads[0], heads[1]) * factor).astype(BF)
+            scores.append((product - p * inner).astype(BF))
+            probs.append(p.astype(BF))
+        dv_acc[keys, :] += dotf(
+            jnp.concatenate(probs, axis=1), jnp.concatenate(da_own, axis=0), 1, 0
+        )
+        dk_acc[keys, :] += dotf(
+            jnp.concatenate(scores, axis=1), jnp.concatenate(q_own, axis=0), 1, 0
+        )
+        dq = dotf(jnp.concatenate(scores, axis=0), jnp.concatenate(k_own, axis=0), 0, 0)
+        dq_ref[here, :] = (dq * factor).astype(BF)
     dk_ref[...] = dk_acc[...].astype(BF)
     dv_ref[...] = dv_acc[...].astype(BF)
 
@@ -1121,7 +1127,7 @@
 
     def grad_half(n, a, b, name, turn=False):
         keep, send = weight_grad(
-            tables[n], a, [b], grid_of, n * half_cols, half_cols, name, turn, not turn
+            tables[n], a, [b], grid_of, n * half_cols, half_cols, name, turn, True
         )
         return Scatter(keep, send, steps[n])
 
@@ -1193,7 +1199,6 @@
         q_last.keep, q_last.send, rows_out.arrived = lax.optimization_barrier(
             (q_last.keep, q_last.send, rows_out.arrived)
         )
-        rows_out.end()
     dresid = launch(dresid, [q_last])
     dresid = land(dresid, [q_last])
     beside = halves + [o0] + ([] if parts > 1 else [rows_out])
@@ -1228,6 +1233,7 @@
     for one, value in zip(tail, values):
         one.go(value)
     rows_back.go(sent)
+    rows_out.arrived = held(rows_out.arrived, [one.arrived for one in tail])
     for one in tail:
         one.end()
     while last.steps:
@@ -1239,6 +1245,7 @@
     last.value = held(last.value, arrived)
     for one in tail:
         one.end()
+    rows_out.end()
     rows_back.end()
     block_out, grad_in = rows_out.result, rows_back.result
     d_totals, u_totals, o_totals, q_totals = (

time: 476 us -> 474 us (level)
  Pallas kernels: 258 us -> 247 us
  waiting for transfers between devices: 84.6 us -> 92.4 us
    pallas_call x2, Pallas kernels: 41.6 us -> 34.8 us  [attend_back(): pl.pallas_call(functools.partial(attend_back_kernel, rows, block, factor)...]
  transfers between devices with their start and end apart: 73 -> 73, of which waited for: 31 -> 29; matrix products, arithmetic and copies ran while one was open for 6% -> 6% of each run, Pallas kernels for 55% -> 53%
where the time goes in v6:
time: 474 us; the launch traced here: 465 us
  Pallas kernels  247 us (52%)
  waiting for transfers between devices  92.4 us (19%)
  starting transfers between devices  70.1 us (15%)
  other arithmetic  27.9 us (6%)
  local copies, waits for them, and re-layouts  25.5 us (5%)
    ppermute x66, waiting for transfers between devices, swap(): return lax.ppermute(value, axis, [(i, i ^ flip) for i in range(count)])  82.4 us
    ppermute x66, starting transfers between devices, swap(): return lax.ppermute(value, axis, [(i, i ^ flip) for i in range(count)])  62.1 us
    pallas_call x7, Pallas kernels, weight_grad(): pl.pallas_call(functools.partial(grad_kernel, grid_of, count, turn, chunk...  59.3 us
    pallas_call x1, Pallas kernels, feed_back(): pl.pallas_call(functools.partial(back_kernel, grid_of), grid_spec=pltpu.P...  46.5 us
    pallas_call x2, Pallas kernels, attend_back(): pl.pallas_call(functools.partial(attend_back_kernel, rows, block, factor)...  34.8 us
    pallas_call x2, Pallas kernels, hidden_forward(): pl.pallas_call(kernel, grid_spec=pltpu.PrefetchScalarGridSpec(num_scalar_...  34.7 us
    pallas_call x2, Pallas kernels, attend(): pl.pallas_call(kernel, grid_spec=pltpu.PrefetchScalarGridSpec(num_scalar_...  26.2 us
    convert_element_type x25, other arithmetic, end(): (keep[:half].astype(F32) + arrived[:half].astype(F32)).astype(BF)  19.3 us
  transfers between devices with their start and end apart: 73, of which 29 were waited for; matrix products, arithmetic and copies ran while one was open for 6% of the time, Pallas kernels for 53%

profile of v6, /device:TPU:0, one launch (start us, length us, event | category | flops | bytes accessed | tf_op | source)
XLA Modules:
  0.0 465.3 jit_solution(13064535168579423855)
XLA Ops:
  4.2 2.9 collective-permute-start
  7.1 2.6 collective-permute-start.1
  9.7 8.9 %collective-permute-done.1 = bf16[1,3,64,512]{3,2,1,0:T(8,128)(2,1)S(1)} collective-permute-done((bf16[1,3,64,512]{3,2,1,0:T(8,128)(2,1)S(1)}, bf16[1,3,64,512]{3,2,1,0:T(8,128)(2,1)S(1)}, u32[]{:S(2)}, u32[]{:S(2)}) %collective-permute-start.1) | collective-permute-done | bytes 196640 | tf_op jit(solution)/shard_map/ppermute | solution.py:81
  19.4 9.3 %collective-permute-done.2 = bf16[2,3,64,512]{3,2,1,0:T(8,128)(2,1)S(1)} collective-permute-done((bf16[2,3,64,512]{3,2,1,0:T(8,128)(2,1)S(1)}, bf16[2,3,64,512]{3,2,1,0:T(8,128)(2,1)S(1)}, u32[]{:S(2)}, u32[]{:S(2)}) %collective-permute-start.2) | collective-permute-done | bytes 393248 | tf_op jit(solution)/shard_map/ppermute | solution.py:81
  33.6 2.7 collective-permute-start.7
  36.2 4.3 collective-permute-done.4
  43.9 5.7 %collective-permute-done.7 = bf16[1,64,2560]{2,1,0:T(8,128)(2,1)S(1)} collective-permute-done((bf16[1,64,2560]{2,1,0:T(8,128)(2,1)S(1)}, bf16[1,64,2560]{2,1,0:T(8,128)(2,1)S(1)}, u32[]{:S(2)}, u32[]{:S(2)}) %collective-permute-start.7) | collective-permute-done | bytes 327712 | tf_op jit(solution)/shard_map/ppermute | solution.py:81
  52.0 7.2 %collective-permute-done.5.refs_1_.refs_10_ = bf16[8,3,64,256]{3,2,1,0:T(8,128)(2,1)} collective-permute-done((bf16[8,3,64,256]{3,2,1,0:T(8,128)(2,1)S(1)}, bf16[8,3,64,256]{3,2,1,0:T(8,128)(2,1)}, u32[]{:S(2)}, u32[]{:S(2)}) %collective-permute-start.5) | collective-permute-done | bytes 786464 | tf_op jit(solution)/shard_map/ppermute | solution.py:81
  61.2 4.1 collective-permute-done.8
  66.7 14.3 %project.1 = (bf16[1024,1024]{1,0:T(8,128)(2,1)}, bf16[1024,1024]{1,0:T(8,128)(2,1)}, bf16[1024,1024]{1,0:T(8,128)(2,1)}, bf16[1024,1024]{1,0:T(8,128)(2,1)}) custom-call(s32[64]{0:T(128)S(1)} %pad_add_fusion.order_ref, bf16[1024,1024]{1,0:T(8,128)(2,1)} %bitcast.3.x_ref.refs_1_.refs_6_, f32[3,1024]{1,0:T(4,128)S(1)} %copy-done.4, ...), custom_call_target="tpu_custom_call" | custom-call | flops 12999999488 | bytes 1048576 | tf_op jit(solution)/shard_map/project/pallas_call | solution.py:343
  84.5 3.4 collective-permute-start.16
  87.9 13.1 %attend.2 = (bf16[1024,1024]{1,0:T(8,128)(2,1)}, f32[8,2,1024]{2,1,0:T(2,128)}) custom-call(s32[4]{0:T(128)S(1)} %bitcast.33, bf16[1024,1024]{1,0:T(8,128)(2,1)} %get-tuple-element.293.q_ref, bf16[1024,1024]{1,0:T(8,128)(2,1)} %get-tuple-element.294.k_ref, bf16[1024,1024]{1,0:T(8,128)(2,1)} %get-tuple-element.295.v_ref, ...), custom_call_target="tpu_custom_call" | custom-call | flops 12000000000 | bytes 1048576 | tf_op jit(solution)/shard_map/attend/pallas_call | solution.py:472
  101.0 1.8 collective-permute-start.19
  102.8 13.1 %attend.3 = (bf16[1024,1024]{1,0:T(8,128)(2,1)}, f32[8,2,1024]{2,1,0:T(2,128)}) custom-call(s32[4]{0:T(128)S(1)} %bitcast.34, bf16[1024,1024]{1,0:T(8,128)(2,1)} %get-tuple-element.293.q_ref, bf16[1024,1024]{1,0:T(8,128)(2,1)} %get-tuple-element.294.k_ref, ...), custom_call_target="tpu_custom_call", output_to_operand_aliasing={{0}: (5, {}), {1}: (6, {})} | custom-call | flops 12000000000 | bytes 1048576 | tf_op jit(solution)/shard_map/attend/pallas_call | solution.py:472
  119.1 1.9 collective-permute-done.21.refs_11_.b3
  125.6 17.5 %hidden_forward.2 = (f32[1024,1024]{1,0:T(8,128)}, bf16[1024,1024]{1,0:T(8,128)(2,1)}, f32[1024,4096]{1,0:T(8,128)}, bf16[1024,4096]{1,0:T(8,128)(2,1)}, f32[1024,128]{1,0:T(8,128)}) custom-call(s32[64]{0:T(128)S(1)} %pad_add_fusion.order_ref, bf16[1024,1024]{1,0:T(8,128)(2,1)} %get-tuple-element.315.refs_0_, ...), custom_call_target="tpu_custom_call" | custom-call | flops 15000000512 | bytes 1048576 | tf_op jit(solution)/shard_map/hidden_forward/pallas_call | solution.py:608
  144.8 17.2 %hidden_forward.3 = (f32[1024,1024]{1,0:T(8,128)}, bf16[1024,1024]{1,0:T(8,128)(2,1)}, f32[1024,4096]{1,0:T(8,128)}, bf16[1024,4096]{1,0:T(8,128)(2,1)}, f32[1024,128]{1,0:T(8,128)}) custom-call(s32[64]{0:T(128)S(1)} %pad_add_fusion.order_ref, ...), custom_call_target="tpu_custom_call", output_to_operand_aliasing={{0}: (13, {}), {1}: (14, {}), {2}: (15, {}), {3}: (16, {}),... | custom-call | flops 15000000512 | bytes 1048576 | tf_op jit(solution)/shard_map/hidden_forward/pallas_call | solution.py:608
  162.1 5.7 %collective-permute-done.27.da1.a1 = bf16[8,64,1024]{2,1,0:T(8,128)(2,1)S(1)} collective-permute-done((bf16[8,64,1024]{2,1,0:T(8,128)(2,1)S(1)}, bf16[8,64,1024]{2,1,0:T(8,128)(2,1)S(1)}, u32[]{:S(2)}, u32[]{:S(2)}) %collective-permute-start.27) | collective-permute-done | bytes 1048608 | tf_op jit(solution)/shard_map/ppermute | solution.py:81
  169.4 8.7 %grad_down.2 = (bf16[16,64,1024]{2,1,0:T(8,128)(2,1)S(1)}, bf16[16,64,1024]{2,1,0:T(8,128)(2,1)S(1)}) custom-call(s32[32]{0:T(128)S(1)} %get-tuple-element.604.order_ref, bf16[1024,1024]{1,0:T(8,128)(2,1)} %bitcast.37, bf16[1024,4096]{1,0:T(8,128)(2,1)} %get-tuple-element.426.refs_0_.narrow_ref), custom_call_target="tpu_custom_call" | custom-call | flops 4800000000 | bytes 1048576 | tf_op jit(solution)/shard_map/grad_down/pallas_call | solution.py:898
  180.4 9.1 %grad_down.3 = (bf16[16,64,1024]{2,1,0:T(8,128)(2,1)S(1)}, bf16[16,64,1024]{2,1,0:T(8,128)(2,1)S(1)}) custom-call(s32[32]{0:T(128)S(1)} %get-tuple-element.603.order_ref, bf16[1024,1024]{1,0:T(8,128)(2,1)} %bitcast.38, bf16[1024,4096]{1,0:T(8,128)(2,1)} %get-tuple-element.426.refs_0_.narrow_ref), custom_call_target="tpu_custom_call" | custom-call | flops 4800000000 | bytes 1048576 | tf_op jit(solution)/shard_map/grad_down/pallas_call | solution.py:898
  189.5 2.1 add_convert_fusion.6
  193.8 2.1 collective-permute-done.32
  195.9 2.0 add_convert_fusion.4
  199.9 46.5 %feed_back.1 = (bf16[1024,4096]{1,0:T(8,128)(2,1)}, f32[1024,1024]{1,0:T(8,128)}, bf16[1024,1024]{1,0:T(8,128)(2,1)}, bf16[1024,1024]{1,0:T(8,128)(2,1)}, f32[16,1024]{1,0:T(8,128)}, /*index=5*/f32[8,4096]{1,0:T(8,128)}) custom-call(s32[64]{0:T(128)} %copy-done.6, f32[1024,4096]{1,0:T(8,128)} %get-tuple-element.362.hidden_ref, ...), custom_call_target="tpu_custom_call" | custom-call | flops 60000002048 | bytes 1048576 | tf_op jit(solution)/shard_map/feed_back/pallas_call | solution.py:799
  250.6 8.0 %grad_up.2 = (bf16[16,64,1024]{2,1,0:T(8,128)(2,1)S(1)}, bf16[16,64,1024]{2,1,0:T(8,128)(2,1)S(1)}) custom-call(s32[32]{0:T(128)S(1)} %get-tuple-element.604.order_ref, bf16[1024,1024]{1,0:T(8,128)(2,1)} %get-tuple-element.382.a_ref, bf16[1024,4096]{1,0:T(8,128)(2,1)} %get-tuple-element.394.refs_0_), custom_call_target="tpu_custom_call" | custom-call | flops 4800000000 | bytes 1048576 | tf_op jit(solution)/shard_map/grad_up/pallas_call | solution.py:898
  258.7 4.0 collective-permute-done.37
  264.5 8.0 %grad_up.3 = (bf16[16,64,1024]{2,1,0:T(8,128)(2,1)S(1)}, bf16[16,64,1024]{2,1,0:T(8,128)(2,1)S(1)}) custom-call(s32[32]{0:T(128)S(1)} %get-tuple-element.603.order_ref, bf16[1024,1024]{1,0:T(8,128)(2,1)} %get-tuple-element.382.a_ref, bf16[1024,4096]{1,0:T(8,128)(2,1)} %get-tuple-element.394.refs_0_), custom_call_target="tpu_custom_call" | custom-call | flops 4800000000 | bytes 1048576 | tf_op jit(solution)/shard_map/grad_up/pallas_call | solution.py:898
  272.5 5.6 %collective-permute-done.40 = bf16[2,64,2048]{2,1,0:T(8,128)(2,1)S(1)} collective-permute-done((bf16[2,64,2048]{2,1,0:T(8,128)(2,1)S(1)}, bf16[2,64,2048]{2,1,0:T(8,128)(2,1)S(1)}, u32[]{:S(2)}, u32[]{:S(2)}) %collective-permute-start.40) | collective-permute-done | bytes 524320 | tf_op jit(solution)/shard_map/ppermute | solution.py:81
  278.1 5.2 %grad_out.1 = (bf16[16,64,512]{2,1,0:T(8,128)(2,1)S(1)}, bf16[16,64,512]{2,1,0:T(8,128)(2,1)S(1)}) custom-call(s32[32]{0:T(128)S(1)} %get-tuple-element.604.order_ref, bf16[1024,1024]{1,0:T(8,128)(2,1)} %get-tuple-element.404.a_ref, bf16[1024,1024]{1,0:T(8,128)(2,1)} %get-tuple-element.315.refs_0_), custom_call_target="tpu_custom_call" | custom-call | flops 2400000000 | bytes 1048576 | tf_op jit(solution)/shard_map/grad_out/pallas_call | solution.py:898
  288.0 1.9 collective-permute-start.45
  289.9 17.4 %attend_back.2 = (bf16[1024,512]{1,0:T(8,128)(2,1)}, bf16[1024,512]{1,0:T(8,128)(2,1)}, bf16[1024,512]{1,0:T(8,128)(2,1)}, f32[4,2,1024]{2,1,0:T(2,128)}) custom-call(s32[4]{0:T(128)S(1)} %bitcast.35, bf16[1024,1024]{1,0:T(8,128)(2,1)} %get-tuple-element.293.q_ref, bf16[1024,1024]{1,0:T(8,128)(2,1)} %get-tuple-element.294.k_ref, ...), custom_call_target="tpu_custom_call" | custom-call | flops 20999999488 | bytes 1048576 | tf_op jit(solution)/shard_map/attend_back/pallas_call | solution.py:501
  307.3 3.9 collective-permute-done.42
  315.1 16.6 %feed_forward.1 = bf16[1024,1024]{1,0:T(8,128)(2,1)} custom-call(s32[64]{0:T(128)S(1)} %copy-done.7, bf16[1024,4096]{1,0:T(8,128)(2,1)} %get-tuple-element.426.refs_0_.narrow_ref, f32[1024,1024]{1,0:T(8,128)} %get-tuple-element.364.unit_ref, bf16[1024,1024]{1,0:T(8,128)(2,1)} %bitcast.3.x_ref.refs_1_.refs_6_, f32[3,1024]{1,0:T(4,128)S(1)} %copy-done.5, ...), custom_call_target="tpu_custom_call" | custom-call | flops 14000000000 | bytes 1048576 | tf_op jit(solution)/shard_map/feed_forward/pallas_call | solution.py:675
  337.3 9.4 %grad_qkv.2 = (bf16[16,3,64,256]{3,2,1,0:T(8,128)(2,1)S(1)}, bf16[16,3,64,256]{3,2,1,0:T(8,128)(2,1)S(1)}) custom-call(s32[32]{0:T(128)S(1)} %get-tuple-element.604.order_ref, bf16[1024,1024]{1,0:T(8,128)(2,1)} %get-tuple-element.430.a_ref, bf16[1024,512]{1,0:T(8,128)(2,1)} %get-tuple-element.440.refs_0_, bf16[1024,512]{1,0:T(8,128)(2,1)} %get-tuple-element.441.refs_1_, ...), custom_call_target="tpu_custom_call" | custom-call | flops 3600000000 | bytes 1048576 | tf_op jit(solution)/shard_map/grad_qkv/pallas_call | solution.py:898
  349.6 2.6 collective-permute-start.51
  354.2 17.4 %attend_back.3 = (bf16[1024,512]{1,0:T(8,128)(2,1)}, bf16[1024,512]{1,0:T(8,128)(2,1)}, bf16[1024,512]{1,0:T(8,128)(2,1)}, f32[4,2,1024]{2,1,0:T(2,128)}) custom-call(s32[4]{0:T(128)S(1)} %bitcast.36, bf16[1024,1024]{1,0:T(8,128)(2,1)} %get-tuple-element.293.q_ref, bf16[1024,1024]{1,0:T(8,128)(2,1)} %get-tuple-element.294.k_ref, ...), custom_call_target="tpu_custom_call" | custom-call | flops 20999999488 | bytes 1048576 | tf_op jit(solution)/shard_map/attend_back/pallas_call | solution.py:501
  374.1 10.9 %grad_qkv.3 = (bf16[16,3,64,256]{3,2,1,0:T(8,128)(2,1)S(1)}, bf16[16,3,64,256]{3,2,1,0:T(8,128)(2,1)}) custom-call(s32[32]{0:T(128)S(1)} %get-tuple-element.603.order_ref, bf16[1024,1024]{1,0:T(8,128)(2,1)} %get-tuple-element.430.a_ref, bf16[1024,512]{1,0:T(8,128)(2,1)} %get-tuple-element.469.refs_0_.refs_3_, ...), custom_call_target="tpu_custom_call" | custom-call | flops 3600000000 | bytes 1048576 | tf_op jit(solution)/shard_map/grad_qkv/pallas_call | solution.py:898
  386.8 1.9 add_bitcast_fusion
  391.7 2.8 add_convert_fusion.10
  394.6 1.8 add_convert_fusion.8
  399.8 14.7 %input_grad.1 = (bf16[1024,1024]{1,0:T(8,128)(2,1)}, f32[8,1024]{1,0:T(8,128)}) custom-call(s32[64]{0:T(128)S(1)} %copy-done.7, bf16[1024,512]{1,0:T(8,128)(2,1)} %get-tuple-element.440.refs_0_, bf16[1024,512]{1,0:T(8,128)(2,1)} %get-tuple-element.441.refs_1_, bf16[1024,512]{1,0:T(8,128)(2,1)} %get-tuple-element.442.refs_2_, ...), custom_call_target="tpu_custom_call" | custom-call | flops 15000000512 | bytes 1048576 | tf_op jit(solution)/shard_map/input_grad/pallas_call | solution.py:960
  414.6 1.9 collective-permute-done.57
  426.2 6.5 %collective-permute-done.63 = f32[7184]{0:T(1024)S(1)} collective-permute-done((f32[7184]{0:T(1024)S(1)}, f32[7184]{0:T(1024)S(1)}, u32[]{:S(2)}, u32[]{:S(2)}) %collective-permute-start.63) | collective-permute-done | bytes 28768 | tf_op jit(solution)/shard_map/ppermute | solution.py:169
  436.8 2.7 collective-permute-start.69
  441.2 3.5 collective-permute-done.67
  448.3 1.9 constant_dynamic-update-slice_fusion.5
  450.2 5.4 %collective-permute-done.72 = bf16[1,3,64,512]{3,2,1,0:T(8,128)(2,1)S(1)} collective-permute-done((bf16[1,3,64,512]{3,2,1,0:T(8,128)(2,1)S(1)}, bf16[1,3,64,512]{3,2,1,0:T(8,128)(2,1)S(1)}, u32[]{:S(2)}, u32[]{:S(2)}) %collective-permute-start.72) | collective-permute-done | bytes 196640 | tf_op jit(solution)/shard_map/ppermute | solution.py:81
  460.2 3.1 collective-permute-done.71
  (328 shorter events, 99.8 us)
Async XLA Ops:
  4.2 26.1 %collective-permute-start = (bf16[1,512,1024]{2,1,0:T(8,128)(2,1)S(1)}, bf16[1,512,1024]{2,1,0:T(8,128)(2,1)S(1)}, u32[]{:S(2)}, u32[]{:S(2)}) collective-permute-start(bf16[1,512,1024]{2,1,0:T(8,128)(2,1)S(1)} %get-tuple-element.273), channel_id=1, source_target_pairs={{0,1},{1,0},{2,3},{3,2},{4,5},{5,4},{6,7},{7,6},{8,9},{9,8},{10,11... | collective-permute-start | bytes 3145736 | tf_op jit(solution)/shard_map/ppermute | solution.py:81
  7.1 11.5 %collective-permute-start.1 = (bf16[1,3,64,512]{3,2,1,0:T(8,128)(2,1)S(1)}, bf16[1,3,64,512]{3,2,1,0:T(8,128)(2,1)S(1)}, u32[]{:S(2)}, u32[]{:S(2)}) collective-permute-start(bf16[1,3,64,512]{3,2,1,0:T(8,128)(2,1)S(1)} %bitcast.46), channel_id=1, source_target_pairs={{0,16},{2,18},{4,20},{6,22},{8,24},{10,26},{12,28},{14,30},{16,0},... | collective-permute-start | bytes 589832 | tf_op jit(solution)/shard_map/ppermute | solution.py:81
  33.6 16.0 %collective-permute-start.7 = (bf16[1,64,2560]{2,1,0:T(8,128)(2,1)S(1)}, bf16[1,64,2560]{2,1,0:T(8,128)(2,1)S(1)}, u32[]{:S(2)}, u32[]{:S(2)}) collective-permute-start(bf16[1,64,2560]{2,1,0:T(8,128)(2,1)S(1)} %maximum_bitcast_fusion), channel_id=1, source_target_pairs={{0,16},{2,18},{4,20},{6,22},{8,24},{10,26},{12,28},{14,30},{16,0},... | collective-permute-start | bytes 983048 | tf_op jit(solution)/shard_map/ppermute | solution.py:81
  41.8 17.4 %collective-permute-start.5 = (bf16[8,3,64,256]{3,2,1,0:T(8,128)(2,1)S(1)}, bf16[8,3,64,256]{3,2,1,0:T(8,128)(2,1)}, u32[]{:S(2)}, u32[]{:S(2)}) collective-permute-start(bf16[8,3,64,256]{3,2,1,0:T(8,128)(2,1)S(1)} %pad_maximum_fusion.4.refs_0_.refs_9_), channel_id=1, source_target_pairs={{0,4},{2,6},{4,0},{6,2},{8,12},{10,14},{12,8},{14,10},{16,20},{18,... | collective-permute-start | bytes 2359304 | tf_op jit(solution)/shard_map/ppermute | solution.py:81
  42.5 17.5 %collective-permute-start.6 = (bf16[8,3,64,256]{3,2,1,0:T(8,128)(2,1)S(1)}, bf16[8,3,64,256]{3,2,1,0:T(8,128)(2,1)}, u32[]{:S(2)}, u32[]{:S(2)}) collective-permute-start(bf16[8,3,64,256]{3,2,1,0:T(8,128)(2,1)S(1)} %pad_maximum_fusion.5.refs_4_.refs_13_), channel_id=1, source_target_pairs={{0,1},{1,0},{2,3},{3,2},{4,5},{5,4},{6,7},{7,6},{8,9},{9,8},{10,11... | collective-permute-start | bytes 2359304 | tf_op jit(solution)/shard_map/ppermute | solution.py:81
  49.6 15.7 %collective-permute-start.8 = (bf16[2,64,2560]{2,1,0:T(8,128)(2,1)S(1)}, bf16[2,64,2560]{2,1,0:T(8,128)(2,1)S(1)}, u32[]{:S(2)}, u32[]{:S(2)}) collective-permute-start(bf16[2,64,2560]{2,1,0:T(8,128)(2,1)S(1)} %pad_maximum_fusion.7), channel_id=1, source_target_pairs={{0,8},{2,10},{4,12},{6,14},{8,0},{10,2},{12,4},{14,6},{16,24},{18,... | collective-permute-start | bytes 1966088 | tf_op jit(solution)/shard_map/ppermute | solution.py:81
  52.0 14.0 %collective-permute-start.11 = (bf16[8,3,64,256]{3,2,1,0:T(8,128)(2,1)S(1)}, bf16[8,3,64,256]{3,2,1,0:T(8,128)(2,1)}, u32[]{:S(2)}, u32[]{:S(2)}) collective-permute-start(bf16[8,3,64,256]{3,2,1,0:T(8,128)(2,1)S(1)} %pad_maximum_fusion.5.refs_4_.refs_13_), channel_id=1, source_target_pairs={{0,2},{2,0},{4,6},{6,4},{8,10},{10,8},{12,14},{14,12},{16,18},{18,... | collective-permute-start | bytes 2359304 | tf_op jit(solution)/shard_map/ppermute | solution.py:81
  65.4 15.6 %collective-permute-start.13 = (bf16[4,64,1280]{2,1,0:T(8,128)(2,1)S(1)}, bf16[4,64,1280]{2,1,0:T(8,128)(2,1)S(1)}, u32[]{:S(2)}, u32[]{:S(2)}) collective-permute-start(bf16[4,64,1280]{2,1,0:T(8,128)(2,1)S(1)} %get-tuple-element.287), channel_id=1, source_target_pairs={{0,1},{1,0},{2,3},{3,2},{4,5},{5,4},{6,7},{7,6},{8,9},{9,8},{10,11... | collective-permute-start | bytes 1966088 | tf_op jit(solution)/shard_map/ppermute | solution.py:81
  66.0 15.0 %collective-permute-start.14 = (bf16[4,64,1280]{2,1,0:T(8,128)(2,1)S(1)}, bf16[4,64,1280]{2,1,0:T(8,128)(2,1)S(1)}, u32[]{:S(2)}, u32[]{:S(2)}) collective-permute-start(bf16[4,64,1280]{2,1,0:T(8,128)(2,1)S(1)} %get-tuple-element.288), channel_id=1, source_target_pairs={{0,4},{2,6},{4,0},{6,2},{8,12},{10,14},{12,8},{14,10},{16,20},{18,... | collective-permute-start | bytes 1966088 | tf_op jit(solution)/shard_map/ppermute | solution.py:81
  81.3 34.7 %collective-permute-start.17 = (bf16[8,64,1280]{2,1,0:T(8,128)(2,1)S(1)}, bf16[8,64,1280]{2,1,0:T(8,128)(2,1)S(1)}, u32[]{:S(2)}, u32[]{:S(2)}) collective-permute-start(bf16[8,64,1280]{2,1,0:T(8,128)(2,1)S(1)} %pad_maximum_fusion.refs_4_.a0), channel_id=1, source_target_pairs={{0,4},{2,6},{4,0},{6,2},{8,12},{10,14},{12,8},{14,10},{16,20},{18,... | collective-permute-start | bytes 3932168 | tf_op jit(solution)/shard_map/ppermute | solution.py:81
  82.8 41.4 %collective-permute-start.22 = (bf16[8,64,1280]{2,1,0:T(8,128)(2,1)S(1)}, bf16[8,64,1280]{2,1,0:T(8,128)(2,1)S(1)}, u32[]{:S(2)}, u32[]{:S(2)}) collective-permute-start(bf16[8,64,1280]{2,1,0:T(8,128)(2,1)S(1)} %pad_maximum_fusion.refs_4_.a0), channel_id=1, source_target_pairs={{0,2},{2,0},{4,6},{6,4},{8,10},{10,8},{12,14},{14,12},{16,18},{18,... | collective-permute-start | bytes 3932168 | tf_op jit(solution)/shard_map/ppermute | solution.py:81
  82.8 33.2 %collective-permute-start.18 = (bf16[8,64,1280]{2,1,0:T(8,128)(2,1)S(1)}, bf16[8,64,1280]{2,1,0:T(8,128)(2,1)S(1)}, u32[]{:S(2)}, u32[]{:S(2)}) collective-permute-start(bf16[8,64,1280]{2,1,0:T(8,128)(2,1)S(1)} %pad_maximum_fusion.1.refs_8_.b0), channel_id=1, source_target_pairs={{0,1},{1,0},{2,3},{3,2},{4,5},{5,4},{6,7},{7,6},{8,9},{9,8},{10,11... | collective-permute-start | bytes 3932168 | tf_op jit(solution)/shard_map/ppermute | solution.py:81
  84.2 39.9 %collective-permute-start.23 = (bf16[8,64,1280]{2,1,0:T(8,128)(2,1)S(1)}, bf16[8,64,1280]{2,1,0:T(8,128)(2,1)S(1)}, u32[]{:S(2)}, u32[]{:S(2)}) collective-permute-start(bf16[8,64,1280]{2,1,0:T(8,128)(2,1)S(1)} %pad_maximum_fusion.1.refs_8_.b0), channel_id=1, source_target_pairs={{0,2},{2,0},{4,6},{6,4},{8,10},{10,8},{12,14},{14,12},{16,18},{18,... | collective-permute-start | bytes 3932168 | tf_op jit(solution)/shard_map/ppermute | solution.py:81
  84.5 16.5 %collective-permute-start.16 = (bf16[1,64,2048]{2,1,0:T(8,128)(2,1)S(1)}, bf16[1,64,2048]{2,1,0:T(8,128)(2,1)S(1)}, u32[]{:S(2)}, u32[]{:S(2)}) collective-permute-start(bf16[1,64,2048]{2,1,0:T(8,128)(2,1)S(1)} %bitcast.44), channel_id=1, source_target_pairs={{0,16},{2,18},{4,20},{6,22},{8,24},{10,26},{12,28},{14,30},{16,0},... | collective-permute-start | bytes 786440 | tf_op jit(solution)/shard_map/ppermute | solution.py:81
  101.0 14.9 %collective-permute-start.19 = (bf16[2,64,2048]{2,1,0:T(8,128)(2,1)S(1)}, bf16[2,64,2048]{2,1,0:T(8,128)(2,1)S(1)}, u32[]{:S(2)}, u32[]{:S(2)}) collective-permute-start(bf16[2,64,2048]{2,1,0:T(8,128)(2,1)S(1)} %pad_maximum_fusion.8), channel_id=1, source_target_pairs={{0,8},{2,10},{4,12},{6,14},{8,0},{10,2},{12,4},{14,6},{16,24},{18,... | collective-permute-start | bytes 1572872 | tf_op jit(solution)/shard_map/ppermute | solution.py:81
  120.9 22.1 %collective-permute-start.24 = (bf16[4,64,1024]{2,1,0:T(8,128)(2,1)S(1)}, bf16[4,64,1024]{2,1,0:T(8,128)(2,1)S(1)}, u32[]{:S(2)}, u32[]{:S(2)}) collective-permute-start(bf16[4,64,1024]{2,1,0:T(8,128)(2,1)S(1)} %get-tuple-element.319), channel_id=1, source_target_pairs={{0,1},{1,0},{2,3},{3,2},{4,5},{5,4},{6,7},{7,6},{8,9},{9,8},{10,11... | collective-permute-start | bytes 1572872 | tf_op jit(solution)/shard_map/ppermute | solution.py:81
  121.5 21.6 %collective-permute-start.25 = (bf16[4,64,1024]{2,1,0:T(8,128)(2,1)S(1)}, bf16[4,64,1024]{2,1,0:T(8,128)(2,1)S(1)}, u32[]{:S(2)}, u32[]{:S(2)}) collective-permute-start(bf16[4,64,1024]{2,1,0:T(8,128)(2,1)S(1)} %get-tuple-element.320), channel_id=1, source_target_pairs={{0,4},{2,6},{4,0},{6,2},{8,12},{10,14},{12,8},{14,10},{16,20},{18,... | collective-permute-start | bytes 1572872 | tf_op jit(solution)/shard_map/ppermute | solution.py:81
  122.6 39.4 %collective-permute-start.26 = (bf16[1,512,1024]{2,1,0:T(8,128)(2,1)S(1)}, bf16[1,512,1024]{2,1,0:T(8,128)(2,1)S(1)}, u32[]{:S(2)}, u32[]{:S(2)}) collective-permute-start(bf16[1,512,1024]{2,1,0:T(8,128)(2,1)S(1)} %get-tuple-element.334), channel_id=1, source_target_pairs={{0,1},{1,0},{2,3},{3,2},{4,5},{5,4},{6,7},{7,6},{8,9},{9,8},{10,11... | collective-permute-start | bytes 3145736 | tf_op jit(solution)/shard_map/ppermute | solution.py:81
  143.3 24.4 %collective-permute-start.27 = (bf16[8,64,1024]{2,1,0:T(8,128)(2,1)S(1)}, bf16[8,64,1024]{2,1,0:T(8,128)(2,1)S(1)}, u32[]{:S(2)}, u32[]{:S(2)}) collective-permute-start(bf16[8,64,1024]{2,1,0:T(8,128)(2,1)S(1)} %pad_maximum_fusion.2.da0.a0), channel_id=1, source_target_pairs={{0,4},{2,6},{4,0},{6,2},{8,12},{10,14},{12,8},{14,10},{16,20},{18,... | collective-permute-start | bytes 3145736 | tf_op jit(solution)/shard_map/ppermute | solution.py:81
  144.3 35.6 %collective-permute-start.28 = (bf16[8,64,1024]{2,1,0:T(8,128)(2,1)S(1)}, bf16[8,64,1024]{2,1,0:T(8,128)(2,1)S(1)}, u32[]{:S(2)}, u32[]{:S(2)}) collective-permute-start(bf16[8,64,1024]{2,1,0:T(8,128)(2,1)S(1)} %pad_maximum_fusion.3.db0.b0), channel_id=1, source_target_pairs={{0,1},{1,0},{2,3},{3,2},{4,5},{5,4},{6,7},{7,6},{8,9},{9,8},{10,11... | collective-permute-start | bytes 3145736 | tf_op jit(solution)/shard_map/ppermute | solution.py:81
  192.6 53.8 %collective-permute-start.35 = (bf16[8,64,1024]{2,1,0:T(8,128)(2,1)}, bf16[8,64,1024]{2,1,0:T(8,128)(2,1)S(1)}, u32[]{:S(2)}, u32[]{:S(2)}) collective-permute-start(bf16[8,64,1024]{2,1,0:T(8,128)(2,1)} %get-tuple-element.373), channel_id=1, source_target_pairs={{0,4},{2,6},{4,0},{6,2},{8,12},{10,14},{12,8},{14,10},{16,20},{18,... | collective-permute-start | bytes 3145736 | tf_op jit(solution)/shard_map/ppermute | solution.py:81
  197.9 48.5 %collective-permute-start.36 = (bf16[8,64,1024]{2,1,0:T(8,128)(2,1)}, bf16[8,64,1024]{2,1,0:T(8,128)(2,1)}, u32[]{:S(2)}, u32[]{:S(2)}) collective-permute-start(bf16[8,64,1024]{2,1,0:T(8,128)(2,1)} %get-tuple-element.374), channel_id=1, source_target_pairs={{0,1},{1,0},{2,3},{3,2},{4,5},{5,4},{6,7},{7,6},{8,9},{9,8},{10,11... | collective-permute-start | bytes 3145736 | tf_op jit(solution)/shard_map/ppermute | solution.py:81
  248.4 14.3 %collective-permute-start.37 = (bf16[4,64,1024]{2,1,0:T(8,128)(2,1)S(1)}, bf16[4,64,1024]{2,1,0:T(8,128)(2,1)S(1)}, u32[]{:S(2)}, u32[]{:S(2)}) collective-permute-start(bf16[4,64,1024]{2,1,0:T(8,128)(2,1)S(1)} %get-tuple-element.385), channel_id=1, source_target_pairs={{0,1},{1,0},{2,3},{3,2},{4,5},{5,4},{6,7},{7,6},{8,9},{9,8},{10,11... | collective-permute-start | bytes 1572872 | tf_op jit(solution)/shard_map/ppermute | solution.py:81
  249.5 13.7 %collective-permute-start.38 = (bf16[4,64,1024]{2,1,0:T(8,128)(2,1)S(1)}, bf16[4,64,1024]{2,1,0:T(8,128)(2,1)S(1)}, u32[]{:S(2)}, u32[]{:S(2)}) collective-permute-start(bf16[4,64,1024]{2,1,0:T(8,128)(2,1)S(1)} %get-tuple-element.386), channel_id=1, source_target_pairs={{0,4},{2,6},{4,0},{6,2},{8,12},{10,14},{12,8},{14,10},{16,20},{18,... | collective-permute-start | bytes 1572872 | tf_op jit(solution)/shard_map/ppermute | solution.py:81
  263.6 14.4 %collective-permute-start.39 = (bf16[16,64,1024]{2,1,0:T(8,128)(2,1)S(1)}, bf16[16,64,1024]{2,1,0:T(8,128)(2,1)S(1)}, u32[]{:S(2)}, u32[]{:S(2)}) collective-permute-start(bf16[16,64,1024]{2,1,0:T(8,128)(2,1)S(1)} %get-tuple-element.397), channel_id=1, source_target_pairs={{0,2},{2,0},{4,6},{6,4},{8,10},{10,8},{12,14},{14,12},{16,18},{18,... | collective-permute-start | bytes 6291464 | tf_op jit(solution)/shard_map/ppermute | solution.py:81
  263.7 14.3 %collective-permute-start.40 = (bf16[2,64,2048]{2,1,0:T(8,128)(2,1)S(1)}, bf16[2,64,2048]{2,1,0:T(8,128)(2,1)S(1)}, u32[]{:S(2)}, u32[]{:S(2)}) collective-permute-start(bf16[2,64,2048]{2,1,0:T(8,128)(2,1)S(1)} %pad_maximum_fusion.9), channel_id=1, source_target_pairs={{0,8},{2,10},{4,12},{6,14},{8,0},{10,2},{12,4},{14,6},{16,24},{18,... | collective-permute-start | bytes 1572872 | tf_op jit(solution)/shard_map/ppermute | solution.py:81
  285.5 25.6 %collective-permute-start.42 = (bf16[8,64,1024]{2,1,0:T(8,128)(2,1)S(1)}, bf16[8,64,1024]{2,1,0:T(8,128)(2,1)S(1)}, u32[]{:S(2)}, u32[]{:S(2)}) collective-permute-start(bf16[8,64,1024]{2,1,0:T(8,128)(2,1)S(1)} %get-tuple-element.419), channel_id=1, source_target_pairs={{0,4},{2,6},{4,0},{6,2},{8,12},{10,14},{12,8},{14,10},{16,20},{18,... | collective-permute-start | bytes 3145736 | tf_op jit(solution)/shard_map/ppermute | solution.py:81
  286.7 25.3 %collective-permute-start.43 = (bf16[8,64,1024]{2,1,0:T(8,128)(2,1)S(1)}, bf16[8,64,1024]{2,1,0:T(8,128)(2,1)S(1)}, u32[]{:S(2)}, u32[]{:S(2)}) collective-permute-start(bf16[8,64,1024]{2,1,0:T(8,128)(2,1)S(1)} %get-tuple-element.420), channel_id=1, source_target_pairs={{0,1},{1,0},{2,3},{3,2},{4,5},{5,4},{6,7},{7,6},{8,9},{9,8},{10,11... | collective-permute-start | bytes 3145736 | tf_op jit(solution)/shard_map/ppermute | solution.py:81
  288.0 24.1 %collective-permute-start.44 = (bf16[16,64,512]{2,1,0:T(8,128)(2,1)S(1)}, bf16[16,64,512]{2,1,0:T(8,128)(2,1)S(1)}, u32[]{:S(2)}, u32[]{:S(2)}) collective-permute-start(bf16[16,64,512]{2,1,0:T(8,128)(2,1)S(1)} %get-tuple-element.421), channel_id=1, source_target_pairs={{0,2},{2,0},{4,6},{6,4},{8,10},{10,8},{12,14},{14,12},{16,18},{18,... | collective-permute-start | bytes 3145736 | tf_op jit(solution)/shard_map/ppermute | solution.py:81
  288.0 19.3 %collective-permute-start.45 = (bf16[1,64,2048]{2,1,0:T(8,128)(2,1)S(1)}, bf16[1,64,2048]{2,1,0:T(8,128)(2,1)S(1)}, u32[]{:S(2)}, u32[]{:S(2)}) collective-permute-start(bf16[1,64,2048]{2,1,0:T(8,128)(2,1)S(1)} %get-tuple-element.422), channel_id=1, source_target_pairs={{0,16},{2,18},{4,20},{6,22},{8,24},{10,26},{12,28},{14,30},{16,0},... | collective-permute-start | bytes 786440 | tf_op jit(solution)/shard_map/ppermute | solution.py:81
  312.9 20.0 %collective-permute-start.46 = (bf16[4,64,1024]{2,1,0:T(8,128)(2,1)S(1)}, bf16[4,64,1024]{2,1,0:T(8,128)(2,1)S(1)}, u32[]{:S(2)}, u32[]{:S(2)}) collective-permute-start(bf16[4,64,1024]{2,1,0:T(8,128)(2,1)S(1)} %get-tuple-element.427), channel_id=1, source_target_pairs={{0,1},{1,0},{2,3},{3,2},{4,5},{5,4},{6,7},{7,6},{8,9},{9,8},{10,11... | collective-permute-start | bytes 1572872 | tf_op jit(solution)/shard_map/ppermute | solution.py:81
  314.2 18.7 %collective-permute-start.47 = (bf16[4,64,1024]{2,1,0:T(8,128)(2,1)S(1)}, bf16[4,64,1024]{2,1,0:T(8,128)(2,1)S(1)}, u32[]{:S(2)}, u32[]{:S(2)}) collective-permute-start(bf16[4,64,1024]{2,1,0:T(8,128)(2,1)S(1)} %get-tuple-element.428), channel_id=1, source_target_pairs={{0,4},{2,6},{4,0},{6,2},{8,12},{10,14},{12,8},{14,10},{16,20},{18,... | collective-permute-start | bytes 1572872 | tf_op jit(solution)/shard_map/ppermute | solution.py:81
  334.2 12.9 %collective-permute-start.48 = (bf16[2,64,2048]{2,1,0:T(8,128)(2,1)}, bf16[2,64,2048]{2,1,0:T(8,128)(2,1)S(1)}, u32[]{:S(2)}, u32[]{:S(2)}) collective-permute-start(bf16[2,64,2048]{2,1,0:T(8,128)(2,1)} %pad_maximum_fusion.11), channel_id=1, source_target_pairs={{0,8},{2,10},{4,12},{6,14},{8,0},{10,2},{12,4},{14,6},{16,24},{18,... | collective-permute-start | bytes 1572872 | tf_op jit(solution)/shard_map/ppermute | solution.py:81
  334.8 12.7 %collective-permute-start.49 = (bf16[8,64,512]{2,1,0:T(8,128)(2,1)}, bf16[8,64,512]{2,1,0:T(8,128)(2,1)}, u32[]{:S(2)}, u32[]{:S(2)}) collective-permute-start(bf16[8,64,512]{2,1,0:T(8,128)(2,1)} %get-tuple-element.446), channel_id=1, source_target_pairs={{0,4},{2,6},{4,0},{6,2},{8,12},{10,14},{12,8},{14,10},{16,20},{18,... | collective-permute-start | bytes 1572872 | tf_op jit(solution)/shard_map/ppermute | solution.py:81
  349.6 23.3 %collective-permute-start.50 = (bf16[16,3,64,256]{3,2,1,0:T(8,128)(2,1)S(1)}, bf16[16,3,64,256]{3,2,1,0:T(8,128)(2,1)S(1)}, u32[]{:S(2)}, u32[]{:S(2)}) collective-permute-start(bf16[16,3,64,256]{3,2,1,0:T(8,128)(2,1)S(1)} %get-tuple-element.457), channel_id=1, source_target_pairs={{0,2},{2,0},{4,6},{6,4},{8,10},{10,8},{12,14},{14,12},{16,18},{18,... | collective-permute-start | bytes 4718600 | tf_op jit(solution)/shard_map/ppermute | solution.py:81
  349.6 23.3 %collective-permute-start.51 = (bf16[1,64,2048]{2,1,0:T(8,128)(2,1)S(1)}, bf16[1,64,2048]{2,1,0:T(8,128)(2,1)S(1)}, u32[]{:S(2)}, u32[]{:S(2)}) collective-permute-start(bf16[1,64,2048]{2,1,0:T(8,128)(2,1)S(1)} %get-tuple-element.458), channel_id=1, source_target_pairs={{0,16},{2,18},{4,20},{6,22},{8,24},{10,26},{12,28},{14,30},{16,0},... | collective-permute-start | bytes 786440 | tf_op jit(solution)/shard_map/ppermute | solution.py:81
  352.1 20.8 %collective-permute-start.52 = (bf16[4,64,512]{2,1,0:T(8,128)(2,1)S(1)}, bf16[4,64,512]{2,1,0:T(8,128)(2,1)S(1)}, u32[]{:S(2)}, u32[]{:S(2)}) collective-permute-start(bf16[4,64,512]{2,1,0:T(8,128)(2,1)S(1)} %get-tuple-element.459), channel_id=1, source_target_pairs={{0,1},{1,0},{2,3},{3,2},{4,5},{5,4},{6,7},{7,6},{8,9},{9,8},{10,11... | collective-permute-start | bytes 786440 | tf_op jit(solution)/shard_map/ppermute | solution.py:81
  353.4 19.5 %collective-permute-start.53 = (bf16[1,256,1024]{2,1,0:T(8,128)(2,1)S(1)}, bf16[1,256,1024]{2,1,0:T(8,128)(2,1)S(1)}, u32[]{:S(2)}, u32[]{:S(2)}) collective-permute-start(bf16[1,256,1024]{2,1,0:T(8,128)(2,1)S(1)} %get-tuple-element.463), channel_id=1, source_target_pairs={{0,1},{1,0},{2,3},{3,2},{4,5},{5,4},{6,7},{7,6},{8,9},{9,8},{10,11... | collective-permute-start | bytes 1572872 | tf_op jit(solution)/shard_map/ppermute | solution.py:81
  371.5 13.7 %collective-permute-start.55 = (bf16[1,256,1024]{2,1,0:T(8,128)(2,1)S(1)}, bf16[1,256,1024]{2,1,0:T(8,128)(2,1)}, u32[]{:S(2)}, u32[]{:S(2)}) collective-permute-start(bf16[1,256,1024]{2,1,0:T(8,128)(2,1)S(1)} %get-tuple-element.478), channel_id=1, source_target_pairs={{0,1},{1,0},{2,3},{3,2},{4,5},{5,4},{6,7},{7,6},{8,9},{9,8},{10,11... | collective-permute-start | bytes 1572872 | tf_op jit(solution)/shard_map/ppermute | solution.py:81
  373.8 11.2 %collective-permute-start.54 = (bf16[2,64,512]{2,1,0:T(8,128)(2,1)S(1)}, bf16[2,64,512]{2,1,0:T(8,128)(2,1)S(1)}, u32[]{:S(2)}, u32[]{:S(2)}) collective-permute-start(bf16[2,64,512]{2,1,0:T(8,128)(2,1)S(1)} %get-tuple-element.474), channel_id=1, source_target_pairs={{0,8},{2,10},{4,12},{6,14},{8,0},{10,2},{12,4},{14,6},{16,24},{18,... | collective-permute-start | bytes 393224 | tf_op jit(solution)/shard_map/ppermute | solution.py:81
  396.5 20.0 %collective-permute-start.57 = (bf16[8,3,64,256]{3,2,1,0:T(8,128)(2,1)S(1)}, bf16[8,3,64,256]{3,2,1,0:T(8,128)(2,1)S(1)}, u32[]{:S(2)}, u32[]{:S(2)}) collective-permute-start(bf16[8,3,64,256]{3,2,1,0:T(8,128)(2,1)S(1)} %get-tuple-element.497), channel_id=1, source_target_pairs={{0,4},{2,6},{4,0},{6,2},{8,12},{10,14},{12,8},{14,10},{16,20},{18,... | collective-permute-start | bytes 2359304 | tf_op jit(solution)/shard_map/ppermute | solution.py:81
  397.9 19.7 %collective-permute-start.58 = (bf16[8,3,64,256]{3,2,1,0:T(8,128)(2,1)S(1)}, bf16[8,3,64,256]{3,2,1,0:T(8,128)(2,1)S(1)}, u32[]{:S(2)}, u32[]{:S(2)}) collective-permute-start(bf16[8,3,64,256]{3,2,1,0:T(8,128)(2,1)S(1)} %get-tuple-element.498), channel_id=1, source_target_pairs={{0,1},{1,0},{2,3},{3,2},{4,5},{5,4},{6,7},{7,6},{8,9},{9,8},{10,11... | collective-permute-start | bytes 2359304 | tf_op jit(solution)/shard_map/ppermute | solution.py:81
  398.8 15.8 %collective-permute-start.59 = (bf16[1,64,512]{2,1,0:T(8,128)(2,1)S(1)}, bf16[1,64,512]{2,1,0:T(8,128)(2,1)S(1)}, u32[]{:S(2)}, u32[]{:S(2)}) collective-permute-start(bf16[1,64,512]{2,1,0:T(8,128)(2,1)S(1)} %get-tuple-element.499), channel_id=1, source_target_pairs={{0,16},{2,18},{4,20},{6,22},{8,24},{10,26},{12,28},{14,30},{16,0},... | collective-permute-start | bytes 196616 | tf_op jit(solution)/shard_map/ppermute | solution.py:81
  419.2 13.5 %collective-permute-start.60 = (bf16[4,3,64,256]{3,2,1,0:T(8,128)(2,1)S(1)}, bf16[4,3,64,256]{3,2,1,0:T(8,128)(2,1)S(1)}, u32[]{:S(2)}, u32[]{:S(2)}) collective-permute-start(bf16[4,3,64,256]{3,2,1,0:T(8,128)(2,1)S(1)} %get-tuple-element.509), channel_id=1, source_target_pairs={{0,1},{1,0},{2,3},{3,2},{4,5},{5,4},{6,7},{7,6},{8,9},{9,8},{10,11... | collective-permute-start | bytes 1179656 | tf_op jit(solution)/shard_map/ppermute | solution.py:81
  420.1 12.6 %collective-permute-start.61 = (bf16[4,3,64,256]{3,2,1,0:T(8,128)(2,1)S(1)}, bf16[4,3,64,256]{3,2,1,0:T(8,128)(2,1)S(1)}, u32[]{:S(2)}, u32[]{:S(2)}) collective-permute-start(bf16[4,3,64,256]{3,2,1,0:T(8,128)(2,1)S(1)} %get-tuple-element.510), channel_id=1, source_target_pairs={{0,4},{2,6},{4,0},{6,2},{8,12},{10,14},{12,8},{14,10},{16,20},{18,... | collective-permute-start | bytes 1179656 | tf_op jit(solution)/shard_map/ppermute | solution.py:81
  433.0 13.1 %collective-permute-start.66 = (bf16[2,3,64,512]{3,2,1,0:T(8,128)(2,1)S(1)}, bf16[2,3,64,512]{3,2,1,0:T(8,128)(2,1)S(1)}, u32[]{:S(2)}, u32[]{:S(2)}) collective-permute-start(bf16[2,3,64,512]{3,2,1,0:T(8,128)(2,1)S(1)} %pad_maximum_fusion.15), channel_id=1, source_target_pairs={{0,8},{2,10},{4,12},{6,14},{8,0},{10,2},{12,4},{14,6},{16,24},{18,... | collective-permute-start | bytes 1179656 | tf_op jit(solution)/shard_map/ppermute | solution.py:81
  439.8 20.3 %collective-permute-start.70 = (bf16[1,256,1024]{2,1,0:T(8,128)(2,1)}, bf16[1,256,1024]{2,1,0:T(8,128)(2,1)S(1)}, u32[]{:S(2)}, u32[]{:S(2)}) collective-permute-start(bf16[1,256,1024]{2,1,0:T(8,128)(2,1)} %get-tuple-element.523), channel_id=1, source_target_pairs={{0,1},{1,0},{2,3},{3,2},{4,5},{5,4},{6,7},{7,6},{8,9},{9,8},{10,11... | collective-permute-start | bytes 1572872 | tf_op jit(solution)/shard_map/ppermute | solution.py:81
  444.7 18.6 %collective-permute-start.71 = (bf16[1,256,1024]{2,1,0:T(8,128)(2,1)}, bf16[1,256,1024]{2,1,0:T(8,128)(2,1)S(1)}, u32[]{:S(2)}, u32[]{:S(2)}) collective-permute-start(bf16[1,256,1024]{2,1,0:T(8,128)(2,1)} %get-tuple-element.524), channel_id=1, source_target_pairs={{0,1},{1,0},{2,3},{3,2},{4,5},{5,4},{6,7},{7,6},{8,9},{9,8},{10,11... | collective-permute-start | bytes 1572872 | tf_op jit(solution)/shard_map/ppermute | solution.py:81
  (80 other events, 942.3 us)
